TPU v7x, 32 devices: a whole 2x2x4 slice. The times are simulated.
32 devices in a mesh: dp: 2 (over core), rows: 4 (over y, x), cols: 4 (over z).
Axes of the slice: x: 2, y: 2, z: 4, core: 2. Of those that a mesh axis runs over, the one named last changes fastest.
Arguments:
- tokens: bfloat16 [8192, 2048], P(('dp', 'rows', 'cols')), may hold values from -6 to 6
- attention_gain: float32 [2048], replicated, may hold values from 0.5 to 1.5
- mlp_gain: float32 [2048], replicated, may hold values from 0.5 to 1.5
- w_query: bfloat16 [2048, 2048], P('rows', 'cols'), may hold values from -0.25 to 0.25
- w_key: bfloat16 [2048, 256], P('rows'), may hold values from -0.125 to 0.125
- w_value: bfloat16 [2048, 256], P('rows'), may hold values from -0.125 to 0.125
- w_out: bfloat16 [2048, 2048], P(None, 'rows'), may hold values from -0.5 to 0.5
- w_gate: bfloat16 [2048, 5632], P('rows', 'cols'), may hold values from -0.125 to 0.125
- w_up: bfloat16 [2048, 5632], P('rows', 'cols'), may hold values from -0.125 to 0.125
- w_down: bfloat16 [5632, 2048], P('cols', 'rows'), may hold values from -0.078125 to 0.078125
- segment_ids: int32 [8, 1024], P(('dp', 'rows')), may hold values from 0 to 3, never falling along the last dimension, each value on 1 to 512 neighbouring positions
- skip_mask: int32 [8], P(('dp', 'rows')), may hold values 0 or 1
- cotangent: float32 [8192, 2048], P(('dp', 'rows', 'cols')), may hold values from -6 to 6
Outputs:
- output: bfloat16 [8192, 2048], P(('dp', 'rows', 'cols'))
- input_grad: float32 [8192, 2048], P(('dp', 'rows', 'cols'))
- attention_gain_grad: float32 [2048], replicated
- mlp_gain_grad: float32 [2048], replicated
- query_grad: float32 [2048, 2048], P(('dp', 'rows'), 'cols')
- key_grad: float32 [2048, 256], replicated
- value_grad: float32 [2048, 256], replicated
- out_grad: float32 [2048, 2048], P('cols', ('dp', 'rows'))
- gate_grad: float32 [2048, 5632], P(('dp', 'rows'), 'cols')
- up_grad: float32 [2048, 5632], P(('dp', 'rows'), 'cols')
- down_grad: float32 [5632, 2048], P('cols', ('dp', 'rows'))
Inputs may be any that keep to these rules, and one draw needn't show every extreme that they name: `segment_ids`: segment numbers never fall along a sequence of 1024 tokens; each sequence holds max(4, 4) documents, a document holds at most 512 tokens, and some document holds exactly that many.
All inputs are finite; a program needn't handle non-finite values. No bound on the sum of `skip_mask` on one device may be relied on, other than what follows from the above.
Results may differ from a plain program's by a relative error of at most 0.014.
Values may be sent and summed in bfloat16 or wider, within the bound.
No kernel may reach another device: no remote copies, remote signals or barrier semaphores. Data moves between devices by JAX's collectives and lax.ppermute only.
A program may use at most 320 MiB of HBM per device.

v0:
```python
import jax
import jax.numpy as jnp
from jax import lax
from jax.sharding import PartitionSpec as P

HEADS = 16
KV_HEADS = 2
HEAD_DIM = 128


epsilon = 1e-05
negative = -1e30
rope_base = 10000.0


def root_norm(values, gain_values):
    factor = lax.rsqrt(jnp.mean(values * values, axis=-1, keepdims=True) + epsilon)
    return values * factor * gain_values


def rotary(values, positions, direction):
    half_width = values.shape[-1] // 2
    frequency = rope_base ** (-2.0 * jnp.arange(half_width, dtype=jnp.float32) / values.shape[-1])
    angles = positions.astype(jnp.float32)[:, None] * frequency[None, :]
    cosine = jnp.cos(angles)[:, None, :]
    sine_part = direction * jnp.sin(angles)[:, None, :]
    leading = values[..., :half_width]
    trailing = values[..., half_width:]
    return jnp.concatenate(
        [leading * cosine - trailing * sine_part, trailing * cosine + leading * sine_part], axis=-1
    )


def matmul(left_side, right_side):
    return jnp.dot(left_side, right_side, preferred_element_type=jnp.float32)


def times_transposed(left_side, right_side):
    return lax.dot_general(
        left_side, right_side, (((1,), (1,)), ((), ())), preferred_element_type=jnp.float32
    )


def transposed_times(left_side, right_side):
    return lax.dot_general(
        left_side, right_side, (((0,), (0,)), ((), ())), preferred_element_type=jnp.float32
    )


def rows_from(source, start_row, row_count):
    return lax.dynamic_slice_in_dim(source, start_row, row_count, 0)


def take_block(source, sequence, start_row, row_count):
    return rows_from(lax.dynamic_index_in_dim(source, sequence, 0, False), start_row, row_count)


def block_scores(query_rows, key_rows, segments, sequence, start_row, row_count, score_scale):
    query_block = take_block(query_rows, sequence, start_row, row_count)
    sequence_keys = lax.dynamic_index_in_dim(key_rows, sequence, 0, False)
    sequence_ids = lax.dynamic_index_in_dim(segments, sequence, 0, False)
    block_ids = rows_from(sequence_ids, start_row, row_count)
    causal = (start_row + jnp.arange(row_count))[:, None] >= jnp.arange(sequence_ids.shape[0])[
        None, :
    ]
    allowed = (block_ids[:, None] == sequence_ids[None, :]) & causal
    scores = (
        jnp.einsum("bhe,ke->hbk", query_block, sequence_keys, preferred_element_type=jnp.float32)
        * score_scale
    )
    return (jnp.where(allowed[None], scores, negative), query_block, sequence_keys)


def attend_forward(query_rows, key_rows, value_rows, segments, score_scale):
    sequences, length = segments.shape
    block_rows = min(512, length)
    block_count = length // block_rows

    def attend_one_block(block_index):
        sequence = block_index // block_count
        start_row = block_index % block_count * block_rows
        scores, query_block, sequence_keys = block_scores(
            query_rows, key_rows, segments, sequence, start_row, block_rows, score_scale
        )
        sequence_values = lax.dynamic_index_in_dim(value_rows, sequence, 0, False)
        row_top = jnp.max(scores, axis=-1, keepdims=True)
        exponent = jnp.exp(scores - row_top)
        row_total = jnp.sum(exponent, axis=-1, keepdims=True)
        attend_weights = (exponent / row_total).astype(jnp.bfloat16)
        mixed_heads = jnp.einsum(
            "hbk,ke->bhe", attend_weights, sequence_values, preferred_element_type=jnp.float32
        )
        return (mixed_heads.astype(jnp.bfloat16), (row_top + jnp.log(row_total))[..., 0])

    return lax.map(attend_one_block, jnp.arange(sequences * block_count))


def attend_backward(
    query_rows, key_rows, value_rows, segments, log_totals, mixed_back, score_scale
):
    sequences, length = segments.shape
    block_rows = min(512, length)
    block_count = length // block_rows
    head_width = key_rows.shape[-1]

    def one_sequence(sequence):
        sequence_values = lax.dynamic_index_in_dim(value_rows, sequence, 0, False)

        def one_one_block(carried, block_number):
            key_sum, value_sum = carried
            start_row = block_number * block_rows
            scores, query_block, sequence_keys = block_scores(
                query_rows, key_rows, segments, sequence, start_row, block_rows, score_scale
            )
            block_totals = lax.dynamic_index_in_dim(
                log_totals, sequence * block_count + block_number, 0, False
            )
            probability = jnp.exp(scores - block_totals[..., None])
            attend_weights = probability.astype(jnp.bfloat16)
            back_block = take_block(mixed_back, sequence, start_row, block_rows)
            weight_back = jnp.einsum(
                "bhe,ke->hbk", back_block, sequence_values, preferred_element_type=jnp.float32
            )
            inner_sum = jnp.sum(weight_back * probability, axis=-1, keepdims=True)
            score_back = (probability * (weight_back - inner_sum)).astype(jnp.bfloat16)
            query_back = (
                jnp.einsum(
                    "hbk,ke->bhe", score_back, sequence_keys, preferred_element_type=jnp.float32
                )
                * score_scale
            )
            key_sum = (
                key_sum
                + jnp.einsum(
                    "hbk,bhe->ke", score_back, query_block, preferred_element_type=jnp.float32
                )
                * score_scale
            )
            value_sum = value_sum + jnp.einsum(
                "hbk,bhe->ke", attend_weights, back_block, preferred_element_type=jnp.float32
            )
            return ((key_sum, value_sum), query_back)

        zeros_rows = jnp.zeros((length, head_width), jnp.float32)
        (key_sum, value_sum), query_back = lax.scan(
            one_one_block, (zeros_rows, zeros_rows), jnp.arange(block_count)
        )
        return (query_back, key_sum, value_sum)

    return lax.map(one_sequence, jnp.arange(sequences))


def local(
    tokens,
    attention_gain,
    mlp_gain,
    w_query,
    w_key,
    w_value,
    w_out,
    w_gate,
    w_up,
    w_down,
    segment_ids,
    skip_mask,
    cotangent,
):
    column_index = lax.axis_index("cols")
    own_rows = tokens.shape[0]
    sequences, length = segment_ids.shape
    group_rows = sequences * length
    query_width = w_query.shape[1]
    local_heads = query_width // HEAD_DIM
    shared_head = column_index * local_heads // (HEADS // KV_HEADS)
    score_scale = HEAD_DIM ** (-0.5)
    positions = jnp.arange(group_rows) % length
    keep_group = jnp.repeat((1 - skip_mask).astype(jnp.float32), length)
    keep_own = rows_from(keep_group, column_index * own_rows, own_rows)[:, None]
    out_piece = rows_from(w_out, column_index * query_width, query_width)
    query_matrix, key_matrix, value_matrix, gate_matrix, up_matrix, out_matrix, down_matrix = (
        lax.all_gather(w_query, "rows", axis=0, tiled=True),
        lax.all_gather(w_key, "rows", axis=0, tiled=True),
        lax.all_gather(w_value, "rows", axis=0, tiled=True),
        lax.all_gather(w_gate, "rows", axis=0, tiled=True),
        lax.all_gather(w_up, "rows", axis=0, tiled=True),
        lax.all_gather(out_piece, "rows", axis=1, tiled=True),
        lax.all_gather(w_down, "rows", axis=1, tiled=True),
    )
    inputs = tokens.astype(jnp.float32)
    attention_normed, attention_pull = jax.vjp(root_norm, inputs, attention_gain)
    normed = attention_normed.astype(jnp.bfloat16)
    normed_group = lax.all_gather(normed, "cols", axis=0, tiled=True)
    query_pre = matmul(normed_group, query_matrix)
    query_rows = rotary(
        query_pre.reshape(group_rows, local_heads, HEAD_DIM), positions, 1.0
    ).astype(jnp.bfloat16)
    key_pre = matmul(
        normed_group, lax.dynamic_slice_in_dim(key_matrix, shared_head * HEAD_DIM, HEAD_DIM, 1)
    )
    value_rows = matmul(
        normed_group, lax.dynamic_slice_in_dim(value_matrix, shared_head * HEAD_DIM, HEAD_DIM, 1)
    ).astype(jnp.bfloat16)
    key_rows = (
        rotary(key_pre.reshape(group_rows, 1, HEAD_DIM), positions, 1.0)
        .reshape(group_rows, HEAD_DIM)
        .astype(jnp.bfloat16)
    )
    query_seqs = query_rows.reshape(sequences, length, local_heads, HEAD_DIM)
    key_seqs = key_rows.reshape(sequences, length, HEAD_DIM)
    value_seqs = value_rows.reshape(sequences, length, HEAD_DIM)
    mixed_blocks, log_totals = attend_forward(
        query_seqs, key_seqs, value_seqs, segment_ids, score_scale
    )
    mixed_group = mixed_blocks.reshape(group_rows, query_width)
    branch = lax.psum_scatter(
        matmul(rows_from(mixed_group, jnp.int32(0), lax.axis_size("cols") * own_rows), out_matrix),
        "cols",
        scatter_dimension=0,
        tiled=True,
    )
    middle = inputs + keep_own * branch
    hidden_normed, mlp_pull = jax.vjp(root_norm, middle, mlp_gain)
    hidden_in = hidden_normed.astype(jnp.bfloat16)
    hidden_group = lax.all_gather(hidden_in, "cols", axis=0, tiled=True)
    gate_values = matmul(hidden_group, gate_matrix)
    up_values = matmul(hidden_group, up_matrix)
    hidden = (jax.nn.silu(gate_values) * up_values).astype(jnp.bfloat16)
    feed_values = lax.psum_scatter(
        matmul(
            rows_from(hidden, jnp.int32(0), own_rows * lax.axis_size("cols")), down_matrix
        ).astype(jnp.bfloat16),
        "cols",
        scatter_dimension=0,
        tiled=True,
    ).astype(jnp.float32)
    output = (middle + keep_own * feed_values).astype(jnp.bfloat16)
    feed_back = (keep_own * cotangent).astype(jnp.bfloat16)
    feed_group = lax.all_gather(feed_back, "cols", axis=0, tiled=True)
    hidden_back = times_transposed(feed_group, down_matrix)
    down_grad = transposed_times(hidden, feed_group)
    sigmoid = jax.nn.sigmoid(gate_values)
    gate_back = (hidden_back * up_values * sigmoid * (1.0 + gate_values * (1.0 - sigmoid))).astype(
        jnp.bfloat16
    )
    up_back = (hidden_back * gate_values * sigmoid).astype(jnp.bfloat16)
    gate_grad = transposed_times(hidden_group, gate_back)
    up_grad = transposed_times(hidden_group, up_back)
    start_row = jnp.int32(0)
    gate_part = times_transposed(
        rows_from(gate_back, start_row, lax.axis_size("cols") * own_rows), gate_matrix
    )
    hidden_in_back = lax.psum_scatter(
        gate_part
        + times_transposed(
            rows_from(up_back, start_row, lax.axis_size("cols") * own_rows), up_matrix
        ),
        "cols",
        scatter_dimension=0,
        tiled=True,
    )
    middle_from_norm, mlp_gain_grad = mlp_pull(hidden_in_back)
    middle_grad = cotangent + middle_from_norm
    branch_back = (keep_own * middle_grad).astype(jnp.bfloat16)
    branch_group = lax.all_gather(branch_back, "cols", axis=0, tiled=True)
    mixed_back = times_transposed(branch_group, out_matrix).astype(jnp.bfloat16)
    out_grad = transposed_times(mixed_group, branch_group)
    query_back, key_back, value_back = attend_backward(
        query_seqs,
        key_seqs,
        value_seqs,
        segment_ids,
        log_totals,
        mixed_back.reshape(sequences, length, local_heads, HEAD_DIM),
        score_scale,
    )
    query_pre_back = (
        rotary(query_back.reshape(group_rows, local_heads, HEAD_DIM), positions, -1.0)
        .reshape(group_rows, query_width)
        .astype(jnp.bfloat16)
    )
    key_pre_back = rotary(key_back.reshape(group_rows, 1, HEAD_DIM), positions, -1.0).reshape(
        group_rows, HEAD_DIM
    )
    head_select = (jnp.arange(KV_HEADS) == shared_head).astype(jnp.float32)[None, :, None]
    key_spread = (head_select * key_pre_back[:, None, :]).reshape(group_rows, KV_HEADS * HEAD_DIM)
    value_spread = (head_select * value_back.reshape(group_rows, HEAD_DIM)[:, None, :]).reshape(
        group_rows, KV_HEADS * HEAD_DIM
    )
    model_width = query_matrix.shape[0]
    shared_width = KV_HEADS * HEAD_DIM
    query_grad = transposed_times(normed_group, query_pre_back)
    start_row = jnp.int32(0)
    query_part = times_transposed(
        rows_from(query_pre_back, start_row, lax.axis_size("cols") * own_rows), query_matrix
    )
    normed_share = lax.psum_scatter(
        jnp.concatenate(
            [
                query_part,
                rows_from(key_spread, start_row, lax.axis_size("cols") * own_rows),
                rows_from(value_spread, start_row, lax.axis_size("cols") * own_rows),
            ],
            axis=1,
        ),
        "cols",
        scatter_dimension=0,
        tiled=True,
    )
    query_normed = normed_share[:, :model_width]
    key_share = normed_share[:, model_width : model_width + shared_width].astype(jnp.bfloat16)
    value_share = normed_share[:, model_width + shared_width :].astype(jnp.bfloat16)
    normed_back = (
        query_normed
        + times_transposed(key_share, key_matrix)
        + times_transposed(value_share, value_matrix)
    )
    input_from_norm, attention_gain_grad = attention_pull(normed_back)
    input_grad = middle_grad + input_from_norm
    key_part = transposed_times(normed, key_share)
    value_part = transposed_times(normed, value_share)
    key_grad, value_grad, attention_total, mlp_total = lax.psum(
        (key_part, value_part, attention_gain_grad, mlp_gain_grad), ("dp", "rows", "cols")
    )
    query_sum, gate_sum, up_sum, out_sum, down_sum = (
        lax.psum_scatter(query_grad, ("dp", "rows"), scatter_dimension=0, tiled=True),
        lax.psum_scatter(gate_grad, ("dp", "rows"), scatter_dimension=0, tiled=True),
        lax.psum_scatter(up_grad, ("dp", "rows"), scatter_dimension=0, tiled=True),
        lax.psum_scatter(out_grad, ("dp", "rows"), scatter_dimension=1, tiled=True),
        lax.psum_scatter(down_grad, ("dp", "rows"), scatter_dimension=1, tiled=True),
    )
    return (
        output,
        input_grad,
        attention_total,
        mlp_total,
        query_sum,
        key_grad,
        value_grad,
        out_sum,
        gate_sum,
        up_sum,
        down_sum,
    )


def solution(mesh):
    return jax.shard_map(
        local,
        mesh=mesh,
        in_specs=(
            P(("dp", "rows", "cols"), None),
            P(),
            P(),
            P("rows", "cols"),
            P("rows", None),
            P("rows", None),
            P(None, "rows"),
            P("rows", "cols"),
            P("rows", "cols"),
            P("cols", "rows"),
            P(("dp", "rows"), None),
            P(("dp", "rows")),
            P(("dp", "rows", "cols"), None),
        ),
        out_specs=(
            P(("dp", "rows", "cols"), None),
            P(("dp", "rows", "cols"), None),
            P(),
            P(),
            P(("dp", "rows"), "cols"),
            P(),
            P(),
            P("cols", ("dp", "rows")),
            P(("dp", "rows"), "cols"),
            P(("dp", "rows"), "cols"),
            P("cols", ("dp", "rows")),
        ),
        check_vma=False,
    )
```

profile of v0, /device:TPU:11, one launch (start us, length us, event | category | flops | bytes accessed | tf_op | source)
XLA Modules:
  0.0 1893.6 jit_solution(18043483729602340258)
XLA Ops:
  18.6 19.0 %all-gather.16.cloned.1.call-done = bf16[2048,256]{1,0:T(8,128)(2,1)} async-done(((bf16[512,256]{1,0:T(8,128)(2,1)}), bf16[2048,256]{1,0:T(8,128)(2,1)}) %all-gather.16.cloned.1.call-update) | async-done | bytes 1048592 | tf_op jit(solution)/shard_map/all_gather | solution.py:182
  37.7 80.5 %all-gather.12.cloned.1.call-done = bf16[1024,2048]{1,0:T(8,128)(2,1)} async-done(((bf16[256,2048]{1,0:T(8,128)(2,1)}), bf16[1024,2048]{1,0:T(8,128)(2,1)}) %all-gather.12.cloned.1.call-update) | async-done | bytes 4194320 | tf_op jit(solution)/shard_map/all_gather | solution.py:192
  118.2 3.8 convolution_bitcast_fusion.1
  123.4 33.0 %all-gather.14.cloned.1.call-done = bf16[2048,512]{1,0:T(8,128)(2,1)} async-done(((bf16[512,512]{1,0:T(8,128)(2,1)}), bf16[2048,512]{1,0:T(8,128)(2,1)}) %all-gather.14.cloned.1.call-update) | async-done | bytes 2097168 | tf_op jit(solution)/shard_map/all_gather | solution.py:181
  156.3 5.2 fusion.101
  169.1 15.5 all-gather.18.cloned.1.call-done
  188.3 22.3 %while.43 = (s32[]{:T(128)}, bf16[2,512,4,128]{3,2,1,0:T(4,128)(2,1)S(1)}, f32[2,4,512]{2,1,0:T(4,128)S(1)}, s32[2]{0:T(128)S(1)}, s32[1,1024]{1,0:T(1,128)S(1)}...) while((s32[]{:T(128)}, ...), condition=%wide.region_4.5_spmd, body=%wide.region_1.4_spmd.sunk | while | flops 1100741120 | bytes 29964600 | solution.py:95
  210.6 11.5 all-gather.20.cloned.1.call-done
  222.1 7.2 fusion.64
  230.8 142.9 %reduce-scatter.10.cloned.1.call-done = f32[256,2048]{1,0:T(8,128)} async-done(((f32[1024,2048]{1,0:T(8,128)}), f32[256,2048]{1,0:T(8,128)}) %reduce-scatter.10.cloned.1.call-update) | async-done | bytes 2097168 | tf_op jit(solution)/shard_map/reduce_scatter | solution.py:215
  382.7 59.8 %all-gather.24.cloned.1.call-done = bf16[2048,1408]{1,0:T(8,128)(2,1)} async-done(((bf16[512,1408]{1,0:T(8,128)(2,1)}), bf16[2048,1408]{1,0:T(8,128)(2,1)}) %all-gather.24.cloned.1.call-update) | async-done | bytes 5767184 | tf_op jit(solution)/shard_map/all_gather | solution.py:184
  442.4 80.5 %all-gather.22.cloned.1.call-done = bf16[1024,2048]{1,0:T(8,128)(2,1)} async-done(((bf16[256,2048]{1,0:T(8,128)(2,1)}), bf16[1024,2048]{1,0:T(8,128)(2,1)}) %all-gather.22.cloned.1.call-update) | async-done | bytes 4194320 | tf_op jit(solution)/shard_map/all_gather | solution.py:224
  522.9 12.1 fusion.102
  535.1 56.5 %all-gather.26.cloned.1.call-done = bf16[2048,1408]{1,0:T(8,128)(2,1)} async-done(((bf16[512,1408]{1,0:T(8,128)(2,1)}), bf16[2048,1408]{1,0:T(8,128)(2,1)}) %all-gather.26.cloned.1.call-update) | async-done | bytes 5767184 | tf_op jit(solution)/shard_map/all_gather | solution.py:185
  591.6 11.7 fusion.103
  603.3 68.7 %all-gather.30.cloned.1.call-done = bf16[1024,2048]{1,0:T(8,128)(2,1)} async-done(((bf16[256,2048]{1,0:T(8,128)(2,1)}), bf16[1024,2048]{1,0:T(8,128)(2,1)}) %all-gather.30.cloned.1.call-update) | async-done | bytes 4194320 | tf_op jit(solution)/shard_map/all_gather | solution.py:238
  671.9 68.5 %all-gather.28.cloned.1.call-done = bf16[1408,2048]{1,0:T(8,128)(2,1)} async-done(((bf16[1408,512]{1,0:T(8,128)(2,1)}), bf16[1408,2048]{1,0:T(8,128)(2,1)}) %all-gather.28.cloned.1.call-update) | async-done | bytes 5767184 | tf_op jit(solution)/shard_map/all_gather | solution.py:187
  740.4 15.7 multiply_convert_fusion
  756.1 10.9 fusion.104
  767.0 9.0 convolution_add_fusion
  776.1 11.1 convolution_convert_fusion
  787.2 133.2 %reduce-scatter.14.cloned.1.call-done = f32[256,2048]{1,0:T(8,128)} async-done(((f32[1024,2048]{1,0:T(8,128)}), f32[256,2048]{1,0:T(8,128)}) %reduce-scatter.14.cloned.1.call-update) | async-done | bytes 2097168 | tf_op jit(solution)/shard_map/reduce_scatter | solution.py:252
  923.8 76.8 %reduce-scatter.12.cloned.1.call-done = bf16[256,2048]{1,0:T(8,128)(2,1)} async-done(((bf16[1024,2048]{1,0:T(8,128)(2,1)}), bf16[256,2048]{1,0:T(8,128)(2,1)}) %reduce-scatter.12.cloned.1.call-update) | async-done | bytes 1048592 | tf_op jit(solution)/shard_map/reduce_scatter | solution.py:228
  1000.6 6.1 multiply_convert_fusion.3
  1006.8 78.8 %all-gather.32.cloned.1.call-done = bf16[1024,2048]{1,0:T(8,128)(2,1)} async-done(((bf16[256,2048]{1,0:T(8,128)(2,1)}), bf16[1024,2048]{1,0:T(8,128)(2,1)}) %all-gather.32.cloned.1.call-update) | async-done | bytes 4194320 | tf_op jit(solution)/shard_map/all_gather | solution.py:264
  1085.6 6.2 convolution_convert_fusion.1
  1091.8 62.6 %while.44 = (s32[]{:T(128)}, f32[1024,128]{1,0:T(8,128)S(1)}, f32[1024,128]{1,0:T(8,128)}, f32[2,512,4,128]{3,1,0,2:T(8,128)}, s32[2]{0:T(128)S(1)}, /*index=5*/...) while((s32[]{:T(128)}, f32[1024,128]{1,0:T(8,128)S(1)}, ...), condition=%wide.region_12.13_spmd.clone, body=%wide.region_10.12_spmd.clone.sunk | while | flops 2718300672 | bytes 117250952 | solution.py:145
  1093.5 4.6 fusion.177
  1099.8 6.1 fusion.179
  1116.3 6.7 fusion.182
  1124.8 4.6 fusion.177
  1131.0 6.1 fusion.179
  1147.6 6.8 fusion.182
  1166.2 4.2 pad_maximum_fusion
  1170.5 11.9 fusion.107
  1182.4 11.9 fusion.108
  1194.4 11.7 fusion.109
  1206.2 6.6 fusion.106
  1214.1 6.5 fusion.62
  1220.7 129.0 %reduce-scatter.16.cloned.1.call-done = f32[256,2560]{1,0:T(8,128)} async-done(((f32[1024,2560]{1,0:T(8,128)}), f32[256,2560]{1,0:T(8,128)}) %reduce-scatter.16.cloned.1.call-update) | async-done | bytes 2621456 | tf_op jit(solution)/shard_map/reduce_scatter | solution.py:296
  1360.8 40.3 %all-reduce = (f32[2048]{0:T(1024)}, f32[2048]{0:T(1024)}) all-reduce(f32[2048]{0:T(1024)S(1)} %get-tuple-element.400, f32[2048]{0:T(1024)S(1)} %copy-done.23), channel_id=1, replica_groups=mesh['dp'=2,'rows'=4,'cols'=4] {'dp','rows','cols'}, use_global_device_ids=true, to_apply=%region_16.17 | all-reduce | flops 4096 | bytes 32768 | tf_op jit(solution)/shard_map/psum | solution.py:321
  1401.1 4.5 fusion.57
  1405.6 36.7 %reduce-scatter.22.cloned.1.call-done = f32[256,1408]{1,0:T(8,128)} async-done(((f32[2048,1408]{1,0:T(8,128)}), f32[256,1408]{1,0:T(8,128)}) %reduce-scatter.22.cloned.1.call-update) | async-done | bytes 1441808 | tf_op jit(solution)/shard_map/reduce_scatter | solution.py:326
  1442.3 91.1 %reduce-scatter.24.cloned.1.call-done = f32[256,1408]{1,0:T(8,128)} async-done(((f32[2048,1408]{1,0:T(8,128)}), f32[256,1408]{1,0:T(8,128)}) %reduce-scatter.24.cloned.1.call-update) | async-done | bytes 1441808 | tf_op jit(solution)/shard_map/reduce_scatter | solution.py:327
  1533.4 91.1 %reduce-scatter.26.cloned.1.call-done = f32[1408,256]{1,0:T(8,128)} async-done(((f32[1408,2048]{1,0:T(8,128)}), f32[1408,256]{1,0:T(8,128)}) %reduce-scatter.26.cloned.1.call-update) | async-done | bytes 1441808 | tf_op jit(solution)/shard_map/reduce_scatter | solution.py:329
  1624.6 55.7 %reduce-scatter.18.cloned.1.call-done = f32[256,512]{1,0:T(8,128)} async-done(((f32[2048,512]{1,0:T(8,128)}), f32[256,512]{1,0:T(8,128)}) %reduce-scatter.18.cloned.1.call-update) | async-done | bytes 524304 | tf_op jit(solution)/shard_map/reduce_scatter | solution.py:325
  1680.3 55.1 %reduce-scatter.20.cloned.1.call-done = f32[512,256]{1,0:T(8,128)} async-done(((f32[512,2048]{1,0:T(8,128)}), f32[512,256]{1,0:T(8,128)}) %reduce-scatter.20.cloned.1.call-update) | async-done | bytes 524304 | tf_op jit(solution)/shard_map/reduce_scatter | solution.py:328
  1735.4 146.6 %all-reduce.4.cloned.1.call-done = (f32[2048,256]{1,0:T(8,128)}, f32[2048,256]{1,0:T(8,128)}) async-done(((f32[2048,256]{1,0:T(8,128)}, f32[2048,256]{1,0:T(8,128)}), (f32[2048,256]{1,0:T(8,128)}, f32[2048,256]{1,0:T(8,128)})) %all-reduce.4.cloned.1.call-update) | async-done | bytes 4194320 | tf_op jit(solution)/shard_map/psum | solution.py:321
  (208 shorter events, 107.2 us)
Async XLA Ops:
  7.2 7.4 copy-start
  7.2 30.5 %all-gather.16.cloned.1.call-start = ((), (), s32[]{:S(2)}) async-start(), calls=%async_computation.11 | async-start | bytes 1310720 | tf_op jit(solution)/shard_map/all_gather | solution.py:182
  7.9 110.2 %all-gather.12.cloned.1.call-start = ((), (), s32[]{:S(2)}) async-start(), calls=%async_computation.9 | async-start | bytes 5242880 | tf_op jit(solution)/shard_map/all_gather | solution.py:192
  13.2 143.1 %all-gather.14.cloned.1.call-start = ((), (), s32[]{:S(2)}) async-start(), calls=%async_computation.10 | async-start | bytes 2621440 | tf_op jit(solution)/shard_map/all_gather | solution.py:181
  13.9 170.8 %all-gather.18.cloned.1.call-start = ((), (), s32[]{:S(2)}) async-start(), calls=%async_computation.12 | async-start | bytes 1310720 | tf_op jit(solution)/shard_map/all_gather | solution.py:183
  14.5 207.6 %all-gather.20.cloned.1.call-start = ((), (), s32[]{:S(2)}) async-start(), calls=%async_computation.13 | async-start | bytes 2621440 | tf_op jit(solution)/shard_map/all_gather | solution.py:186
  15.4 358.4 %reduce-scatter.10.cloned.1.call-start = ((), (), s32[]{:S(2)}) async-start(), calls=%async_computation.14 | async-start | bytes 10485760 | tf_op jit(solution)/shard_map/reduce_scatter | solution.py:215
  15.5 106.5 %copy-start.21 = (f32[1024]{0:T(1024)}, f32[1024]{0:T(1024)S(1)}, u32[]{:S(2)}) copy-start(f32[1024]{0:T(1024)S(1)} %fusion.91) | copy-start | bytes 12292
  15.5 106.5 %copy-start.28 = (f32[64]{0:T(128)}, f32[64]{0:T(128)S(1)}, u32[]{:S(2)}) copy-start(f32[64]{0:T(128)S(1)} %multiply_power_fusion) | copy-start | bytes 772
  18.6 147.0 %copy-start.8 = (f32[1024,64]{1,0:T(8,128)}, f32[1024,64]{1,0:T(8,128)S(1)}, u32[]{:S(2)}) copy-start(f32[1024,64]{1,0:T(8,128)S(1)} %get-tuple-element.468) | copy-start | bytes 786436
  169.1 19.1 %copy-start.11 = (bf16[2,512,4,128]{3,2,1,0:T(4,128)(2,1)S(1)}, bf16[2,512,4,128]{3,2,1,0:T(4,128)(2,1)}, u32[]{:S(2)}) copy-start(bf16[2,512,4,128]{3,2,1,0:T(4,128)(2,1)} %custom-call.2) | copy-start | bytes 3145732
  169.1 19.1 %copy-start.18 = (s32[1,1024]{1,0:T(1,128)S(1)}, s32[1,1024]{1,0:T(1,128)}, u32[]{:S(2)}) copy-start(s32[1,1024]{1,0:T(1,128)} %param.27) | copy-start | bytes 12292
  210.6 18.7 copy-start.12
  229.4 144.4 %copy-start.4 = (bf16[256,2048]{1,0:T(8,128)(2,1)S(1)}, bf16[256,2048]{1,0:T(8,128)(2,1)}, u32[]{:S(2)}) copy-start(bf16[256,2048]{1,0:T(8,128)(2,1)} %param.17) | copy-start | bytes 3145732
  229.4 213.1 %all-gather.24.cloned.1.call-start = ((), (), s32[]{:S(2)}) async-start(), calls=%async_computation.16 | async-start | bytes 7208960 | tf_op jit(solution)/shard_map/all_gather | solution.py:184
  230.1 147.0 %copy-start.20 = (f32[2048]{0:T(1024)S(1)}, f32[2048]{0:T(1024)}, u32[]{:S(2)}) copy-start(f32[2048]{0:T(1024)} %param.19) | copy-start | bytes 24580
  230.1 292.8 %all-gather.22.cloned.1.call-start = ((), (), s32[]{:S(2)}) async-start(), calls=%async_computation.15 | async-start | bytes 5242880 | tf_op jit(solution)/shard_map/all_gather | solution.py:224
  378.4 213.2 %all-gather.26.cloned.1.call-start = ((), (), s32[]{:S(2)}) async-start(), calls=%async_computation.17 | async-start | bytes 7208960 | tf_op jit(solution)/shard_map/all_gather | solution.py:185
  379.1 292.8 %all-gather.30.cloned.1.call-start = ((), (), s32[]{:S(2)}) async-start(), calls=%async_computation.20 | async-start | bytes 5242880 | tf_op jit(solution)/shard_map/all_gather | solution.py:238
  381.9 358.5 %all-gather.28.cloned.1.call-start = ((), (), s32[]{:S(2)}) async-start(), calls=%async_computation.18 | async-start | bytes 7208960 | tf_op jit(solution)/shard_map/all_gather | solution.py:187
  382.6 537.8 %reduce-scatter.14.cloned.1.call-start = ((), (), s32[]{:S(2)}) async-start(), calls=%async_computation.21 | async-start | bytes 10485760 | tf_op jit(solution)/shard_map/reduce_scatter | solution.py:252
  756.1 10.9 copy-start.33
  756.1 10.9 copy-start.32
  756.1 10.9 copy-start.30
  776.0 224.5 %reduce-scatter.12.cloned.1.call-start = ((), (), s32[]{:S(2)}) async-start(), calls=%async_computation.19 | async-start | bytes 5242880 | tf_op jit(solution)/shard_map/reduce_scatter | solution.py:228
  787.2 298.4 %all-gather.32.cloned.1.call-start = ((), (), s32[]{:S(2)}) async-start(), calls=%async_computation.22 | async-start | bytes 5242880 | tf_op jit(solution)/shard_map/all_gather | solution.py:264
  1006.7 343.0 %reduce-scatter.16.cloned.1.call-start = ((), (), s32[]{:S(2)}) async-start(), calls=%async_computation.23 | async-start | bytes 13107200 | tf_op jit(solution)/shard_map/reduce_scatter | solution.py:296
  1091.8 62.6 %copy-start.9 = (f32[1024,64]{1,0:T(8,128)S(1)}, f32[1024,64]{1,0:T(8,128)}, u32[]{:S(2)}) copy-start(f32[1024,64]{1,0:T(8,128)} %copy-done.8) | copy-start | bytes 786436
  1099.8 6.1 slice-start
  1099.8 6.1 slice-start.1
  1112.6 3.7 copy-start.7
  1131.0 6.1 slice-start
  1131.0 6.1 slice-start.1
  1143.8 3.7 copy-start.7
  1170.4 271.9 %reduce-scatter.22.cloned.1.call-start = ((), (), s32[]{:S(2)}) async-start(), calls=%async_computation.26 | async-start | bytes 12976128 | tf_op jit(solution)/shard_map/reduce_scatter | solution.py:326
  1182.4 351.1 %reduce-scatter.24.cloned.1.call-start = ((), (), s32[]{:S(2)}) async-start(), calls=%async_computation.27 | async-start | bytes 12976128 | tf_op jit(solution)/shard_map/reduce_scatter | solution.py:327
  1194.4 430.2 %reduce-scatter.26.cloned.1.call-start = ((), (), s32[]{:S(2)}) async-start(), calls=%async_computation.28 | async-start | bytes 12976128 | tf_op jit(solution)/shard_map/reduce_scatter | solution.py:329
  1206.1 474.1 %reduce-scatter.18.cloned.1.call-start = ((), (), s32[]{:S(2)}) async-start(), calls=%async_computation.24 | async-start | bytes 4718592 | tf_op jit(solution)/shard_map/reduce_scatter | solution.py:325
  1212.8 522.5 %reduce-scatter.20.cloned.1.call-start = ((), (), s32[]{:S(2)}) async-start(), calls=%async_computation.25 | async-start | bytes 4718592 | tf_op jit(solution)/shard_map/reduce_scatter | solution.py:328
  1220.6 130.9 %copy-start.6 = (bf16[256,2048]{1,0:T(8,128)(2,1)S(1)}, bf16[256,2048]{1,0:T(8,128)(2,1)}, u32[]{:S(2)}) copy-start(bf16[256,2048]{1,0:T(8,128)(2,1)} %fusion.54) | copy-start | bytes 3145732
  1220.6 661.4 %all-reduce.4.cloned.1.call-start = ((), (), s32[]{:S(2)}) async-start(), calls=%async_computation.29 | async-start | bytes 8388608 | tf_op jit(solution)/shard_map/psum | solution.py:321
  1356.4 2.2 copy-start.5
  1356.4 2.2 copy-start.17
  1356.4 2.2 copy-start.19
  1356.4 2.2 copy-start.25
  1358.7 42.5 %copy-start.27 = (f32[256]{0:T(256)S(1)}, f32[256]{0:T(256)}, u32[]{:S(2)}) copy-start(f32[256]{0:T(256)} %copy-done.26) | copy-start | bytes 3076
  1882.0 3.2 copy-start.15
  1882.0 4.5 copy-start.1
  (13 other events, 21.3 us)
Sparse Core Ops, SparseCore 0:
  9.9 27.7 all-gather.15
  39.8 78.3 all-gather.11
  120.0 36.2 all-gather.13
  158.0 26.6 all-gather.17
  186.9 35.1 all-gather.19
  229.5 144.2 reduce-scatter.9
  375.6 66.7 all-gather.23
  444.6 78.3 all-gather.21
  524.8 66.7 all-gather.25
  593.6 78.3 all-gather.29
  673.8 66.5 all-gather.27
  776.1 144.2 reduce-scatter.13
  922.7 77.7 reduce-scatter.11
  1006.8 78.7 all-gather.31
  1170.6 179.0 reduce-scatter.15
  1354.0 88.3 reduce-scatter.21
  1446.7 86.7 reduce-scatter.23
  1537.8 86.7 reduce-scatter.25
  1628.9 51.3 reduce-scatter.17
  1684.1 51.2 reduce-scatter.19
  1742.1 139.8 all-reduce.3
where the time goes:
time: 1900 us; the launch traced here: 1890 us
  waiting for transfers between devices  1530 us (81%)
  matrix products  212 us (11%)
  other arithmetic  55.2 us (3%)
  blocking collectives  40.3 us (2%)
  local copies, waits for them, and re-layouts  26 us (1%)
    psum x1, waiting for transfers between devices, local(): lax.psum((key_part, value_part, attention_gain_grad, mlp_gain_grad), ('dp...  147 us
    reduce_scatter x1, waiting for transfers between devices, local(): lax.psum_scatter(matmul(rows_from(mixed_group, jnp.int32(0), lax.axis_siz...  143 us
    reduce_scatter x1, waiting for transfers between devices, local(): lax.psum_scatter(gate_part + times_transposed(rows_from(up_back, start_ro...  133 us
    reduce_scatter x1, waiting for transfers between devices, local(): lax.psum_scatter(jnp.concatenate([query_part, rows_from(key_spread, start...  129 us
    reduce_scatter x1, waiting for transfers between devices, local(): lax.psum_scatter(down_grad, ('dp', 'rows'), scatter_dimension=1, tiled=True)  91.1 us
    reduce_scatter x1, waiting for transfers between devices, local(): lax.psum_scatter(up_grad, ('dp', 'rows'), scatter_dimension=0, tiled=True)  91.1 us
    all_gather x1, waiting for transfers between devices, local(): normed_group = lax.all_gather(normed, 'cols', axis=0, tiled=True)  80.5 us
    all_gather x1, waiting for transfers between devices, local(): hidden_group = lax.all_gather(hidden_in, 'cols', axis=0, tiled=True)  80.5 us
  transfers between devices with their start and end apart: 21, of which 21 were waited for; matrix products, arithmetic and copies ran while one was open for 8% of the time, Pallas kernels for 0%

commit v1 on v0

v1 whole, which is shorter than its diff:
```python
import jax
import jax.numpy as jnp
from jax import lax
from jax.sharding import PartitionSpec as P

HEADS = 16
KV_HEADS = 2
HEAD_DIM = 128

epsilon = 1e-05
negative = -1e30
rope_base = 10000.0
bf16 = jnp.bfloat16
f32 = jnp.float32


def dot(left, right, dims):
    return lax.dot_general(left, right, ((dims[:1], dims[1:]), ((), ())), preferred_element_type=f32)


def nn(left, right):
    return dot(left, right, (1, 0))


def nt(left, right):
    return dot(left, right, (1, 1))


def tn(left, right):
    return dot(left, right, (0, 0))


def after(value, *earlier):
    return lax.optimization_barrier((value,) + earlier)[0]


def xor_blocks(blocks, index):
    bit = 1
    while bit < len(blocks):
        swap = (index & bit) != 0
        blocks = [jnp.where(swap, blocks[j ^ bit], blocks[j]) for j in range(len(blocks))]
        bit *= 2
    return blocks


def xor_order(value, index, count, axis):
    return jnp.concatenate(xor_blocks(jnp.split(value, count, axis), index), axis)


def rotary_tables(positions):
    half = HEAD_DIM // 2
    frequency = rope_base ** (-2.0 * jnp.arange(half, dtype=f32) / HEAD_DIM)
    angles = positions.astype(f32)[:, None] * frequency[None, :]
    return jnp.cos(angles)[:, None, :], jnp.sin(angles)[:, None, :]


def rotate(values, cosine, sine, direction):
    heads = values.reshape(values.shape[0], -1, HEAD_DIM)
    half = HEAD_DIM // 2
    a, b = heads[..., :half], heads[..., half:]
    s = sine * direction
    turned = jnp.concatenate([a * cosine - b * s, b * cosine + a * s], axis=-1)
    return turned.reshape(values.shape)


def norm_factor(values):
    return lax.rsqrt(jnp.mean(values * values, axis=-1, keepdims=True) + epsilon)


def norm_back(grad, values, factor, gain):
    y = grad * gain
    pulled = factor * y - values * factor**3 * jnp.mean(y * values, axis=-1, keepdims=True)
    return pulled, jnp.sum(grad * values * factor, axis=0)


def local(
    tokens,
    attention_gain,
    mlp_gain,
    w_query,
    w_key,
    w_value,
    w_out,
    w_gate,
    w_up,
    w_down,
    segment_ids,
    skip_mask,
    cotangent,
):
    cols, rows = lax.axis_size("cols"), lax.axis_size("rows")
    c, r, d = lax.axis_index("cols"), lax.axis_index("rows"), lax.axis_index("dp")
    own, width = tokens.shape
    sequences, length = segment_ids.shape
    place = 2 * r + d
    blocks = 2 * rows
    step = width // blocks
    scale = HEAD_DIM ** (-0.5)

    def to_rows(value, a):
        return lax.ppermute(value, "rows", [(i, i ^ a) for i in range(rows)])

    def to_core(value):
        return lax.ppermute(value, "dp", [(0, 1), (1, 0)])

    def to_cols(value, k):
        return lax.ppermute(value, "cols", [(i, (i + k) % cols) for i in range(cols)])

    def along(value, k):
        return lax.ppermute(
            value, "cols", [(i, i + k) for i in range(cols) if 0 <= i + k < cols]
        )

    def to_xor_cols(value, k):
        return lax.ppermute(value, "cols", [(i, i ^ k) for i in range(cols)])

    def fetch_rows(piece, first):
        if rows != 4:
            return [piece] + [to_rows(piece, a) for a in range(1, rows)]
        other = 3 - first
        near = to_rows(piece, first)
        far = to_rows(piece, other)
        both = to_rows(near, other)
        got = [piece, None, None, both]
        got[first], got[other] = near, far
        return got

    def with_core(got, own_other):
        pairs = []
        for j, piece in enumerate(got):
            pairs += [piece, own_other if j == 0 else to_core(piece)]
        return pairs

    def halves(weight, axis):
        low, high = jnp.split(weight, 2, axis)
        return jnp.where(d == 0, low, high), jnp.where(d == 0, high, low)

    inputs = xor_order(tokens, place, blocks, 1).astype(f32)
    upstream = xor_order(cotangent, place, blocks, 1)
    gain_one = xor_order(attention_gain, place, blocks, 0)
    gain_two = xor_order(mlp_gain, place, blocks, 0)
    sequence = (c * own) // length
    start = (c * own) % length
    keep = (1 - lax.dynamic_index_in_dim(skip_mask, sequence, 0, False)).astype(f32)
    feed_own = (keep * upstream).astype(bf16)

    kv_mine, kv_other = halves(jnp.concatenate([w_key, w_value], 1), 0)
    kv_got = fetch_rows(kv_mine, 1)
    kv_matrix = jnp.concatenate(with_core(kv_got, kv_other), 0)
    q_mine, _ = halves(w_query, 0)
    q_parts = [q_mine] + [to_xor_cols(q_mine, k) for k in range(1, cols)]
    q_mine = jnp.concatenate(xor_blocks(q_parts, c), 1)
    q_lo, q_hi = jnp.split(q_mine, 2, 0)
    q_lo_got = fetch_rows(after(q_lo, kv_got[1]), 1)
    q_hi_got = fetch_rows(after(q_hi, kv_got[1]), 2)
    q_got = [jnp.concatenate([lo, hi], 0) for lo, hi in zip(q_lo_got, q_hi_got)]
    q_pairs = []
    for piece in q_got:
        q_pairs += [piece, to_core(piece)]
    q_matrix = jnp.concatenate(q_pairs, 0)
    o_mine, o_other = halves(w_out, 1)
    o_mine = after(o_mine, q_lo_got[1], q_hi_got[2])
    o_lo, o_hi = jnp.split(o_mine, 2, 0)
    o_lo_got, o_hi_got = fetch_rows(o_lo, 1), fetch_rows(o_hi, 2)
    o_got = [jnp.concatenate([lo, hi], 0) for lo, hi in zip(o_lo_got, o_hi_got)]
    o_matrix = jnp.concatenate(with_core(o_got, o_other), 1)

    g_mine, g_other = halves(w_gate, 0)
    u_mine, u_other = halves(w_up, 0)
    g_got = fetch_rows(after(g_mine, o_lo_got[1], o_hi_got[2]), 1)
    u_got = fetch_rows(after(u_mine, o_lo_got[1], o_hi_got[2]), 2)
    g_matrix = jnp.concatenate(with_core(g_got, g_other), 0)
    u_matrix = jnp.concatenate(with_core(u_got, u_other), 0)
    w_mine, w_other = halves(w_down, 1)
    w_mine = after(w_mine, g_got[1], u_got[2])
    w_lo, w_hi = jnp.split(w_mine, 2, 0)
    w_lo_got, w_hi_got = fetch_rows(w_lo, 1), fetch_rows(w_hi, 2)
    w_got = [jnp.concatenate([lo, hi], 0) for lo, hi in zip(w_lo_got, w_hi_got)]
    d_matrix = jnp.concatenate(with_core(w_got, w_other), 1)

    factor_one = norm_factor(inputs)
    normed = (inputs * factor_one * gain_one).astype(bf16)
    cosine, sine = rotary_tables(start + jnp.arange(own))
    kv_pre = nn(normed, kv_matrix)
    kv_width = KV_HEADS * HEAD_DIM
    kv_own = jnp.concatenate(
        [rotate(kv_pre[:, :kv_width], cosine, sine, 1.0), kv_pre[:, kv_width:]], 1
    ).astype(bf16)
    reach = min(-(-(length // 2 - 1) // own), length // own - 1)
    kv_before = [along(kv_own, k) for k in range(reach, 0, -1)]
    kv_all = jnp.concatenate(kv_before + [kv_own], 0)
    span = (reach + 1) * own
    q_rows = rotate(nn(normed, q_matrix), cosine, sine, 1.0).astype(bf16)

    feeds = [after(feed_own, q_parts[1])]
    for k in range(1, cols):
        feeds.append(to_cols(feeds[-1], 1))

    ids = lax.dynamic_index_in_dim(segment_ids, sequence, 0, False)
    ids_padded = jnp.concatenate([jnp.full((reach * own,), -1, ids.dtype), ids])
    ids_keys = lax.dynamic_slice_in_dim(ids_padded, start, span, 0)
    ids_rows = ids_keys[reach * own :]
    allowed = (ids_rows[:, None] == ids_keys[None, :]) & (
        (reach * own + jnp.arange(own))[:, None] >= jnp.arange(span)[None, :]
    )
    share = HEADS // KV_HEADS
    q_heads = q_rows.reshape(own, KV_HEADS, share, HEAD_DIM)
    k_heads = kv_all[:, :kv_width].reshape(span, KV_HEADS, HEAD_DIM)
    v_heads = kv_all[:, kv_width:].reshape(span, KV_HEADS, HEAD_DIM)

    def ein(form, a, b):
        return jnp.einsum(form, a, b, preferred_element_type=f32)

    scores = ein("bghe,kge->ghbk", q_heads, k_heads) * scale
    scores = jnp.where(allowed[None, None], scores, negative)
    top = jnp.max(scores, -1, keepdims=True)
    exponent = jnp.exp(scores - top)
    probs = exponent / jnp.sum(exponent, -1, keepdims=True)
    attend = probs.astype(bf16)
    mixed = ein("ghbk,kge->bghe", attend, v_heads).reshape(own, width).astype(bf16)
    branch = nn(mixed, o_matrix)
    middle = inputs + keep * branch
    factor_two = norm_factor(middle)
    hidden_own = (middle * factor_two * gain_two).astype(bf16)

    chunks = [hidden_own]
    for k in range(1, cols):
        chunks.append(to_cols(chunks[-1], 1))
    hiddens, gate_backs, up_backs, feed_parts, in_parts = {}, {}, {}, {}, {}
    carry_in = None
    for k in list(range(1, cols)) + [0]:
        gate = nn(chunks[k], g_matrix)
        up = nn(chunks[k], u_matrix)
        back = nt(feeds[k], d_matrix)
        s = jax.nn.sigmoid(gate)
        hiddens[k] = (gate * s * up).astype(bf16)
        gate_backs[k] = (back * up * s * (1.0 + gate * (1.0 - s))).astype(bf16)
        up_backs[k] = (back * gate * s).astype(bf16)
        part = nt(gate_backs[k], g_matrix) + nt(up_backs[k], u_matrix)
        if carry_in is not None:
            part = part + carry_in.astype(f32)
        if k != 0:
            carry_in = to_cols(part.astype(bf16), 1)
        else:
            hidden_in_back = part
    order = list(range(cols))
    h_all = jnp.concatenate([chunks[k] for k in order], 0)
    f_all = jnp.concatenate([feeds[k] for k in order], 0)
    hid_all = jnp.concatenate([hiddens[k] for k in order], 0)
    gb_all = jnp.concatenate([gate_backs[k] for k in order], 0)
    ub_all = jnp.concatenate([up_backs[k] for k in order], 0)
    down_part = tn(hid_all, f_all).astype(bf16)
    gate_part = tn(h_all, gb_all).astype(bf16)
    up_part = tn(h_all, ub_all).astype(bf16)

    from_norm, mlp_gain_part = norm_back(hidden_in_back, middle, factor_two, gain_two)
    middle_grad = upstream + from_norm
    branch_back = (keep * middle_grad).astype(bf16)
    mixed_back = nt(branch_back, o_matrix).astype(bf16)
    out_part = tn(mixed, branch_back).astype(bf16)

    carry_out = None
    for k in list(range(1, cols)) + [0]:
        part = nn(after(hiddens[k], hidden_in_back), d_matrix)
        if carry_out is not None:
            part = part + carry_out.astype(f32)
        if k != 0:
            carry_out = to_cols(part.astype(bf16), 1)
    feed_values = part
    output = (middle + keep * feed_values).astype(bf16)

    mb_heads = mixed_back.reshape(own, KV_HEADS, share, HEAD_DIM)
    weight_back = ein("bghe,kge->ghbk", mb_heads, v_heads)
    inner = jnp.sum(weight_back * probs, -1, keepdims=True)
    score_back = (probs * (weight_back - inner)).astype(bf16)
    q_turned = ein("ghbk,kge->bghe", score_back, k_heads).reshape(own, width) * scale
    k_turned = ein("ghbk,bghe->kge", score_back, q_heads).reshape(span, kv_width) * scale
    v_turned = ein("ghbk,bghe->kge", attend, mb_heads).reshape(span, kv_width)
    kv_turned = jnp.concatenate([k_turned, v_turned], 1)
    kv_back_pre = kv_turned[reach * own :]
    for k in range(1, reach + 1):
        part = kv_turned[(reach - k) * own : (reach - k + 1) * own].astype(bf16)
        kv_back_pre = kv_back_pre + along(part, -k).astype(f32)
    q_back = rotate(q_turned, cosine, sine, -1.0).astype(bf16)
    kv_back = jnp.concatenate(
        [rotate(kv_back_pre[:, :kv_width], cosine, sine, -1.0), kv_back_pre[:, kv_width:]], 1
    ).astype(bf16)
    q_part = tn(normed, q_back).astype(bf16)
    normed_back = nt(q_back, q_matrix) + nt(kv_back, kv_matrix)
    from_norm, attention_gain_part = norm_back(normed_back, inputs, factor_one, gain_one)
    input_grad = xor_order(middle_grad + from_norm, place, blocks, 1)
    kv_part = tn(normed, kv_back).astype(bf16)

    def scatter(part, axis, first):
        parts = xor_blocks(jnp.split(part, blocks, axis), place ^ (d * rows + r))
        keep_half = jnp.concatenate(parts[:rows], axis)
        send_half = jnp.concatenate(parts[rows:], axis)
        half = keep_half.astype(f32) + to_core(send_half).astype(f32)
        pieces = jnp.split(half, rows, axis)
        if rows != 4:
            total = pieces[0]
            for a in range(1, rows):
                total = total + to_rows(pieces[a].astype(bf16), a).astype(f32)
            return total
        other = 3 - first
        near = to_rows(jnp.concatenate([pieces[first], pieces[3]], axis).astype(bf16), first)
        near = jnp.split(near, 2, axis)
        mine = pieces[0] + near[0].astype(f32)
        theirs = pieces[other] + near[1].astype(f32)
        return mine + to_rows(theirs.astype(bf16), other).astype(f32)

    gate_grad = scatter(gate_part, 0, 1)
    up_grad = scatter(up_part, 0, 2)
    down_lo, down_hi = jnp.split(down_part, 2, 0)
    down_grad = jnp.concatenate([scatter(down_lo, 1, 1), scatter(down_hi, 1, 2)], 0)

    def scatter_cols(total, axis):
        pieces = xor_blocks(jnp.split(total.astype(bf16), cols, axis), c)
        result = pieces[0].astype(f32)
        for k in range(1, cols):
            result = result + to_xor_cols(pieces[k], k).astype(f32)
        return result

    out_lo, out_hi = jnp.split(out_part, 2, 0)
    out_sum = jnp.concatenate([scatter(out_lo, 1, 1), scatter(out_hi, 1, 2)], 0)
    out_grad = scatter_cols(out_sum, 0)
    q_lo, q_hi = jnp.split(q_part, 2, 1)
    q_sum = jnp.concatenate([scatter(q_lo, 0, 1), scatter(q_hi, 0, 2)], 1)
    query_grad = scatter_cols(q_sum, 1)

    kv_sum = scatter(kv_part, 0, 1).astype(bf16)
    total = kv_sum.astype(f32)
    for k in range(1, cols):
        total = total + to_xor_cols(kv_sum, k).astype(f32)
    total = total.astype(bf16)
    found = fetch_rows(total, 1)
    found = found + [to_core(x) for x in found]
    found = jnp.concatenate(xor_blocks(found, d * rows + r), 0).astype(f32)
    key_grad, value_grad = found[:, :kv_width], found[:, kv_width:]

    gains = jnp.stack([attention_gain_part, mlp_gain_part])
    gains = lax.psum(xor_order(gains, place, blocks, 1), ("dp", "rows", "cols"))
    return (
        xor_order(output, place, blocks, 1),
        input_grad,
        gains[0],
        gains[1],
        query_grad,
        key_grad,
        value_grad,
        out_grad,
        gate_grad,
        up_grad,
        down_grad,
    )


def solution(mesh):
    return jax.shard_map(
        local,
        mesh=mesh,
        in_specs=(
            P(("dp", "rows", "cols"), None),
            P(),
            P(),
            P("rows", "cols"),
            P("rows", None),
            P("rows", None),
            P(None, "rows"),
            P("rows", "cols"),
            P("rows", "cols"),
            P("cols", "rows"),
            P(("dp", "rows"), None),
            P(("dp", "rows")),
            P(("dp", "rows", "cols"), None),
        ),
        out_specs=(
            P(("dp", "rows", "cols"), None),
            P(("dp", "rows", "cols"), None),
            P(),
            P(),
            P(("dp", "rows"), "cols"),
            P(),
            P(),
            P("cols", ("dp", "rows")),
            P(("dp", "rows"), "cols"),
            P(("dp", "rows"), "cols"),
            P("cols", ("dp", "rows")),
        ),
        check_vma=False,
    )
```

time: 1900 us -> 922 us (0.49)
  waiting for transfers between devices: 1530 us -> 288 us
  starting transfers between devices: 0.85 us -> 132 us
  other arithmetic: 55.2 us -> 159 us
  local copies, waits for them, and re-layouts: 26 us -> 109 us
  matrix products: 212 us -> 174 us
    reduce_scatter x9 -> x0, waiting for transfers between devices: 812 us -> none  [the longest x1 143 us: local(): lax.psum_scatter(matmul(rows_from(mixed_group, jnp.int32(0), lax.axis_siz...]
    all_gather x11 -> x0, waiting for transfers between devices: 572 us -> none  [the longest x1 80.5 us: local(): normed_group = lax.all_gather(normed, 'cols', axis=0, tiled=True)]
    ppermute x0 -> x108, waiting for transfers between devices: none -> 288 us  [the longest x48 176 us: to_rows(): return lax.ppermute(value, 'rows', [(i, i ^ a) for i in range(rows)])]
    psum x1 -> x0, waiting for transfers between devices: 147 us -> none  [local(): lax.psum((key_part, value_part, attention_gain_grad, mlp_gain_grad), ('dp...]
    ppermute x0 -> x108, starting transfers between devices: none -> 132 us  [the longest x32 37.2 us: to_core(): return lax.ppermute(value, 'dp', [(0, 1), (1, 0)])]
    unnamed x68 -> x413, local copies, waits for them, and re-layouts: 13.7 us -> 74.4 us
    dot_general x35 -> x41, matrix products: 212 us -> 164 us  [the longest x36 149 us: dot(): lax.dot_general(left, right, ((dims[:1], dims[1:]), ((), ())), preferred_...]
    select_n x0 -> x34, other arithmetic: none -> 36.8 us  [the longest x30 34.6 us: xor_blocks(): jnp.where(swap, blocks[j ^ bit], blocks[j])]
  transfers between devices with their start and end apart: 21 -> 108, of which waited for: 21 -> 38; matrix products, arithmetic and copies ran while one was open for 8% -> 46% of each run, Pallas kernels for 0% -> 0%
where the time goes in v1:
time: 922 us; the launch traced here: 907 us
  waiting for transfers between devices  288 us (31%)
  matrix products  174 us (19%)
  other arithmetic  159 us (17%)
  starting transfers between devices  132 us (14%)
  local copies, waits for them, and re-layouts  109 us (12%)
  blocking collectives  40 us (4%)
    ppermute x48, waiting for transfers between devices, to_rows(): return lax.ppermute(value, 'rows', [(i, i ^ a) for i in range(rows)])  176 us
    dot_general x36, matrix products, dot(): lax.dot_general(left, right, ((dims[:1], dims[1:]), ((), ())), preferred_...  149 us
    unnamed x413, local copies, waits for them, and re-layouts  74.4 us
    ppermute x12, waiting for transfers between devices, to_xor_cols(): return lax.ppermute(value, 'cols', [(i, i ^ k) for i in range(cols)])  59.7 us
    ppermute x12, waiting for transfers between devices, to_cols(): lax.ppermute(value, 'cols', [(i, (i + k) % cols) for i in range(cols)])  50.7 us
    psum x1, blocking collectives, local(): gains = lax.psum(xor_order(gains, place, blocks, 1), ('dp', 'rows', 'cols'))  40 us
    ppermute x32, starting transfers between devices, to_core(): return lax.ppermute(value, 'dp', [(0, 1), (1, 0)])  37.2 us
    ppermute x48, starting transfers between devices, to_rows(): return lax.ppermute(value, 'rows', [(i, i ^ a) for i in range(rows)])  34.7 us
  transfers between devices with their start and end apart: 108, of which 38 were waited for; matrix products, arithmetic and copies ran while one was open for 46% of the time, Pallas kernels for 0%

profile of v1, /device:TPU:11, one launch (start us, length us, event | category | flops | bytes accessed | tf_op | source)
XLA Modules:
  0.0 906.8 jit_solution(14802513030163577752)
XLA Ops:
  54.3 13.8 %collective-permute-done.16 = bf16[128,2048]{1,0:T(8,128)(2,1)} collective-permute-done((bf16[128,2048]{1,0:T(8,128)(2,1)}, bf16[128,2048]{1,0:T(8,128)(2,1)}, u32[]{:S(2)}, u32[]{:S(2)}) %collective-permute-start.16) | collective-permute-done | bytes 524320 | tf_op jit(solution)/shard_map/ppermute | solution.py:101
  68.1 5.0 collective-permute-start.6
  136.9 13.6 %collective-permute-done.28 = bf16[1024,256]{1,0:T(8,128)(2,1)S(1)} collective-permute-done((bf16[1024,256]{1,0:T(8,128)(2,1)}, bf16[1024,256]{1,0:T(8,128)(2,1)S(1)}, u32[]{:S(2)}, u32[]{:S(2)}) %collective-permute-start.28) | collective-permute-done | bytes 524320 | tf_op jit(solution)/shard_map/ppermute | solution.py:101
  157.2 8.9 collective-permute-done.36
  166.1 11.5 %collective-permute-start.52 = (bf16[256,2048]{1,0:T(8,128)(2,1)}, bf16[256,2048]{1,0:T(8,128)(2,1)}, u32[]{:S(2)}, u32[]{:S(2)}) collective-permute-start(bf16[256,2048]{1,0:T(8,128)(2,1)} %collective-permute-done.51), channel_id=1, source_target_pairs={{0,1},{1,2},{2,3},{3,0},{4,5},{5,6},{6,7},{7,4},{8,9},{9,10},{10,1... | collective-permute-start | bytes 3145736 | tf_op jit(solution)/shard_map/ppermute | solution.py:107
  182.7 5.7 convolution_bitcast_fusion
  191.4 10.4 %fusion.144 = (f32[2,8,256]{2,1,0:T(8,128)}, f32[2,8,256,768]{2,3,1,0:T(8,128)}) fusion(pred[256,768]{0,1:T(8,128)(4,1)} %fusion.85, bf16[768,2,128,1]{0,2,3,1:T(8,128)(2,1)S(1)} %copy-done.88, bf16[256,2,8,128]{3,0,2,1:T(8,128)(2,1)} %bitcast.160), kind=kOutput, calls=%fused_computation.794 | convolution fusion | flops 817890048 | bytes 14237696 | tf_op jit(solution)/shard_map/sub | solution.py:217
  201.9 8.6 fusion.121
  210.5 9.0 copy.51
  265.7 12.2 %collective-permute-done.40 = bf16[256,1408]{1,0:T(8,128)(2,1)S(1)} collective-permute-done((bf16[256,1408]{1,0:T(8,128)(2,1)S(1)}, bf16[256,1408]{1,0:T(8,128)(2,1)S(1)}, u32[]{:S(2)}, u32[]{:S(2)}) %collective-permute-start.40) | collective-permute-done | bytes 720928 | tf_op jit(solution)/shard_map/ppermute | solution.py:101
  285.0 5.9 multiply_reduce_fusion.2
  301.1 5.9 multiply_convert_fusion.13
  329.4 4.5 fusion.41
  337.1 7.1 collective-permute-done.55
  354.8 11.9 %collective-permute-done.57 = bf16[256,2048]{1,0:T(8,128)(2,1)S(1)} collective-permute-done((bf16[256,2048]{1,0:T(8,128)(2,1)S(1)}, bf16[256,2048]{1,0:T(8,128)(2,1)S(1)}, u32[]{:S(2)}, u32[]{:S(2)}) %collective-permute-start.57) | collective-permute-done | bytes 1048608 | tf_op jit(solution)/shard_map/ppermute | solution.py:107
  366.7 4.6 fusion.45
  372.8 16.3 %collective-permute-done.56 = bf16[256,2048]{1,0:T(8,128)(2,1)S(1)} collective-permute-done((bf16[256,2048]{1,0:T(8,128)(2,1)S(1)}, bf16[256,2048]{1,0:T(8,128)(2,1)S(1)}, u32[]{:S(2)}, u32[]{:S(2)}) %collective-permute-start.56) | collective-permute-done | bytes 1048608 | tf_op jit(solution)/shard_map/ppermute | solution.py:107
  389.1 4.8 fusion.149
  399.0 12.7 %collective-permute-done.58 = bf16[256,2048]{1,0:T(8,128)(2,1)S(1)} collective-permute-done((bf16[256,2048]{1,0:T(8,128)(2,1)S(1)}, bf16[256,2048]{1,0:T(8,128)(2,1)S(1)}, u32[]{:S(2)}, u32[]{:S(2)}) %collective-permute-start.58) | collective-permute-done | bytes 1048608 | tf_op jit(solution)/shard_map/ppermute | solution.py:107
  411.6 5.6 fusion.46
  418.4 8.3 convolution_convert_fusion.2
  431.0 5.9 pad_maximum_fusion.1
  438.4 8.3 convolution_convert_fusion.1
  450.8 6.2 pad_maximum_fusion.2
  457.1 8.1 convolution_convert_fusion
  474.1 5.6 multiply_reduce_fusion
  480.4 6.8 fusion.63
  488.3 5.9 fusion.1
  494.2 6.2 fusion.3
  513.9 7.2 fusion.66
  583.4 40.0 %psum.7 = f32[2,2048]{1,0:T(2,128)S(1)} all-reduce(f32[2,2048]{1,0:T(2,128)S(1)} %constant_dynamic-update-slice_fusion.67), channel_id=1, replica_groups=mesh['dp'=2,'rows'=4,'cols'=4] {'dp','rows','cols'}, use_global_device_ids=true, to_apply=%region_9.10 | all-reduce | flops 4096 | bytes 32768 | tf_op jit(solution)/shard_map/psum | solution.py:342
  639.4 10.0 %collective-permute-done.106 = bf16[704,512]{1,0:T(8,128)(2,1)S(1)} collective-permute-done((bf16[704,512]{1,0:T(8,128)(2,1)S(1)}, bf16[704,512]{1,0:T(8,128)(2,1)S(1)}, u32[]{:S(2)}, u32[]{:S(2)}) %collective-permute-start.106) | collective-permute-done | bytes 720928 | tf_op jit(solution)/shard_map/ppermute | solution.py:101
  653.9 6.6 collective-permute-done.107
  666.0 6.2 fusion.122
  672.6 7.0 convert_add_fusion
  679.9 5.8 collective-permute-done.75
  690.9 5.7 fusion.42
  717.5 26.3 %collective-permute-done.79 = bf16[256,512]{1,0:T(8,128)(2,1)} collective-permute-done((bf16[256,512]{1,0:T(8,128)(2,1)}, bf16[256,512]{1,0:T(8,128)(2,1)}, u32[]{:S(2)}, u32[]{:S(2)}) %collective-permute-start.79) | collective-permute-done | bytes 262176 | tf_op jit(solution)/shard_map/ppermute | solution.py:115
  748.5 4.8 fusion.44
  754.1 11.7 %collective-permute-done.66 = bf16[512,1024]{1,0:T(8,128)(2,1)S(1)} collective-permute-done((bf16[512,1024]{1,0:T(8,128)(2,1)S(1)}, bf16[512,1024]{1,0:T(8,128)(2,1)S(1)}, u32[]{:S(2)}, u32[]{:S(2)}) %collective-permute-start.66) | collective-permute-done | bytes 1048608 | tf_op jit(solution)/shard_map/ppermute | solution.py:101
  766.2 22.1 %collective-permute-done.88 = bf16[1024,512]{0,1:T(8,128)(2,1)S(1)} collective-permute-done((bf16[1024,512]{0,1:T(8,128)(2,1)}, bf16[1024,512]{0,1:T(8,128)(2,1)S(1)}, u32[]{:S(2)}, u32[]{:S(2)}) %collective-permute-start.88) | collective-permute-done | bytes 1048608 | tf_op jit(solution)/shard_map/ppermute | solution.py:101
  788.5 7.8 collective-permute-done.80
  801.0 6.5 collective-permute-done.81
  816.7 24.5 %collective-permute-done.100 = bf16[512,1408]{1,0:T(8,128)(2,1)S(1)} collective-permute-done((bf16[512,1408]{1,0:T(8,128)(2,1)S(1)}, bf16[512,1408]{1,0:T(8,128)(2,1)S(1)}, u32[]{:S(2)}, u32[]{:S(2)}) %collective-permute-start.100) | collective-permute-done | bytes 1441824 | tf_op jit(solution)/shard_map/ppermute | solution.py:101
  844.0 8.6 collective-permute-done.70
  863.7 4.8 collective-permute-start.71
  873.8 11.8 %collective-permute-done.72 = bf16[256,512]{1,0:T(8,128)(2,1)S(1)} collective-permute-done((bf16[256,512]{1,0:T(8,128)(2,1)S(1)}, bf16[256,512]{1,0:T(8,128)(2,1)S(1)}, u32[]{:S(2)}, u32[]{:S(2)}) %collective-permute-start.72) | collective-permute-done | bytes 262176 | tf_op jit(solution)/shard_map/ppermute | solution.py:115
  893.0 6.7 collective-permute-done.94
  (859 shorter events, 439.2 us)
Async XLA Ops:
  3.7 27.6 %collective-permute-start = (bf16[256,512]{1,0:T(8,128)(2,1)}, bf16[256,512]{1,0:T(8,128)(2,1)}, u32[]{:S(2)}, u32[]{:S(2)}) collective-permute-start(bf16[256,512]{1,0:T(8,128)(2,1)} %get-tuple-element.217), channel_id=1, source_target_pairs={{0,4},{4,0},{8,12},{12,8},{1,5},{5,1},{9,13},{13,9},{2,6},{6,2},{1... | collective-permute-start | bytes 786440 | tf_op jit(solution)/shard_map/ppermute | solution.py:101
  4.0 36.1 %collective-permute-start.2 = (bf16[256,512]{1,0:T(8,128)(2,1)}, bf16[256,512]{1,0:T(8,128)(2,1)}, u32[]{:S(2)}, u32[]{:S(2)}) collective-permute-start(bf16[256,512]{1,0:T(8,128)(2,1)} %get-tuple-element.217), channel_id=1, source_target_pairs={{0,8},{4,12},{8,0},{12,4},{1,9},{5,13},{9,1},{13,5},{2,10},{6,14},... | collective-permute-start | bytes 786440 | tf_op jit(solution)/shard_map/ppermute | solution.py:101
  34.5 42.0 %collective-permute-start.13 = (bf16[128,2048]{1,0:T(8,128)(2,1)}, bf16[128,2048]{1,0:T(8,128)(2,1)}, u32[]{:S(2)}, u32[]{:S(2)}) collective-permute-start(bf16[128,2048]{1,0:T(8,128)(2,1)} %get-tuple-element.23), channel_id=1, source_target_pairs={{0,4},{4,0},{8,12},{12,8},{1,5},{5,1},{9,13},{13,9},{2,6},{6,2},{1... | collective-permute-start | bytes 1572872 | tf_op jit(solution)/shard_map/ppermute | solution.py:101
  43.2 36.9 %collective-permute-start.15 = (bf16[128,2048]{1,0:T(8,128)(2,1)}, bf16[128,2048]{1,0:T(8,128)(2,1)}, u32[]{:S(2)}, u32[]{:S(2)}) collective-permute-start(bf16[128,2048]{1,0:T(8,128)(2,1)} %get-tuple-element.22), channel_id=1, source_target_pairs={{0,8},{4,12},{8,0},{12,4},{1,9},{5,13},{9,1},{13,5},{2,10},{6,14},... | collective-permute-start | bytes 1572872 | tf_op jit(solution)/shard_map/ppermute | solution.py:101
  47.8 56.9 %collective-permute-start.11 = (bf16[256,2048]{1,0:T(8,128)(2,1)}, bf16[256,2048]{1,0:T(8,128)(2,1)}, u32[]{:S(2)}, u32[]{:S(2)}) collective-permute-start(bf16[256,2048]{1,0:T(8,128)(2,1)} %pad_maximum_fusion.13), channel_id=1, source_target_pairs={{0,16},{16,0},{1,17},{17,1},{2,18},{18,2},{3,19},{19,3},{4,20},{20... | collective-permute-start | bytes 3145736 | tf_op jit(solution)/shard_map/ppermute | solution.py:104
  52.2 31.3 %collective-permute-start.7 = (bf16[256,512]{1,0:T(8,128)(2,1)S(1)}, bf16[256,512]{1,0:T(8,128)(2,1)S(1)}, u32[]{:S(2)}, u32[]{:S(2)}) collective-permute-start(bf16[256,512]{1,0:T(8,128)(2,1)S(1)} %pad_maximum_fusion.32), channel_id=1, source_target_pairs={{0,1},{1,2},{2,3},{4,5},{5,6},{6,7},{8,9},{9,10},{10,11},{12,13},{... | collective-permute-start | bytes 786440 | tf_op jit(solution)/shard_map/ppermute | solution.py:110
  83.6 73.3 %collective-permute-start.51 = (bf16[256,2048]{1,0:T(8,128)(2,1)}, bf16[256,2048]{1,0:T(8,128)(2,1)}, u32[]{:S(2)}, u32[]{:S(2)}) collective-permute-start(bf16[256,2048]{1,0:T(8,128)(2,1)} %multiply_convert_fusion.1), channel_id=1, source_target_pairs={{0,1},{1,2},{2,3},{3,0},{4,5},{5,6},{6,7},{7,4},{8,9},{9,10},{10,1... | collective-permute-start | bytes 3145736 | tf_op jit(solution)/shard_map/ppermute | solution.py:107
  92.2 32.3 %collective-permute-start.14 = (bf16[256,2048]{1,0:T(8,128)(2,1)}, bf16[256,2048]{1,0:T(8,128)(2,1)S(1)}, u32[]{:S(2)}, u32[]{:S(2)}) collective-permute-start(bf16[256,2048]{1,0:T(8,128)(2,1)} %pad_maximum_fusion.14), channel_id=1, source_target_pairs={{0,16},{16,0},{1,17},{17,1},{2,18},{18,2},{3,19},{19,3},{4,20},{20... | collective-permute-start | bytes 3145736 | tf_op jit(solution)/shard_map/ppermute | solution.py:104
  100.2 30.4 %collective-permute-start.17 = (bf16[256,2048]{1,0:T(8,128)(2,1)S(1)}, bf16[256,2048]{1,0:T(8,128)(2,1)S(1)}, u32[]{:S(2)}, u32[]{:S(2)}) collective-permute-start(bf16[256,2048]{1,0:T(8,128)(2,1)S(1)} %copy-done.114), channel_id=1, source_target_pairs={{0,16},{16,0},{1,17},{17,1},{2,18},{18,2},{3,19},{19,3},{4,20},{20... | collective-permute-start | bytes 3145736 | tf_op jit(solution)/shard_map/ppermute | solution.py:104
  120.6 32.4 %collective-permute-start.30 = (bf16[256,1408]{1,0:T(8,128)(2,1)}, bf16[256,1408]{1,0:T(8,128)(2,1)S(1)}, u32[]{:S(2)}, u32[]{:S(2)}) collective-permute-start(bf16[256,1408]{1,0:T(8,128)(2,1)} %get-tuple-element.25), channel_id=1, source_target_pairs={{0,4},{4,0},{8,12},{12,8},{1,5},{5,1},{9,13},{13,9},{2,6},{6,2},{1... | collective-permute-start | bytes 2162696 | tf_op jit(solution)/shard_map/ppermute | solution.py:101
  135.7 30.4 %collective-permute-start.36 = (bf16[256,1408]{1,0:T(8,128)(2,1)S(1)}, bf16[256,1408]{1,0:T(8,128)(2,1)S(1)}, u32[]{:S(2)}, u32[]{:S(2)}) collective-permute-start(bf16[256,1408]{1,0:T(8,128)(2,1)S(1)} %copy-done.36), channel_id=1, source_target_pairs={{0,4},{4,0},{8,12},{12,8},{1,5},{5,1},{9,13},{13,9},{2,6},{6,2},{1... | collective-permute-start | bytes 2162696 | tf_op jit(solution)/shard_map/ppermute | solution.py:101
  150.6 104.2 %collective-permute-start.32 = (bf16[256,1408]{1,0:T(8,128)(2,1)}, bf16[256,1408]{1,0:T(8,128)(2,1)}, u32[]{:S(2)}, u32[]{:S(2)}) collective-permute-start(bf16[256,1408]{1,0:T(8,128)(2,1)} %get-tuple-element.25), channel_id=1, source_target_pairs={{0,8},{4,12},{8,0},{12,4},{1,9},{5,13},{9,1},{13,5},{2,10},{6,14},... | collective-permute-start | bytes 2162696 | tf_op jit(solution)/shard_map/ppermute | solution.py:101
  153.0 27.4 %collective-permute-start.20 = (bf16[256,2048]{1,0:T(8,128)(2,1)S(1)}, bf16[256,2048]{1,0:T(8,128)(2,1)S(1)}, u32[]{:S(2)}, u32[]{:S(2)}) collective-permute-start(bf16[256,2048]{1,0:T(8,128)(2,1)S(1)} %pad_maximum_fusion.16), channel_id=1, source_target_pairs={{0,16},{16,0},{1,17},{17,1},{2,18},{18,2},{3,19},{19,3},{4,20},{20... | collective-permute-start | bytes 3145736 | tf_op jit(solution)/shard_map/ppermute | solution.py:104
  154.8 64.7 %collective-permute-start.23 = (bf16[2048,256]{1,0:T(8,128)(2,1)}, bf16[2048,256]{1,0:T(8,128)(2,1)}, u32[]{:S(2)}, u32[]{:S(2)}) collective-permute-start(bf16[2048,256]{1,0:T(8,128)(2,1)} %pad_maximum_fusion.18), channel_id=1, source_target_pairs={{0,16},{16,0},{1,17},{17,1},{2,18},{18,2},{3,19},{19,3},{4,20},{20... | collective-permute-start | bytes 3145736 | tf_op jit(solution)/shard_map/ppermute | solution.py:104
  156.9 72.9 %collective-permute-start.26 = (bf16[2048,256]{1,0:T(8,128)(2,1)}, bf16[2048,256]{1,0:T(8,128)(2,1)}, u32[]{:S(2)}, u32[]{:S(2)}) collective-permute-start(bf16[2048,256]{1,0:T(8,128)(2,1)} %pad_maximum_fusion.19), channel_id=1, source_target_pairs={{0,16},{16,0},{1,17},{17,1},{2,18},{18,2},{3,19},{19,3},{4,20},{20... | collective-permute-start | bytes 3145736 | tf_op jit(solution)/shard_map/ppermute | solution.py:104
  166.1 98.1 %collective-permute-start.52 = (bf16[256,2048]{1,0:T(8,128)(2,1)}, bf16[256,2048]{1,0:T(8,128)(2,1)}, u32[]{:S(2)}, u32[]{:S(2)}) collective-permute-start(bf16[256,2048]{1,0:T(8,128)(2,1)} %collective-permute-done.51), channel_id=1, source_target_pairs={{0,1},{1,2},{2,3},{3,0},{4,5},{5,6},{6,7},{7,4},{8,9},{9,10},{10,1... | collective-permute-start | bytes 3145736 | tf_op jit(solution)/shard_map/ppermute | solution.py:107
  180.3 55.8 %collective-permute-start.42 = (bf16[704,256]{1,0:T(8,128)(2,1)}, bf16[704,256]{1,0:T(8,128)(2,1)}, u32[]{:S(2)}, u32[]{:S(2)}) collective-permute-start(bf16[704,256]{1,0:T(8,128)(2,1)} %get-tuple-element.388), channel_id=1, source_target_pairs={{0,4},{4,0},{8,12},{12,8},{1,5},{5,1},{9,13},{13,9},{2,6},{6,2},{1... | collective-permute-start | bytes 1081352 | tf_op jit(solution)/shard_map/ppermute | solution.py:101
  264.7 52.2 %collective-permute-start.53 = (bf16[256,2048]{1,0:T(8,128)(2,1)}, bf16[256,2048]{1,0:T(8,128)(2,1)S(1)}, u32[]{:S(2)}, u32[]{:S(2)}) collective-permute-start(bf16[256,2048]{1,0:T(8,128)(2,1)} %collective-permute-done.52), channel_id=1, source_target_pairs={{0,1},{1,2},{2,3},{3,0},{4,5},{5,6},{6,7},{7,4},{8,9},{9,10},{10,1... | collective-permute-start | bytes 3145736 | tf_op jit(solution)/shard_map/ppermute | solution.py:107
  333.9 32.7 %collective-permute-start.57 = (bf16[256,2048]{1,0:T(8,128)(2,1)S(1)}, bf16[256,2048]{1,0:T(8,128)(2,1)S(1)}, u32[]{:S(2)}, u32[]{:S(2)}) collective-permute-start(bf16[256,2048]{1,0:T(8,128)(2,1)S(1)} %fusion.41), channel_id=1, source_target_pairs={{0,1},{1,2},{2,3},{3,0},{4,5},{5,6},{6,7},{7,4},{8,9},{9,10},{10,1... | collective-permute-start | bytes 3145736 | tf_op jit(solution)/shard_map/ppermute | solution.py:107
  344.2 44.9 %collective-permute-start.56 = (bf16[256,2048]{1,0:T(8,128)(2,1)S(1)}, bf16[256,2048]{1,0:T(8,128)(2,1)S(1)}, u32[]{:S(2)}, u32[]{:S(2)}) collective-permute-start(bf16[256,2048]{1,0:T(8,128)(2,1)S(1)} %collective-permute-done.55), channel_id=1, source_target_pairs={{0,1},{1,2},{2,3},{3,0},{4,5},{5,6},{6,7},{7,4},{8,9},{9,10},{10,1... | collective-permute-start | bytes 3145736 | tf_op jit(solution)/shard_map/ppermute | solution.py:107
  371.2 40.4 %collective-permute-start.58 = (bf16[256,2048]{1,0:T(8,128)(2,1)S(1)}, bf16[256,2048]{1,0:T(8,128)(2,1)S(1)}, u32[]{:S(2)}, u32[]{:S(2)}) collective-permute-start(bf16[256,2048]{1,0:T(8,128)(2,1)S(1)} %fusion.45), channel_id=1, source_target_pairs={{0,1},{1,2},{2,3},{3,0},{4,5},{5,6},{6,7},{7,4},{8,9},{9,10},{10,1... | collective-permute-start | bytes 3145736 | tf_op jit(solution)/shard_map/ppermute | solution.py:107
  417.3 56.8 %collective-permute-start.59 = (bf16[256,2048]{1,0:T(8,128)(2,1)}, bf16[256,2048]{1,0:T(8,128)(2,1)S(1)}, u32[]{:S(2)}, u32[]{:S(2)}) collective-permute-start(bf16[256,2048]{1,0:T(8,128)(2,1)} %fusion.46), channel_id=1, source_target_pairs={{0,1},{1,2},{2,3},{3,0},{4,5},{5,6},{6,7},{7,4},{8,9},{9,10},{10,1... | collective-permute-start | bytes 3145736 | tf_op jit(solution)/shard_map/ppermute | solution.py:107
  437.0 228.2 %collective-permute-start.96 = (bf16[1024,1408]{1,0:T(8,128)(2,1)}, bf16[1024,1408]{1,0:T(8,128)(2,1)}, u32[]{:S(2)}, u32[]{:S(2)}) collective-permute-start(bf16[1024,1408]{1,0:T(8,128)(2,1)} %pad_maximum_fusion.1), channel_id=1, source_target_pairs={{0,16},{16,0},{1,17},{17,1},{2,18},{18,2},{3,19},{19,3},{4,20},{20... | collective-permute-start | bytes 8650760 | tf_op jit(solution)/shard_map/ppermute | solution.py:104
  457.0 215.2 %collective-permute-start.99 = (bf16[1024,1408]{1,0:T(8,128)(2,1)}, bf16[1024,1408]{1,0:T(8,128)(2,1)}, u32[]{:S(2)}, u32[]{:S(2)}) collective-permute-start(bf16[1024,1408]{1,0:T(8,128)(2,1)} %pad_maximum_fusion.2), channel_id=1, source_target_pairs={{0,16},{16,0},{1,17},{17,1},{2,18},{18,2},{3,19},{19,3},{4,20},{20... | collective-permute-start | bytes 8650760 | tf_op jit(solution)/shard_map/ppermute | solution.py:104
  469.4 157.6 %collective-permute-start.105 = (bf16[704,1024]{1,0:T(8,128)(2,1)}, bf16[704,1024]{1,0:T(8,128)(2,1)}, u32[]{:S(2)}, u32[]{:S(2)}) collective-permute-start(bf16[704,1024]{1,0:T(8,128)(2,1)} %pad_maximum_fusion.10), channel_id=1, source_target_pairs={{0,16},{16,0},{1,17},{17,1},{2,18},{18,2},{3,19},{19,3},{4,20},{20... | collective-permute-start | bytes 4325384 | tf_op jit(solution)/shard_map/ppermute | solution.py:104
  564.9 66.7 %collective-permute-start.102 = (bf16[704,1024]{1,0:T(8,128)(2,1)}, bf16[704,1024]{1,0:T(8,128)(2,1)}, u32[]{:S(2)}, u32[]{:S(2)}) collective-permute-start(bf16[704,1024]{1,0:T(8,128)(2,1)} %pad_maximum_fusion.9), channel_id=1, source_target_pairs={{0,16},{16,0},{1,17},{17,1},{2,18},{18,2},{3,19},{19,3},{4,20},{20... | collective-permute-start | bytes 4325384 | tf_op jit(solution)/shard_map/ppermute | solution.py:104
  567.1 67.0 %collective-permute-start.60 = (bf16[256,2048]{1,0:T(8,128)(2,1)}, bf16[256,2048]{1,0:T(8,128)(2,1)}, u32[]{:S(2)}, u32[]{:S(2)}) collective-permute-start(bf16[256,2048]{1,0:T(8,128)(2,1)} %convolution_convert_fusion.7), channel_id=1, source_target_pairs={{0,1},{1,2},{2,3},{3,0},{4,5},{5,6},{6,7},{7,4},{8,9},{9,10},{10,1... | collective-permute-start | bytes 3145736 | tf_op jit(solution)/shard_map/ppermute | solution.py:107
  649.3 47.2 %collective-permute-start.65 = (bf16[1024,1024]{1,0:T(8,128)(2,1)}, bf16[1024,1024]{1,0:T(8,128)(2,1)}, u32[]{:S(2)}, u32[]{:S(2)}) collective-permute-start(bf16[1024,1024]{1,0:T(8,128)(2,1)} %pad_maximum_fusion.3), channel_id=1, source_target_pairs={{0,16},{16,0},{1,17},{17,1},{2,18},{18,2},{3,19},{19,3},{4,20},{20... | collective-permute-start | bytes 6291464 | tf_op jit(solution)/shard_map/ppermute | solution.py:104
  660.4 46.4 %collective-permute-start.68 = (bf16[1024,1024]{1,0:T(8,128)(2,1)}, bf16[1024,1024]{1,0:T(8,128)(2,1)}, u32[]{:S(2)}, u32[]{:S(2)}) collective-permute-start(bf16[1024,1024]{1,0:T(8,128)(2,1)} %pad_maximum_fusion.4), channel_id=1, source_target_pairs={{0,16},{16,0},{1,17},{17,1},{2,18},{18,2},{3,19},{19,3},{4,20},{20... | collective-permute-start | bytes 6291464 | tf_op jit(solution)/shard_map/ppermute | solution.py:104
  662.7 39.9 %collective-permute-start.87 = (bf16[1024,1024]{0,1:T(8,128)(2,1)}, bf16[1024,1024]{0,1:T(8,128)(2,1)}, u32[]{:S(2)}, u32[]{:S(2)}) collective-permute-start(bf16[1024,1024]{0,1:T(8,128)(2,1)} %pad_maximum_fusion.5), channel_id=1, source_target_pairs={{0,16},{16,0},{1,17},{17,1},{2,18},{18,2},{3,19},{19,3},{4,20},{20... | collective-permute-start | bytes 6291464 | tf_op jit(solution)/shard_map/ppermute | solution.py:104
  685.6 26.5 %collective-permute-start.90 = (bf16[1024,1024]{0,1:T(8,128)(2,1)}, bf16[1024,1024]{0,1:T(8,128)(2,1)S(1)}, u32[]{:S(2)}, u32[]{:S(2)}) collective-permute-start(bf16[1024,1024]{0,1:T(8,128)(2,1)} %pad_maximum_fusion.6), channel_id=1, source_target_pairs={{0,16},{16,0},{1,17},{17,1},{2,18},{18,2},{3,19},{19,3},{4,20},{20... | collective-permute-start | bytes 6291464 | tf_op jit(solution)/shard_map/ppermute | solution.py:104
  696.5 118.8 %collective-permute-start.97 = (bf16[512,1408]{1,0:T(8,128)(2,1)S(1)}, bf16[512,1408]{1,0:T(8,128)(2,1)}, u32[]{:S(2)}, u32[]{:S(2)}) collective-permute-start(bf16[512,1408]{1,0:T(8,128)(2,1)S(1)} %pad_maximum_fusion.8), channel_id=1, source_target_pairs={{0,4},{4,0},{8,12},{12,8},{1,5},{5,1},{9,13},{13,9},{2,6},{6,2},{1... | collective-permute-start | bytes 4325384 | tf_op jit(solution)/shard_map/ppermute | solution.py:101
  701.4 47.0 %collective-permute-start.62 = (bf16[256,2048]{1,0:T(8,128)(2,1)}, bf16[256,2048]{1,0:T(8,128)(2,1)}, u32[]{:S(2)}, u32[]{:S(2)}) collective-permute-start(bf16[256,2048]{1,0:T(8,128)(2,1)} %fusion.42), channel_id=1, source_target_pairs={{0,1},{1,2},{2,3},{3,0},{4,5},{5,6},{6,7},{7,4},{8,9},{9,10},{10,1... | collective-permute-start | bytes 3145736 | tf_op jit(solution)/shard_map/ppermute | solution.py:107
  702.6 41.2 %collective-permute-start.79 = (bf16[256,512]{1,0:T(8,128)(2,1)}, bf16[256,512]{1,0:T(8,128)(2,1)}, u32[]{:S(2)}, u32[]{:S(2)}) collective-permute-start(bf16[256,512]{1,0:T(8,128)(2,1)} %fusion.95), channel_id=1, source_target_pairs={{0,3},{1,2},{2,1},{3,0},{4,7},{5,6},{6,5},{7,4},{8,11},{9,10},{10,... | collective-permute-start | bytes 786440 | tf_op jit(solution)/shard_map/ppermute | solution.py:115
  706.8 38.9 %collective-permute-start.78 = (bf16[256,512]{1,0:T(8,128)(2,1)}, bf16[256,512]{1,0:T(8,128)(2,1)S(1)}, u32[]{:S(2)}, u32[]{:S(2)}) collective-permute-start(bf16[256,512]{1,0:T(8,128)(2,1)} %fusion.95), channel_id=1, source_target_pairs={{0,2},{1,3},{2,0},{3,1},{4,6},{5,7},{6,4},{7,5},{8,10},{9,11},{10,... | collective-permute-start | bytes 786440 | tf_op jit(solution)/shard_map/ppermute | solution.py:115
  712.1 33.6 %collective-permute-start.77 = (bf16[256,512]{1,0:T(8,128)(2,1)}, bf16[256,512]{1,0:T(8,128)(2,1)S(1)}, u32[]{:S(2)}, u32[]{:S(2)}) collective-permute-start(bf16[256,512]{1,0:T(8,128)(2,1)} %fusion.95), channel_id=1, source_target_pairs={{0,1},{1,0},{2,3},{3,2},{4,5},{5,4},{6,7},{7,6},{8,9},{9,8},{10,11... | collective-permute-start | bytes 786440 | tf_op jit(solution)/shard_map/ppermute | solution.py:115
  745.7 53.9 %collective-permute-start.69 = (bf16[512,1024]{1,0:T(8,128)(2,1)}, bf16[512,1024]{1,0:T(8,128)(2,1)S(1)}, u32[]{:S(2)}, u32[]{:S(2)}) collective-permute-start(bf16[512,1024]{1,0:T(8,128)(2,1)} %pad_maximum_fusion.22), channel_id=1, source_target_pairs={{0,4},{4,0},{8,12},{12,8},{1,5},{5,1},{9,13},{13,9},{2,6},{6,2},{1... | collective-permute-start | bytes 3145736 | tf_op jit(solution)/shard_map/ppermute | solution.py:101
  745.8 42.4 %collective-permute-start.88 = (bf16[1024,512]{0,1:T(8,128)(2,1)}, bf16[1024,512]{0,1:T(8,128)(2,1)S(1)}, u32[]{:S(2)}, u32[]{:S(2)}) collective-permute-start(bf16[1024,512]{0,1:T(8,128)(2,1)} %concatenate.300), channel_id=1, source_target_pairs={{0,8},{4,12},{8,0},{12,4},{1,9},{5,13},{9,1},{13,5},{2,10},{6,14},... | collective-permute-start | bytes 3145736 | tf_op jit(solution)/shard_map/ppermute | solution.py:101
  748.4 59.9 %collective-permute-start.91 = (bf16[1024,512]{0,1:T(8,128)(2,1)}, bf16[1024,512]{0,1:T(8,128)(2,1)S(1)}, u32[]{:S(2)}, u32[]{:S(2)}) collective-permute-start(bf16[1024,512]{0,1:T(8,128)(2,1)} %pad_maximum_fusion.24), channel_id=1, source_target_pairs={{0,4},{4,0},{8,12},{12,8},{1,5},{5,1},{9,13},{13,9},{2,6},{6,2},{1... | collective-permute-start | bytes 3145736 | tf_op jit(solution)/shard_map/ppermute | solution.py:101
  765.8 30.6 %collective-permute-start.80 = (bf16[256,512]{1,0:T(8,128)(2,1)S(1)}, bf16[256,512]{1,0:T(8,128)(2,1)S(1)}, u32[]{:S(2)}, u32[]{:S(2)}) collective-permute-start(bf16[256,512]{1,0:T(8,128)(2,1)S(1)} %add_convert_fusion.2), channel_id=1, source_target_pairs={{0,4},{4,0},{8,12},{12,8},{1,5},{5,1},{9,13},{13,9},{2,6},{6,2},{1... | collective-permute-start | bytes 786440 | tf_op jit(solution)/shard_map/ppermute | solution.py:101
  808.5 32.7 %collective-permute-start.100 = (bf16[512,1408]{1,0:T(8,128)(2,1)S(1)}, bf16[512,1408]{1,0:T(8,128)(2,1)S(1)}, u32[]{:S(2)}, u32[]{:S(2)}) collective-permute-start(bf16[512,1408]{1,0:T(8,128)(2,1)S(1)} %copy-done.98), channel_id=1, source_target_pairs={{0,8},{4,12},{8,0},{12,4},{1,9},{5,13},{9,1},{13,5},{2,10},{6,14},... | collective-permute-start | bytes 4325384 | tf_op jit(solution)/shard_map/ppermute | solution.py:101
  808.6 33.6 %collective-permute-start.67 = (bf16[256,1024]{1,0:T(8,128)(2,1)S(1)}, bf16[256,1024]{1,0:T(8,128)(2,1)S(1)}, u32[]{:S(2)}, u32[]{:S(2)}) collective-permute-start(bf16[256,1024]{1,0:T(8,128)(2,1)S(1)} %fusion.77), channel_id=1, source_target_pairs={{0,4},{4,0},{8,12},{12,8},{1,5},{5,1},{9,13},{13,9},{2,6},{6,2},{1... | collective-permute-start | bytes 1572872 | tf_op jit(solution)/shard_map/ppermute | solution.py:101
  810.1 42.5 %collective-permute-start.70 = (bf16[256,1024]{1,0:T(8,128)(2,1)}, bf16[256,1024]{1,0:T(8,128)(2,1)S(1)}, u32[]{:S(2)}, u32[]{:S(2)}) collective-permute-start(bf16[256,1024]{1,0:T(8,128)(2,1)} %fusion.74), channel_id=1, source_target_pairs={{0,8},{4,12},{8,0},{12,4},{1,9},{5,13},{9,1},{13,5},{2,10},{6,14},... | collective-permute-start | bytes 1572872 | tf_op jit(solution)/shard_map/ppermute | solution.py:101
  810.2 45.8 %collective-permute-start.89 = (bf16[1024,256]{0,1:T(8,128)(2,1)S(1)}, bf16[1024,256]{0,1:T(8,128)(2,1)S(1)}, u32[]{:S(2)}, u32[]{:S(2)}) collective-permute-start(bf16[1024,256]{0,1:T(8,128)(2,1)S(1)} %fusion.71), channel_id=1, source_target_pairs={{0,4},{4,0},{8,12},{12,8},{1,5},{5,1},{9,13},{13,9},{2,6},{6,2},{1... | collective-permute-start | bytes 1572872 | tf_op jit(solution)/shard_map/ppermute | solution.py:101
  815.4 48.3 %collective-permute-start.92 = (bf16[1024,256]{0,1:T(8,128)(2,1)S(1)}, bf16[1024,256]{0,1:T(8,128)(2,1)S(1)}, u32[]{:S(2)}, u32[]{:S(2)}) collective-permute-start(bf16[1024,256]{0,1:T(8,128)(2,1)S(1)} %fusion.68), channel_id=1, source_target_pairs={{0,8},{4,12},{8,0},{12,4},{1,9},{5,13},{9,1},{13,5},{2,10},{6,14},... | collective-permute-start | bytes 1572872 | tf_op jit(solution)/shard_map/ppermute | solution.py:101
  841.2 59.7 %collective-permute-start.98 = (bf16[256,1408]{1,0:T(8,128)(2,1)S(1)}, bf16[256,1408]{1,0:T(8,128)(2,1)S(1)}, u32[]{:S(2)}, u32[]{:S(2)}) collective-permute-start(bf16[256,1408]{1,0:T(8,128)(2,1)S(1)} %fusion.59), channel_id=1, source_target_pairs={{0,8},{4,12},{8,0},{12,4},{1,9},{5,13},{9,1},{13,5},{2,10},{6,14},... | collective-permute-start | bytes 2162696 | tf_op jit(solution)/shard_map/ppermute | solution.py:101
  842.3 61.5 %collective-permute-start.101 = (bf16[256,1408]{1,0:T(8,128)(2,1)}, bf16[256,1408]{1,0:T(8,128)(2,1)}, u32[]{:S(2)}, u32[]{:S(2)}) collective-permute-start(bf16[256,1408]{1,0:T(8,128)(2,1)} %fusion.57), channel_id=1, source_target_pairs={{0,4},{4,0},{8,12},{12,8},{1,5},{5,1},{9,13},{13,9},{2,6},{6,2},{1... | collective-permute-start | bytes 2162696 | tf_op jit(solution)/shard_map/ppermute | solution.py:101
  856.0 29.7 %collective-permute-start.72 = (bf16[256,512]{1,0:T(8,128)(2,1)S(1)}, bf16[256,512]{1,0:T(8,128)(2,1)S(1)}, u32[]{:S(2)}, u32[]{:S(2)}) collective-permute-start(bf16[256,512]{1,0:T(8,128)(2,1)S(1)} %get-tuple-element.371), channel_id=1, source_target_pairs={{0,2},{1,3},{2,0},{3,1},{4,6},{5,7},{6,4},{7,5},{8,10},{9,11},{10,... | collective-permute-start | bytes 786440 | tf_op jit(solution)/shard_map/ppermute | solution.py:115
  (239 other events, 3533.4 us)

commit v2 on v1

v2 whole, which is shorter than its diff:
```python
import jax
import jax.numpy as jnp
from jax import lax
from jax.experimental import pallas as pl
from jax.experimental.pallas import tpu as pltpu
from jax.sharding import PartitionSpec as P

HEADS = 16
KV_HEADS = 2
HEAD_DIM = 128

epsilon = 1e-05
negative = -1e30
rope_base = 10000.0
log2e = 1.4426950408889634
bf16 = jnp.bfloat16
f32 = jnp.float32


def dot(left, right, dims):
    return lax.dot_general(left, right, ((dims[:1], dims[1:]), ((), ())), preferred_element_type=f32)


def turn(values, cosine, sine):
    return values * cosine + pltpu.roll(values, HEAD_DIM // 2, 1) * sine


def mask_bias(row_ids, key_ids):
    span, own = key_ids.shape[0], row_ids.shape[1]
    key_place = lax.broadcasted_iota(jnp.int32, (span, own), 0)
    row_place = lax.broadcasted_iota(jnp.int32, (span, own), 1) + (span - own)
    return jnp.where((key_ids == row_ids) & (row_place >= key_place), 0.0, negative)


PER = 4


def forward_kernel(pre_ref, k_ref, v_ref, cos_ref, sin_ref, rid_ref, kid_ref, mixed_ref, q_ref, top_ref, bias_ref, vt_ref):
    head = pl.program_id(0) * PER

    @pl.when(head == 0)
    def _():
        bias_ref[...] = mask_bias(rid_ref[...], kid_ref[...])

    @pl.when(head % (HEADS // KV_HEADS) == 0)
    def _():
        vt_ref[...] = v_ref[...].astype(f32).T.astype(bf16)

    for n in range(PER):
        lanes = slice(n * HEAD_DIM, (n + 1) * HEAD_DIM)
        q = turn(pre_ref[:, lanes], cos_ref[...], sin_ref[...]).astype(bf16)
        q_ref[:, lanes] = q
        scores = dot(k_ref[...], q, (1, 1)) * (HEAD_DIM ** (-0.5) * log2e) + bias_ref[...]
        top = jnp.max(scores, axis=0, keepdims=True)
        exponent = jnp.exp2(scores - top)
        total = jnp.sum(exponent, axis=0, keepdims=True)
        mixed = dot(vt_ref[...], exponent.astype(bf16), (1, 0)) * (1.0 / total)
        mixed_ref[:, lanes] = mixed.T.astype(bf16)
        top_ref[n] = top + jnp.log2(total)


def attend_forward(pre, kv_all, cosine, sine, row_ids, key_ids):
    own, width = pre.shape
    span = kv_all.shape[0]
    share = HEADS // KV_HEADS
    whole = lambda shape: pl.BlockSpec(shape, lambda h: (0, 0))
    head = pl.BlockSpec((own, PER * HEAD_DIM), lambda h: (0, h))
    return pl.pallas_call(
        forward_kernel,
        grid=(HEADS // PER,),
        in_specs=[
            head,
            pl.BlockSpec((span, HEAD_DIM), lambda h: (0, h * PER // share)),
            pl.BlockSpec((span, HEAD_DIM), lambda h: (0, KV_HEADS + h * PER // share)),
            whole((own, HEAD_DIM)),
            whole((own, HEAD_DIM)),
            whole((1, own)),
            whole((span, 1)),
        ],
        out_specs=[head, head, pl.BlockSpec((PER, 1, own), lambda h: (h, 0, 0))],
        out_shape=[
            jax.ShapeDtypeStruct((own, width), bf16),
            jax.ShapeDtypeStruct((own, width), bf16),
            jax.ShapeDtypeStruct((HEADS, 1, own), f32),
        ],
        scratch_shapes=[pltpu.VMEM((span, own), f32), pltpu.VMEM((HEAD_DIM, span), bf16)],
        compiler_params=pltpu.CompilerParams(dimension_semantics=("arbitrary",), vmem_limit_bytes=32 << 20),
        cost_estimate=pl.CostEstimate(flops=0, transcendentals=0, bytes_accessed=0),
    )(pre, kv_all, kv_all, cosine, sine, row_ids[None, :], key_ids[:, None])


def backward_kernel(q_ref, k_ref, v_ref, back_ref, top_ref, cos_ref, sin_ref, rid_ref, kid_ref, dq_ref, dk_ref, dv_ref, bias_ref, kt_ref):
    step = pl.program_id(0)

    @pl.when(step == 0)
    def _():
        bias_ref[...] = mask_bias(rid_ref[...], kid_ref[...])

    @pl.when(step % (HEADS // KV_HEADS // PER) == 0)
    def _():
        kt_ref[...] = k_ref[...].astype(f32).T.astype(bf16)
        dk_ref[...] = jnp.zeros_like(dk_ref)
        dv_ref[...] = jnp.zeros_like(dv_ref)

    scale = HEAD_DIM ** (-0.5)
    for n in range(PER):
        lanes = slice(n * HEAD_DIM, (n + 1) * HEAD_DIM)
        q = q_ref[:, lanes]
        back = back_ref[:, lanes]
        scores = dot(k_ref[...], q, (1, 1)) * (scale * log2e) + bias_ref[...]
        probs = jnp.exp2(scores - top_ref[n])
        dv_ref[...] += dot(probs.astype(bf16), back, (1, 0))
        weight_back = dot(v_ref[...], back, (1, 1))
        inner = jnp.sum(weight_back * probs, axis=0, keepdims=True)
        score_back = (probs * (weight_back - inner)).astype(bf16)
        dk_ref[...] += dot(score_back, q, (1, 0)) * scale
        turned = (dot(kt_ref[...], score_back, (1, 0)) * scale).T
        dq_ref[:, lanes] = turn(turned, cos_ref[...], sin_ref[...]).astype(bf16)


def attend_backward(q_rows, kv_all, mixed_back, top, cosine, sine, row_ids, key_ids):
    own, width = q_rows.shape
    span = kv_all.shape[0]
    steps = HEADS // KV_HEADS // PER
    whole = lambda shape: pl.BlockSpec(shape, lambda h: (0, 0))
    head = pl.BlockSpec((own, PER * HEAD_DIM), lambda h: (0, h))
    shared = pl.BlockSpec((span, HEAD_DIM), lambda h: (0, h // steps))
    return pl.pallas_call(
        backward_kernel,
        grid=(HEADS // PER,),
        in_specs=[
            head,
            shared,
            pl.BlockSpec((span, HEAD_DIM), lambda h: (0, KV_HEADS + h // steps)),
            head,
            pl.BlockSpec((PER, 1, own), lambda h: (h, 0, 0)),
            whole((own, HEAD_DIM)),
            whole((own, HEAD_DIM)),
            whole((1, own)),
            whole((span, 1)),
        ],
        out_specs=[head, shared, shared],
        out_shape=[
            jax.ShapeDtypeStruct((own, width), bf16),
            jax.ShapeDtypeStruct((span, KV_HEADS * HEAD_DIM), f32),
            jax.ShapeDtypeStruct((span, KV_HEADS * HEAD_DIM), f32),
        ],
        scratch_shapes=[pltpu.VMEM((span, own), f32), pltpu.VMEM((HEAD_DIM, span), bf16)],
        compiler_params=pltpu.CompilerParams(dimension_semantics=("arbitrary",), vmem_limit_bytes=32 << 20),
        cost_estimate=pl.CostEstimate(flops=0, transcendentals=0, bytes_accessed=0),
    )(q_rows, kv_all, kv_all, mixed_back, top, cosine, sine, row_ids[None, :], key_ids[:, None])


FREE = pl.CostEstimate(flops=0, transcendentals=0, bytes_accessed=0)


def call(kernel, grid, in_specs, out_specs, out_shape, scratch=()):
    return pl.pallas_call(
        kernel,
        grid=grid,
        in_specs=in_specs,
        out_specs=out_specs,
        out_shape=out_shape,
        scratch_shapes=list(scratch),
        compiler_params=pltpu.CompilerParams(
            dimension_semantics=("arbitrary",) * len(grid), vmem_limit_bytes=48 << 20
        ),
        cost_estimate=FREE,
    )


def fixed(shape):
    return pl.BlockSpec(shape, lambda i: (0,) * len(shape))


def through_kernel(h_ref, f_ref, g_ref, u_ref, d_ref, hid_ref, gb_ref, ub_ref):
    gate = dot(h_ref[...], g_ref[...], (1, 0))
    up = dot(h_ref[...], u_ref[...], (1, 0))
    back = dot(f_ref[...], d_ref[...], (1, 1))
    s = jax.nn.sigmoid(gate)
    swish = gate * s
    hid_ref[...] = (swish * up).astype(bf16)
    ub_ref[...] = (back * swish).astype(bf16)
    gb_ref[...] = (back * up * s * (1.0 + gate * (1.0 - s))).astype(bf16)


def feed_through(hidden, feed, g_matrix, u_matrix, d_matrix):
    count, width = hidden.shape
    units = g_matrix.shape[1]
    tile = min(256, units)
    across = pl.BlockSpec((width, tile), lambda i: (0, i))
    out = pl.BlockSpec((count, tile), lambda i: (0, i))
    return call(
        through_kernel,
        (pl.cdiv(units, tile),),
        [fixed((count, width))] * 2 + [across, across, pl.BlockSpec((tile, width), lambda i: (i, 0))],
        [out] * 3,
        [jax.ShapeDtypeStruct((count, units), bf16)] * 3,
    )(hidden, feed, g_matrix, u_matrix, d_matrix)


def finish_kernel(f_ref, gate_ref, up_ref, d_ref, hid_ref, gb_ref, ub_ref):
    gate = gate_ref[...]
    back = dot(f_ref[...], d_ref[...], (1, 1))
    s = jax.nn.sigmoid(gate)
    swish = gate * s
    hid_ref[...] = (swish * up_ref[...]).astype(bf16)
    ub_ref[...] = (back * swish).astype(bf16)
    gb_ref[...] = (back * up_ref[...] * s * (1.0 + gate * (1.0 - s))).astype(bf16)


def feed_finish(feed, gate, up, d_matrix):
    count, units = gate.shape
    width = feed.shape[1]
    tile = min(256, units)
    out = pl.BlockSpec((count, tile), lambda i: (0, i))
    return call(
        finish_kernel,
        (pl.cdiv(units, tile),),
        [fixed((count, width)), out, out, pl.BlockSpec((tile, width), lambda i: (i, 0))],
        [out] * 3,
        [jax.ShapeDtypeStruct((count, units), bf16)] * 3,
    )(feed, gate, up, d_matrix)


def rows_product(lefts, rights, turned, dtype, block=0, count=None):
    n = len(lefts)
    count = lefts[0].shape[0] if count is None else count
    columns = rights[0].shape[0 if turned else 1]
    tile = min(512, columns)

    def kernel(*refs):
        total = 0.0
        for k in range(n):
            total = total + dot(refs[k][...], refs[n + k][...], (1, 1 if turned else 0))
        refs[-1][...] = total.astype(dtype)

    specs = [pl.BlockSpec((count, x.shape[1]), lambda i: (block, 0)) for x in lefts]
    for x in rights:
        if turned:
            specs.append(pl.BlockSpec((tile, x.shape[1]), lambda i: (i, 0)))
        else:
            specs.append(pl.BlockSpec((x.shape[0], tile), lambda i: (0, i)))
    return call(
        kernel,
        (columns // tile,),
        specs,
        pl.BlockSpec((count, tile), lambda i: (0, i)),
        jax.ShapeDtypeStruct((count, columns), dtype),
    )(*lefts, *rights)


def token_sum(lefts, left_lanes, rights, right_lanes, received=None):
    n = len(lefts)
    start, rows_out = left_lanes
    tile = min(256, rows_out)
    base, columns = right_lanes

    def kernel(*refs):
        total = dot(refs[0][...], refs[n][...], (0, 0))
        for k in range(1, n):
            total = total + dot(refs[k][...], refs[n + k][...], (0, 0))
        if received is not None:
            total = total + refs[2 * n][...].astype(f32)
        refs[-1][...] = total.astype(bf16)

    first, second = start // tile, base // columns
    specs = [pl.BlockSpec((x.shape[0], tile), lambda i: (0, first + i)) for x in lefts]
    specs += [pl.BlockSpec((x.shape[0], columns), lambda i: (0, second)) for x in rights]
    out = pl.BlockSpec((tile, columns), lambda i: (i, 0))
    operands = list(lefts) + list(rights)
    if received is not None:
        specs.append(out)
        operands.append(received)
    return call(
        kernel,
        (pl.cdiv(rows_out, tile),),
        specs,
        out,
        jax.ShapeDtypeStruct((rows_out, columns), bf16),
    )(*operands)


def nn(left, right):
    return dot(left, right, (1, 0))


def nt(left, right):
    return dot(left, right, (1, 1))


def tn(left, right):
    return dot(left, right, (0, 0))


def after(value, *earlier):
    return lax.optimization_barrier((value,) + earlier)[0]


def fence(*values):
    return lax.optimization_barrier(values)


def blank(shape):
    return pl.pallas_call(
        lambda out: None,
        out_specs=pl.BlockSpec(memory_space=pl.ANY),
        out_shape=jax.ShapeDtypeStruct(shape, bf16),
    )()


def xor_blocks(blocks, index):
    bit = 1
    while bit < len(blocks):
        swap = (index & bit) != 0
        blocks = [jnp.where(swap, blocks[j ^ bit], blocks[j]) for j in range(len(blocks))]
        bit *= 2
    return blocks


def xor_order(value, index, count, axis):
    return jnp.concatenate(xor_blocks(jnp.split(value, count, axis), index), axis)


def tree_sum(values):
    while len(values) > 1:
        values = [values[i] + values[i + 1] for i in range(0, len(values), 2)]
    return values[0]


def rotary_tables(positions):
    half = HEAD_DIM // 2
    frequency = rope_base ** (-2.0 * jnp.arange(half, dtype=f32) / HEAD_DIM)
    angles = positions.astype(f32)[:, None] * frequency[None, :]
    cosine, sine = jnp.cos(angles), jnp.sin(angles)
    return jnp.concatenate([cosine, cosine], 1), jnp.concatenate([-sine, sine], 1)


def rotate(values, cosine, sine):
    heads = jnp.split(values, values.shape[1] // HEAD_DIM, 1)
    half = HEAD_DIM // 2
    swapped = [jnp.concatenate([h[:, half:], h[:, :half]], 1) for h in heads]
    return jnp.concatenate([h * cosine + s * sine for h, s in zip(heads, swapped)], 1)


def norm_factor(values):
    return lax.rsqrt(jnp.mean(values * values, axis=-1, keepdims=True) + epsilon)


def norm_back(grad, values, factor, gain):
    y = grad * gain
    pulled = factor * y - values * factor**3 * jnp.mean(y * values, axis=-1, keepdims=True)
    return pulled, jnp.sum(grad * values * factor, axis=0)


def local(
    tokens,
    attention_gain,
    mlp_gain,
    w_query,
    w_key,
    w_value,
    w_out,
    w_gate,
    w_up,
    w_down,
    segment_ids,
    skip_mask,
    cotangent,
):
    cols, rows = lax.axis_size("cols"), lax.axis_size("rows")
    c, r, d = lax.axis_index("cols"), lax.axis_index("rows"), lax.axis_index("dp")
    own, width = tokens.shape
    half = width // 2
    sequences, length = segment_ids.shape
    blocks = 2 * rows
    step = width // blocks
    target = d * rows + r
    kv_width = KV_HEADS * HEAD_DIM

    def to_rows(value, a):
        return lax.ppermute(value, "rows", [(i, i ^ a) for i in range(rows)])

    def to_near(value, turn):
        pairs = []
        for core in range(2):
            a = 1 + (core ^ turn)
            pairs += [(core * rows + i, core * rows + (i ^ a)) for i in range(rows)]
        return lax.ppermute(value, ("dp", "rows"), pairs)

    first = 1 + d

    def to_core(value):
        return lax.ppermute(value, "dp", [(0, 1), (1, 0)])

    def to_cols(value, k):
        return lax.ppermute(value, "cols", [(i, (i + k) % cols) for i in range(cols)])

    def along(value, k):
        return lax.ppermute(
            value, "cols", [(i, i + k) for i in range(cols) if 0 <= i + k < cols]
        )

    def to_xor_cols(value, k):
        return lax.ppermute(value, "cols", [(i, i ^ k) for i in range(cols)])

    def spot(j, e):
        return ((2 * (r ^ j) + (d ^ e)) ^ target) * step

    def put(full, piece, axis, start, offset):
        at = (start + offset, 0) if axis == 0 else (offset, start)
        return lax.dynamic_update_slice(full, piece, at)

    def fill(full, axis, one, two, e):
        near, far = (first, 3 - first) if e == 0 else (3 - first, first)
        size = two.shape[0] // 2
        full = put(full, one, axis, spot(near, e), 0)
        full = put(full, two[:size], axis, spot(far, e), 0)
        return put(full, two[size:], axis, spot(3, e), 0)

    def halves(weight, axis):
        low, high = jnp.split(weight, 2, axis)
        return jnp.where(d == 0, low, high), jnp.where(d == 0, high, low)

    sequence = (c * own) // length
    start = (c * own) % length
    reach = min(-(-(length // 2 - 1) // own), length // own - 1)
    span = (reach + 1) * own
    units = w_gate.shape[1]

    kv_mine, kv_rest = halves(jnp.concatenate([w_key, w_value], 1), 0)
    q_mine, _ = halves(w_query, 0)
    kv_one = to_near(kv_mine, 0)
    q_parts = [q_mine] + [to_xor_cols(q_mine, k) for k in range(1, cols)]
    kv_one, tokens, attention_gain, mlp_gain, w_out, segment_ids, skip_mask, cotangent = fence(
        kv_one, tokens, attention_gain, mlp_gain, w_out, segment_ids, skip_mask, cotangent
    )
    kv_two = to_near(jnp.concatenate([kv_mine, kv_one], 0), 1)
    o_mine, o_rest = halves(w_out, 1)
    o_one = to_near(o_mine, 0)
    inputs = xor_order(tokens, target, blocks, 1).astype(f32)
    gain_one = xor_order(attention_gain, target, blocks, 0)
    gain_two = xor_order(mlp_gain, target, blocks, 0)
    factor_one = norm_factor(inputs)
    normed = (inputs * factor_one * gain_one).astype(bf16)
    cosine, sine = rotary_tables(start + jnp.arange(own))
    keep = (1 - lax.dynamic_index_in_dim(skip_mask, sequence, 0, False)).astype(f32)
    upstream = xor_order(cotangent, target, blocks, 1)
    feed_own = (keep * upstream).astype(bf16)

    (kv_two, q_parts, normed, o_one, cosine, sine, feed_own, upstream, w_down, w_gate, w_up) = fence(
        kv_two, q_parts, normed, o_one, cosine, sine, feed_own, upstream, w_down, w_gate, w_up
    )
    feeds = [feed_own, to_cols(feed_own, 1)]
    q_mine = jnp.concatenate(xor_blocks(q_parts, c), 1)
    q_one = to_near(q_mine, 0)
    kv_other = (to_core(kv_one), to_core(kv_two))
    q_own_other = to_core(q_mine)
    q_one, q_own_other, kv_other, w_down, o_one = fence(
        q_one, q_own_other, kv_other, w_down, o_one
    )
    q_sent = jnp.concatenate([q_mine, q_one], 0)
    q_two = to_near(q_sent, 1)
    kv_mine, kv_rest, kv_one, kv_two, kv_other, _ = fence(
        kv_mine, kv_rest, kv_one, kv_two, kv_other, q_sent
    )
    kv_matrix = blank((width, 2 * kv_width))
    kv_matrix = put(kv_matrix, kv_mine, 0, spot(0, 0), 0)
    kv_matrix = put(kv_matrix, kv_rest, 0, spot(0, 1), 0)
    kv_matrix = fill(kv_matrix, 0, kv_one, kv_two, 0)
    kv_matrix = fill(kv_matrix, 0, *kv_other, 1)
    kv_pre = nn(normed, kv_matrix)
    kv_own = jnp.concatenate(
        [rotate(kv_pre[:, :kv_width], cosine, sine), kv_pre[:, kv_width:]], 1
    ).astype(bf16)

    w_mine, w_rest = halves(w_down, 1)
    w_one = to_near(w_mine, 0)
    kv_own, feeds[1] = fence(kv_own, feeds[1])
    kv_before = [along(kv_own, k) for k in range(reach, 0, -1)]
    q_one_other = to_core(q_one)
    q_matrix = blank((width, width))
    q_matrix = put(q_matrix, q_mine, 0, spot(0, 0), 0)
    q_matrix = put(q_matrix, q_own_other, 0, spot(0, 1), 0)
    q_matrix = put(q_matrix, q_one, 0, spot(first, 0), 0)
    q_matrix = put(q_matrix, q_one_other, 0, spot(3 - first, 1), 0)
    ids = lax.dynamic_index_in_dim(segment_ids, sequence, 0, False)
    ids_padded = jnp.concatenate([jnp.full((reach * own,), -1, ids.dtype), ids])
    key_ids = lax.dynamic_slice_in_dim(ids_padded, start, span, 0)
    row_ids = key_ids[reach * own :]

    (q_two, w_one, q_matrix, o_mine, o_rest, o_one, w_gate, w_up) = fence(
        q_two, w_one, q_matrix, o_mine, o_rest, o_one, w_gate, w_up
    )
    feeds[1] = after(feeds[1], *kv_before)
    for k in range(2, cols - 1):
        feeds.append(to_cols(feeds[-1], 1))
    o_two = to_near(jnp.concatenate([o_mine, o_one], 0), 1)
    q_two_other = to_core(q_two)
    g_mine, g_rest = halves(w_gate, 0)
    u_mine, u_rest = halves(w_up, 0)
    gu_mine = jnp.concatenate([g_mine, u_mine], 0)
    gu_one = to_near(gu_mine, 0)
    o_one_other = to_core(o_one)
    kv_all = jnp.concatenate(list(kv_before) + [kv_own], 0)
    rows_two = q_two.shape[0] // 2
    for e, two in ((0, q_two), (1, q_two_other)):
        far = 3 - first if e == 0 else first
        q_matrix = put(q_matrix, two[:rows_two], 0, spot(far, e), 0)
        q_matrix = put(q_matrix, two[rows_two:], 0, spot(3, e), 0)
    q_pre = nn(normed, q_matrix)
    mixed, q_rows, top = attend_forward(q_pre, kv_all, cosine, sine, row_ids, key_ids)
    o_matrix = blank((width, width))
    o_matrix = put(o_matrix, o_mine, 1, spot(0, 0), 0)
    o_matrix = put(o_matrix, o_rest, 1, spot(0, 1), 0)
    o_matrix = put(o_matrix, o_one, 1, spot(first, 0), 0)
    o_matrix = put(o_matrix, o_one_other, 1, spot(3 - first, 1), 0)

    (o_two, gu_one, mixed, q_rows, top, feeds, o_matrix, w_mine, w_rest, w_one, gu_mine) = fence(
        o_two, gu_one, mixed, q_rows, top, feeds, o_matrix, w_mine, w_rest, w_one, gu_mine
    )
    feeds = list(feeds) + [to_cols(feeds[-1], 1)]
    gu_two = to_near(jnp.concatenate([gu_mine, gu_one], 0), 1)
    o_two_other = to_core(o_two)
    gu_one_other = to_core(gu_one)
    w_one_other = to_core(w_one)
    rows_two = o_two.shape[0] // 2
    for e, two in ((0, o_two), (1, o_two_other)):
        far = 3 - first if e == 0 else first
        o_matrix = put(o_matrix, two[:rows_two], 1, spot(far, e), 0)
        o_matrix = put(o_matrix, two[rows_two:], 1, spot(3, e), 0)
    branch = nn(mixed, o_matrix)
    middle = inputs + keep * branch
    factor_two = norm_factor(middle)
    hidden_own = (middle * factor_two * gain_two).astype(bf16)
    hidden_own, o_matrix, gu_one_other, w_one_other, gu_one, w_one, gu_mine, g_rest, u_rest, feeds = fence(
        hidden_own, o_matrix, gu_one_other, w_one_other, gu_one, w_one, gu_mine, g_rest, u_rest, feeds
    )
    chunks = [hidden_own, to_cols(hidden_own, 1)]
    g_matrix, u_matrix = blank((width, units)), blank((width, units))
    g_matrix = put(g_matrix, gu_mine[:step], 0, spot(0, 0), 0)
    u_matrix = put(u_matrix, gu_mine[step:], 0, spot(0, 0), 0)
    g_matrix = put(g_matrix, g_rest, 0, spot(0, 1), 0)
    u_matrix = put(u_matrix, u_rest, 0, spot(0, 1), 0)
    for e, one in ((0, gu_one), (1, gu_one_other)):
        near = first if e == 0 else 3 - first
        g_matrix = put(g_matrix, one[:step], 0, spot(near, e), 0)
        u_matrix = put(u_matrix, one[step:], 0, spot(near, e), 0)
    d_matrix = blank((units, width))
    d_matrix = put(d_matrix, w_mine, 1, spot(0, 0), 0)
    d_matrix = put(d_matrix, w_rest, 1, spot(0, 1), 0)
    d_matrix = put(d_matrix, w_one, 1, spot(first, 0), 0)
    d_matrix = put(d_matrix, w_one_other, 1, spot(3 - first, 1), 0)

    gu_two, g_matrix, u_matrix, d_matrix, w_mine, w_one, chunks = fence(
        gu_two, g_matrix, u_matrix, d_matrix, w_mine, w_one, chunks
    )
    chunks = list(chunks)
    w_two = to_near(jnp.concatenate([w_mine, w_one], 0), 1)
    gu_two_other = to_core(gu_two)
    for e, two in ((0, gu_two), (1, gu_two_other)):
        far = 3 - first if e == 0 else first
        for n, at in enumerate((spot(far, e), spot(3, e))):
            piece = two[n * 2 * step : (n + 1) * 2 * step]
            g_matrix = put(g_matrix, piece[:step], 0, at, 0)
            u_matrix = put(u_matrix, piece[step:], 0, at, 0)
    chunks.append(to_cols(chunks[1], 1))

    def gate_up(hidden):
        gate, up = nn(hidden, g_matrix), nn(hidden, u_matrix)
        return gate, up

    gate, up = gate_up(chunks[1])
    w_two, gate, up, d_matrix, arrived = fence(w_two, gate, up, d_matrix, chunks[2])
    chunks[2] = arrived
    chunks.append(to_cols(chunks[2], 1))
    w_two_other = to_core(w_two)
    rows_two = w_two.shape[0] // 2
    for e, two in ((0, w_two), (1, w_two_other)):
        far = 3 - first if e == 0 else first
        d_matrix = put(d_matrix, two[:rows_two], 1, spot(far, e), 0)
        d_matrix = put(d_matrix, two[rows_two:], 1, spot(3, e), 0)
    weights = (g_matrix, u_matrix)
    done = [feed_finish(feeds[1], gate, up, d_matrix)]
    part = rows_product(done[0][1:], weights, True, bf16)
    for k in range(2, cols - 1):
        done.append(feed_through(chunks[k], feeds[k], g_matrix, u_matrix, d_matrix))
        if k == 2:
            part, arrived, done = fence(part, chunks[3], done)
        else:
            part, carry, arrived, done = fence(part, carry, chunks[k + 1], done)
            part = (part + carry.astype(f32)).astype(bf16)
            part, done = fence(part, done)
        chunks[k + 1] = arrived
        carry = to_cols(part, 1)
        done = list(done)
        if k + 2 < cols:
            chunks.append(to_cols(chunks[k + 1], 1))
        part = rows_product(done[-1][1:], weights, True, f32)
    last_hidden = jnp.concatenate([chunks[cols - 1], chunks[0]], 0)
    last_feed = jnp.concatenate([feeds[cols - 1], feeds[0]], 0)
    done.append(feed_through(last_hidden, last_feed, g_matrix, u_matrix, d_matrix))
    hids, gbs, ubs = ([x[n] for x in done] for n in range(3))
    h_parts, f_parts = chunks[1 : cols - 1] + [last_hidden], feeds[1 : cols - 1] + [last_feed]
    low, high, full = (0, half), (half, half), (0, units)
    d_sent = token_sum(hids, full, f_parts, high)
    part, carry, d_sent, hids, gbs, ubs, h_parts, f_parts = fence(
        part, carry, d_sent, hids, gbs, ubs, h_parts, f_parts
    )
    part = (part + carry.astype(f32)).astype(bf16)
    part, d_sent, hids, gbs, ubs = fence(part, d_sent, hids, gbs, ubs)

    carry = to_cols(part, 1)
    d_received = to_core(d_sent)
    part = rows_product((gbs[-1], ubs[-1]), weights, True, f32, 0, own)
    g_sent = token_sum(h_parts, high, gbs, full)
    u_sent = token_sum(h_parts, high, ubs, full)
    d_sum = token_sum(hids, full, f_parts, low, d_received)
    part, carry, d_sum, g_sent, u_sent, hids, gbs, ubs = fence(
        part, carry, d_sum, g_sent, u_sent, hids, gbs, ubs
    )
    part = (part + carry.astype(f32)).astype(bf16)
    part, d_sum, g_sent, u_sent, gbs, ubs, hids = fence(
        part, d_sum, g_sent, u_sent, gbs, ubs, hids
    )

    def row_sum_start(total, axis):
        pieces = jnp.split(total, rows, axis)
        sent = jnp.concatenate([jnp.where(d == 0, pieces[1], pieces[2]), pieces[3]], axis)
        return [pieces, to_near(sent, 0), axis]

    def row_sum_next(state):
        pieces, near, axis = state
        mine, theirs = jnp.split(near, 2, axis)
        kept = jnp.where(d == 0, pieces[2], pieces[1])
        theirs = (kept.astype(f32) + theirs.astype(f32)).astype(bf16)
        return [pieces[0], mine, to_near(theirs, 1)]

    def row_sum_end(state):
        return state[0].astype(f32) + state[1].astype(f32) + state[2].astype(f32)

    def around(carry, part):
        return to_cols((part.astype(f32) + carry.astype(f32)).astype(bf16), 1)

    carry = to_cols(part, 1)
    d_state = row_sum_start(d_sum, 1)
    g_received = to_core(g_sent)
    u_received = to_core(u_sent)
    part = rows_product((gbs[-1], ubs[-1]), weights, True, f32, 1, own)
    outs = [rows_product([hids[0]], [d_matrix], False, bf16)]
    g_sum = token_sum(h_parts, low, gbs, full, g_received)
    u_sum = token_sum(h_parts, low, ubs, full, u_received)
    part, carry, d_state[1], g_sum, u_sum, outs, hids = fence(
        part, carry, d_state[1], g_sum, u_sum, outs, hids
    )
    outs = list(outs)

    d_state = row_sum_next(d_state)
    g_state = row_sum_start(g_sum, 0)
    out_carry = to_cols(outs[0], 1)
    hidden_in_back = part + carry.astype(f32)
    from_norm, mlp_gain_part = norm_back(hidden_in_back, middle, factor_two, gain_two)
    middle_grad = upstream + from_norm
    branch_back = (keep * middle_grad).astype(bf16)
    mixed_back = rows_product([branch_back], [o_matrix], True, bf16)
    o_sent = token_sum([mixed], (0, width), [branch_back], high)
    outs += [rows_product([x], [d_matrix], False, bf16) for x in hids[1:-1]]
    last_out = rows_product([hids[-1]], [d_matrix], False, bf16)
    outs += jnp.split(last_out, 2, 0)
    mixed_back, branch_back, o_sent, d_state[2], g_state[1], out_carry, outs = fence(
        mixed_back, branch_back, o_sent, d_state[2], g_state[1], out_carry, outs
    )

    g_state = row_sum_next(g_state)
    u_state = row_sum_start(u_sum, 0)
    for k in range(1, cols - 2):
        out_carry = around(out_carry, outs[k])
    o_received = to_core(o_sent)
    dq, dk, dv = attend_backward(
        q_rows, kv_all, mixed_back, top, cosine, -sine, row_ids, key_ids
    )
    q_sent = token_sum([normed], high, [dq], (0, width))
    o_sum = token_sum([mixed], (0, width), [branch_back], low, o_received)
    dq, dk, dv, q_sent, o_sum, g_state[2], u_state[1], out_carry = fence(
        dq, dk, dv, q_sent, o_sum, g_state[2], u_state[1], out_carry
    )

    u_state = row_sum_next(u_state)
    o_low, o_high = jnp.split(o_sum, 2, 0)
    o_low = row_sum_start(o_low, 1)
    kv_turned = jnp.concatenate([dk, dv], 1)
    kv_back_pre = kv_turned[reach * own :]
    back_parts = []
    for k in range(1, reach + 1):
        piece = kv_turned[(reach - k) * own : (reach - k + 1) * own].astype(bf16)
        back_parts.append(along(piece, -k))
    q_received = to_core(q_sent)
    down_grad = row_sum_end(d_state)
    back_parts, q_received, down_grad, u_state[2], o_low[1] = fence(
        back_parts, q_received, down_grad, u_state[2], o_low[1]
    )

    o_high = row_sum_start(o_high, 1)
    for piece in back_parts:
        kv_back_pre = kv_back_pre + piece.astype(f32)
    kv_back = jnp.concatenate(
        [rotate(kv_back_pre[:, :kv_width], cosine, -sine), kv_back_pre[:, kv_width:]], 1
    ).astype(bf16)
    kv_sent = token_sum([normed], high, [kv_back], (0, 2 * kv_width))
    kv_received = to_core(kv_sent)
    q_sum = token_sum([normed], low, [dq], (0, width), q_received)
    kv_sum = token_sum([normed], low, [kv_back], (0, 2 * kv_width), kv_received)
    kv_sum, q_sum, kv_back, o_high[1] = fence(kv_sum, q_sum, kv_back, o_high[1])

    kv_state = row_sum_start(kv_sum, 0)
    q_low, q_high = jnp.split(q_sum, 2, 1)
    q_low = row_sum_start(q_low, 0)
    out_carry = around(out_carry, outs[cols - 2])
    normed_back = rows_product([dq, kv_back], [q_matrix, kv_matrix], True, f32)
    from_norm, attention_gain_part = norm_back(normed_back, inputs, factor_one, gain_one)
    input_grad = xor_order(middle_grad + from_norm, target, blocks, 1)
    gains = xor_order(jnp.stack([attention_gain_part, mlp_gain_part]), target, blocks, 1)
    hops = [to_core, lambda x: to_rows(x, 1), lambda x: to_rows(x, 2)]
    hops += [(lambda x, k=1 << n: to_xor_cols(x, k)) for n in range(cols.bit_length() - 1)]

    def shared(values, some):
        for hop in some:
            values = values + hop(values)
        return values

    kv_state[1], q_low[1], input_grad, gains = fence(kv_state[1], q_low[1], input_grad, gains)

    kv_state = row_sum_next(kv_state)
    o_low = row_sum_next(o_low)
    gains = shared(gains, hops[:2])
    gate_grad = row_sum_end(g_state)
    kv_state[2], gains, o_low[2], gate_grad, out_carry = fence(
        kv_state[2], gains, o_low[2], gate_grad, out_carry
    )

    kv_sum = row_sum_end(kv_state).astype(bf16)
    o_high = row_sum_next(o_high)
    q_high = row_sum_start(q_high, 0)
    total = [kv_sum] + [to_xor_cols(kv_sum, k) for k in range(1, cols)]
    up_grad = row_sum_end(u_state)
    piece = outs[cols - 1].astype(f32) + out_carry.astype(f32)
    output = xor_order((middle + keep * piece).astype(bf16), target, blocks, 1)
    total, o_high[2], q_high[1], output, up_grad, gains = fence(
        total, o_high[2], q_high[1], output, up_grad, gains
    )

    def col_sum(total, axis):
        pieces = xor_blocks(jnp.split(total.astype(bf16), cols, axis), c)
        return [pieces[0]] + [to_xor_cols(pieces[k], k) for k in range(1, cols)]

    def added(values):
        return tree_sum([x.astype(f32) for x in values])

    total = tree_sum([x.astype(f32) for x in total]).astype(bf16)
    one = to_near(total, 0)
    q_low, q_high = row_sum_next(q_low), row_sum_next(q_high)
    out_sum = jnp.concatenate([row_sum_end(o_low), row_sum_end(o_high)], 0)
    gains = shared(gains, hops[2:4])
    one, q_low[2], q_high[2], out_sum, gains = fence(one, q_low[2], q_high[2], out_sum, gains)
    two = to_near(jnp.concatenate([total, one], 0), 1)
    gains = shared(gains, hops[4:])
    out_parts = col_sum(out_sum, 0)
    q_sum = jnp.concatenate([row_sum_end(q_low), row_sum_end(q_high)], 1)
    two, out_parts, q_sum, gains = fence(two, out_parts, q_sum, gains)
    mine = jnp.concatenate([total, one, two], 0)
    theirs = to_core(mine)
    q_parts = col_sum(q_sum, 1)
    out_grad = added(out_parts)
    theirs, out_grad = fence(theirs, out_grad)
    found = blank((width, 2 * kv_width))
    for e, part in enumerate((mine, theirs)):
        near, far = (first, 3 - first) if e == 0 else (3 - first, first)
        for n, j in enumerate((0, near, far, 3)):
            at = ((d ^ e) * rows + (r ^ j)) * step
            found = put(found, part[n * step : (n + 1) * step], 0, at, 0)
    found = found.astype(f32)
    key_grad, value_grad = found[:, :kv_width], found[:, kv_width:]
    q_parts, key_grad, value_grad = fence(q_parts, key_grad, value_grad)
    query_grad = added(q_parts)
    return (
        output,
        input_grad,
        gains[0],
        gains[1],
        query_grad,
        key_grad,
        value_grad,
        out_grad,
        gate_grad,
        up_grad,
        down_grad,
    )


def solution(mesh):
    return jax.shard_map(
        local,
        mesh=mesh,
        in_specs=(
            P(("dp", "rows", "cols"), None),
            P(),
            P(),
            P("rows", "cols"),
            P("rows", None),
            P("rows", None),
            P(None, "rows"),
            P("rows", "cols"),
            P("rows", "cols"),
            P("cols", "rows"),
            P(("dp", "rows"), None),
            P(("dp", "rows")),
            P(("dp", "rows", "cols"), None),
        ),
        out_specs=(
            P(("dp", "rows", "cols"), None),
            P(("dp", "rows", "cols"), None),
            P(),
            P(),
            P(("dp", "rows"), "cols"),
            P(),
            P(),
            P("cols", ("dp", "rows")),
            P(("dp", "rows"), "cols"),
            P(("dp", "rows"), "cols"),
            P("cols", ("dp", "rows")),
        ),
        check_vma=False,
    )
```

time: 922 us -> 599 us (0.65)
  Pallas kernels: 0 us -> 179 us
  matrix products: 174 us -> 9.24 us
  other arithmetic: 159 us -> 58.2 us
  waiting for transfers between devices: 288 us -> 201 us
  local copies, waits for them, and re-layouts: 109 us -> 49.6 us
  starting transfers between devices: 132 us -> 87.1 us
  blocking collectives: 40 us -> 0 us
    pallas_call x0 -> x33, Pallas kernels: none -> 179 us  [the longest x12 65.2 us: token_sum(): call(kernel, (pl.cdiv(rows_out, tile),), specs, out, jax.ShapeDtypeStruct...]
    ppermute x48 -> x2, waiting for transfers between devices: 176 us -> 8.62 us  [to_rows(): return lax.ppermute(value, 'rows', [(i, i ^ a) for i in range(rows)])]
    dot_general x36 -> x5, matrix products: 149 us -> 9.24 us  [dot(): lax.dot_general(left, right, ((dims[:1], dims[1:]), ((), ())), preferred_...]
    ppermute x0 -> x28, waiting for transfers between devices: none -> 59.4 us  [to_near(): return lax.ppermute(value, ('dp', 'rows'), pairs)]
    unnamed x413 -> x194, local copies, waits for them, and re-layouts: 74.4 us -> 23.5 us
    psum x1 -> x0, blocking collectives: 40 us -> none  [local(): gains = lax.psum(xor_order(gains, place, blocks, 1), ('dp', 'rows', 'cols'))]
    select_n x30 -> x3, other arithmetic: 34.6 us -> 1.3 us  [xor_blocks(): jnp.where(swap, blocks[j ^ bit], blocks[j])]
    concatenate x33 -> x22, other arithmetic: 41.2 us -> 8.28 us  [the longest x8 5.72 us: row_sum_start(): jnp.concatenate([jnp.where(d == 0, pieces[1], pieces[2]), pieces[3]], axis)]
  transfers between devices with their start and end apart: 108 -> 79, of which waited for: 38 -> 31; matrix products, arithmetic and copies ran while one was open for 46% -> 15% of each run, Pallas kernels for 0% -> 30%
where the time goes in v2:
time: 599 us; the launch traced here: 588 us
  waiting for transfers between devices  201 us (34%)
  Pallas kernels  179 us (30%)
  starting transfers between devices  87.1 us (15%)
  other arithmetic  58.2 us (10%)
  local copies, waits for them, and re-layouts  49.6 us (8%)
  matrix products  9.24 us (2%)
    pallas_call x12, Pallas kernels, token_sum(): call(kernel, (pl.cdiv(rows_out, tile),), specs, out, jax.ShapeDtypeStruct...  65.2 us
    ppermute x28, waiting for transfers between devices, to_near(): return lax.ppermute(value, ('dp', 'rows'), pairs)  59.4 us
    pallas_call x9, Pallas kernels, rows_product(): call(kernel, (columns // tile,), specs, pl.BlockSpec((count, tile), lambd...  57 us
    ppermute x12, waiting for transfers between devices, to_cols(): lax.ppermute(value, 'cols', [(i, (i + k) % cols) for i in range(cols)])  55.3 us
    ppermute x14, waiting for transfers between devices, to_xor_cols(): return lax.ppermute(value, 'cols', [(i, i ^ k) for i in range(cols)])  49 us
    pallas_call x2, Pallas kernels, feed_through(): call(through_kernel, (pl.cdiv(units, tile),), [fixed((count, width))] * 2...  25.6 us
    ppermute x4, waiting for transfers between devices, along(): lax.ppermute(value, 'cols', [(i, i + k) for i in range(cols) if 0 <= i +...  24.4 us
    unnamed x194, local copies, waits for them, and re-layouts  23.5 us
  transfers between devices with their start and end apart: 79, of which 31 were waited for; matrix products, arithmetic and copies ran while one was open for 15% of the time, Pallas kernels for 30%

profile of v2, /device:TPU:11, one launch (start us, length us, event | category | flops | bytes accessed | tf_op | source)
XLA Modules:
  0.0 588.0 jit_solution(1175384661981949783)
XLA Ops:
  22.1 4.8 collective-permute-done.4
  26.9 7.0 %collective-permute-done.5 = bf16[2048,256]{1,0:T(8,128)(2,1)S(1)} collective-permute-done((bf16[2048,256]{1,0:T(8,128)(2,1)S(1)}, bf16[2048,256]{1,0:T(8,128)(2,1)S(1)}, u32[]{:S(2)}, u32[]{:S(2)}) %collective-permute-start.5) | collective-permute-done | bytes 1048608 | tf_op jit(solution)/shard_map/ppermute | solution.py:389
  40.0 9.3 %collective-permute-done.6 = bf16[256,2048]{1,0:T(8,128)(2,1)S(1)} collective-permute-done((bf16[256,2048]{1,0:T(8,128)(2,1)S(1)}, bf16[256,2048]{1,0:T(8,128)(2,1)S(1)}, u32[]{:S(2)}, u32[]{:S(2)}) %collective-permute-start.6) | collective-permute-done | bytes 1048608 | tf_op jit(solution)/shard_map/ppermute | solution.py:389
  52.5 9.8 %collective-permute-done.16.f_ref.refs_3_ = bf16[256,2048]{1,0:T(8,128)(2,1)S(1)} collective-permute-done((bf16[256,2048]{1,0:T(8,128)(2,1)S(1)}, bf16[256,2048]{1,0:T(8,128)(2,1)S(1)}, u32[]{:S(2)}, u32[]{:S(2)}) %collective-permute-start.16) | collective-permute-done | bytes 1048608 | tf_op jit(solution)/shard_map/ppermute | solution.py:397
  62.3 5.2 collective-permute-start.17
  70.1 8.1 %collective-permute-done.17 = bf16[256,512]{1,0:T(8,128)(2,1)S(1)} collective-permute-done((bf16[256,512]{1,0:T(8,128)(2,1)S(1)}, bf16[256,512]{1,0:T(8,128)(2,1)S(1)}, u32[]{:S(2)}, u32[]{:S(2)}) %collective-permute-start.17) | collective-permute-done | bytes 262176 | tf_op jit(solution)/shard_map/ppermute | solution.py:400
  78.2 5.6 collective-permute-done.18
  96.9 10.9 %shard_map.214 = (bf16[256,2048]{1,0:T(8,128)(2,1)S(1)}, bf16[256,2048]{1,0:T(8,128)(2,1)S(1)}, f32[16,1,256]{2,1,0:T(1,128)S(1)}) custom-call(f32[256,2048]{1,0:T(8,128)S(1)} %fusion.39.pre_ref, bf16[768,512]{1,0:T(8,128)(2,1)S(1)} %constant_dynamic-update-slice_fusion.3.k_ref.v_ref, bf16[768,512]{1,0:T(8,128)(2,1)S(1)} %constant_dynamic-update-slice_fusion.3.k_ref.v_ref, ...), custom_call_target="tpu_custom_call" | custom-call | tf_op jit(solution)/shard_map/pallas_call | solution.py:68
  108.3 15.1 %collective-permute-done.14 = bf16[512,1408]{1,0:T(8,128)(2,1)S(1)} collective-permute-done((bf16[512,1408]{1,0:T(8,128)(2,1)S(1)}, bf16[512,1408]{1,0:T(8,128)(2,1)S(1)}, u32[]{:S(2)}, u32[]{:S(2)}) %collective-permute-start.14) | collective-permute-done | bytes 1441824 | tf_op jit(solution)/shard_map/ppermute | solution.py:389
  123.4 6.3 %collective-permute-done.13 = bf16[4096,256]{1,0:T(8,128)(2,1)} collective-permute-done((bf16[4096,256]{1,0:T(8,128)(2,1)}, bf16[4096,256]{1,0:T(8,128)(2,1)}, u32[]{:S(2)}, u32[]{:S(2)}) %collective-permute-start.13) | collective-permute-done | bytes 2097184 | tf_op jit(solution)/shard_map/ppermute | solution.py:389
  141.5 14.5 %collective-permute-done.24 = bf16[256,2048]{1,0:T(8,128)(2,1)} collective-permute-done((bf16[256,2048]{1,0:T(8,128)(2,1)S(1)}, bf16[256,2048]{1,0:T(8,128)(2,1)}, u32[]{:S(2)}, u32[]{:S(2)}) %collective-permute-start.24) | collective-permute-done | bytes 1048608 | tf_op jit(solution)/shard_map/ppermute | solution.py:397
  160.3 4.9 collective-permute-done.25
  165.1 14.7 %collective-permute-done.26.refs_0_ = bf16[256,2048]{1,0:T(8,128)(2,1)S(1)} collective-permute-done((bf16[256,2048]{1,0:T(8,128)(2,1)S(1)}, bf16[256,2048]{1,0:T(8,128)(2,1)S(1)}, u32[]{:S(2)}, u32[]{:S(2)}) %collective-permute-start.26) | collective-permute-done | bytes 1048608 | tf_op jit(solution)/shard_map/ppermute | solution.py:397
  193.1 15.9 %collective-permute-done.29.h_ref.refs_1_ = bf16[256,2048]{1,0:T(8,128)(2,1)S(1)} collective-permute-done((bf16[256,2048]{1,0:T(8,128)(2,1)S(1)}, bf16[256,2048]{1,0:T(8,128)(2,1)S(1)}, u32[]{:S(2)}, u32[]{:S(2)}) %collective-permute-start.29) | collective-permute-done | bytes 1048608 | tf_op jit(solution)/shard_map/ppermute | solution.py:397
  214.4 10.3 %shard_map.221 = (bf16[256,1408]{1,0:T(8,128)(2,1)S(1)}, bf16[256,1408]{1,0:T(8,128)(2,1)S(1)}, bf16[256,1408]{1,0:T(8,128)(2,1)S(1)}) custom-call(bf16[256,2048]{1,0:T(8,128)(2,1)S(1)} %collective-permute-done.29.h_ref.refs_1_, bf16[256,2048]{1,0:T(8,128)(2,1)S(1)} %collective-permute-done.19.f_ref.refs_4_, bf16[2048,1408]{1,0:T(8,128)(2,1)} %copy-done.35, ...), custom_call_target="tpu_custom_call" | custom-call | tf_op jit(solution)/shard_map/pallas_call | solution.py:193
  225.6 6.9 %shard_map.219 = (bf16[256,1408]{1,0:T(8,128)(2,1)S(1)}, bf16[256,1408]{1,0:T(8,128)(2,1)S(1)}, bf16[256,1408]{1,0:T(8,128)(2,1)S(1)}) custom-call(bf16[256,2048]{1,0:T(8,128)(2,1)S(1)} %collective-permute-done.16.f_ref.refs_3_, f32[256,1408]{1,0:T(8,128)S(1)} %fusion.41.gate_ref, f32[256,1408]{1,0:T(8,128)S(1)} %fusion.42.up_ref, ...), custom_call_target="tpu_custom_call" | custom-call | tf_op jit(solution)/shard_map/pallas_call | solution.py:217
  232.6 7.6 %shard_map.220 = bf16[256,2048]{1,0:T(8,128)(2,1)S(1)} custom-call(bf16[256,1408]{1,0:T(8,128)(2,1)S(1)} %get-tuple-element.396.refs_0_.refs_3_, bf16[256,1408]{1,0:T(8,128)(2,1)S(1)} %get-tuple-element.399.refs_1_.refs_3_, bf16[2048,1408]{1,0:T(8,128)(2,1)} %copy-done.35, bf16[2048,1408]{1,0:T(8,128)(2,1)} %copy-done.34), custom_call_target="tpu_custom_call" | custom-call | tf_op jit(solution)/shard_map/pallas_call | solution.py:244
  242.5 7.7 %shard_map.222 = f32[256,2048]{1,0:T(8,128)S(1)} custom-call(bf16[256,1408]{1,0:T(8,128)(2,1)S(1)} %get-tuple-element.397.refs_0_.refs_4_, bf16[256,1408]{1,0:T(8,128)(2,1)S(1)} %get-tuple-element.400.refs_1_.refs_4_, bf16[2048,1408]{1,0:T(8,128)(2,1)} %copy-done.35, bf16[2048,1408]{1,0:T(8,128)(2,1)} %copy-done.34), custom_call_target="tpu_custom_call" | custom-call | tf_op jit(solution)/shard_map/pallas_call | solution.py:244
  252.9 15.2 %shard_map.223 = (bf16[512,1408]{1,0:T(8,128)(2,1)S(1)}, bf16[512,1408]{1,0:T(8,128)(2,1)S(1)}, bf16[512,1408]{1,0:T(8,128)(2,1)S(1)}) custom-call(bf16[512,2048]{1,0:T(8,128)(2,1)} %constant_dynamic-update-slice_fusion.7.h_ref.refs_2_, bf16[512,2048]{1,0:T(8,128)(2,1)} %copy-done.43, bf16[2048,1408]{1,0:T(8,128)(2,1)} %copy-done.35, ...), custom_call_target="tpu_custom_call" | custom-call | tf_op jit(solution)/shard_map/pallas_call | solution.py:193
  268.1 7.1 %shard_map.224 = bf16[1408,1024]{1,0:T(8,128)(2,1)} custom-call(bf16[256,1408]{1,0:T(8,128)(2,1)S(1)} %copy-done.13, bf16[256,1408]{1,0:T(8,128)(2,1)S(1)} %copy-done.4, bf16[512,1408]{1,0:T(8,128)(2,1)S(1)} %get-tuple-element.412.refs_2_.refs_0_, bf16[256,2048]{1,0:T(8,128)(2,1)S(1)} %collective-permute-done.16.f_ref.refs_3_, ...), custom_call_target="tpu_custom_call" | custom-call | tf_op jit(solution)/shard_map/pallas_call | solution.py:275
  278.3 4.2 collective-permute-start.33
  282.5 6.9 %shard_map.225 = f32[256,2048]{1,0:T(8,128)S(1)} custom-call(bf16[512,1408]{1,0:T(8,128)(2,1)S(1)} %get-tuple-element.392.refs_0_.refs_5_, bf16[512,1408]{1,0:T(8,128)(2,1)S(1)} %get-tuple-element.393.refs_1_.refs_5_, bf16[2048,1408]{1,0:T(8,128)(2,1)} %copy-done.35, bf16[2048,1408]{1,0:T(8,128)(2,1)} %copy-done.34), custom_call_target="tpu_custom_call" | custom-call | tf_op jit(solution)/shard_map/pallas_call | solution.py:244
  289.4 6.3 %shard_map.227 = bf16[1024,1408]{1,0:T(8,128)(2,1)} custom-call(bf16[256,2048]{1,0:T(8,128)(2,1)S(1)} %collective-permute-done.26.refs_0_, bf16[256,2048]{1,0:T(8,128)(2,1)S(1)} %collective-permute-done.29.h_ref.refs_1_, bf16[512,2048]{1,0:T(8,128)(2,1)} %constant_dynamic-update-slice_fusion.7.h_ref.refs_2_, bf16[256,1408]{1,0:T(8,128)(2,1)S(1)} %copy-done.19, ...), custom_call_target="tpu_custom_call" | custom-call | tf_op jit(solution)/shard_map/pallas_call | solution.py:275
  296.8 6.3 %shard_map.228 = bf16[1024,1408]{1,0:T(8,128)(2,1)} custom-call(bf16[256,2048]{1,0:T(8,128)(2,1)S(1)} %collective-permute-done.26.refs_0_, bf16[256,2048]{1,0:T(8,128)(2,1)S(1)} %collective-permute-done.29.h_ref.refs_1_, bf16[512,2048]{1,0:T(8,128)(2,1)} %constant_dynamic-update-slice_fusion.7.h_ref.refs_2_, bf16[256,1408]{1,0:T(8,128)(2,1)S(1)} %copy-done.16, ...), custom_call_target="tpu_custom_call" | custom-call | tf_op jit(solution)/shard_map/pallas_call | solution.py:275
  303.1 7.8 %shard_map.226 = bf16[1408,1024]{1,0:T(8,128)(2,1)} custom-call(bf16[256,1408]{1,0:T(8,128)(2,1)S(1)} %copy-done.14, bf16[256,1408]{1,0:T(8,128)(2,1)S(1)} %copy-done.5, bf16[512,1408]{1,0:T(8,128)(2,1)S(1)} %get-tuple-element.412.refs_2_.refs_0_, bf16[256,2048]{1,0:T(8,128)(2,1)S(1)} %collective-permute-done.16.f_ref.refs_3_, ...), custom_call_target="tpu_custom_call" | custom-call | tf_op jit(solution)/shard_map/pallas_call | solution.py:275
  315.7 5.4 shard_map.232
  321.1 7.1 %shard_map.229 = f32[256,2048]{1,0:T(8,128)S(1)} custom-call(bf16[512,1408]{1,0:T(8,128)(2,1)S(1)} %get-tuple-element.392.refs_0_.refs_5_, bf16[512,1408]{1,0:T(8,128)(2,1)S(1)} %get-tuple-element.393.refs_1_.refs_5_, bf16[2048,1408]{1,0:T(8,128)(2,1)} %copy-done.35, bf16[2048,1408]{1,0:T(8,128)(2,1)} %copy-done.34), custom_call_target="tpu_custom_call" | custom-call | tf_op jit(solution)/shard_map/pallas_call | solution.py:244
  328.2 6.9 %shard_map.230 = bf16[1024,1408]{1,0:T(8,128)(2,1)} custom-call(bf16[256,2048]{1,0:T(8,128)(2,1)S(1)} %collective-permute-done.26.refs_0_, bf16[256,2048]{1,0:T(8,128)(2,1)S(1)} %collective-permute-done.29.h_ref.refs_1_, bf16[512,2048]{1,0:T(8,128)(2,1)} %constant_dynamic-update-slice_fusion.7.h_ref.refs_2_, bf16[256,1408]{1,0:T(8,128)(2,1)S(1)} %copy-done.20, ...), custom_call_target="tpu_custom_call" | custom-call | tf_op jit(solution)/shard_map/pallas_call | solution.py:275
  335.1 6.8 %shard_map.231 = bf16[1024,1408]{1,0:T(8,128)(2,1)} custom-call(bf16[256,2048]{1,0:T(8,128)(2,1)S(1)} %collective-permute-done.26.refs_0_, bf16[256,2048]{1,0:T(8,128)(2,1)S(1)} %collective-permute-done.29.h_ref.refs_1_, bf16[512,2048]{1,0:T(8,128)(2,1)} %constant_dynamic-update-slice_fusion.7.h_ref.refs_2_, bf16[256,1408]{1,0:T(8,128)(2,1)S(1)} %copy-done.17, ...), custom_call_target="tpu_custom_call" | custom-call | tf_op jit(solution)/shard_map/pallas_call | solution.py:275
  351.4 5.1 shard_map.234
  356.4 5.6 shard_map.233.back_ref
  362.1 4.6 shard_map.235
  366.7 5.9 shard_map.236
  383.9 13.5 %shard_map.237 = (bf16[256,2048]{1,0:T(8,128)(2,1)S(1)}, f32[768,256]{1,0:T(8,128)S(1)}, f32[768,256]{1,0:T(8,128)S(1)}) custom-call(bf16[256,2048]{1,0:T(8,128)(2,1)S(1)} %copy-done.30, bf16[768,512]{1,0:T(8,128)(2,1)S(1)} %constant_dynamic-update-slice_fusion.3.k_ref.v_ref, bf16[768,512]{1,0:T(8,128)(2,1)S(1)} %constant_dynamic-update-slice_fusion.3.k_ref.v_ref, ...), custom_call_target="tpu_custom_call" | custom-call | tf_op jit(solution)/shard_map/pallas_call | solution.py:128
  403.6 7.6 %shard_map.239 = bf16[2048,1024]{1,0:T(8,128)(2,1)} custom-call(bf16[256,2048]{1,0:T(8,128)(2,1)S(1)} %copy-done.22, bf16[256,2048]{1,0:T(8,128)(2,1)S(1)} %get-tuple-element.418.refs_0_.refs_1_, bf16[2048,1024]{1,0:T(8,128)(2,1)} %copy-done.56), custom_call_target="tpu_custom_call" | custom-call | tf_op jit(solution)/shard_map/pallas_call | solution.py:275
  427.1 4.2 collective-permute-done.46
  431.3 6.6 %collective-permute-done.47 = bf16[256,512]{1,0:T(8,128)(2,1)S(1)} collective-permute-done((bf16[256,512]{1,0:T(8,128)(2,1)S(1)}, bf16[256,512]{1,0:T(8,128)(2,1)S(1)}, u32[]{:S(2)}, u32[]{:S(2)}) %collective-permute-start.47) | collective-permute-done | bytes 262176 | tf_op jit(solution)/shard_map/ppermute | solution.py:400
  443.7 3.9 collective-permute-start.59
  450.4 5.6 shard_map.242
  461.1 6.1 %shard_map.243 = f32[256,2048]{1,0:T(8,128)S(1)} custom-call(bf16[256,2048]{1,0:T(8,128)(2,1)S(1)} %get-tuple-element.432.refs_1_.refs_0_, bf16[256,512]{1,0:T(8,128)(2,1)S(1)} %pad_maximum_fusion.20.refs_1_, bf16[2048,2048]{1,0:T(8,128)(2,1)} %copy-done.37, bf16[2048,512]{1,0:T(8,128)(2,1)S(1)} %copy-done.2), custom_call_target="tpu_custom_call" | custom-call | tf_op jit(solution)/shard_map/pallas_call | solution.py:244
  474.4 4.0 collective-permute-done.54
  486.9 7.1 %collective-permute-done.57 = f32[2,2048]{1,0:T(2,128)S(1)} collective-permute-done((f32[2,2048]{1,0:T(2,128)S(1)}, f32[2,2048]{1,0:T(2,128)S(1)}, u32[]{:S(2)}, u32[]{:S(2)}) %collective-permute-start.57) | collective-permute-done | bytes 16416 | tf_op jit(solution)/shard_map/ppermute | solution.py:382
  505.0 4.5 collective-permute-done.64
  509.5 8.4 %collective-permute-done.61 = bf16[256,512]{1,0:T(8,128)(2,1)S(1)} collective-permute-done((bf16[256,512]{1,0:T(8,128)(2,1)S(1)}, bf16[256,512]{1,0:T(8,128)(2,1)S(1)}, u32[]{:S(2)}, u32[]{:S(2)}) %collective-permute-start.61) | collective-permute-done | bytes 262176 | tf_op jit(solution)/shard_map/ppermute | solution.py:405
  531.7 5.6 collective-permute-done.67
  545.0 17.3 %collective-permute-done.74 = f32[2,2048]{1,0:T(2,128)S(1)} collective-permute-done((f32[2,2048]{1,0:T(2,128)S(1)}, f32[2,2048]{1,0:T(2,128)S(1)}, u32[]{:S(2)}, u32[]{:S(2)}) %collective-permute-start.74) | collective-permute-done | bytes 16416 | tf_op jit(solution)/shard_map/ppermute | solution.py:405
  565.7 4.0 collective-permute-start.78
  574.4 12.2 %collective-permute-done.77 = bf16[256,512]{1,0:T(8,128)(2,1)S(1)} collective-permute-done((bf16[256,512]{1,0:T(8,128)(2,1)S(1)}, bf16[256,512]{1,0:T(8,128)(2,1)S(1)}, u32[]{:S(2)}, u32[]{:S(2)}) %collective-permute-start.77) | collective-permute-done | bytes 262176 | tf_op jit(solution)/shard_map/ppermute | solution.py:405
  (550 shorter events, 207.6 us)
Async XLA Ops:
  1.9 20.1 %collective-permute-start.3 = (bf16[256,512]{1,0:T(8,128)(2,1)S(1)}, bf16[256,512]{1,0:T(8,128)(2,1)}, u32[]{:S(2)}, u32[]{:S(2)}) collective-permute-start(bf16[256,512]{1,0:T(8,128)(2,1)S(1)} %slice_select_fusion), channel_id=1, source_target_pairs={{0,2},{1,3},{2,0},{3,1},{4,6},{5,7},{6,4},{7,5},{8,10},{9,11},{10,... | collective-permute-start | bytes 786440 | tf_op jit(solution)/shard_map/ppermute | solution.py:405
  4.3 22.6 %collective-permute-start.4 = (bf16[256,512]{1,0:T(8,128)(2,1)S(1)}, bf16[256,512]{1,0:T(8,128)(2,1)}, u32[]{:S(2)}, u32[]{:S(2)}) collective-permute-start(bf16[256,512]{1,0:T(8,128)(2,1)S(1)} %slice_select_fusion), channel_id=1, source_target_pairs={{0,3},{1,2},{2,1},{3,0},{4,7},{5,6},{6,5},{7,4},{8,11},{9,10},{10,... | collective-permute-start | bytes 786440 | tf_op jit(solution)/shard_map/ppermute | solution.py:405
  14.5 19.3 %collective-permute-start.5 = (bf16[2048,256]{1,0:T(8,128)(2,1)S(1)}, bf16[2048,256]{1,0:T(8,128)(2,1)S(1)}, u32[]{:S(2)}, u32[]{:S(2)}) collective-permute-start(bf16[2048,256]{1,0:T(8,128)(2,1)S(1)} %get-tuple-element.267), channel_id=1, source_target_pairs={{0,4},{4,0},{8,12},{12,8},{16,24},{20,28},{24,16},{28,20},{1,5},{5... | collective-permute-start | bytes 3145736 | tf_op jit(solution)/shard_map/ppermute | solution.py:389
  18.4 20.6 %collective-permute-start.8 = (bf16[256,512]{1,0:T(8,128)(2,1)S(1)}, bf16[256,512]{1,0:T(8,128)(2,1)S(1)}, u32[]{:S(2)}, u32[]{:S(2)}) collective-permute-start(bf16[256,512]{1,0:T(8,128)(2,1)S(1)} %collective-permute-done), channel_id=1, source_target_pairs={{0,16},{16,0},{1,17},{17,1},{2,18},{18,2},{3,19},{19,3},{4,20},{20... | collective-permute-start | bytes 786440 | tf_op jit(solution)/shard_map/ppermute | solution.py:394
  37.5 24.8 %collective-permute-start.16 = (bf16[256,2048]{1,0:T(8,128)(2,1)S(1)}, bf16[256,2048]{1,0:T(8,128)(2,1)S(1)}, u32[]{:S(2)}, u32[]{:S(2)}) collective-permute-start(bf16[256,2048]{1,0:T(8,128)(2,1)S(1)} %multiply_convert_fusion.2), channel_id=1, source_target_pairs={{0,1},{1,2},{2,3},{3,0},{4,5},{5,6},{6,7},{7,4},{8,9},{9,10},{10,1... | collective-permute-start | bytes 3145736 | tf_op jit(solution)/shard_map/ppermute | solution.py:397
  49.4 36.8 %collective-permute-start.12 = (bf16[256,2048]{1,0:T(8,128)(2,1)S(1)}, bf16[256,2048]{1,0:T(8,128)(2,1)S(1)}, u32[]{:S(2)}, u32[]{:S(2)}) collective-permute-start(bf16[256,2048]{1,0:T(8,128)(2,1)S(1)} %collective-permute-done.6), channel_id=1, source_target_pairs={{0,16},{16,0},{1,17},{17,1},{2,18},{18,2},{3,19},{19,3},{4,20},{20... | collective-permute-start | bytes 3145736 | tf_op jit(solution)/shard_map/ppermute | solution.py:394
  49.5 36.9 %collective-permute-start.10 = (bf16[512,2048]{1,0:T(8,128)(2,1)S(1)}, bf16[512,2048]{1,0:T(8,128)(2,1)S(1)}, u32[]{:S(2)}, u32[]{:S(2)}) collective-permute-start(bf16[512,2048]{1,0:T(8,128)(2,1)S(1)} %pad_maximum_fusion.1), channel_id=1, source_target_pairs={{0,8},{4,12},{8,0},{12,4},{16,20},{20,16},{24,28},{28,24},{1,9},{5... | collective-permute-start | bytes 6291464 | tf_op jit(solution)/shard_map/ppermute | solution.py:389
  69.6 16.8 %collective-permute-start.11 = (bf16[1408,256]{1,0:T(8,128)(2,1)S(1)}, bf16[1408,256]{1,0:T(8,128)(2,1)S(1)}, u32[]{:S(2)}, u32[]{:S(2)}) collective-permute-start(bf16[1408,256]{1,0:T(8,128)(2,1)S(1)} %get-tuple-element.316), channel_id=1, source_target_pairs={{0,4},{4,0},{8,12},{12,8},{16,24},{20,28},{24,16},{28,20},{1,5},{5... | collective-permute-start | bytes 2162696 | tf_op jit(solution)/shard_map/ppermute | solution.py:389
  83.8 24.5 %collective-permute-start.19 = (bf16[256,2048]{1,0:T(8,128)(2,1)S(1)}, bf16[256,2048]{1,0:T(8,128)(2,1)S(1)}, u32[]{:S(2)}, u32[]{:S(2)}) collective-permute-start(bf16[256,2048]{1,0:T(8,128)(2,1)S(1)} %collective-permute-done.16.f_ref.refs_3_), channel_id=1, source_target_pairs={{0,1},{1,2},{2,3},{3,0},{4,5},{5,6},{6,7},{7,4},{8,9},{9,10},{10,1... | collective-permute-start | bytes 3145736 | tf_op jit(solution)/shard_map/ppermute | solution.py:397
  88.7 40.9 %collective-permute-start.13 = (bf16[4096,256]{1,0:T(8,128)(2,1)}, bf16[4096,256]{1,0:T(8,128)(2,1)}, u32[]{:S(2)}, u32[]{:S(2)}) collective-permute-start(bf16[4096,256]{1,0:T(8,128)(2,1)} %pad_maximum_fusion.2), channel_id=1, source_target_pairs={{0,8},{4,12},{8,0},{12,4},{16,20},{20,16},{24,28},{28,24},{1,9},{5... | collective-permute-start | bytes 6291464 | tf_op jit(solution)/shard_map/ppermute | solution.py:389
  89.6 33.8 %collective-permute-start.14 = (bf16[512,1408]{1,0:T(8,128)(2,1)S(1)}, bf16[512,1408]{1,0:T(8,128)(2,1)S(1)}, u32[]{:S(2)}, u32[]{:S(2)}) collective-permute-start(bf16[512,1408]{1,0:T(8,128)(2,1)S(1)} %pad_maximum_fusion.5), channel_id=1, source_target_pairs={{0,4},{4,0},{8,12},{12,8},{16,24},{20,28},{24,16},{28,20},{1,5},{5... | collective-permute-start | bytes 4325384 | tf_op jit(solution)/shard_map/ppermute | solution.py:389
  130.5 25.4 %collective-permute-start.22 = (bf16[512,1408]{1,0:T(8,128)(2,1)S(1)}, bf16[512,1408]{1,0:T(8,128)(2,1)}, u32[]{:S(2)}, u32[]{:S(2)}) collective-permute-start(bf16[512,1408]{1,0:T(8,128)(2,1)S(1)} %collective-permute-done.14), channel_id=1, source_target_pairs={{0,16},{16,0},{1,17},{17,1},{2,18},{18,2},{3,19},{19,3},{4,20},{20... | collective-permute-start | bytes 4325384 | tf_op jit(solution)/shard_map/ppermute | solution.py:394
  131.1 24.8 %collective-permute-start.24 = (bf16[256,2048]{1,0:T(8,128)(2,1)S(1)}, bf16[256,2048]{1,0:T(8,128)(2,1)}, u32[]{:S(2)}, u32[]{:S(2)}) collective-permute-start(bf16[256,2048]{1,0:T(8,128)(2,1)S(1)} %collective-permute-done.19.f_ref.refs_4_), channel_id=1, source_target_pairs={{0,1},{1,2},{2,3},{3,0},{4,5},{5,6},{6,7},{7,4},{8,9},{9,10},{10,1... | collective-permute-start | bytes 3145736 | tf_op jit(solution)/shard_map/ppermute | solution.py:397
  131.4 33.8 %collective-permute-start.25 = (bf16[1024,1408]{1,0:T(8,128)(2,1)S(1)}, bf16[1024,1408]{1,0:T(8,128)(2,1)}, u32[]{:S(2)}, u32[]{:S(2)}) collective-permute-start(bf16[1024,1408]{1,0:T(8,128)(2,1)S(1)} %pad_maximum_fusion), channel_id=1, source_target_pairs={{0,8},{4,12},{8,0},{12,4},{16,20},{20,16},{24,28},{28,24},{1,9},{5... | collective-permute-start | bytes 8650760 | tf_op jit(solution)/shard_map/ppermute | solution.py:389
  156.0 23.8 %collective-permute-start.26 = (bf16[256,2048]{1,0:T(8,128)(2,1)S(1)}, bf16[256,2048]{1,0:T(8,128)(2,1)S(1)}, u32[]{:S(2)}, u32[]{:S(2)}) collective-permute-start(bf16[256,2048]{1,0:T(8,128)(2,1)S(1)} %multiply_convert_fusion.1), channel_id=1, source_target_pairs={{0,1},{1,2},{2,3},{3,0},{4,5},{5,6},{6,7},{7,4},{8,9},{9,10},{10,1... | collective-permute-start | bytes 3145736 | tf_op jit(solution)/shard_map/ppermute | solution.py:397
  181.6 27.3 %collective-permute-start.27 = (bf16[2816,256]{1,0:T(8,128)(2,1)S(1)}, bf16[2816,256]{1,0:T(8,128)(2,1)S(1)}, u32[]{:S(2)}, u32[]{:S(2)}) collective-permute-start(bf16[2816,256]{1,0:T(8,128)(2,1)S(1)} %pad_maximum_fusion.6), channel_id=1, source_target_pairs={{0,8},{4,12},{8,0},{12,4},{16,20},{20,16},{24,28},{28,24},{1,9},{5... | collective-permute-start | bytes 4325384 | tf_op jit(solution)/shard_map/ppermute | solution.py:389
  182.2 26.8 %collective-permute-start.29 = (bf16[256,2048]{1,0:T(8,128)(2,1)S(1)}, bf16[256,2048]{1,0:T(8,128)(2,1)S(1)}, u32[]{:S(2)}, u32[]{:S(2)}) collective-permute-start(bf16[256,2048]{1,0:T(8,128)(2,1)S(1)} %collective-permute-done.26.refs_0_), channel_id=1, source_target_pairs={{0,1},{1,2},{2,3},{3,0},{4,5},{5,6},{6,7},{7,4},{8,9},{9,10},{10,1... | collective-permute-start | bytes 3145736 | tf_op jit(solution)/shard_map/ppermute | solution.py:397
  209.6 30.7 %collective-permute-start.31 = (bf16[256,2048]{1,0:T(8,128)(2,1)S(1)}, bf16[256,2048]{1,0:T(8,128)(2,1)S(1)}, u32[]{:S(2)}, u32[]{:S(2)}) collective-permute-start(bf16[256,2048]{1,0:T(8,128)(2,1)S(1)} %collective-permute-done.29.h_ref.refs_1_), channel_id=1, source_target_pairs={{0,1},{1,2},{2,3},{3,0},{4,5},{5,6},{6,7},{7,4},{8,9},{9,10},{10,1... | collective-permute-start | bytes 3145736 | tf_op jit(solution)/shard_map/ppermute | solution.py:397
  240.3 35.0 %collective-permute-start.32 = (bf16[256,2048]{1,0:T(8,128)(2,1)S(1)}, bf16[256,2048]{1,0:T(8,128)(2,1)}, u32[]{:S(2)}, u32[]{:S(2)}) collective-permute-start(bf16[256,2048]{1,0:T(8,128)(2,1)S(1)} %shard_map.220), channel_id=1, source_target_pairs={{0,1},{1,2},{2,3},{3,0},{4,5},{5,6},{6,7},{7,4},{8,9},{9,10},{10,1... | collective-permute-start | bytes 3145736 | tf_op jit(solution)/shard_map/ppermute | solution.py:397
  277.8 25.4 %collective-permute-start.34 = (bf16[1408,1024]{1,0:T(8,128)(2,1)}, bf16[1408,1024]{1,0:T(8,128)(2,1)}, u32[]{:S(2)}, u32[]{:S(2)}) collective-permute-start(bf16[1408,1024]{1,0:T(8,128)(2,1)} %shard_map.224), channel_id=1, source_target_pairs={{0,16},{16,0},{1,17},{17,1},{2,18},{18,2},{3,19},{19,3},{4,20},{20... | collective-permute-start | bytes 8650760 | tf_op jit(solution)/shard_map/ppermute | solution.py:394
  278.3 32.6 %collective-permute-start.33 = (bf16[256,2048]{1,0:T(8,128)(2,1)}, bf16[256,2048]{1,0:T(8,128)(2,1)S(1)}, u32[]{:S(2)}, u32[]{:S(2)}) collective-permute-start(bf16[256,2048]{1,0:T(8,128)(2,1)} %add_convert_fusion.4), channel_id=1, source_target_pairs={{0,1},{1,2},{2,3},{3,0},{4,5},{5,6},{6,7},{7,4},{8,9},{9,10},{10,1... | collective-permute-start | bytes 3145736 | tf_op jit(solution)/shard_map/ppermute | solution.py:397
  312.6 22.5 %collective-permute-start.38 = (bf16[1024,1408]{1,0:T(8,128)(2,1)}, bf16[1024,1408]{1,0:T(8,128)(2,1)}, u32[]{:S(2)}, u32[]{:S(2)}) collective-permute-start(bf16[1024,1408]{1,0:T(8,128)(2,1)} %shard_map.228), channel_id=1, source_target_pairs={{0,16},{16,0},{1,17},{17,1},{2,18},{18,2},{3,19},{19,3},{4,20},{20... | collective-permute-start | bytes 8650760 | tf_op jit(solution)/shard_map/ppermute | solution.py:394
  314.5 27.5 %collective-permute-start.36 = (bf16[1408,512]{1,0:T(8,128)(2,1)}, bf16[1408,512]{1,0:T(8,128)(2,1)}, u32[]{:S(2)}, u32[]{:S(2)}) collective-permute-start(bf16[1408,512]{1,0:T(8,128)(2,1)} %pad_maximum_fusion.7), channel_id=1, source_target_pairs={{0,4},{4,0},{8,12},{12,8},{16,24},{20,28},{24,16},{28,20},{1,5},{5... | collective-permute-start | bytes 4325384 | tf_op jit(solution)/shard_map/ppermute | solution.py:389
  314.7 27.2 %collective-permute-start.35 = (bf16[256,2048]{1,0:T(8,128)(2,1)}, bf16[256,2048]{1,0:T(8,128)(2,1)S(1)}, u32[]{:S(2)}, u32[]{:S(2)}) collective-permute-start(bf16[256,2048]{1,0:T(8,128)(2,1)} %add_convert_fusion.3), channel_id=1, source_target_pairs={{0,1},{1,2},{2,3},{3,0},{4,5},{5,6},{6,7},{7,4},{8,9},{9,10},{10,1... | collective-permute-start | bytes 3145736 | tf_op jit(solution)/shard_map/ppermute | solution.py:397
  344.7 29.3 %collective-permute-start.39 = (bf16[1408,256]{1,0:T(8,128)(2,1)}, bf16[1408,256]{1,0:T(8,128)(2,1)S(1)}, u32[]{:S(2)}, u32[]{:S(2)}) collective-permute-start(bf16[1408,256]{1,0:T(8,128)(2,1)} %add_convert_fusion.7), channel_id=1, source_target_pairs={{0,8},{4,12},{8,0},{12,4},{16,20},{20,16},{24,28},{28,24},{1,9},{5... | collective-permute-start | bytes 2162696 | tf_op jit(solution)/shard_map/ppermute | solution.py:389
  347.1 26.9 %collective-permute-start.40 = (bf16[512,1408]{1,0:T(8,128)(2,1)}, bf16[512,1408]{1,0:T(8,128)(2,1)}, u32[]{:S(2)}, u32[]{:S(2)}) collective-permute-start(bf16[512,1408]{1,0:T(8,128)(2,1)} %pad_maximum_fusion.8), channel_id=1, source_target_pairs={{0,4},{4,0},{8,12},{12,8},{16,24},{20,28},{24,16},{28,20},{1,5},{5... | collective-permute-start | bytes 4325384 | tf_op jit(solution)/shard_map/ppermute | solution.py:389
  348.3 25.7 %collective-permute-start.41 = (bf16[256,2048]{1,0:T(8,128)(2,1)}, bf16[256,2048]{1,0:T(8,128)(2,1)}, u32[]{:S(2)}, u32[]{:S(2)}) collective-permute-start(bf16[256,2048]{1,0:T(8,128)(2,1)} %shard_map.232), channel_id=1, source_target_pairs={{0,1},{1,2},{2,3},{3,0},{4,5},{5,6},{6,7},{7,4},{8,9},{9,10},{10,1... | collective-permute-start | bytes 3145736 | tf_op jit(solution)/shard_map/ppermute | solution.py:397
  374.0 27.6 %collective-permute-start.42 = (bf16[2048,1024]{1,0:T(8,128)(2,1)}, bf16[2048,1024]{1,0:T(8,128)(2,1)S(1)}, u32[]{:S(2)}, u32[]{:S(2)}) collective-permute-start(bf16[2048,1024]{1,0:T(8,128)(2,1)} %shard_map.234), channel_id=1, source_target_pairs={{0,16},{16,0},{1,17},{17,1},{2,18},{18,2},{3,19},{19,3},{4,20},{20... | collective-permute-start | bytes 12582920 | tf_op jit(solution)/shard_map/ppermute | solution.py:394
  376.7 34.5 %collective-permute-start.44 = (bf16[512,1408]{1,0:T(8,128)(2,1)}, bf16[512,1408]{1,0:T(8,128)(2,1)}, u32[]{:S(2)}, u32[]{:S(2)}) collective-permute-start(bf16[512,1408]{1,0:T(8,128)(2,1)} %pad_maximum_fusion.9), channel_id=1, source_target_pairs={{0,4},{4,0},{8,12},{12,8},{16,24},{20,28},{24,16},{28,20},{1,5},{5... | collective-permute-start | bytes 4325384 | tf_op jit(solution)/shard_map/ppermute | solution.py:389
  380.4 30.9 %collective-permute-start.45 = (bf16[256,2048]{1,0:T(8,128)(2,1)}, bf16[256,2048]{1,0:T(8,128)(2,1)}, u32[]{:S(2)}, u32[]{:S(2)}) collective-permute-start(bf16[256,2048]{1,0:T(8,128)(2,1)} %add_convert_fusion.2), channel_id=1, source_target_pairs={{0,1},{1,2},{2,3},{3,0},{4,5},{5,6},{6,7},{7,4},{8,9},{9,10},{10,1... | collective-permute-start | bytes 3145736 | tf_op jit(solution)/shard_map/ppermute | solution.py:397
  382.9 28.3 %collective-permute-start.43 = (bf16[256,1408]{1,0:T(8,128)(2,1)}, bf16[256,1408]{1,0:T(8,128)(2,1)}, u32[]{:S(2)}, u32[]{:S(2)}) collective-permute-start(bf16[256,1408]{1,0:T(8,128)(2,1)} %add_convert_fusion.6), channel_id=1, source_target_pairs={{0,8},{4,12},{8,0},{12,4},{16,20},{20,16},{24,28},{28,24},{1,9},{5... | collective-permute-start | bytes 2162696 | tf_op jit(solution)/shard_map/ppermute | solution.py:389
  411.2 26.6 %collective-permute-start.48 = (bf16[1024,2048]{1,0:T(8,128)(2,1)}, bf16[1024,2048]{1,0:T(8,128)(2,1)}, u32[]{:S(2)}, u32[]{:S(2)}) collective-permute-start(bf16[1024,2048]{1,0:T(8,128)(2,1)} %shard_map.238), channel_id=1, source_target_pairs={{0,16},{16,0},{1,17},{17,1},{2,18},{18,2},{3,19},{19,3},{4,20},{20... | collective-permute-start | bytes 12582920 | tf_op jit(solution)/shard_map/ppermute | solution.py:394
  415.4 22.4 %collective-permute-start.50 = (bf16[1024,512]{1,0:T(8,128)(2,1)S(1)}, bf16[1024,512]{1,0:T(8,128)(2,1)S(1)}, u32[]{:S(2)}, u32[]{:S(2)}) collective-permute-start(bf16[1024,512]{1,0:T(8,128)(2,1)S(1)} %pad_maximum_fusion.11), channel_id=1, source_target_pairs={{0,4},{4,0},{8,12},{12,8},{16,24},{20,28},{24,16},{28,20},{1,5},{5... | collective-permute-start | bytes 3145736 | tf_op jit(solution)/shard_map/ppermute | solution.py:389
  419.0 18.9 %collective-permute-start.49 = (bf16[256,1408]{1,0:T(8,128)(2,1)S(1)}, bf16[256,1408]{1,0:T(8,128)(2,1)S(1)}, u32[]{:S(2)}, u32[]{:S(2)}) collective-permute-start(bf16[256,1408]{1,0:T(8,128)(2,1)S(1)} %add_convert_fusion.5), channel_id=1, source_target_pairs={{0,8},{4,12},{8,0},{12,4},{16,20},{20,16},{24,28},{28,24},{1,9},{5... | collective-permute-start | bytes 2162696 | tf_op jit(solution)/shard_map/ppermute | solution.py:389
  431.3 25.9 %collective-permute-start.52 = (bf16[1024,512]{1,0:T(8,128)(2,1)S(1)}, bf16[1024,512]{1,0:T(8,128)(2,1)S(1)}, u32[]{:S(2)}, u32[]{:S(2)}) collective-permute-start(bf16[1024,512]{1,0:T(8,128)(2,1)S(1)} %pad_maximum_fusion.12), channel_id=1, source_target_pairs={{0,4},{4,0},{8,12},{12,8},{16,24},{20,28},{24,16},{28,20},{1,5},{5... | collective-permute-start | bytes 3145736 | tf_op jit(solution)/shard_map/ppermute | solution.py:389
  443.7 53.3 %collective-permute-start.59 = (bf16[256,2048]{1,0:T(8,128)(2,1)}, bf16[256,2048]{1,0:T(8,128)(2,1)}, u32[]{:S(2)}, u32[]{:S(2)}) collective-permute-start(bf16[256,2048]{1,0:T(8,128)(2,1)} %add_convert_fusion.1), channel_id=1, source_target_pairs={{0,1},{1,2},{2,3},{3,0},{4,5},{5,6},{6,7},{7,4},{8,9},{9,10},{10,1... | collective-permute-start | bytes 3145736 | tf_op jit(solution)/shard_map/ppermute | solution.py:397
  459.7 18.7 %collective-permute-start.54 = (bf16[512,1024]{1,0:T(8,128)(2,1)}, bf16[512,1024]{1,0:T(8,128)(2,1)}, u32[]{:S(2)}, u32[]{:S(2)}) collective-permute-start(bf16[512,1024]{1,0:T(8,128)(2,1)} %pad_maximum_fusion.13), channel_id=1, source_target_pairs={{0,4},{4,0},{8,12},{12,8},{16,24},{20,28},{24,16},{28,20},{1,5},{5... | collective-permute-start | bytes 3145736 | tf_op jit(solution)/shard_map/ppermute | solution.py:389
  473.9 23.1 %collective-permute-start.58 = (bf16[1024,256]{1,0:T(8,128)(2,1)S(1)}, bf16[1024,256]{1,0:T(8,128)(2,1)S(1)}, u32[]{:S(2)}, u32[]{:S(2)}) collective-permute-start(bf16[1024,256]{1,0:T(8,128)(2,1)S(1)} %get-tuple-element.580), channel_id=1, source_target_pairs={{0,8},{4,12},{8,0},{12,4},{16,20},{20,16},{24,28},{28,24},{1,9},{5... | collective-permute-start | bytes 1572872 | tf_op jit(solution)/shard_map/ppermute | solution.py:389
  479.4 17.7 %collective-permute-start.55 = (bf16[256,512]{1,0:T(8,128)(2,1)S(1)}, bf16[256,512]{1,0:T(8,128)(2,1)S(1)}, u32[]{:S(2)}, u32[]{:S(2)}) collective-permute-start(bf16[256,512]{1,0:T(8,128)(2,1)S(1)} %add_convert_fusion.14), channel_id=1, source_target_pairs={{0,8},{4,12},{8,0},{12,4},{16,20},{20,16},{24,28},{28,24},{1,9},{5... | collective-permute-start | bytes 786440 | tf_op jit(solution)/shard_map/ppermute | solution.py:389
  485.3 19.8 %collective-permute-start.63 = (bf16[1024,256]{1,0:T(8,128)(2,1)S(1)}, bf16[1024,256]{1,0:T(8,128)(2,1)S(1)}, u32[]{:S(2)}, u32[]{:S(2)}) collective-permute-start(bf16[1024,256]{1,0:T(8,128)(2,1)S(1)} %get-tuple-element.579), channel_id=1, source_target_pairs={{0,8},{4,12},{8,0},{12,4},{16,20},{20,16},{24,28},{28,24},{1,9},{5... | collective-permute-start | bytes 1572872 | tf_op jit(solution)/shard_map/ppermute | solution.py:389
  499.6 18.4 %collective-permute-start.61 = (bf16[256,512]{1,0:T(8,128)(2,1)S(1)}, bf16[256,512]{1,0:T(8,128)(2,1)S(1)}, u32[]{:S(2)}, u32[]{:S(2)}) collective-permute-start(bf16[256,512]{1,0:T(8,128)(2,1)S(1)} %add_convert_fusion.13), channel_id=1, source_target_pairs={{0,2},{1,3},{2,0},{3,1},{4,6},{5,7},{6,4},{7,5},{8,10},{9,11},{10,... | collective-permute-start | bytes 786440 | tf_op jit(solution)/shard_map/ppermute | solution.py:405
  502.3 19.1 %collective-permute-start.62 = (bf16[256,512]{1,0:T(8,128)(2,1)S(1)}, bf16[256,512]{1,0:T(8,128)(2,1)S(1)}, u32[]{:S(2)}, u32[]{:S(2)}) collective-permute-start(bf16[256,512]{1,0:T(8,128)(2,1)S(1)} %add_convert_fusion.13), channel_id=1, source_target_pairs={{0,3},{1,2},{2,1},{3,0},{4,7},{5,6},{6,5},{7,4},{8,11},{9,10},{10,... | collective-permute-start | bytes 786440 | tf_op jit(solution)/shard_map/ppermute | solution.py:405
  537.4 25.0 %collective-permute-start.70 = (bf16[512,512]{1,0:T(8,128)(2,1)S(1)}, bf16[512,512]{1,0:T(8,128)(2,1)S(1)}, u32[]{:S(2)}, u32[]{:S(2)}) collective-permute-start(bf16[512,512]{1,0:T(8,128)(2,1)S(1)} %pad_maximum_fusion.18), channel_id=1, source_target_pairs={{0,8},{4,12},{8,0},{12,4},{16,20},{20,16},{24,28},{28,24},{1,9},{5... | collective-permute-start | bytes 1572872 | tf_op jit(solution)/shard_map/ppermute | solution.py:389
  538.5 23.8 %collective-permute-start.71 = (bf16[512,256]{1,0:T(8,128)(2,1)S(1)}, bf16[512,256]{1,0:T(8,128)(2,1)S(1)}, u32[]{:S(2)}, u32[]{:S(2)}) collective-permute-start(bf16[512,256]{1,0:T(8,128)(2,1)S(1)} %get-tuple-element.618), channel_id=1, source_target_pairs={{0,1},{1,0},{2,3},{3,2},{4,5},{5,4},{6,7},{7,6},{8,9},{9,8},{10,11... | collective-permute-start | bytes 786440 | tf_op jit(solution)/shard_map/ppermute | solution.py:405
  538.6 23.7 %collective-permute-start.72 = (bf16[512,256]{1,0:T(8,128)(2,1)S(1)}, bf16[512,256]{1,0:T(8,128)(2,1)S(1)}, u32[]{:S(2)}, u32[]{:S(2)}) collective-permute-start(bf16[512,256]{1,0:T(8,128)(2,1)S(1)} %get-tuple-element.619), channel_id=1, source_target_pairs={{0,2},{1,3},{2,0},{3,1},{4,6},{5,7},{6,4},{7,5},{8,10},{9,11},{10,... | collective-permute-start | bytes 786440 | tf_op jit(solution)/shard_map/ppermute | solution.py:405
  541.0 21.3 %collective-permute-start.73 = (bf16[512,256]{1,0:T(8,128)(2,1)S(1)}, bf16[512,256]{1,0:T(8,128)(2,1)S(1)}, u32[]{:S(2)}, u32[]{:S(2)}) collective-permute-start(bf16[512,256]{1,0:T(8,128)(2,1)S(1)} %get-tuple-element.617), channel_id=1, source_target_pairs={{0,3},{1,2},{2,1},{3,0},{4,7},{5,6},{6,5},{7,4},{8,11},{9,10},{10,... | collective-permute-start | bytes 786440 | tf_op jit(solution)/shard_map/ppermute | solution.py:405
  541.2 21.0 %collective-permute-start.74 = (f32[2,2048]{1,0:T(2,128)S(1)}, f32[2,2048]{1,0:T(2,128)S(1)}, u32[]{:S(2)}, u32[]{:S(2)}) collective-permute-start(f32[2,2048]{1,0:T(2,128)S(1)} %add.450), channel_id=1, source_target_pairs={{0,2},{1,3},{2,0},{3,1},{4,6},{5,7},{6,4},{7,5},{8,10},{9,11},{10,... | collective-permute-start | bytes 49160 | tf_op jit(solution)/shard_map/ppermute | solution.py:405
  565.5 21.1 %collective-permute-start.77 = (bf16[256,512]{1,0:T(8,128)(2,1)S(1)}, bf16[256,512]{1,0:T(8,128)(2,1)S(1)}, u32[]{:S(2)}, u32[]{:S(2)}) collective-permute-start(bf16[256,512]{1,0:T(8,128)(2,1)S(1)} %get-tuple-element.613), channel_id=1, source_target_pairs={{0,3},{1,2},{2,1},{3,0},{4,7},{5,6},{6,5},{7,4},{8,11},{9,10},{10,... | collective-permute-start | bytes 786440 | tf_op jit(solution)/shard_map/ppermute | solution.py:405
  (125 other events, 1641.0 us)

commit v3 on v2

--- a/solution.py
+++ b/solution.py
@@ -223,62 +223,83 @@
     )(feed, gate, up, d_matrix)
 
 
-def rows_product(lefts, rights, turned, dtype, block=0, count=None):
-    n = len(lefts)
-    count = lefts[0].shape[0] if count is None else count
+def rows_products(sets, rights, turned, dtype, count):
+    n, many = len(rights), len(sets)
     columns = rights[0].shape[0 if turned else 1]
     tile = min(512, columns)
 
     def kernel(*refs):
-        total = 0.0
-        for k in range(n):
-            total = total + dot(refs[k][...], refs[n + k][...], (1, 1 if turned else 0))
-        refs[-1][...] = total.astype(dtype)
-
-    specs = [pl.BlockSpec((count, x.shape[1]), lambda i: (block, 0)) for x in lefts]
+        for m in range(many):
+            total = 0.0
+            for k in range(n):
+                total = total + dot(refs[n + n * m + k][...], refs[k][...], (1, 1 if turned else 0))
+            refs[m - many][...] = total.astype(dtype)
+
+    specs = []
     for x in rights:
         if turned:
             specs.append(pl.BlockSpec((tile, x.shape[1]), lambda i: (i, 0)))
         else:
             specs.append(pl.BlockSpec((x.shape[0], tile), lambda i: (0, i)))
+    operands = list(rights)
+    for lefts, block in sets:
+        specs += [pl.BlockSpec((count, x.shape[1]), lambda i, block=block: (block, 0)) for x in lefts]
+        operands += list(lefts)
     return call(
         kernel,
         (columns // tile,),
         specs,
-        pl.BlockSpec((count, tile), lambda i: (0, i)),
-        jax.ShapeDtypeStruct((count, columns), dtype),
-    )(*lefts, *rights)
-
-
-def token_sum(lefts, left_lanes, rights, right_lanes, received=None):
-    n = len(lefts)
+        [pl.BlockSpec((count, tile), lambda i: (0, i))] * many,
+        [jax.ShapeDtypeStruct((count, columns), dtype)] * many,
+    )(*operands)
+
+
+def rows_product(lefts, rights, turned, dtype, block=0, count=None):
+    count = lefts[0].shape[0] if count is None else count
+    return rows_products([(lefts, block)], rights, turned, dtype, count)[0]
+
+
+def token_sums(lefts, left_lanes, rights, right_lanes, received=None):
+    n, many = len(lefts), len(rights)
     start, rows_out = left_lanes
     tile = min(256, rows_out)
     base, columns = right_lanes
 
     def kernel(*refs):
-        total = dot(refs[0][...], refs[n][...], (0, 0))
-        for k in range(1, n):
-            total = total + dot(refs[k][...], refs[n + k][...], (0, 0))
-        if received is not None:
-            total = total + refs[2 * n][...].astype(f32)
-        refs[-1][...] = total.astype(bf16)
+        for k in range(n):
+            left = refs[k][...]
+            for m in range(many):
+                part = dot(left, refs[n * (m + 1) + k][...], (0, 0))
+                totals = [part] * many if k == 0 and m == 0 else totals
+                totals[m] = part if k == 0 else totals[m] + part
+        for m in range(many):
+            total = totals[m]
+            if received is not None:
+                total = total + refs[n * (many + 1) + m][...].astype(f32)
+            refs[m - many][...] = total.astype(bf16)
 
     first, second = start // tile, base // columns
     specs = [pl.BlockSpec((x.shape[0], tile), lambda i: (0, first + i)) for x in lefts]
-    specs += [pl.BlockSpec((x.shape[0], columns), lambda i: (0, second)) for x in rights]
+    operands = list(lefts)
+    for group in rights:
+        specs += [pl.BlockSpec((x.shape[0], columns), lambda i: (0, second)) for x in group]
+        operands += list(group)
     out = pl.BlockSpec((tile, columns), lambda i: (i, 0))
-    operands = list(lefts) + list(rights)
     if received is not None:
-        specs.append(out)
-        operands.append(received)
+        specs += [out] * many
+        operands += list(received)
     return call(
         kernel,
         (pl.cdiv(rows_out, tile),),
         specs,
-        out,
-        jax.ShapeDtypeStruct((rows_out, columns), bf16),
+        [out] * many,
+        [jax.ShapeDtypeStruct((rows_out, columns), bf16)] * many,
     )(*operands)
+
+
+def token_sum(lefts, left_lanes, rights, right_lanes, received=None):
+    received = None if received is None else [received]
+    return token_sums(lefts, left_lanes, [rights], right_lanes, received)[0]
 
 
 def nn(left, right):
@@ -448,8 +469,8 @@
     upstream = xor_order(cotangent, target, blocks, 1)
     feed_own = (keep * upstream).astype(bf16)
 
-    (kv_two, q_parts, normed, o_one, cosine, sine, feed_own, upstream, w_down, w_gate, w_up) = fence(
-        kv_two, q_parts, normed, o_one, cosine, sine, feed_own, upstream, w_down, w_gate, w_up
+    (kv_two, q_parts, normed, cosine, sine, feed_own, upstream, w_down, w_gate, w_up) = fence(
+        kv_two, q_parts, normed, cosine, sine, feed_own, upstream, w_down, w_gate, w_up
     )
     feeds = [feed_own, to_cols(feed_own, 1)]
     q_mine = jnp.concatenate(xor_blocks(q_parts, c), 1)
@@ -478,6 +499,8 @@
     w_one = to_near(w_mine, 0)
     kv_own, feeds[1] = fence(kv_own, feeds[1])
     kv_before = [along(kv_own, k) for k in range(reach, 0, -1)]
+    for k in range(2, cols - 1):
+        feeds.append(to_cols(feeds[-1], 1))
     q_one_other = to_core(q_one)
     q_matrix = blank((width, width))
     q_matrix = put(q_matrix, q_mine, 0, spot(0, 0), 0)
@@ -492,9 +515,8 @@
     (q_two, w_one, q_matrix, o_mine, o_rest, o_one, w_gate, w_up) = fence(
         q_two, w_one, q_matrix, o_mine, o_rest, o_one, w_gate, w_up
     )
-    feeds[1] = after(feeds[1], *kv_before)
-    for k in range(2, cols - 1):
-        feeds.append(to_cols(feeds[-1], 1))
+    feeds.append(to_cols(after(feeds[-1], q_two), 1))
+
     o_two = to_near(jnp.concatenate([o_mine, o_one], 0), 1)
     q_two_other = to_core(q_two)
     g_mine, g_rest = halves(w_gate, 0)
@@ -519,7 +541,6 @@
     (o_two, gu_one, mixed, q_rows, top, feeds, o_matrix, w_mine, w_rest, w_one, gu_mine) = fence(
         o_two, gu_one, mixed, q_rows, top, feeds, o_matrix, w_mine, w_rest, w_one, gu_mine
     )
-    feeds = list(feeds) + [to_cols(feeds[-1], 1)]
     gu_two = to_near(jnp.concatenate([gu_mine, gu_one], 0), 1)
     o_two_other = to_core(o_two)
     gu_one_other = to_core(gu_one)
@@ -533,8 +554,8 @@
     middle = inputs + keep * branch
     factor_two = norm_factor(middle)
     hidden_own = (middle * factor_two * gain_two).astype(bf16)
-    hidden_own, o_matrix, gu_one_other, w_one_other, gu_one, w_one, gu_mine, g_rest, u_rest, feeds = fence(
-        hidden_own, o_matrix, gu_one_other, w_one_other, gu_one, w_one, gu_mine, g_rest, u_rest, feeds
+    hidden_own, o_matrix, gu_one_other, w_one_other, gu_one, w_one, gu_mine, g_rest, u_rest = fence(
+        hidden_own, o_matrix, gu_one_other, w_one_other, gu_one, w_one, gu_mine, g_rest, u_rest
     )
     chunks = [hidden_own, to_cols(hidden_own, 1)]
     g_matrix, u_matrix = blank((width, units)), blank((width, units))
@@ -570,7 +591,9 @@
         gate, up = nn(hidden, g_matrix), nn(hidden, u_matrix)
         return gate, up
 
-    gate, up = gate_up(chunks[1])
+    near_hidden = jnp.concatenate([chunks[1], chunks[0]], 0)
+    near_feed = jnp.concatenate([feeds[1], feeds[0]], 0)
+    gate, up = gate_up(near_hidden)
     w_two, gate, up, d_matrix, arrived = fence(w_two, gate, up, d_matrix, chunks[2])
     chunks[2] = arrived
     chunks.append(to_cols(chunks[2], 1))
@@ -581,28 +604,30 @@
         d_matrix = put(d_matrix, two[:rows_two], 1, spot(far, e), 0)
         d_matrix = put(d_matrix, two[rows_two:], 1, spot(3, e), 0)
     weights = (g_matrix, u_matrix)
-    done = [feed_finish(feeds[1], gate, up, d_matrix)]
-    part = rows_product(done[0][1:], weights, True, bf16)
-    for k in range(2, cols - 1):
+    done = [feed_finish(near_feed, gate, up, d_matrix)]
+    part = rows_product(done[0][1:], weights, True, bf16, 0, own)
+    part, arrived = fence(part, chunks[3])
+    chunks[3] = arrived
+    for k in range(2, cols - 2):
+        carry = to_cols(part, 1)
+        chunks.append(to_cols(chunks[k + 1], 1))
         done.append(feed_through(chunks[k], feeds[k], g_matrix, u_matrix, d_matrix))
-        if k == 2:
-            part, arrived, done = fence(part, chunks[3], done)
-        else:
-            part, carry, arrived, done = fence(part, carry, chunks[k + 1], done)
-            part = (part + carry.astype(f32)).astype(bf16)
-            part, done = fence(part, done)
-        chunks[k + 1] = arrived
-        carry = to_cols(part, 1)
+        part = rows_product(done[-1][1:], weights, True, f32)
+        part, carry, arrived, done = fence(part, carry, chunks[k + 2], done)
         done = list(done)
-        if k + 2 < cols:
-            chunks.append(to_cols(chunks[k + 1], 1))
-        part = rows_product(done[-1][1:], weights, True, f32)
-    last_hidden = jnp.concatenate([chunks[cols - 1], chunks[0]], 0)
-    last_feed = jnp.concatenate([feeds[cols - 1], feeds[0]], 0)
-    done.append(feed_through(last_hidden, last_feed, g_matrix, u_matrix, d_matrix))
+        chunks[k + 2] = arrived
+        part = (part + carry.astype(f32)).astype(bf16)
+        (part,) = fence(part)
+    k = cols - 2
+    carry = to_cols(part, 1)
+    far_hidden = jnp.concatenate(chunks[k:], 0)
+    far_feed = jnp.concatenate(feeds[k:], 0)
+    done.append(feed_through(after(far_hidden, part), far_feed, g_matrix, u_matrix, d_matrix))
     hids, gbs, ubs = ([x[n] for x in done] for n in range(3))
-    h_parts, f_parts = chunks[1 : cols - 1] + [last_hidden], feeds[1 : cols - 1] + [last_feed]
+    h_parts = [near_hidden] + chunks[2:k] + [far_hidden]
+    f_parts = [near_feed] + feeds[2:k] + [far_feed]
     low, high, full = (0, half), (half, half), (0, units)
+    part = rows_product((gbs[-1], ubs[-1]), weights, True, f32, 0, own)
     d_sent = token_sum(hids, full, f_parts, high)
     part, carry, d_sent, hids, gbs, ubs, h_parts, f_parts = fence(
         part, carry, d_sent, hids, gbs, ubs, h_parts, f_parts
@@ -612,16 +637,17 @@
 
     carry = to_cols(part, 1)
     d_received = to_core(d_sent)
-    part = rows_product((gbs[-1], ubs[-1]), weights, True, f32, 0, own)
-    g_sent = token_sum(h_parts, high, gbs, full)
-    u_sent = token_sum(h_parts, high, ubs, full)
+    part, own_part = rows_products(
+        [((gbs[-1], ubs[-1]), 1), ((gbs[0], ubs[0]), 1)], weights, True, f32, own
+    )
+    g_sent, u_sent = token_sums(h_parts, high, [gbs, ubs], full)
     d_sum = token_sum(hids, full, f_parts, low, d_received)
-    part, carry, d_sum, g_sent, u_sent, hids, gbs, ubs = fence(
-        part, carry, d_sum, g_sent, u_sent, hids, gbs, ubs
+    part, own_part, carry, d_sum, g_sent, u_sent, hids, gbs, ubs = fence(
+        part, own_part, carry, d_sum, g_sent, u_sent, hids, gbs, ubs
     )
     part = (part + carry.astype(f32)).astype(bf16)
-    part, d_sum, g_sent, u_sent, gbs, ubs, hids = fence(
-        part, d_sum, g_sent, u_sent, gbs, ubs, hids
+    part, own_part, d_sum, g_sent, u_sent, gbs, ubs, hids = fence(
+        part, own_part, d_sum, g_sent, u_sent, gbs, ubs, hids
     )
 
     def row_sum_start(total, axis):
@@ -646,35 +672,33 @@
     d_state = row_sum_start(d_sum, 1)
     g_received = to_core(g_sent)
     u_received = to_core(u_sent)
-    part = rows_product((gbs[-1], ubs[-1]), weights, True, f32, 1, own)
-    outs = [rows_product([hids[0]], [d_matrix], False, bf16)]
-    g_sum = token_sum(h_parts, low, gbs, full, g_received)
-    u_sum = token_sum(h_parts, low, ubs, full, u_received)
-    part, carry, d_state[1], g_sum, u_sum, outs, hids = fence(
-        part, carry, d_state[1], g_sum, u_sum, outs, hids
-    )
-    outs = list(outs)
+    outs = jnp.split(rows_product([hids[0]], [d_matrix], False, bf16), 2, 0)
+    g_sum, u_sum = token_sums(h_parts, low, [gbs, ubs], full, [g_received, u_received])
+    part, carry, d_state[1], g_sum, u_sum, hids, outs = fence(
+        own_part, carry, d_state[1], g_sum, u_sum, hids, outs
+    )
+    out_carry = to_cols(outs[0], 1)
+    out_last = outs[1]
 
     d_state = row_sum_next(d_state)
     g_state = row_sum_start(g_sum, 0)
-    out_carry = to_cols(outs[0], 1)
     hidden_in_back = part + carry.astype(f32)
     from_norm, mlp_gain_part = norm_back(hidden_in_back, middle, factor_two, gain_two)
     middle_grad = upstream + from_norm
     branch_back = (keep * middle_grad).astype(bf16)
     mixed_back = rows_product([branch_back], [o_matrix], True, bf16)
     o_sent = token_sum([mixed], (0, width), [branch_back], high)
-    outs += [rows_product([x], [d_matrix], False, bf16) for x in hids[1:-1]]
-    last_out = rows_product([hids[-1]], [d_matrix], False, bf16)
-    outs += jnp.split(last_out, 2, 0)
-    mixed_back, branch_back, o_sent, d_state[2], g_state[1], out_carry, outs = fence(
-        mixed_back, branch_back, o_sent, d_state[2], g_state[1], out_carry, outs
-    )
+    outs = [None] + [rows_product([x], [d_matrix], False, bf16) for x in hids[1:-1]]
+    outs += jnp.split(rows_product([hids[-1]], [d_matrix], False, bf16), 2, 0)
+    mixed_back, branch_back, o_sent, d_state[2], g_state[1], outs, hids, out_carry = fence(
+        mixed_back, branch_back, o_sent, d_state[2], g_state[1], outs, hids, out_carry
+    )
+    outs = list(outs)
+    for k in range(1, cols - 2):
+        out_carry = around(out_carry, outs[k])
 
     g_state = row_sum_next(g_state)
     u_state = row_sum_start(u_sum, 0)
-    for k in range(1, cols - 2):
-        out_carry = around(out_carry, outs[k])
     o_received = to_core(o_sent)
     dq, dk, dv = attend_backward(
         q_rows, kv_all, mixed_back, top, cosine, -sine, row_ids, key_ids
@@ -695,10 +719,10 @@
         piece = kv_turned[(reach - k) * own : (reach - k + 1) * own].astype(bf16)
         back_parts.append(along(piece, -k))
     q_received = to_core(q_sent)
-    down_grad = row_sum_end(d_state)
-    back_parts, q_received, down_grad, u_state[2], o_low[1] = fence(
-        back_parts, q_received, down_grad, u_state[2], o_low[1]
-    )
+    back_parts, q_received, u_state[2], o_low[1] = fence(
+        back_parts, q_received, u_state[2], o_low[1]
+    )
+    out_carry = around(out_carry, outs[cols - 2])
 
     o_high = row_sum_start(o_high, 1)
     for piece in back_parts:
@@ -711,31 +735,25 @@
     q_sum = token_sum([normed], low, [dq], (0, width), q_received)
     kv_sum = token_sum([normed], low, [kv_back], (0, 2 * kv_width), kv_received)
     kv_sum, q_sum, kv_back, o_high[1] = fence(kv_sum, q_sum, kv_back, o_high[1])
+    down_grad = row_sum_end(d_state)
 
     kv_state = row_sum_start(kv_sum, 0)
     q_low, q_high = jnp.split(q_sum, 2, 1)
     q_low = row_sum_start(q_low, 0)
-    out_carry = around(out_carry, outs[cols - 2])
     normed_back = rows_product([dq, kv_back], [q_matrix, kv_matrix], True, f32)
     from_norm, attention_gain_part = norm_back(normed_back, inputs, factor_one, gain_one)
     input_grad = xor_order(middle_grad + from_norm, target, blocks, 1)
     gains = xor_order(jnp.stack([attention_gain_part, mlp_gain_part]), target, blocks, 1)
-    hops = [to_core, lambda x: to_rows(x, 1), lambda x: to_rows(x, 2)]
-    hops += [(lambda x, k=1 << n: to_xor_cols(x, k)) for n in range(cols.bit_length() - 1)]
-
-    def shared(values, some):
-        for hop in some:
-            values = values + hop(values)
-        return values
-
-    kv_state[1], q_low[1], input_grad, gains = fence(kv_state[1], q_low[1], input_grad, gains)
-
+    kv_state[1], q_low[1], input_grad, gains, out_carry, down_grad = fence(
+        kv_state[1], q_low[1], input_grad, gains, out_carry, down_grad
+    )
     kv_state = row_sum_next(kv_state)
     o_low = row_sum_next(o_low)
-    gains = shared(gains, hops[:2])
+    for n in range(cols.bit_length() - 1):
+        gains = gains + to_xor_cols(gains, 1 << n)
     gate_grad = row_sum_end(g_state)
-    kv_state[2], gains, o_low[2], gate_grad, out_carry = fence(
-        kv_state[2], gains, o_low[2], gate_grad, out_carry
+    kv_state[2], gains, o_low[2], gate_grad, o_high[1], q_high = fence(
+        kv_state[2], gains, o_low[2], gate_grad, o_high[1], q_high
     )
 
     kv_sum = row_sum_end(kv_state).astype(bf16)
@@ -743,11 +761,7 @@
     q_high = row_sum_start(q_high, 0)
     total = [kv_sum] + [to_xor_cols(kv_sum, k) for k in range(1, cols)]
     up_grad = row_sum_end(u_state)
-    piece = outs[cols - 1].astype(f32) + out_carry.astype(f32)
-    output = xor_order((middle + keep * piece).astype(bf16), target, blocks, 1)
-    total, o_high[2], q_high[1], output, up_grad, gains = fence(
-        total, o_high[2], q_high[1], output, up_grad, gains
-    )
+    total, o_high[2], q_high[1], up_grad = fence(total, o_high[2], q_high[1], up_grad)
 
     def col_sum(total, axis):
         pieces = xor_blocks(jnp.split(total.astype(bf16), cols, axis), c)
@@ -758,20 +772,29 @@
 
     total = tree_sum([x.astype(f32) for x in total]).astype(bf16)
     one = to_near(total, 0)
-    q_low, q_high = row_sum_next(q_low), row_sum_next(q_high)
-    out_sum = jnp.concatenate([row_sum_end(o_low), row_sum_end(o_high)], 0)
-    gains = shared(gains, hops[2:4])
-    one, q_low[2], q_high[2], out_sum, gains = fence(one, q_low[2], q_high[2], out_sum, gains)
+    low_pieces, low_near, _ = q_low
+    high_pieces, high_near, _ = q_high
+    q_state = row_sum_next(
+        [
+            [jnp.concatenate(pair, 1) for pair in zip(low_pieces, high_pieces)],
+            jnp.concatenate([low_near, high_near], 1),
+            0,
+        ]
+    )
+    out_parts = col_sum(jnp.concatenate([row_sum_end(o_low), row_sum_end(o_high)], 0), 0)
+    piece = out_last.astype(f32) + out_carry.astype(f32)
+    output = xor_order((middle + keep * piece).astype(bf16), target, blocks, 1)
+    one, q_state[2], out_parts, output, gains = fence(one, q_state[2], out_parts, output, gains)
     two = to_near(jnp.concatenate([total, one], 0), 1)
-    gains = shared(gains, hops[4:])
-    out_parts = col_sum(out_sum, 0)
-    q_sum = jnp.concatenate([row_sum_end(q_low), row_sum_end(q_high)], 1)
-    two, out_parts, q_sum, gains = fence(two, out_parts, q_sum, gains)
+    gains = gains + to_near(gains, 0)
+    gains = gains + to_near(gains, 1)
+    q_parts = col_sum(row_sum_end(q_state), 1)
+    out_grad = added(out_parts)
+    two, q_parts, out_grad, gains = fence(two, q_parts, out_grad, gains)
     mine = jnp.concatenate([total, one, two], 0)
     theirs = to_core(mine)
-    q_parts = col_sum(q_sum, 1)
-    out_grad = added(out_parts)
-    theirs, out_grad = fence(theirs, out_grad)
+    gains = gains + to_core(gains)
+    query_grad = added(q_parts)
     found = blank((width, 2 * kv_width))
     for e, part in enumerate((mine, theirs)):
         near, far = (first, 3 - first) if e == 0 else (3 - first, first)
@@ -780,8 +803,6 @@
             found = put(found, part[n * step : (n + 1) * step], 0, at, 0)
     found = found.astype(f32)
     key_grad, value_grad = found[:, :kv_width], found[:, kv_width:]
-    q_parts, key_grad, value_grad = fence(q_parts, key_grad, value_grad)
-    query_grad = added(q_parts)
     return (
         output,
         input_grad,

time: 599 us -> 567 us (0.947)
  Pallas kernels: 179 us -> 156 us
  waiting for transfers between devices: 201 us -> 184 us
  matrix products: 9.24 us -> 15.6 us
  other arithmetic: 58.2 us -> 64.2 us
    ppermute x12, waiting for transfers between devices: 55.3 us -> 39.1 us  [to_cols(): lax.ppermute(value, 'cols', [(i, (i + k) % cols) for i in range(cols)])]
    pallas_call x21 -> x17, Pallas kernels: 122 us -> 107 us  [the longest x10 58 us: token_sums(): call(kernel, (pl.cdiv(rows_out, tile),), specs, [out] * many, [jax.ShapeD...]
    ppermute x14, waiting for transfers between devices: 49 us -> 61.2 us  [to_xor_cols(): return lax.ppermute(value, 'cols', [(i, i ^ k) for i in range(cols)])]
    pallas_call x2 -> x1, Pallas kernels: 25.6 us -> 15.1 us  [feed_through(): call(through_kernel, (pl.cdiv(units, tile),), [fixed((count, width))] * 2...]
    ppermute x2 -> x0, waiting for transfers between devices: 8.62 us -> none  [to_rows(): return lax.ppermute(value, 'rows', [(i, i ^ a) for i in range(rows)])]
    dot_general x5, matrix products: 9.24 us -> 15.6 us  [dot(): lax.dot_general(left, right, ((dims[:1], dims[1:]), ((), ())), preferred_...]
    unnamed x194 -> x183, local copies, waits for them, and re-layouts: 23.5 us -> 20.9 us
    ppermute x28 -> x29, waiting for transfers between devices: 59.4 us -> 56.9 us  [to_near(): return lax.ppermute(value, ('dp', 'rows'), pairs)]
  transfers between devices with their start and end apart: 79 -> 78, of which waited for: 31 -> 36; matrix products, arithmetic and copies ran while one was open for 15% -> 17% of each run, Pallas kernels for 30% -> 28%
where the time goes in v3:
time: 567 us; the launch traced here: 557 us
  waiting for transfers between devices  184 us (32%)
  Pallas kernels  156 us (28%)
  starting transfers between devices  89.2 us (16%)
  other arithmetic  64.2 us (11%)
  local copies, waits for them, and re-layouts  44.1 us (8%)
  matrix products  15.6 us (3%)
    ppermute x14, waiting for transfers between devices, to_xor_cols(): return lax.ppermute(value, 'cols', [(i, i ^ k) for i in range(cols)])  61.2 us
    pallas_call x10, Pallas kernels, token_sums(): call(kernel, (pl.cdiv(rows_out, tile),), specs, [out] * many, [jax.ShapeD...  58 us
    ppermute x29, waiting for transfers between devices, to_near(): return lax.ppermute(value, ('dp', 'rows'), pairs)  56.9 us
    pallas_call x7, Pallas kernels, rows_products(): call(kernel, (columns // tile,), specs, [pl.BlockSpec((count, tile), lamb...  49.3 us
    ppermute x12, waiting for transfers between devices, to_cols(): lax.ppermute(value, 'cols', [(i, (i + k) % cols) for i in range(cols)])  39.1 us
    ppermute x29, starting transfers between devices, to_near(): return lax.ppermute(value, ('dp', 'rows'), pairs)  23.7 us
    ppermute x4, waiting for transfers between devices, along(): lax.ppermute(value, 'cols', [(i, i + k) for i in range(cols) if 0 <= i +...  21.9 us
    unnamed x183, local copies, waits for them, and re-layouts  20.9 us
  transfers between devices with their start and end apart: 78, of which 36 were waited for; matrix products, arithmetic and copies ran while one was open for 17% of the time, Pallas kernels for 28%

profile of v3, /device:TPU:11, one launch (start us, length us, event | category | flops | bytes accessed | tf_op | source)
XLA Modules:
  0.0 557.0 jit_solution(3110884472005258847)
XLA Ops:
  36.7 11.2 %collective-permute-done.5 = bf16[256,2048]{1,0:T(8,128)(2,1)S(1)} collective-permute-done((bf16[256,2048]{1,0:T(8,128)(2,1)S(1)}, bf16[256,2048]{1,0:T(8,128)(2,1)S(1)}, u32[]{:S(2)}, u32[]{:S(2)}) %collective-permute-start.5) | collective-permute-done | bytes 1048608 | tf_op jit(solution)/shard_map/ppermute | solution.py:410
  55.4 3.2 collective-permute-start.17
  62.3 7.1 %collective-permute-done.17 = bf16[256,512]{1,0:T(8,128)(2,1)S(1)} collective-permute-done((bf16[256,512]{1,0:T(8,128)(2,1)S(1)}, bf16[256,512]{1,0:T(8,128)(2,1)S(1)}, u32[]{:S(2)}, u32[]{:S(2)}) %collective-permute-start.17) | collective-permute-done | bytes 262176 | tf_op jit(solution)/shard_map/ppermute | solution.py:421
  69.4 5.6 %collective-permute-done.18 = bf16[256,512]{1,0:T(8,128)(2,1)S(1)} collective-permute-done((bf16[256,512]{1,0:T(8,128)(2,1)S(1)}, bf16[256,512]{1,0:T(8,128)(2,1)S(1)}, u32[]{:S(2)}, u32[]{:S(2)}) %collective-permute-start.18) | collective-permute-done | bytes 262176 | tf_op jit(solution)/shard_map/ppermute | solution.py:421
  75.2 3.9 collective-permute-done.11
  79.1 4.3 collective-permute-done.10
  89.1 8.4 %collective-permute-done.19 = bf16[256,2048]{1,0:T(8,128)(2,1)} collective-permute-done((bf16[256,2048]{1,0:T(8,128)(2,1)S(1)}, bf16[256,2048]{1,0:T(8,128)(2,1)}, u32[]{:S(2)}, u32[]{:S(2)}) %collective-permute-start.19) | collective-permute-done | bytes 1048608 | tf_op jit(solution)/shard_map/ppermute | solution.py:418
  104.4 10.8 %shard_map.214 = (bf16[256,2048]{1,0:T(8,128)(2,1)S(1)}, bf16[256,2048]{1,0:T(8,128)(2,1)S(1)}, f32[16,1,256]{2,1,0:T(1,128)S(1)}) custom-call(f32[256,2048]{1,0:T(8,128)S(1)} %fusion.42.pre_ref, bf16[768,512]{1,0:T(8,128)(2,1)S(1)} %constant_dynamic-update-slice_fusion.3.k_ref.v_ref, bf16[768,512]{1,0:T(8,128)(2,1)S(1)} %constant_dynamic-update-slice_fusion.3.k_ref.v_ref, ...), custom_call_target="tpu_custom_call" | custom-call | tf_op jit(solution)/shard_map/pallas_call | solution.py:68
  115.2 6.1 %collective-permute-done.20 = bf16[256,2048]{1,0:T(8,128)(2,1)} collective-permute-done((bf16[256,2048]{1,0:T(8,128)(2,1)}, bf16[256,2048]{1,0:T(8,128)(2,1)}, u32[]{:S(2)}, u32[]{:S(2)}) %collective-permute-start.20) | collective-permute-done | bytes 1048608 | tf_op jit(solution)/shard_map/ppermute | solution.py:418
  121.6 5.0 collective-permute-done.13
  146.8 16.5 %collective-permute-done.25 = bf16[1024,1408]{1,0:T(8,128)(2,1)S(1)} collective-permute-done((bf16[1024,1408]{1,0:T(8,128)(2,1)S(1)}, bf16[1024,1408]{1,0:T(8,128)(2,1)S(1)}, u32[]{:S(2)}, u32[]{:S(2)}) %collective-permute-start.25) | collective-permute-done | bytes 2883616 | tf_op jit(solution)/shard_map/ppermute | solution.py:410
  169.6 5.0 fusion.44.gate_ref
  174.5 5.1 fusion.45.up_ref
  179.6 12.5 %collective-permute-done.29 = bf16[256,2048]{1,0:T(8,128)(2,1)} collective-permute-done((bf16[256,2048]{1,0:T(8,128)(2,1)S(1)}, bf16[256,2048]{1,0:T(8,128)(2,1)}, u32[]{:S(2)}, u32[]{:S(2)}) %collective-permute-start.29) | collective-permute-done | bytes 1048608 | tf_op jit(solution)/shard_map/ppermute | solution.py:418
  197.6 9.2 %shard_map.219 = (bf16[512,1408]{1,0:T(8,128)(2,1)S(1)}, bf16[512,1408]{1,0:T(8,128)(2,1)S(1)}, bf16[512,1408]{1,0:T(8,128)(2,1)S(1)}) custom-call(bf16[512,2048]{1,0:T(8,128)(2,1)} %copy-done, f32[512,1408]{1,0:T(8,128)} %fusion.44.gate_ref, f32[512,1408]{1,0:T(8,128)} %fusion.45.up_ref, bf16[1408,2048]{1,0:T(8,128)(2,1)} %slice_dynamic-update-slice_fusion.8.d_ref.refs_0_), custom_call_target="tpu_custom_call" | custom-call | tf_op jit(solution)/shard_map/pallas_call | solution.py:217
  206.8 8.2 %shard_map.220 = bf16[256,2048]{1,0:T(8,128)(2,1)} custom-call(bf16[2048,1408]{1,0:T(8,128)(2,1)} %copy-done.20, bf16[2048,1408]{1,0:T(8,128)(2,1)} %copy-done.19, bf16[512,1408]{1,0:T(8,128)(2,1)S(1)} %get-tuple-element.354.refs_2_.refs_4_, bf16[512,1408]{1,0:T(8,128)(2,1)S(1)} %get-tuple-element.356.refs_3_.refs_5_.refs_4_), custom_call_target="tpu_custom_call" | custom-call | tf_op jit(solution)/shard_map/pallas_call | solution.py:248
  215.0 5.0 collective-permute-done.31
  226.3 15.1 %shard_map.221 = (bf16[512,1408]{1,0:T(8,128)(2,1)S(1)}, bf16[512,1408]{1,0:T(8,128)(2,1)S(1)}, bf16[512,1408]{1,0:T(8,128)(2,1)S(1)}) custom-call(bf16[512,2048]{1,0:T(8,128)(2,1)} %copy-done.28, bf16[512,2048]{1,0:T(8,128)(2,1)} %copy-done.27, bf16[2048,1408]{1,0:T(8,128)(2,1)} %copy-done.20, bf16[2048,1408]{1,0:T(8,128)(2,1)} %copy-done.19, ...), custom_call_target="tpu_custom_call" | custom-call | tf_op jit(solution)/shard_map/pallas_call | solution.py:193
  241.5 7.5 %shard_map.222 = f32[256,2048]{1,0:T(8,128)S(1)} custom-call(bf16[2048,1408]{1,0:T(8,128)(2,1)} %copy-done.20, bf16[2048,1408]{1,0:T(8,128)(2,1)} %copy-done.19, bf16[512,1408]{1,0:T(8,128)(2,1)S(1)} %get-tuple-element.355.refs_2_.refs_3_, bf16[512,1408]{1,0:T(8,128)(2,1)S(1)} %get-tuple-element.357.refs_3_.refs_5_), custom_call_target="tpu_custom_call" | custom-call | tf_op jit(solution)/shard_map/pallas_call | solution.py:248
  249.0 6.9 %shard_map.223 = bf16[1408,1024]{1,0:T(8,128)(2,1)} custom-call(bf16[512,1408]{1,0:T(8,128)(2,1)S(1)} %get-tuple-element.362.refs_0_.refs_1_, bf16[512,1408]{1,0:T(8,128)(2,1)S(1)} %get-tuple-element.368.refs_1_, bf16[512,2048]{1,0:T(8,128)(2,1)S(1)} %copy-done.1, bf16[512,2048]{1,0:T(8,128)(2,1)} %copy-done.27), custom_call_target="tpu_custom_call" | custom-call | tf_op jit(solution)/shard_map/pallas_call | solution.py:291
  261.1 10.1 %shard_map.224 = (f32[256,2048]{1,0:T(8,128)}, f32[256,2048]{1,0:T(8,128)}) custom-call(bf16[2048,1408]{1,0:T(8,128)(2,1)} %copy-done.20, bf16[2048,1408]{1,0:T(8,128)(2,1)} %copy-done.19, bf16[512,1408]{1,0:T(8,128)(2,1)S(1)} %get-tuple-element.355.refs_2_.refs_3_, bf16[512,1408]{1,0:T(8,128)(2,1)S(1)} %get-tuple-element.357.refs_3_.refs_5_, ...), custom_call_target="tpu_custom_call" | custom-call | tf_op jit(solution)/shard_map/pallas_call | solution.py:248
  271.3 9.3 %shard_map.226 = (bf16[1024,1408]{1,0:T(8,128)(2,1)}, bf16[1024,1408]{1,0:T(8,128)(2,1)}) custom-call(bf16[512,2048]{1,0:T(8,128)(2,1)} %copy-done.33, bf16[512,2048]{1,0:T(8,128)(2,1)} %copy-done.28, bf16[512,1408]{1,0:T(8,128)(2,1)S(1)} %get-tuple-element.354.refs_2_.refs_4_, bf16[512,1408]{1,0:T(8,128)(2,1)S(1)} %get-tuple-element.355.refs_2_.refs_3_, ...), custom_call_target="tpu_custom_call" | custom-call | tf_op jit(solution)/shard_map/pallas_call | solution.py:291
  280.6 7.7 %shard_map.225 = bf16[1408,1024]{1,0:T(8,128)(2,1)} custom-call(bf16[512,1408]{1,0:T(8,128)(2,1)S(1)} %get-tuple-element.362.refs_0_.refs_1_, bf16[512,1408]{1,0:T(8,128)(2,1)S(1)} %get-tuple-element.368.refs_1_, bf16[512,2048]{1,0:T(8,128)(2,1)S(1)} %copy-done.1, bf16[512,2048]{1,0:T(8,128)(2,1)} %copy-done.27, ...), custom_call_target="tpu_custom_call" | custom-call | tf_op jit(solution)/shard_map/pallas_call | solution.py:291
  289.3 3.3 add_convert_fusion.5
  294.8 3.9 collective-permute-start.35
  298.7 5.8 %shard_map.228 = bf16[512,2048]{1,0:T(8,128)(2,1)S(1)} custom-call(bf16[1408,2048]{1,0:T(8,128)(2,1)} %slice_dynamic-update-slice_fusion.8.d_ref.refs_0_, bf16[512,1408]{1,0:T(8,128)(2,1)S(1)} %copy-done.5), custom_call_target="tpu_custom_call" | custom-call | tf_op jit(solution)/shard_map/pallas_call | solution.py:248
  306.2 9.8 %shard_map.227 = (bf16[1024,1408]{1,0:T(8,128)(2,1)}, bf16[1024,1408]{1,0:T(8,128)(2,1)}) custom-call(bf16[512,2048]{1,0:T(8,128)(2,1)} %copy-done.33, bf16[512,2048]{1,0:T(8,128)(2,1)} %copy-done.28, bf16[512,1408]{1,0:T(8,128)(2,1)S(1)} %get-tuple-element.354.refs_2_.refs_4_, bf16[512,1408]{1,0:T(8,128)(2,1)S(1)} %get-tuple-element.355.refs_2_.refs_3_, ...), custom_call_target="tpu_custom_call" | custom-call | tf_op jit(solution)/shard_map/pallas_call | solution.py:291
  315.9 4.3 collective-permute-done.35
  331.6 3.3 multiply_convert_fusion
  334.8 5.0 shard_map.230
  339.9 5.7 %shard_map.229.back_ref = bf16[256,2048]{1,0:T(8,128)(2,1)S(1)} custom-call(bf16[2048,2048]{1,0:T(8,128)(2,1)} %copy-done.21, bf16[256,2048]{1,0:T(8,128)(2,1)S(1)} %get-tuple-element.375.refs_1_), custom_call_target="tpu_custom_call" | custom-call | tf_op jit(solution)/shard_map/pallas_call | solution.py:248
  345.6 5.9 %shard_map.231 = bf16[512,2048]{1,0:T(8,128)(2,1)S(1)} custom-call(bf16[1408,2048]{1,0:T(8,128)(2,1)} %slice_dynamic-update-slice_fusion.8.d_ref.refs_0_, bf16[512,1408]{1,0:T(8,128)(2,1)S(1)} %copy-done.3), custom_call_target="tpu_custom_call" | custom-call | tf_op jit(solution)/shard_map/pallas_call | solution.py:248
  359.4 13.4 %shard_map.232 = (bf16[256,2048]{1,0:T(8,128)(2,1)S(1)}, f32[768,256]{1,0:T(8,128)S(1)}, f32[768,256]{1,0:T(8,128)S(1)}) custom-call(bf16[256,2048]{1,0:T(8,128)(2,1)S(1)} %copy-done.14, bf16[768,512]{1,0:T(8,128)(2,1)S(1)} %constant_dynamic-update-slice_fusion.3.k_ref.v_ref, bf16[768,512]{1,0:T(8,128)(2,1)S(1)} %constant_dynamic-update-slice_fusion.3.k_ref.v_ref, ...), custom_call_target="tpu_custom_call" | custom-call | tf_op jit(solution)/shard_map/pallas_call | solution.py:128
  374.6 3.4 shard_map.233
  378.0 7.6 %shard_map.234 = bf16[2048,1024]{1,0:T(8,128)(2,1)} custom-call(bf16[256,2048]{1,0:T(8,128)(2,1)S(1)} %get-tuple-element.269.refs_0_, bf16[256,2048]{1,0:T(8,128)(2,1)S(1)} %get-tuple-element.375.refs_1_, bf16[2048,1024]{1,0:T(8,128)(2,1)} %collective-permute-done.42.refs_2_), custom_call_target="tpu_custom_call" | custom-call | tf_op jit(solution)/shard_map/pallas_call | solution.py:291
  407.2 6.1 %collective-permute-done.47 = bf16[256,512]{1,0:T(8,128)(2,1)S(1)} collective-permute-done((bf16[256,512]{1,0:T(8,128)(2,1)S(1)}, bf16[256,512]{1,0:T(8,128)(2,1)S(1)}, u32[]{:S(2)}, u32[]{:S(2)}) %collective-permute-start.47) | collective-permute-done | bytes 262176 | tf_op jit(solution)/shard_map/ppermute | solution.py:421
  413.3 3.5 collective-permute-start.55
  425.5 5.6 %shard_map.237 = bf16[1024,2048]{1,0:T(8,128)(2,1)} custom-call(bf16[256,2048]{1,0:T(8,128)(2,1)S(1)} %fusion.2.refs_0_, bf16[256,2048]{1,0:T(8,128)(2,1)S(1)} %get-tuple-element.388.refs_1_.refs_2_, bf16[1024,2048]{1,0:T(8,128)(2,1)} %collective-permute-done.48.refs_2_), custom_call_target="tpu_custom_call" | custom-call | tf_op jit(solution)/shard_map/pallas_call | solution.py:291
  439.9 6.1 %shard_map.238 = f32[256,2048]{1,0:T(8,128)S(1)} custom-call(bf16[2048,2048]{1,0:T(8,128)(2,1)} %copy-done.22, bf16[2048,512]{1,0:T(8,128)(2,1)S(1)} %copy-done.8, bf16[256,2048]{1,0:T(8,128)(2,1)S(1)} %get-tuple-element.388.refs_1_.refs_2_, bf16[256,512]{1,0:T(8,128)(2,1)S(1)} %pad_maximum_fusion.18.refs_1_.refs_3_), custom_call_target="tpu_custom_call" | custom-call | tf_op jit(solution)/shard_map/pallas_call | solution.py:248
  449.2 6.2 %collective-permute-done.54 = bf16[512,1024]{1,0:T(8,128)(2,1)S(1)} collective-permute-done((bf16[512,1024]{1,0:T(8,128)(2,1)}, bf16[512,1024]{1,0:T(8,128)(2,1)S(1)}, u32[]{:S(2)}, u32[]{:S(2)}) %collective-permute-start.54) | collective-permute-done | bytes 1048608 | tf_op jit(solution)/shard_map/ppermute | solution.py:410
  472.7 4.9 collective-permute-done.60
  477.5 10.6 %collective-permute-done.61 = bf16[256,512]{1,0:T(8,128)(2,1)S(1)} collective-permute-done((bf16[256,512]{1,0:T(8,128)(2,1)S(1)}, bf16[256,512]{1,0:T(8,128)(2,1)S(1)}, u32[]{:S(2)}, u32[]{:S(2)}) %collective-permute-start.61) | collective-permute-done | bytes 262176 | tf_op jit(solution)/shard_map/ppermute | solution.py:426
  488.1 5.8 %collective-permute-done.62 = bf16[256,512]{1,0:T(8,128)(2,1)S(1)} collective-permute-done((bf16[256,512]{1,0:T(8,128)(2,1)S(1)}, bf16[256,512]{1,0:T(8,128)(2,1)S(1)}, u32[]{:S(2)}, u32[]{:S(2)}) %collective-permute-start.62) | collective-permute-done | bytes 262176 | tf_op jit(solution)/shard_map/ppermute | solution.py:426
  498.6 3.4 collective-permute-start.68
  504.9 6.1 %collective-permute-done.68 = bf16[512,256]{1,0:T(8,128)(2,1)S(1)} collective-permute-done((bf16[512,256]{1,0:T(8,128)(2,1)S(1)}, bf16[512,256]{1,0:T(8,128)(2,1)S(1)}, u32[]{:S(2)}, u32[]{:S(2)}) %collective-permute-start.68) | collective-permute-done | bytes 262176 | tf_op jit(solution)/shard_map/ppermute | solution.py:426
  511.0 12.1 %collective-permute-done.69 = bf16[512,256]{1,0:T(8,128)(2,1)S(1)} collective-permute-done((bf16[512,256]{1,0:T(8,128)(2,1)S(1)}, bf16[512,256]{1,0:T(8,128)(2,1)S(1)}, u32[]{:S(2)}, u32[]{:S(2)}) %collective-permute-start.69) | collective-permute-done | bytes 262176 | tf_op jit(solution)/shard_map/ppermute | solution.py:426
  524.5 3.4 collective-permute-start.72
  537.2 11.8 %collective-permute-done.73 = bf16[256,512]{1,0:T(8,128)(2,1)S(1)} collective-permute-done((bf16[256,512]{1,0:T(8,128)(2,1)S(1)}, bf16[256,512]{1,0:T(8,128)(2,1)S(1)}, u32[]{:S(2)}, u32[]{:S(2)}) %collective-permute-start.73) | collective-permute-done | bytes 262176 | tf_op jit(solution)/shard_map/ppermute | solution.py:426
  (538 shorter events, 211.8 us)
Async XLA Ops:
  1.7 20.9 %collective-permute-start.2 = (bf16[256,512]{1,0:T(8,128)(2,1)S(1)}, bf16[256,512]{1,0:T(8,128)(2,1)S(1)}, u32[]{:S(2)}, u32[]{:S(2)}) collective-permute-start(bf16[256,512]{1,0:T(8,128)(2,1)S(1)} %slice_select_fusion), channel_id=1, source_target_pairs={{0,1},{1,0},{2,3},{3,2},{4,5},{5,4},{6,7},{7,6},{8,9},{9,8},{10,11... | collective-permute-start | bytes 786440 | tf_op jit(solution)/shard_map/ppermute | solution.py:426
  1.9 22.0 %collective-permute-start.3 = (bf16[256,512]{1,0:T(8,128)(2,1)S(1)}, bf16[256,512]{1,0:T(8,128)(2,1)S(1)}, u32[]{:S(2)}, u32[]{:S(2)}) collective-permute-start(bf16[256,512]{1,0:T(8,128)(2,1)S(1)} %slice_select_fusion), channel_id=1, source_target_pairs={{0,2},{1,3},{2,0},{3,1},{4,6},{5,7},{6,4},{7,5},{8,10},{9,11},{10,... | collective-permute-start | bytes 786440 | tf_op jit(solution)/shard_map/ppermute | solution.py:426
  4.3 22.6 %collective-permute-start.4 = (bf16[256,512]{1,0:T(8,128)(2,1)S(1)}, bf16[256,512]{1,0:T(8,128)(2,1)}, u32[]{:S(2)}, u32[]{:S(2)}) collective-permute-start(bf16[256,512]{1,0:T(8,128)(2,1)S(1)} %slice_select_fusion), channel_id=1, source_target_pairs={{0,3},{1,2},{2,1},{3,0},{4,7},{5,6},{6,5},{7,4},{8,11},{9,10},{10,... | collective-permute-start | bytes 786440 | tf_op jit(solution)/shard_map/ppermute | solution.py:426
  12.7 18.4 %collective-permute-start.7 = (bf16[256,512]{1,0:T(8,128)(2,1)S(1)}, bf16[256,512]{1,0:T(8,128)(2,1)S(1)}, u32[]{:S(2)}, u32[]{:S(2)}) collective-permute-start(bf16[256,512]{1,0:T(8,128)(2,1)S(1)} %collective-permute-done), channel_id=1, source_target_pairs={{0,16},{16,0},{1,17},{17,1},{2,18},{18,2},{3,19},{19,3},{4,20},{20... | collective-permute-start | bytes 786440 | tf_op jit(solution)/shard_map/ppermute | solution.py:415
  28.2 19.7 %collective-permute-start.5 = (bf16[256,2048]{1,0:T(8,128)(2,1)S(1)}, bf16[256,2048]{1,0:T(8,128)(2,1)S(1)}, u32[]{:S(2)}, u32[]{:S(2)}) collective-permute-start(bf16[256,2048]{1,0:T(8,128)(2,1)S(1)} %get-tuple-element.578), channel_id=1, source_target_pairs={{0,4},{4,0},{8,12},{12,8},{16,24},{20,28},{24,16},{28,20},{1,5},{5... | collective-permute-start | bytes 3145736 | tf_op jit(solution)/shard_map/ppermute | solution.py:410
  29.5 18.4 %collective-permute-start.6 = (bf16[256,2048]{1,0:T(8,128)(2,1)S(1)}, bf16[256,2048]{1,0:T(8,128)(2,1)S(1)}, u32[]{:S(2)}, u32[]{:S(2)}) collective-permute-start(bf16[256,2048]{1,0:T(8,128)(2,1)S(1)} %get-tuple-element.578), channel_id=1, source_target_pairs={{0,16},{16,0},{1,17},{17,1},{2,18},{18,2},{3,19},{19,3},{4,20},{20... | collective-permute-start | bytes 3145736 | tf_op jit(solution)/shard_map/ppermute | solution.py:415
  31.1 24.3 %collective-permute-start.16 = (bf16[256,2048]{1,0:T(8,128)(2,1)S(1)}, bf16[256,2048]{1,0:T(8,128)(2,1)S(1)}, u32[]{:S(2)}, u32[]{:S(2)}) collective-permute-start(bf16[256,2048]{1,0:T(8,128)(2,1)S(1)} %multiply_convert_fusion.2), channel_id=1, source_target_pairs={{0,1},{1,2},{2,3},{3,0},{4,5},{5,6},{6,7},{7,4},{8,9},{9,10},{10,1... | collective-permute-start | bytes 3145736 | tf_op jit(solution)/shard_map/ppermute | solution.py:418
  48.2 26.8 %collective-permute-start.12 = (bf16[256,2048]{1,0:T(8,128)(2,1)S(1)}, bf16[256,2048]{1,0:T(8,128)(2,1)S(1)}, u32[]{:S(2)}, u32[]{:S(2)}) collective-permute-start(bf16[256,2048]{1,0:T(8,128)(2,1)S(1)} %collective-permute-done.5), channel_id=1, source_target_pairs={{0,16},{16,0},{1,17},{17,1},{2,18},{18,2},{3,19},{19,3},{4,20},{20... | collective-permute-start | bytes 3145736 | tf_op jit(solution)/shard_map/ppermute | solution.py:415
  50.4 33.0 %collective-permute-start.10 = (bf16[512,2048]{1,0:T(8,128)(2,1)S(1)}, bf16[512,2048]{1,0:T(8,128)(2,1)S(1)}, u32[]{:S(2)}, u32[]{:S(2)}) collective-permute-start(bf16[512,2048]{1,0:T(8,128)(2,1)S(1)} %pad_maximum_fusion.1), channel_id=1, source_target_pairs={{0,8},{4,12},{8,0},{12,4},{16,20},{20,16},{24,28},{28,24},{1,9},{5... | collective-permute-start | bytes 6291464 | tf_op jit(solution)/shard_map/ppermute | solution.py:410
  58.7 16.3 %collective-permute-start.18 = (bf16[256,512]{1,0:T(8,128)(2,1)S(1)}, bf16[256,512]{1,0:T(8,128)(2,1)S(1)}, u32[]{:S(2)}, u32[]{:S(2)}) collective-permute-start(bf16[256,512]{1,0:T(8,128)(2,1)S(1)} %pad_maximum_fusion.17), channel_id=1, source_target_pairs={{0,1},{1,2},{2,3},{4,5},{5,6},{6,7},{8,9},{9,10},{10,11},{12,13},{... | collective-permute-start | bytes 786440 | tf_op jit(solution)/shard_map/ppermute | solution.py:421
  60.7 18.4 %collective-permute-start.11 = (bf16[1408,256]{1,0:T(8,128)(2,1)S(1)}, bf16[1408,256]{1,0:T(8,128)(2,1)}, u32[]{:S(2)}, u32[]{:S(2)}) collective-permute-start(bf16[1408,256]{1,0:T(8,128)(2,1)S(1)} %get-tuple-element.291), channel_id=1, source_target_pairs={{0,4},{4,0},{8,12},{12,8},{16,24},{20,28},{24,16},{28,20},{1,5},{5... | collective-permute-start | bytes 2162696 | tf_op jit(solution)/shard_map/ppermute | solution.py:410
  69.3 28.1 %collective-permute-start.19 = (bf16[256,2048]{1,0:T(8,128)(2,1)S(1)}, bf16[256,2048]{1,0:T(8,128)(2,1)}, u32[]{:S(2)}, u32[]{:S(2)}) collective-permute-start(bf16[256,2048]{1,0:T(8,128)(2,1)S(1)} %collective-permute-done.16), channel_id=1, source_target_pairs={{0,1},{1,2},{2,3},{3,0},{4,5},{5,6},{6,7},{7,4},{8,9},{9,10},{10,1... | collective-permute-start | bytes 3145736 | tf_op jit(solution)/shard_map/ppermute | solution.py:418
  83.4 17.2 %collective-permute-start.21 = (bf16[2048,256]{1,0:T(8,128)(2,1)S(1)}, bf16[2048,256]{1,0:T(8,128)(2,1)S(1)}, u32[]{:S(2)}, u32[]{:S(2)}) collective-permute-start(bf16[2048,256]{1,0:T(8,128)(2,1)S(1)} %collective-permute-done.9), channel_id=1, source_target_pairs={{0,16},{16,0},{1,17},{17,1},{2,18},{18,2},{3,19},{19,3},{4,20},{20... | collective-permute-start | bytes 3145736 | tf_op jit(solution)/shard_map/ppermute | solution.py:415
  85.7 40.8 %collective-permute-start.13 = (bf16[4096,256]{1,0:T(8,128)(2,1)}, bf16[4096,256]{1,0:T(8,128)(2,1)S(1)}, u32[]{:S(2)}, u32[]{:S(2)}) collective-permute-start(bf16[4096,256]{1,0:T(8,128)(2,1)} %pad_maximum_fusion.2), channel_id=1, source_target_pairs={{0,8},{4,12},{8,0},{12,4},{16,20},{20,16},{24,28},{28,24},{1,9},{5... | collective-permute-start | bytes 6291464 | tf_op jit(solution)/shard_map/ppermute | solution.py:410
  87.8 33.8 %collective-permute-start.14 = (bf16[512,1408]{1,0:T(8,128)(2,1)S(1)}, bf16[512,1408]{1,0:T(8,128)(2,1)}, u32[]{:S(2)}, u32[]{:S(2)}) collective-permute-start(bf16[512,1408]{1,0:T(8,128)(2,1)S(1)} %pad_maximum_fusion.3), channel_id=1, source_target_pairs={{0,4},{4,0},{8,12},{12,8},{16,24},{20,28},{24,16},{28,20},{1,5},{5... | collective-permute-start | bytes 4325384 | tf_op jit(solution)/shard_map/ppermute | solution.py:410
  97.4 23.8 %collective-permute-start.20 = (bf16[256,2048]{1,0:T(8,128)(2,1)}, bf16[256,2048]{1,0:T(8,128)(2,1)}, u32[]{:S(2)}, u32[]{:S(2)}) collective-permute-start(bf16[256,2048]{1,0:T(8,128)(2,1)} %collective-permute-done.19), channel_id=1, source_target_pairs={{0,1},{1,2},{2,3},{3,0},{4,5},{5,6},{6,7},{7,4},{8,9},{9,10},{10,1... | collective-permute-start | bytes 3145736 | tf_op jit(solution)/shard_map/ppermute | solution.py:418
  129.6 33.7 %collective-permute-start.25 = (bf16[1024,1408]{1,0:T(8,128)(2,1)S(1)}, bf16[1024,1408]{1,0:T(8,128)(2,1)S(1)}, u32[]{:S(2)}, u32[]{:S(2)}) collective-permute-start(bf16[1024,1408]{1,0:T(8,128)(2,1)S(1)} %pad_maximum_fusion), channel_id=1, source_target_pairs={{0,8},{4,12},{8,0},{12,4},{16,20},{20,16},{24,28},{28,24},{1,9},{5... | collective-permute-start | bytes 8650760 | tf_op jit(solution)/shard_map/ppermute | solution.py:410
  138.1 25.1 %collective-permute-start.26 = (bf16[256,2048]{1,0:T(8,128)(2,1)S(1)}, bf16[256,2048]{1,0:T(8,128)(2,1)S(1)}, u32[]{:S(2)}, u32[]{:S(2)}) collective-permute-start(bf16[256,2048]{1,0:T(8,128)(2,1)S(1)} %multiply_convert_fusion.1), channel_id=1, source_target_pairs={{0,1},{1,2},{2,3},{3,0},{4,5},{5,6},{6,7},{7,4},{8,9},{9,10},{10,1... | collective-permute-start | bytes 3145736 | tf_op jit(solution)/shard_map/ppermute | solution.py:418
  165.4 26.7 %collective-permute-start.28 = (bf16[2816,256]{1,0:T(8,128)(2,1)S(1)}, bf16[2816,256]{1,0:T(8,128)(2,1)S(1)}, u32[]{:S(2)}, u32[]{:S(2)}) collective-permute-start(bf16[2816,256]{1,0:T(8,128)(2,1)S(1)} %pad_maximum_fusion.4), channel_id=1, source_target_pairs={{0,8},{4,12},{8,0},{12,4},{16,20},{20,16},{24,28},{28,24},{1,9},{5... | collective-permute-start | bytes 4325384 | tf_op jit(solution)/shard_map/ppermute | solution.py:410
  165.7 26.3 %collective-permute-start.29 = (bf16[256,2048]{1,0:T(8,128)(2,1)S(1)}, bf16[256,2048]{1,0:T(8,128)(2,1)}, u32[]{:S(2)}, u32[]{:S(2)}) collective-permute-start(bf16[256,2048]{1,0:T(8,128)(2,1)S(1)} %collective-permute-done.26), channel_id=1, source_target_pairs={{0,1},{1,2},{2,3},{3,0},{4,5},{5,6},{6,7},{7,4},{8,9},{9,10},{10,1... | collective-permute-start | bytes 3145736 | tf_op jit(solution)/shard_map/ppermute | solution.py:418
  193.0 27.0 %collective-permute-start.31 = (bf16[256,2048]{1,0:T(8,128)(2,1)}, bf16[256,2048]{1,0:T(8,128)(2,1)S(1)}, u32[]{:S(2)}, u32[]{:S(2)}) collective-permute-start(bf16[256,2048]{1,0:T(8,128)(2,1)} %collective-permute-done.29), channel_id=1, source_target_pairs={{0,1},{1,2},{2,3},{3,0},{4,5},{5,6},{6,7},{7,4},{8,9},{9,10},{10,1... | collective-permute-start | bytes 3145736 | tf_op jit(solution)/shard_map/ppermute | solution.py:418
  220.1 35.8 %collective-permute-start.32 = (bf16[256,2048]{1,0:T(8,128)(2,1)}, bf16[256,2048]{1,0:T(8,128)(2,1)}, u32[]{:S(2)}, u32[]{:S(2)}) collective-permute-start(bf16[256,2048]{1,0:T(8,128)(2,1)} %shard_map.220), channel_id=1, source_target_pairs={{0,1},{1,2},{2,3},{3,0},{4,5},{5,6},{6,7},{7,4},{8,9},{9,10},{10,1... | collective-permute-start | bytes 3145736 | tf_op jit(solution)/shard_map/ppermute | solution.py:418
  258.4 22.2 %collective-permute-start.34 = (bf16[1408,1024]{1,0:T(8,128)(2,1)}, bf16[1408,1024]{1,0:T(8,128)(2,1)}, u32[]{:S(2)}, u32[]{:S(2)}) collective-permute-start(bf16[1408,1024]{1,0:T(8,128)(2,1)} %shard_map.223), channel_id=1, source_target_pairs={{0,16},{16,0},{1,17},{17,1},{2,18},{18,2},{3,19},{19,3},{4,20},{20... | collective-permute-start | bytes 8650760 | tf_op jit(solution)/shard_map/ppermute | solution.py:415
  259.0 29.3 %collective-permute-start.33 = (bf16[256,2048]{1,0:T(8,128)(2,1)}, bf16[256,2048]{1,0:T(8,128)(2,1)S(1)}, u32[]{:S(2)}, u32[]{:S(2)}) collective-permute-start(bf16[256,2048]{1,0:T(8,128)(2,1)} %add_convert_fusion.6), channel_id=1, source_target_pairs={{0,1},{1,2},{2,3},{3,0},{4,5},{5,6},{6,7},{7,4},{8,9},{9,10},{10,1... | collective-permute-start | bytes 3145736 | tf_op jit(solution)/shard_map/ppermute | solution.py:418
  294.4 25.8 %collective-permute-start.36 = (bf16[1408,512]{1,0:T(8,128)(2,1)}, bf16[1408,512]{1,0:T(8,128)(2,1)}, u32[]{:S(2)}, u32[]{:S(2)}) collective-permute-start(bf16[1408,512]{1,0:T(8,128)(2,1)} %pad_maximum_fusion.5), channel_id=1, source_target_pairs={{0,4},{4,0},{8,12},{12,8},{16,24},{20,28},{24,16},{28,20},{1,5},{5... | collective-permute-start | bytes 4325384 | tf_op jit(solution)/shard_map/ppermute | solution.py:410
  294.8 25.4 %collective-permute-start.35 = (bf16[256,2048]{1,0:T(8,128)(2,1)}, bf16[256,2048]{1,0:T(8,128)(2,1)}, u32[]{:S(2)}, u32[]{:S(2)}) collective-permute-start(bf16[256,2048]{1,0:T(8,128)(2,1)} %add_convert_fusion.5), channel_id=1, source_target_pairs={{0,1},{1,2},{2,3},{3,0},{4,5},{5,6},{6,7},{7,4},{8,9},{9,10},{10,1... | collective-permute-start | bytes 3145736 | tf_op jit(solution)/shard_map/ppermute | solution.py:418
  322.5 30.2 %collective-permute-start.39 = (bf16[1408,256]{1,0:T(8,128)(2,1)}, bf16[1408,256]{1,0:T(8,128)(2,1)}, u32[]{:S(2)}, u32[]{:S(2)}) collective-permute-start(bf16[1408,256]{1,0:T(8,128)(2,1)} %add_convert_fusion.9), channel_id=1, source_target_pairs={{0,8},{4,12},{8,0},{12,4},{16,20},{20,16},{24,28},{28,24},{1,9},{5... | collective-permute-start | bytes 2162696 | tf_op jit(solution)/shard_map/ppermute | solution.py:410
  325.6 27.1 %collective-permute-start.40 = (bf16[512,1408]{1,0:T(8,128)(2,1)}, bf16[512,1408]{1,0:T(8,128)(2,1)}, u32[]{:S(2)}, u32[]{:S(2)}) collective-permute-start(bf16[512,1408]{1,0:T(8,128)(2,1)} %pad_maximum_fusion.6), channel_id=1, source_target_pairs={{0,4},{4,0},{8,12},{12,8},{16,24},{20,28},{24,16},{28,20},{1,5},{5... | collective-permute-start | bytes 4325384 | tf_op jit(solution)/shard_map/ppermute | solution.py:410
  327.5 25.2 %collective-permute-start.41 = (bf16[256,2048]{1,0:T(8,128)(2,1)}, bf16[256,2048]{1,0:T(8,128)(2,1)}, u32[]{:S(2)}, u32[]{:S(2)}) collective-permute-start(bf16[256,2048]{1,0:T(8,128)(2,1)} %get-tuple-element.369), channel_id=1, source_target_pairs={{0,1},{1,2},{2,3},{3,0},{4,5},{5,6},{6,7},{7,4},{8,9},{9,10},{10,1... | collective-permute-start | bytes 3145736 | tf_op jit(solution)/shard_map/ppermute | solution.py:418
  352.6 25.4 %collective-permute-start.42 = (bf16[2048,1024]{1,0:T(8,128)(2,1)}, bf16[2048,1024]{1,0:T(8,128)(2,1)}, u32[]{:S(2)}, u32[]{:S(2)}) collective-permute-start(bf16[2048,1024]{1,0:T(8,128)(2,1)} %shard_map.230), channel_id=1, source_target_pairs={{0,16},{16,0},{1,17},{17,1},{2,18},{18,2},{3,19},{19,3},{4,20},{20... | collective-permute-start | bytes 12582920 | tf_op jit(solution)/shard_map/ppermute | solution.py:415
  354.5 31.1 %collective-permute-start.44 = (bf16[512,1408]{1,0:T(8,128)(2,1)S(1)}, bf16[512,1408]{1,0:T(8,128)(2,1)}, u32[]{:S(2)}, u32[]{:S(2)}) collective-permute-start(bf16[512,1408]{1,0:T(8,128)(2,1)S(1)} %pad_maximum_fusion.7), channel_id=1, source_target_pairs={{0,4},{4,0},{8,12},{12,8},{16,24},{20,28},{24,16},{28,20},{1,5},{5... | collective-permute-start | bytes 4325384 | tf_op jit(solution)/shard_map/ppermute | solution.py:410
  356.7 29.0 %collective-permute-start.45 = (bf16[256,2048]{1,0:T(8,128)(2,1)S(1)}, bf16[256,2048]{1,0:T(8,128)(2,1)}, u32[]{:S(2)}, u32[]{:S(2)}) collective-permute-start(bf16[256,2048]{1,0:T(8,128)(2,1)S(1)} %add_convert_fusion.4), channel_id=1, source_target_pairs={{0,1},{1,2},{2,3},{3,0},{4,5},{5,6},{6,7},{7,4},{8,9},{9,10},{10,1... | collective-permute-start | bytes 3145736 | tf_op jit(solution)/shard_map/ppermute | solution.py:418
  359.3 26.3 %collective-permute-start.43 = (bf16[256,1408]{1,0:T(8,128)(2,1)S(1)}, bf16[256,1408]{1,0:T(8,128)(2,1)S(1)}, u32[]{:S(2)}, u32[]{:S(2)}) collective-permute-start(bf16[256,1408]{1,0:T(8,128)(2,1)S(1)} %add_convert_fusion.8), channel_id=1, source_target_pairs={{0,8},{4,12},{8,0},{12,4},{16,20},{20,16},{24,28},{28,24},{1,9},{5... | collective-permute-start | bytes 2162696 | tf_op jit(solution)/shard_map/ppermute | solution.py:410
  386.5 30.4 %collective-permute-start.48 = (bf16[1024,2048]{1,0:T(8,128)(2,1)}, bf16[1024,2048]{1,0:T(8,128)(2,1)}, u32[]{:S(2)}, u32[]{:S(2)}) collective-permute-start(bf16[1024,2048]{1,0:T(8,128)(2,1)} %shard_map.233), channel_id=1, source_target_pairs={{0,16},{16,0},{1,17},{17,1},{2,18},{18,2},{3,19},{19,3},{4,20},{20... | collective-permute-start | bytes 12582920 | tf_op jit(solution)/shard_map/ppermute | solution.py:415
  393.1 23.7 %collective-permute-start.50 = (bf16[1024,512]{1,0:T(8,128)(2,1)S(1)}, bf16[1024,512]{1,0:T(8,128)(2,1)S(1)}, u32[]{:S(2)}, u32[]{:S(2)}) collective-permute-start(bf16[1024,512]{1,0:T(8,128)(2,1)S(1)} %pad_maximum_fusion.9), channel_id=1, source_target_pairs={{0,4},{4,0},{8,12},{12,8},{16,24},{20,28},{24,16},{28,20},{1,5},{5... | collective-permute-start | bytes 3145736 | tf_op jit(solution)/shard_map/ppermute | solution.py:410
  396.1 20.8 %collective-permute-start.49 = (bf16[256,1408]{1,0:T(8,128)(2,1)S(1)}, bf16[256,1408]{1,0:T(8,128)(2,1)S(1)}, u32[]{:S(2)}, u32[]{:S(2)}) collective-permute-start(bf16[256,1408]{1,0:T(8,128)(2,1)S(1)} %add_convert_fusion.7), channel_id=1, source_target_pairs={{0,8},{4,12},{8,0},{12,4},{16,20},{20,16},{24,28},{28,24},{1,9},{5... | collective-permute-start | bytes 2162696 | tf_op jit(solution)/shard_map/ppermute | solution.py:410
  406.4 28.4 %collective-permute-start.52 = (bf16[1024,512]{1,0:T(8,128)(2,1)S(1)}, bf16[1024,512]{1,0:T(8,128)(2,1)}, u32[]{:S(2)}, u32[]{:S(2)}) collective-permute-start(bf16[1024,512]{1,0:T(8,128)(2,1)S(1)} %pad_maximum_fusion.10), channel_id=1, source_target_pairs={{0,4},{4,0},{8,12},{12,8},{16,24},{20,28},{24,16},{28,20},{1,5},{5... | collective-permute-start | bytes 3145736 | tf_op jit(solution)/shard_map/ppermute | solution.py:410
  413.3 35.8 %collective-permute-start.55 = (bf16[256,2048]{1,0:T(8,128)(2,1)S(1)}, bf16[256,2048]{1,0:T(8,128)(2,1)}, u32[]{:S(2)}, u32[]{:S(2)}) collective-permute-start(bf16[256,2048]{1,0:T(8,128)(2,1)S(1)} %add_convert_fusion.3), channel_id=1, source_target_pairs={{0,1},{1,2},{2,3},{3,0},{4,5},{5,6},{6,7},{7,4},{8,9},{9,10},{10,1... | collective-permute-start | bytes 3145736 | tf_op jit(solution)/shard_map/ppermute | solution.py:418
  425.0 40.4 %collective-permute-start.59 = (bf16[1024,256]{1,0:T(8,128)(2,1)}, bf16[1024,256]{1,0:T(8,128)(2,1)}, u32[]{:S(2)}, u32[]{:S(2)}) collective-permute-start(bf16[1024,256]{1,0:T(8,128)(2,1)} %add_convert_fusion.13), channel_id=1, source_target_pairs={{0,8},{4,12},{8,0},{12,4},{16,20},{20,16},{24,28},{28,24},{1,9},{5... | collective-permute-start | bytes 1572872 | tf_op jit(solution)/shard_map/ppermute | solution.py:410
  438.8 16.6 %collective-permute-start.54 = (bf16[512,1024]{1,0:T(8,128)(2,1)}, bf16[512,1024]{1,0:T(8,128)(2,1)S(1)}, u32[]{:S(2)}, u32[]{:S(2)}) collective-permute-start(bf16[512,1024]{1,0:T(8,128)(2,1)} %pad_maximum_fusion.11), channel_id=1, source_target_pairs={{0,4},{4,0},{8,12},{12,8},{16,24},{20,28},{24,16},{28,20},{1,5},{5... | collective-permute-start | bytes 3145736 | tf_op jit(solution)/shard_map/ppermute | solution.py:410
  465.6 28.3 %collective-permute-start.64 = (bf16[512,1024]{1,0:T(8,128)(2,1)S(1)}, bf16[512,1024]{1,0:T(8,128)(2,1)S(1)}, u32[]{:S(2)}, u32[]{:S(2)}) collective-permute-start(bf16[512,1024]{1,0:T(8,128)(2,1)S(1)} %pad_maximum_fusion.12), channel_id=1, source_target_pairs={{0,4},{4,0},{8,12},{12,8},{16,24},{20,28},{24,16},{28,20},{1,5},{5... | collective-permute-start | bytes 3145736 | tf_op jit(solution)/shard_map/ppermute | solution.py:410
  467.4 26.5 %collective-permute-start.63 = (bf16[1024,256]{1,0:T(8,128)(2,1)S(1)}, bf16[1024,256]{1,0:T(8,128)(2,1)S(1)}, u32[]{:S(2)}, u32[]{:S(2)}) collective-permute-start(bf16[1024,256]{1,0:T(8,128)(2,1)S(1)} %add_convert_fusion.12), channel_id=1, source_target_pairs={{0,8},{4,12},{8,0},{12,4},{16,20},{20,16},{24,28},{28,24},{1,9},{5... | collective-permute-start | bytes 1572872 | tf_op jit(solution)/shard_map/ppermute | solution.py:410
  470.2 17.9 %collective-permute-start.61 = (bf16[256,512]{1,0:T(8,128)(2,1)S(1)}, bf16[256,512]{1,0:T(8,128)(2,1)S(1)}, u32[]{:S(2)}, u32[]{:S(2)}) collective-permute-start(bf16[256,512]{1,0:T(8,128)(2,1)S(1)} %add_convert_fusion.15), channel_id=1, source_target_pairs={{0,2},{1,3},{2,0},{3,1},{4,6},{5,7},{6,4},{7,5},{8,10},{9,11},{10,... | collective-permute-start | bytes 786440 | tf_op jit(solution)/shard_map/ppermute | solution.py:426
  472.5 21.3 %collective-permute-start.62 = (bf16[256,512]{1,0:T(8,128)(2,1)S(1)}, bf16[256,512]{1,0:T(8,128)(2,1)S(1)}, u32[]{:S(2)}, u32[]{:S(2)}) collective-permute-start(bf16[256,512]{1,0:T(8,128)(2,1)S(1)} %add_convert_fusion.15), channel_id=1, source_target_pairs={{0,3},{1,2},{2,1},{3,0},{4,7},{5,6},{6,5},{7,4},{8,11},{9,10},{10,... | collective-permute-start | bytes 786440 | tf_op jit(solution)/shard_map/ppermute | solution.py:426
  495.8 27.3 %collective-permute-start.66 = (bf16[256,2048]{1,0:T(8,128)(2,1)S(1)}, bf16[256,2048]{1,0:T(8,128)(2,1)S(1)}, u32[]{:S(2)}, u32[]{:S(2)}) collective-permute-start(bf16[256,2048]{1,0:T(8,128)(2,1)S(1)} %add_convert_fusion.2), channel_id=1, source_target_pairs={{0,8},{4,12},{8,0},{12,4},{16,20},{20,16},{24,28},{28,24},{1,9},{5... | collective-permute-start | bytes 3145736 | tf_op jit(solution)/shard_map/ppermute | solution.py:410
  502.0 21.1 %collective-permute-start.69 = (bf16[512,256]{1,0:T(8,128)(2,1)S(1)}, bf16[512,256]{1,0:T(8,128)(2,1)S(1)}, u32[]{:S(2)}, u32[]{:S(2)}) collective-permute-start(bf16[512,256]{1,0:T(8,128)(2,1)S(1)} %get-tuple-element.571), channel_id=1, source_target_pairs={{0,3},{1,2},{2,1},{3,0},{4,7},{5,6},{6,5},{7,4},{8,11},{9,10},{10,... | collective-permute-start | bytes 786440 | tf_op jit(solution)/shard_map/ppermute | solution.py:426
  523.1 25.9 %collective-permute-start.70 = (bf16[512,512]{1,0:T(8,128)(2,1)S(1)}, bf16[512,512]{1,0:T(8,128)(2,1)S(1)}, u32[]{:S(2)}, u32[]{:S(2)}) collective-permute-start(bf16[512,512]{1,0:T(8,128)(2,1)S(1)} %pad_maximum_fusion.16), channel_id=1, source_target_pairs={{0,8},{4,12},{8,0},{12,4},{16,20},{20,16},{24,28},{28,24},{1,9},{5... | collective-permute-start | bytes 1572872 | tf_op jit(solution)/shard_map/ppermute | solution.py:410
  527.9 21.1 %collective-permute-start.73 = (bf16[256,512]{1,0:T(8,128)(2,1)S(1)}, bf16[256,512]{1,0:T(8,128)(2,1)S(1)}, u32[]{:S(2)}, u32[]{:S(2)}) collective-permute-start(bf16[256,512]{1,0:T(8,128)(2,1)S(1)} %get-tuple-element.567), channel_id=1, source_target_pairs={{0,3},{1,2},{2,1},{3,0},{4,7},{5,6},{6,5},{7,4},{8,11},{9,10},{10,... | collective-permute-start | bytes 786440 | tf_op jit(solution)/shard_map/ppermute | solution.py:426
  (118 other events, 1579.3 us)

commit v4 on v3

--- a/solution.py
+++ b/solution.py
@@ -650,38 +650,45 @@
         part, own_part, d_sum, g_sent, u_sent, gbs, ubs, hids
     )
 
-    def row_sum_start(total, axis):
+    def prepare(total, axis):
         pieces = jnp.split(total, rows, axis)
         sent = jnp.concatenate([jnp.where(d == 0, pieces[1], pieces[2]), pieces[3]], axis)
-        return [pieces, to_near(sent, 0), axis]
-
-    def row_sum_next(state):
-        pieces, near, axis = state
+        return pieces[0], jnp.where(d == 0, pieces[2], pieces[1]), sent
+
+    def half_way(parts, near, axis):
         mine, theirs = jnp.split(near, 2, axis)
-        kept = jnp.where(d == 0, pieces[2], pieces[1])
-        theirs = (kept.astype(f32) + theirs.astype(f32)).astype(bf16)
-        return [pieces[0], mine, to_near(theirs, 1)]
-
-    def row_sum_end(state):
-        return state[0].astype(f32) + state[1].astype(f32) + state[2].astype(f32)
+        return (parts[0], mine), (parts[1].astype(f32) + theirs.astype(f32)).astype(bf16)
+
+    def finish(kept, far):
+        return kept[0].astype(f32) + kept[1].astype(f32) + far.astype(f32)
 
     def around(carry, part):
         return to_cols((part.astype(f32) + carry.astype(f32)).astype(bf16), 1)
 
+    def col_sum(total, axis):
+        pieces = xor_blocks(jnp.split(total.astype(bf16), cols, axis), c)
+        return [pieces[0]] + [to_xor_cols(pieces[k], k) for k in range(1, cols)]
+
+    def added(values):
+        return tree_sum([x.astype(f32) for x in values])
+
     carry = to_cols(part, 1)
-    d_state = row_sum_start(d_sum, 1)
+    d_parts = prepare(d_sum, 1)
+    d_near = to_near(d_parts[2], 0)
     g_received = to_core(g_sent)
     u_received = to_core(u_sent)
     outs = jnp.split(rows_product([hids[0]], [d_matrix], False, bf16), 2, 0)
     g_sum, u_sum = token_sums(h_parts, low, [gbs, ubs], full, [g_received, u_received])
-    part, carry, d_state[1], g_sum, u_sum, hids, outs = fence(
-        own_part, carry, d_state[1], g_sum, u_sum, hids, outs
-    )
+    g_parts, u_parts = prepare(g_sum, 0), prepare(u_sum, 0)
+    part, carry, d_near, g_parts, u_parts, hids, outs = fence(
+        own_part, carry, d_near, g_parts, u_parts, hids, outs
+    )
+
     out_carry = to_cols(outs[0], 1)
     out_last = outs[1]
-
-    d_state = row_sum_next(d_state)
-    g_state = row_sum_start(g_sum, 0)
+    g_near = to_near(g_parts[2], 0)
+    d_kept, d_theirs = half_way(d_parts, d_near, 1)
+    d_far = to_near(d_theirs, 1)
     hidden_in_back = part + carry.astype(f32)
     from_norm, mlp_gain_part = norm_back(hidden_in_back, middle, factor_two, gain_two)
     middle_grad = upstream + from_norm
@@ -690,41 +697,45 @@
     o_sent = token_sum([mixed], (0, width), [branch_back], high)
     outs = [None] + [rows_product([x], [d_matrix], False, bf16) for x in hids[1:-1]]
     outs += jnp.split(rows_product([hids[-1]], [d_matrix], False, bf16), 2, 0)
-    mixed_back, branch_back, o_sent, d_state[2], g_state[1], outs, hids, out_carry = fence(
-        mixed_back, branch_back, o_sent, d_state[2], g_state[1], outs, hids, out_carry
-    )
-    outs = list(outs)
+    mixed_back, branch_back, o_sent, d_far, g_near, outs, out_carry = fence(
+        mixed_back, branch_back, o_sent, d_far, g_near, outs, out_carry
+    )
+
+    u_near = to_near(u_parts[2], 0)
+    g_kept, g_theirs = half_way(g_parts, g_near, 0)
+    g_far = to_near(g_theirs, 1)
     for k in range(1, cols - 2):
         out_carry = around(out_carry, outs[k])
-
-    g_state = row_sum_next(g_state)
-    u_state = row_sum_start(u_sum, 0)
     o_received = to_core(o_sent)
     dq, dk, dv = attend_backward(
         q_rows, kv_all, mixed_back, top, cosine, -sine, row_ids, key_ids
     )
-    q_sent = token_sum([normed], high, [dq], (0, width))
     o_sum = token_sum([mixed], (0, width), [branch_back], low, o_received)
-    dq, dk, dv, q_sent, o_sum, g_state[2], u_state[1], out_carry = fence(
-        dq, dk, dv, q_sent, o_sum, g_state[2], u_state[1], out_carry
-    )
-
-    u_state = row_sum_next(u_state)
     o_low, o_high = jnp.split(o_sum, 2, 0)
-    o_low = row_sum_start(o_low, 1)
+    o_low = prepare(o_low, 1)
+    dq, dk, dv, o_low, o_high, g_far, u_near, out_carry = fence(
+        dq, dk, dv, o_low, o_high, g_far, u_near, out_carry
+    )
+
     kv_turned = jnp.concatenate([dk, dv], 1)
     kv_back_pre = kv_turned[reach * own :]
     back_parts = []
     for k in range(1, reach + 1):
         piece = kv_turned[(reach - k) * own : (reach - k + 1) * own].astype(bf16)
         back_parts.append(along(piece, -k))
+    u_kept, u_theirs = half_way(u_parts, u_near, 0)
+    u_far = to_near(u_theirs, 1)
+    o_low_near = to_near(o_low[2], 0)
+    q_sent = token_sum([normed], high, [dq], (0, width))
+    o_high = prepare(o_high, 1)
+    back_parts, q_sent, u_far, o_low_near, o_high = fence(
+        back_parts, q_sent, u_far, o_low_near, o_high
+    )
+
+    out_carry = around(out_carry, outs[cols - 2])
+    o_low_kept, o_theirs = half_way(o_low, o_low_near, 1)
+    o_low_far = to_near(o_theirs, 1)
     q_received = to_core(q_sent)
-    back_parts, q_received, u_state[2], o_low[1] = fence(
-        back_parts, q_received, u_state[2], o_low[1]
-    )
-    out_carry = around(out_carry, outs[cols - 2])
-
-    o_high = row_sum_start(o_high, 1)
     for piece in back_parts:
         kv_back_pre = kv_back_pre + piece.astype(f32)
     kv_back = jnp.concatenate(
@@ -732,69 +743,65 @@
     ).astype(bf16)
     kv_sent = token_sum([normed], high, [kv_back], (0, 2 * kv_width))
     kv_received = to_core(kv_sent)
-    q_sum = token_sum([normed], low, [dq], (0, width), q_received)
     kv_sum = token_sum([normed], low, [kv_back], (0, 2 * kv_width), kv_received)
-    kv_sum, q_sum, kv_back, o_high[1] = fence(kv_sum, q_sum, kv_back, o_high[1])
-    down_grad = row_sum_end(d_state)
-
-    kv_state = row_sum_start(kv_sum, 0)
-    q_low, q_high = jnp.split(q_sum, 2, 1)
-    q_low = row_sum_start(q_low, 0)
+    kv_parts = prepare(kv_sum, 0)
+    kv_parts, kv_back, o_low_far, q_received, o_high = fence(
+        kv_parts, kv_back, o_low_far, q_received, o_high
+    )
+
+    kv_near = to_near(kv_parts[2], 0)
+    o_high_near = to_near(o_high[2], 0)
     normed_back = rows_product([dq, kv_back], [q_matrix, kv_matrix], True, f32)
     from_norm, attention_gain_part = norm_back(normed_back, inputs, factor_one, gain_one)
     input_grad = xor_order(middle_grad + from_norm, target, blocks, 1)
     gains = xor_order(jnp.stack([attention_gain_part, mlp_gain_part]), target, blocks, 1)
-    kv_state[1], q_low[1], input_grad, gains, out_carry, down_grad = fence(
-        kv_state[1], q_low[1], input_grad, gains, out_carry, down_grad
-    )
-    kv_state = row_sum_next(kv_state)
-    o_low = row_sum_next(o_low)
-    for n in range(cols.bit_length() - 1):
-        gains = gains + to_xor_cols(gains, 1 << n)
-    gate_grad = row_sum_end(g_state)
-    kv_state[2], gains, o_low[2], gate_grad, o_high[1], q_high = fence(
-        kv_state[2], gains, o_low[2], gate_grad, o_high[1], q_high
-    )
-
-    kv_sum = row_sum_end(kv_state).astype(bf16)
-    o_high = row_sum_next(o_high)
-    q_high = row_sum_start(q_high, 0)
+    q_sum = token_sum([normed], low, [dq], (0, width), q_received)
+    kv_near, o_high_near, input_grad, gains, q_sum, out_carry = fence(
+        kv_near, o_high_near, input_grad, gains, q_sum, out_carry
+    )
+
+    kv_kept, kv_theirs = half_way(kv_parts, kv_near, 0)
+    kv_far = to_near(kv_theirs, 1)
+    o_high_kept, o_theirs = half_way(o_high, o_high_near, 1)
+    o_high_far = to_near(o_theirs, 1)
+    hops = [1 << n for n in range(cols.bit_length() - 1)]
+    gains = gains + to_xor_cols(gains, hops[0])
+    q_parts = prepare(q_sum, 0)
+    kv_far, o_high_far, gains, q_parts = fence(kv_far, o_high_far, gains, q_parts)
+
+    q_near = to_near(q_parts[2], 0)
+    kv_sum = finish(kv_kept, kv_far).astype(bf16)
     total = [kv_sum] + [to_xor_cols(kv_sum, k) for k in range(1, cols)]
-    up_grad = row_sum_end(u_state)
-    total, o_high[2], q_high[1], up_grad = fence(total, o_high[2], q_high[1], up_grad)
-
-    def col_sum(total, axis):
-        pieces = xor_blocks(jnp.split(total.astype(bf16), cols, axis), c)
-        return [pieces[0]] + [to_xor_cols(pieces[k], k) for k in range(1, cols)]
-
-    def added(values):
-        return tree_sum([x.astype(f32) for x in values])
-
-    total = tree_sum([x.astype(f32) for x in total]).astype(bf16)
+    for hop in hops[1:]:
+        gains = gains + to_xor_cols(gains, hop)
+    out_sum = jnp.concatenate(
+        [finish(o_low_kept, o_low_far), finish(o_high_kept, o_high_far)], 0
+    ).astype(bf16)
+    total, q_near, gains, out_sum = fence(total, q_near, gains, out_sum)
+
+    total = added(total).astype(bf16)
     one = to_near(total, 0)
-    low_pieces, low_near, _ = q_low
-    high_pieces, high_near, _ = q_high
-    q_state = row_sum_next(
-        [
-            [jnp.concatenate(pair, 1) for pair in zip(low_pieces, high_pieces)],
-            jnp.concatenate([low_near, high_near], 1),
-            0,
-        ]
-    )
-    out_parts = col_sum(jnp.concatenate([row_sum_end(o_low), row_sum_end(o_high)], 0), 0)
+    q_kept, q_theirs = half_way(q_parts, q_near, 0)
+    q_far = to_near(q_theirs, 1)
+    out_parts = col_sum(out_sum, 0)
+    one, d_far, g_far, u_far, out_carry = fence(one, d_far, g_far, u_far, out_carry)
+    down_grad, gate_grad, up_grad = finish(d_kept, d_far), finish(g_kept, g_far), finish(u_kept, u_far)
     piece = out_last.astype(f32) + out_carry.astype(f32)
     output = xor_order((middle + keep * piece).astype(bf16), target, blocks, 1)
-    one, q_state[2], out_parts, output, gains = fence(one, q_state[2], out_parts, output, gains)
+    one, q_far, out_parts, output, gains, down_grad, gate_grad, up_grad = fence(
+        one, q_far, out_parts, output, gains, down_grad, gate_grad, up_grad
+    )
+
     two = to_near(jnp.concatenate([total, one], 0), 1)
     gains = gains + to_near(gains, 0)
     gains = gains + to_near(gains, 1)
-    q_parts = col_sum(row_sum_end(q_state), 1)
+    q_cols = col_sum(finish(q_kept, q_far), 1)
     out_grad = added(out_parts)
-    two, q_parts, out_grad, gains = fence(two, q_parts, out_grad, gains)
+    two, q_cols, out_grad, gains = fence(two, q_cols, out_grad, gains)
     mine = jnp.concatenate([total, one, two], 0)
     theirs = to_core(mine)
     gains = gains + to_core(gains)
-    query_grad = added(q_parts)
+    query_grad = added(q_cols)
     found = blank((width, 2 * kv_width))
     for e, part in enumerate((mine, theirs)):
         near, far = (first, 3 - first) if e == 0 else (3 - first, first)

time: 567 us -> 552 us (0.974)
  waiting for transfers between devices: 184 us -> 170 us
  starting transfers between devices: 89.2 us -> 81 us
    ppermute x14, waiting for transfers between devices: 61.2 us -> 49.7 us  [to_xor_cols(): return lax.ppermute(value, 'cols', [(i, i ^ k) for i in range(cols)])]
    dynamic_update_slice x49, local copies, waits for them, and re-layouts: 14.3 us -> 20.5 us  [put(): return lax.dynamic_update_slice(full, piece, at)]
    ppermute x29 -> x28, starting transfers between devices: 23.7 us -> 21.5 us  [to_near(): return lax.ppermute(value, ('dp', 'rows'), pairs)]
    ppermute x29 -> x28, waiting for transfers between devices: 56.9 us -> 57.8 us  [to_near(): return lax.ppermute(value, ('dp', 'rows'), pairs)]
    unnamed x183 -> x170, local copies, waits for them, and re-layouts: 20.9 us -> 20.6 us
  transfers between devices with their start and end apart: 78 -> 77, of which waited for: 36 -> 36; matrix products, arithmetic and copies ran while one was open for 17% -> 20% of each run, Pallas kernels for 28% -> 28%
where the time goes in v4:
time: 552 us; the launch traced here: 544 us
  waiting for transfers between devices  170 us (31%)
  Pallas kernels  154 us (28%)
  starting transfers between devices  81 us (15%)
  other arithmetic  69.8 us (13%)
  local copies, waits for them, and re-layouts  49.2 us (9%)
  matrix products  15.6 us (3%)
    pallas_call x10, Pallas kernels, token_sums(): call(kernel, (pl.cdiv(rows_out, tile),), specs, [out] * many, [jax.ShapeD...  57.8 us
    ppermute x28, waiting for transfers between devices, to_near(): return lax.ppermute(value, ('dp', 'rows'), pairs)  57.8 us
    ppermute x14, waiting for transfers between devices, to_xor_cols(): return lax.ppermute(value, 'cols', [(i, i ^ k) for i in range(cols)])  49.7 us
    pallas_call x7, Pallas kernels, rows_products(): call(kernel, (columns // tile,), specs, [pl.BlockSpec((count, tile), lamb...  47.7 us
    ppermute x12, waiting for transfers between devices, to_cols(): lax.ppermute(value, 'cols', [(i, (i + k) % cols) for i in range(cols)])  39.3 us
    ppermute x28, starting transfers between devices, to_near(): return lax.ppermute(value, ('dp', 'rows'), pairs)  21.5 us
    unnamed x170, local copies, waits for them, and re-layouts  20.6 us
    dynamic_update_slice x49, local copies, waits for them, and re-layouts, put(): return lax.dynamic_update_slice(full, piece, at)  20.5 us
  transfers between devices with their start and end apart: 77, of which 36 were waited for; matrix products, arithmetic and copies ran while one was open for 20% of the time, Pallas kernels for 28%

profile of v4, /device:TPU:11, one launch (start us, length us, event | category | flops | bytes accessed | tf_op | source)
XLA Modules:
  0.0 543.9 jit_solution(2901856159600254512)
XLA Ops:
  33.8 3.5 collective-permute-done.9
  37.3 11.2 %collective-permute-done.5 = bf16[256,2048]{1,0:T(8,128)(2,1)S(1)} collective-permute-done((bf16[256,2048]{1,0:T(8,128)(2,1)S(1)}, bf16[256,2048]{1,0:T(8,128)(2,1)S(1)}, u32[]{:S(2)}, u32[]{:S(2)}) %collective-permute-start.5) | collective-permute-done | bytes 1048608 | tf_op jit(solution)/shard_map/ppermute | solution.py:410
  55.5 3.7 collective-permute-start.17
  63.2 7.4 %collective-permute-done.17 = bf16[256,512]{1,0:T(8,128)(2,1)S(1)} collective-permute-done((bf16[256,512]{1,0:T(8,128)(2,1)S(1)}, bf16[256,512]{1,0:T(8,128)(2,1)S(1)}, u32[]{:S(2)}, u32[]{:S(2)}) %collective-permute-start.17) | collective-permute-done | bytes 262176 | tf_op jit(solution)/shard_map/ppermute | solution.py:421
  70.5 5.6 %collective-permute-done.18 = bf16[256,512]{1,0:T(8,128)(2,1)S(1)} collective-permute-done((bf16[256,512]{1,0:T(8,128)(2,1)S(1)}, bf16[256,512]{1,0:T(8,128)(2,1)S(1)}, u32[]{:S(2)}, u32[]{:S(2)}) %collective-permute-start.18) | collective-permute-done | bytes 262176 | tf_op jit(solution)/shard_map/ppermute | solution.py:421
  76.3 4.2 collective-permute-done.11
  80.5 3.6 collective-permute-done.10
  90.3 8.3 %collective-permute-done.19 = bf16[256,2048]{1,0:T(8,128)(2,1)} collective-permute-done((bf16[256,2048]{1,0:T(8,128)(2,1)S(1)}, bf16[256,2048]{1,0:T(8,128)(2,1)}, u32[]{:S(2)}, u32[]{:S(2)}) %collective-permute-start.19) | collective-permute-done | bytes 1048608 | tf_op jit(solution)/shard_map/ppermute | solution.py:418
  105.6 10.8 %shard_map.214 = (bf16[256,2048]{1,0:T(8,128)(2,1)S(1)}, bf16[256,2048]{1,0:T(8,128)(2,1)S(1)}, f32[16,1,256]{2,1,0:T(1,128)S(1)}) custom-call(f32[256,2048]{1,0:T(8,128)S(1)} %fusion.40.pre_ref, bf16[768,512]{1,0:T(8,128)(2,1)S(1)} %constant_dynamic-update-slice_fusion.3.k_ref.v_ref, bf16[768,512]{1,0:T(8,128)(2,1)S(1)} %constant_dynamic-update-slice_fusion.3.k_ref.v_ref, ...), custom_call_target="tpu_custom_call" | custom-call | tf_op jit(solution)/shard_map/pallas_call | solution.py:68
  116.4 6.6 %collective-permute-done.20 = bf16[256,2048]{1,0:T(8,128)(2,1)} collective-permute-done((bf16[256,2048]{1,0:T(8,128)(2,1)}, bf16[256,2048]{1,0:T(8,128)(2,1)}, u32[]{:S(2)}, u32[]{:S(2)}) %collective-permute-start.20) | collective-permute-done | bytes 1048608 | tf_op jit(solution)/shard_map/ppermute | solution.py:418
  123.0 4.3 collective-permute-done.13
  146.4 16.4 %collective-permute-done.25 = bf16[1024,1408]{1,0:T(8,128)(2,1)} collective-permute-done((bf16[1024,1408]{1,0:T(8,128)(2,1)S(1)}, bf16[1024,1408]{1,0:T(8,128)(2,1)}, u32[]{:S(2)}, u32[]{:S(2)}) %collective-permute-start.25) | collective-permute-done | bytes 2883616 | tf_op jit(solution)/shard_map/ppermute | solution.py:410
  172.8 5.0 fusion.42.gate_ref
  177.9 5.0 fusion.43.up_ref
  182.9 9.7 %collective-permute-done.29 = bf16[256,2048]{1,0:T(8,128)(2,1)} collective-permute-done((bf16[256,2048]{1,0:T(8,128)(2,1)S(1)}, bf16[256,2048]{1,0:T(8,128)(2,1)}, u32[]{:S(2)}, u32[]{:S(2)}) %collective-permute-start.29) | collective-permute-done | bytes 1048608 | tf_op jit(solution)/shard_map/ppermute | solution.py:418
  197.8 9.2 %shard_map.219 = (bf16[512,1408]{1,0:T(8,128)(2,1)S(1)}, bf16[512,1408]{1,0:T(8,128)(2,1)S(1)}, bf16[512,1408]{1,0:T(8,128)(2,1)S(1)}) custom-call(bf16[512,2048]{1,0:T(8,128)(2,1)} %copy-done, f32[512,1408]{1,0:T(8,128)} %fusion.42.gate_ref, f32[512,1408]{1,0:T(8,128)} %fusion.43.up_ref, bf16[1408,2048]{1,0:T(8,128)(2,1)} %slice_dynamic-update-slice_fusion.8.d_ref.refs_0_), custom_call_target="tpu_custom_call" | custom-call | tf_op jit(solution)/shard_map/pallas_call | solution.py:217
  207.0 6.9 %shard_map.220 = bf16[256,2048]{1,0:T(8,128)(2,1)S(1)} custom-call(bf16[2048,1408]{1,0:T(8,128)(2,1)} %copy-done.10, bf16[2048,1408]{1,0:T(8,128)(2,1)} %copy-done.9, bf16[512,1408]{1,0:T(8,128)(2,1)S(1)} %get-tuple-element.376.refs_2_.refs_4_, bf16[512,1408]{1,0:T(8,128)(2,1)S(1)} %get-tuple-element.378.refs_3_.refs_5_.refs_4_), custom_call_target="tpu_custom_call" | custom-call | tf_op jit(solution)/shard_map/pallas_call | solution.py:248
  213.9 6.8 %collective-permute-done.31 = bf16[256,2048]{1,0:T(8,128)(2,1)S(1)} collective-permute-done((bf16[256,2048]{1,0:T(8,128)(2,1)}, bf16[256,2048]{1,0:T(8,128)(2,1)S(1)}, u32[]{:S(2)}, u32[]{:S(2)}) %collective-permute-start.31) | collective-permute-done | bytes 1048608 | tf_op jit(solution)/shard_map/ppermute | solution.py:418
  226.8 15.1 %shard_map.221 = (bf16[512,1408]{1,0:T(8,128)(2,1)S(1)}, bf16[512,1408]{1,0:T(8,128)(2,1)S(1)}, bf16[512,1408]{1,0:T(8,128)(2,1)S(1)}) custom-call(bf16[512,2048]{1,0:T(8,128)(2,1)} %copy-done.17, bf16[512,2048]{1,0:T(8,128)(2,1)} %copy-done.16, bf16[2048,1408]{1,0:T(8,128)(2,1)} %copy-done.10, bf16[2048,1408]{1,0:T(8,128)(2,1)} %copy-done.9, ...), custom_call_target="tpu_custom_call" | custom-call | tf_op jit(solution)/shard_map/pallas_call | solution.py:193
  242.0 7.1 %shard_map.222 = f32[256,2048]{1,0:T(8,128)S(1)} custom-call(bf16[2048,1408]{1,0:T(8,128)(2,1)} %copy-done.10, bf16[2048,1408]{1,0:T(8,128)(2,1)} %copy-done.9, bf16[512,1408]{1,0:T(8,128)(2,1)S(1)} %get-tuple-element.377.refs_2_.refs_3_, bf16[512,1408]{1,0:T(8,128)(2,1)S(1)} %get-tuple-element.379.refs_3_.refs_5_), custom_call_target="tpu_custom_call" | custom-call | tf_op jit(solution)/shard_map/pallas_call | solution.py:248
  249.1 7.0 %shard_map.223 = bf16[1408,1024]{1,0:T(8,128)(2,1)} custom-call(bf16[512,1408]{1,0:T(8,128)(2,1)S(1)} %get-tuple-element.384.refs_0_.refs_1_, bf16[512,1408]{1,0:T(8,128)(2,1)S(1)} %get-tuple-element.390.refs_1_, bf16[512,2048]{1,0:T(8,128)(2,1)S(1)} %copy-done.1, bf16[512,2048]{1,0:T(8,128)(2,1)} %copy-done.16), custom_call_target="tpu_custom_call" | custom-call | tf_op jit(solution)/shard_map/pallas_call | solution.py:291
  261.3 10.1 %shard_map.224 = (f32[256,2048]{1,0:T(8,128)}, f32[256,2048]{1,0:T(8,128)}) custom-call(bf16[2048,1408]{1,0:T(8,128)(2,1)} %copy-done.10, bf16[2048,1408]{1,0:T(8,128)(2,1)} %copy-done.9, bf16[512,1408]{1,0:T(8,128)(2,1)S(1)} %get-tuple-element.377.refs_2_.refs_3_, bf16[512,1408]{1,0:T(8,128)(2,1)S(1)} %get-tuple-element.379.refs_3_.refs_5_, ...), custom_call_target="tpu_custom_call" | custom-call | tf_op jit(solution)/shard_map/pallas_call | solution.py:248
  271.5 9.3 %shard_map.226 = (bf16[1024,1408]{1,0:T(8,128)(2,1)}, bf16[1024,1408]{1,0:T(8,128)(2,1)}) custom-call(bf16[512,2048]{1,0:T(8,128)(2,1)} %copy-done.24, bf16[512,2048]{1,0:T(8,128)(2,1)} %copy-done.17, bf16[512,1408]{1,0:T(8,128)(2,1)S(1)} %get-tuple-element.376.refs_2_.refs_4_, bf16[512,1408]{1,0:T(8,128)(2,1)S(1)} %get-tuple-element.377.refs_2_.refs_3_, ...), custom_call_target="tpu_custom_call" | custom-call | tf_op jit(solution)/shard_map/pallas_call | solution.py:291
  282.4 7.7 %shard_map.225 = bf16[1408,1024]{1,0:T(8,128)(2,1)} custom-call(bf16[512,1408]{1,0:T(8,128)(2,1)S(1)} %get-tuple-element.384.refs_0_.refs_1_, bf16[512,1408]{1,0:T(8,128)(2,1)S(1)} %get-tuple-element.390.refs_1_, bf16[512,2048]{1,0:T(8,128)(2,1)S(1)} %copy-done.1, bf16[512,2048]{1,0:T(8,128)(2,1)} %copy-done.16, bf16[1408,1024]{1,0:T(8,128)(2,1)} %copy-done.38), custom_call_target="tpu_custom_call" | custom-call | tf_op jit(solution)/shard_map/pallas_call | solution.py:291
  290.1 3.2 add_convert_fusion.5
  293.8 3.9 collective-permute-start.35
  299.4 5.8 %shard_map.228 = bf16[512,2048]{1,0:T(8,128)(2,1)S(1)} custom-call(bf16[1408,2048]{1,0:T(8,128)(2,1)} %slice_dynamic-update-slice_fusion.8.d_ref.refs_0_, bf16[512,1408]{1,0:T(8,128)(2,1)S(1)} %get-tuple-element.384.refs_0_.refs_1_), custom_call_target="tpu_custom_call" | custom-call | tf_op jit(solution)/shard_map/pallas_call | solution.py:248
  306.8 9.8 %shard_map.227 = (bf16[1024,1408]{1,0:T(8,128)(2,1)}, bf16[1024,1408]{1,0:T(8,128)(2,1)}) custom-call(bf16[512,2048]{1,0:T(8,128)(2,1)} %copy-done.24, bf16[512,2048]{1,0:T(8,128)(2,1)} %copy-done.17, bf16[512,1408]{1,0:T(8,128)(2,1)S(1)} %get-tuple-element.376.refs_2_.refs_4_, bf16[512,1408]{1,0:T(8,128)(2,1)S(1)} %get-tuple-element.377.refs_2_.refs_3_, ...), custom_call_target="tpu_custom_call" | custom-call | tf_op jit(solution)/shard_map/pallas_call | solution.py:291
  316.6 4.4 broadcast_select_fusion.4
  329.4 3.4 multiply_convert_fusion
  332.9 5.0 shard_map.230
  337.9 5.6 %shard_map.229.back_ref = bf16[256,2048]{1,0:T(8,128)(2,1)S(1)} custom-call(bf16[2048,2048]{1,0:T(8,128)(2,1)} %copy-done.11, bf16[256,2048]{1,0:T(8,128)(2,1)S(1)} %get-tuple-element.397.refs_1_), custom_call_target="tpu_custom_call" | custom-call | tf_op jit(solution)/shard_map/pallas_call | solution.py:248
  343.5 5.9 %shard_map.231 = bf16[512,2048]{1,0:T(8,128)(2,1)S(1)} custom-call(bf16[1408,2048]{1,0:T(8,128)(2,1)} %slice_dynamic-update-slice_fusion.8.d_ref.refs_0_, bf16[512,1408]{1,0:T(8,128)(2,1)S(1)} %get-tuple-element.390.refs_1_), custom_call_target="tpu_custom_call" | custom-call | tf_op jit(solution)/shard_map/pallas_call | solution.py:248
  359.8 13.4 %shard_map.232 = (bf16[256,2048]{1,0:T(8,128)(2,1)S(1)}, f32[768,256]{1,0:T(8,128)S(1)}, f32[768,256]{1,0:T(8,128)S(1)}) custom-call(bf16[256,2048]{1,0:T(8,128)(2,1)S(1)} %copy-done.8, bf16[768,512]{1,0:T(8,128)(2,1)S(1)} %constant_dynamic-update-slice_fusion.3.k_ref.v_ref, bf16[768,512]{1,0:T(8,128)(2,1)S(1)} %constant_dynamic-update-slice_fusion.3.k_ref.v_ref, ...), custom_call_target="tpu_custom_call" | custom-call | tf_op jit(solution)/shard_map/pallas_call | solution.py:128
  373.2 7.6 %shard_map.233 = bf16[2048,1024]{1,0:T(8,128)(2,1)} custom-call(bf16[256,2048]{1,0:T(8,128)(2,1)S(1)} %copy-done.6, bf16[256,2048]{1,0:T(8,128)(2,1)S(1)} %get-tuple-element.397.refs_1_, bf16[2048,1024]{1,0:T(8,128)(2,1)} %collective-permute-done.42.refs_2_), custom_call_target="tpu_custom_call" | custom-call | tf_op jit(solution)/shard_map/pallas_call | solution.py:291
  386.6 3.7 collective-permute-start.46
  392.6 3.5 shard_map.234
  397.2 6.2 %collective-permute-done.47 = bf16[256,512]{1,0:T(8,128)(2,1)S(1)} collective-permute-done((bf16[256,512]{1,0:T(8,128)(2,1)S(1)}, bf16[256,512]{1,0:T(8,128)(2,1)S(1)}, u32[]{:S(2)}, u32[]{:S(2)}) %collective-permute-start.47) | collective-permute-done | bytes 262176 | tf_op jit(solution)/shard_map/ppermute | solution.py:421
  418.9 6.2 %shard_map.237 = f32[256,2048]{1,0:T(8,128)S(1)} custom-call(bf16[2048,2048]{1,0:T(8,128)(2,1)} %copy-done.12, bf16[2048,512]{1,0:T(8,128)(2,1)S(1)} %copy-done.4, bf16[256,2048]{1,0:T(8,128)(2,1)S(1)} %get-tuple-element.406.refs_1_.refs_2_, bf16[256,512]{1,0:T(8,128)(2,1)S(1)} %pad_maximum_fusion.18.refs_1_.refs_3_), custom_call_target="tpu_custom_call" | custom-call | tf_op jit(solution)/shard_map/pallas_call | solution.py:248
  428.2 5.7 %shard_map.238 = bf16[1024,2048]{1,0:T(8,128)(2,1)} custom-call(bf16[256,2048]{1,0:T(8,128)(2,1)S(1)} %fusion.2.refs_0_, bf16[256,2048]{1,0:T(8,128)(2,1)S(1)} %get-tuple-element.406.refs_1_.refs_2_, bf16[1024,2048]{1,0:T(8,128)(2,1)} %copy-done.31), custom_call_target="tpu_custom_call" | custom-call | tf_op jit(solution)/shard_map/pallas_call | solution.py:291
  434.0 4.5 collective-permute-done.55
  440.3 2.9 collective-permute-start.58
  445.2 4.6 collective-permute-done.57
  454.6 3.0 collective-permute-start.59
  460.2 18.4 %collective-permute-done.63 = f32[2,2048]{1,0:T(2,128)S(1)} collective-permute-done((f32[2,2048]{1,0:T(2,128)S(1)}, f32[2,2048]{1,0:T(2,128)S(1)}, u32[]{:S(2)}, u32[]{:S(2)}) %collective-permute-start.63) | collective-permute-done | bytes 16416 | tf_op jit(solution)/shard_map/ppermute | solution.py:426
  488.9 2.9 convert_add_fusion.4
  497.4 10.4 %collective-permute-done.68 = bf16[512,256]{1,0:T(8,128)(2,1)S(1)} collective-permute-done((bf16[512,256]{1,0:T(8,128)(2,1)S(1)}, bf16[512,256]{1,0:T(8,128)(2,1)S(1)}, u32[]{:S(2)}, u32[]{:S(2)}) %collective-permute-start.68) | collective-permute-done | bytes 262176 | tf_op jit(solution)/shard_map/ppermute | solution.py:426
  520.4 16.0 %collective-permute-done.72 = bf16[256,512]{1,0:T(8,128)(2,1)S(1)} collective-permute-done((bf16[256,512]{1,0:T(8,128)(2,1)S(1)}, bf16[256,512]{1,0:T(8,128)(2,1)S(1)}, u32[]{:S(2)}, u32[]{:S(2)}) %collective-permute-start.72) | collective-permute-done | bytes 262176 | tf_op jit(solution)/shard_map/ppermute | solution.py:426
  (523 shorter events, 198.9 us)
Async XLA Ops:
  1.7 21.6 %collective-permute-start.2 = (bf16[256,512]{1,0:T(8,128)(2,1)S(1)}, bf16[256,512]{1,0:T(8,128)(2,1)}, u32[]{:S(2)}, u32[]{:S(2)}) collective-permute-start(bf16[256,512]{1,0:T(8,128)(2,1)S(1)} %slice_select_fusion), channel_id=1, source_target_pairs={{0,1},{1,0},{2,3},{3,2},{4,5},{5,4},{6,7},{7,6},{8,9},{9,8},{10,11... | collective-permute-start | bytes 786440 | tf_op jit(solution)/shard_map/ppermute | solution.py:426
  1.9 22.7 %collective-permute-start.3 = (bf16[256,512]{1,0:T(8,128)(2,1)S(1)}, bf16[256,512]{1,0:T(8,128)(2,1)}, u32[]{:S(2)}, u32[]{:S(2)}) collective-permute-start(bf16[256,512]{1,0:T(8,128)(2,1)S(1)} %slice_select_fusion), channel_id=1, source_target_pairs={{0,2},{1,3},{2,0},{3,1},{4,6},{5,7},{6,4},{7,5},{8,10},{9,11},{10,... | collective-permute-start | bytes 786440 | tf_op jit(solution)/shard_map/ppermute | solution.py:426
  4.3 22.6 %collective-permute-start.4 = (bf16[256,512]{1,0:T(8,128)(2,1)S(1)}, bf16[256,512]{1,0:T(8,128)(2,1)}, u32[]{:S(2)}, u32[]{:S(2)}) collective-permute-start(bf16[256,512]{1,0:T(8,128)(2,1)S(1)} %slice_select_fusion), channel_id=1, source_target_pairs={{0,3},{1,2},{2,1},{3,0},{4,7},{5,6},{6,5},{7,4},{8,11},{9,10},{10,... | collective-permute-start | bytes 786440 | tf_op jit(solution)/shard_map/ppermute | solution.py:426
  13.7 17.5 %collective-permute-start.7 = (bf16[256,512]{1,0:T(8,128)(2,1)}, bf16[256,512]{1,0:T(8,128)(2,1)S(1)}, u32[]{:S(2)}, u32[]{:S(2)}) collective-permute-start(bf16[256,512]{1,0:T(8,128)(2,1)} %collective-permute-done), channel_id=1, source_target_pairs={{0,16},{16,0},{1,17},{17,1},{2,18},{18,2},{3,19},{19,3},{4,20},{20... | collective-permute-start | bytes 786440 | tf_op jit(solution)/shard_map/ppermute | solution.py:415
  28.4 20.2 %collective-permute-start.5 = (bf16[256,2048]{1,0:T(8,128)(2,1)S(1)}, bf16[256,2048]{1,0:T(8,128)(2,1)S(1)}, u32[]{:S(2)}, u32[]{:S(2)}) collective-permute-start(bf16[256,2048]{1,0:T(8,128)(2,1)S(1)} %get-tuple-element.624), channel_id=1, source_target_pairs={{0,4},{4,0},{8,12},{12,8},{16,24},{20,28},{24,16},{28,20},{1,5},{5... | collective-permute-start | bytes 3145736 | tf_op jit(solution)/shard_map/ppermute | solution.py:410
  29.7 18.9 %collective-permute-start.6 = (bf16[256,2048]{1,0:T(8,128)(2,1)S(1)}, bf16[256,2048]{1,0:T(8,128)(2,1)S(1)}, u32[]{:S(2)}, u32[]{:S(2)}) collective-permute-start(bf16[256,2048]{1,0:T(8,128)(2,1)S(1)} %get-tuple-element.624), channel_id=1, source_target_pairs={{0,16},{16,0},{1,17},{17,1},{2,18},{18,2},{3,19},{19,3},{4,20},{20... | collective-permute-start | bytes 3145736 | tf_op jit(solution)/shard_map/ppermute | solution.py:415
  31.2 24.3 %collective-permute-start.16 = (bf16[256,2048]{1,0:T(8,128)(2,1)S(1)}, bf16[256,2048]{1,0:T(8,128)(2,1)S(1)}, u32[]{:S(2)}, u32[]{:S(2)}) collective-permute-start(bf16[256,2048]{1,0:T(8,128)(2,1)S(1)} %multiply_convert_fusion.2), channel_id=1, source_target_pairs={{0,1},{1,2},{2,3},{3,0},{4,5},{5,6},{6,7},{7,4},{8,9},{9,10},{10,1... | collective-permute-start | bytes 3145736 | tf_op jit(solution)/shard_map/ppermute | solution.py:418
  48.8 27.3 %collective-permute-start.12 = (bf16[256,2048]{1,0:T(8,128)(2,1)S(1)}, bf16[256,2048]{1,0:T(8,128)(2,1)S(1)}, u32[]{:S(2)}, u32[]{:S(2)}) collective-permute-start(bf16[256,2048]{1,0:T(8,128)(2,1)S(1)} %collective-permute-done.5), channel_id=1, source_target_pairs={{0,16},{16,0},{1,17},{17,1},{2,18},{18,2},{3,19},{19,3},{4,20},{20... | collective-permute-start | bytes 3145736 | tf_op jit(solution)/shard_map/ppermute | solution.py:415
  51.1 33.0 %collective-permute-start.10 = (bf16[512,2048]{1,0:T(8,128)(2,1)S(1)}, bf16[512,2048]{1,0:T(8,128)(2,1)S(1)}, u32[]{:S(2)}, u32[]{:S(2)}) collective-permute-start(bf16[512,2048]{1,0:T(8,128)(2,1)S(1)} %pad_maximum_fusion.1), channel_id=1, source_target_pairs={{0,8},{4,12},{8,0},{12,4},{16,20},{20,16},{24,28},{28,24},{1,9},{5... | collective-permute-start | bytes 6291464 | tf_op jit(solution)/shard_map/ppermute | solution.py:410
  55.5 15.0 %collective-permute-start.17 = (bf16[256,512]{1,0:T(8,128)(2,1)S(1)}, bf16[256,512]{1,0:T(8,128)(2,1)S(1)}, u32[]{:S(2)}, u32[]{:S(2)}) collective-permute-start(bf16[256,512]{1,0:T(8,128)(2,1)S(1)} %pad_maximum_fusion.17), channel_id=1, source_target_pairs={{0,2},{1,3},{4,6},{5,7},{8,10},{9,11},{12,14},{13,15},{16,18},{17,... | collective-permute-start | bytes 786440 | tf_op jit(solution)/shard_map/ppermute | solution.py:421
  59.3 16.9 %collective-permute-start.18 = (bf16[256,512]{1,0:T(8,128)(2,1)S(1)}, bf16[256,512]{1,0:T(8,128)(2,1)S(1)}, u32[]{:S(2)}, u32[]{:S(2)}) collective-permute-start(bf16[256,512]{1,0:T(8,128)(2,1)S(1)} %pad_maximum_fusion.17), channel_id=1, source_target_pairs={{0,1},{1,2},{2,3},{4,5},{5,6},{6,7},{8,9},{9,10},{10,11},{12,13},{... | collective-permute-start | bytes 786440 | tf_op jit(solution)/shard_map/ppermute | solution.py:421
  62.2 18.3 %collective-permute-start.11 = (bf16[1408,256]{1,0:T(8,128)(2,1)S(1)}, bf16[1408,256]{1,0:T(8,128)(2,1)S(1)}, u32[]{:S(2)}, u32[]{:S(2)}) collective-permute-start(bf16[1408,256]{1,0:T(8,128)(2,1)S(1)} %get-tuple-element.313), channel_id=1, source_target_pairs={{0,4},{4,0},{8,12},{12,8},{16,24},{20,28},{24,16},{28,20},{1,5},{5... | collective-permute-start | bytes 2162696 | tf_op jit(solution)/shard_map/ppermute | solution.py:410
  70.5 28.1 %collective-permute-start.19 = (bf16[256,2048]{1,0:T(8,128)(2,1)S(1)}, bf16[256,2048]{1,0:T(8,128)(2,1)}, u32[]{:S(2)}, u32[]{:S(2)}) collective-permute-start(bf16[256,2048]{1,0:T(8,128)(2,1)S(1)} %collective-permute-done.16), channel_id=1, source_target_pairs={{0,1},{1,2},{2,3},{3,0},{4,5},{5,6},{6,7},{7,4},{8,9},{9,10},{10,1... | collective-permute-start | bytes 3145736 | tf_op jit(solution)/shard_map/ppermute | solution.py:418
  84.1 17.7 %collective-permute-start.21 = (bf16[2048,256]{1,0:T(8,128)(2,1)S(1)}, bf16[2048,256]{1,0:T(8,128)(2,1)S(1)}, u32[]{:S(2)}, u32[]{:S(2)}) collective-permute-start(bf16[2048,256]{1,0:T(8,128)(2,1)S(1)} %collective-permute-done.9), channel_id=1, source_target_pairs={{0,16},{16,0},{1,17},{17,1},{2,18},{18,2},{3,19},{19,3},{4,20},{20... | collective-permute-start | bytes 3145736 | tf_op jit(solution)/shard_map/ppermute | solution.py:415
  86.4 40.9 %collective-permute-start.13 = (bf16[4096,256]{1,0:T(8,128)(2,1)}, bf16[4096,256]{1,0:T(8,128)(2,1)}, u32[]{:S(2)}, u32[]{:S(2)}) collective-permute-start(bf16[4096,256]{1,0:T(8,128)(2,1)} %pad_maximum_fusion.2), channel_id=1, source_target_pairs={{0,8},{4,12},{8,0},{12,4},{16,20},{20,16},{24,28},{28,24},{1,9},{5... | collective-permute-start | bytes 6291464 | tf_op jit(solution)/shard_map/ppermute | solution.py:410
  89.1 33.9 %collective-permute-start.14 = (bf16[512,1408]{1,0:T(8,128)(2,1)S(1)}, bf16[512,1408]{1,0:T(8,128)(2,1)S(1)}, u32[]{:S(2)}, u32[]{:S(2)}) collective-permute-start(bf16[512,1408]{1,0:T(8,128)(2,1)S(1)} %pad_maximum_fusion.4), channel_id=1, source_target_pairs={{0,4},{4,0},{8,12},{12,8},{16,24},{20,28},{24,16},{28,20},{1,5},{5... | collective-permute-start | bytes 4325384 | tf_op jit(solution)/shard_map/ppermute | solution.py:410
  98.6 24.4 %collective-permute-start.20 = (bf16[256,2048]{1,0:T(8,128)(2,1)}, bf16[256,2048]{1,0:T(8,128)(2,1)}, u32[]{:S(2)}, u32[]{:S(2)}) collective-permute-start(bf16[256,2048]{1,0:T(8,128)(2,1)} %collective-permute-done.19), channel_id=1, source_target_pairs={{0,1},{1,2},{2,3},{3,0},{4,5},{5,6},{6,7},{7,4},{8,9},{9,10},{10,1... | collective-permute-start | bytes 3145736 | tf_op jit(solution)/shard_map/ppermute | solution.py:418
  129.0 33.8 %collective-permute-start.25 = (bf16[1024,1408]{1,0:T(8,128)(2,1)S(1)}, bf16[1024,1408]{1,0:T(8,128)(2,1)}, u32[]{:S(2)}, u32[]{:S(2)}) collective-permute-start(bf16[1024,1408]{1,0:T(8,128)(2,1)S(1)} %pad_maximum_fusion), channel_id=1, source_target_pairs={{0,8},{4,12},{8,0},{12,4},{16,20},{20,16},{24,28},{28,24},{1,9},{5... | collective-permute-start | bytes 8650760 | tf_op jit(solution)/shard_map/ppermute | solution.py:410
  139.0 24.4 %collective-permute-start.26 = (bf16[256,2048]{1,0:T(8,128)(2,1)S(1)}, bf16[256,2048]{1,0:T(8,128)(2,1)S(1)}, u32[]{:S(2)}, u32[]{:S(2)}) collective-permute-start(bf16[256,2048]{1,0:T(8,128)(2,1)S(1)} %multiply_convert_fusion.1), channel_id=1, source_target_pairs={{0,1},{1,2},{2,3},{3,0},{4,5},{5,6},{6,7},{7,4},{8,9},{9,10},{10,1... | collective-permute-start | bytes 3145736 | tf_op jit(solution)/shard_map/ppermute | solution.py:418
  164.8 27.8 %collective-permute-start.28 = (bf16[2816,256]{1,0:T(8,128)(2,1)S(1)}, bf16[2816,256]{1,0:T(8,128)(2,1)S(1)}, u32[]{:S(2)}, u32[]{:S(2)}) collective-permute-start(bf16[2816,256]{1,0:T(8,128)(2,1)S(1)} %pad_maximum_fusion.5), channel_id=1, source_target_pairs={{0,8},{4,12},{8,0},{12,4},{16,20},{20,16},{24,28},{28,24},{1,9},{5... | collective-permute-start | bytes 4325384 | tf_op jit(solution)/shard_map/ppermute | solution.py:410
  166.0 26.5 %collective-permute-start.29 = (bf16[256,2048]{1,0:T(8,128)(2,1)S(1)}, bf16[256,2048]{1,0:T(8,128)(2,1)}, u32[]{:S(2)}, u32[]{:S(2)}) collective-permute-start(bf16[256,2048]{1,0:T(8,128)(2,1)S(1)} %collective-permute-done.26), channel_id=1, source_target_pairs={{0,1},{1,2},{2,3},{3,0},{4,5},{5,6},{6,7},{7,4},{8,9},{9,10},{10,1... | collective-permute-start | bytes 3145736 | tf_op jit(solution)/shard_map/ppermute | solution.py:418
  193.2 27.5 %collective-permute-start.31 = (bf16[256,2048]{1,0:T(8,128)(2,1)}, bf16[256,2048]{1,0:T(8,128)(2,1)S(1)}, u32[]{:S(2)}, u32[]{:S(2)}) collective-permute-start(bf16[256,2048]{1,0:T(8,128)(2,1)} %collective-permute-done.29), channel_id=1, source_target_pairs={{0,1},{1,2},{2,3},{3,0},{4,5},{5,6},{6,7},{7,4},{8,9},{9,10},{10,1... | collective-permute-start | bytes 3145736 | tf_op jit(solution)/shard_map/ppermute | solution.py:418
  220.6 35.5 %collective-permute-start.32 = (bf16[256,2048]{1,0:T(8,128)(2,1)S(1)}, bf16[256,2048]{1,0:T(8,128)(2,1)}, u32[]{:S(2)}, u32[]{:S(2)}) collective-permute-start(bf16[256,2048]{1,0:T(8,128)(2,1)S(1)} %shard_map.220), channel_id=1, source_target_pairs={{0,1},{1,2},{2,3},{3,0},{4,5},{5,6},{6,7},{7,4},{8,9},{9,10},{10,1... | collective-permute-start | bytes 3145736 | tf_op jit(solution)/shard_map/ppermute | solution.py:418
  258.5 22.3 %collective-permute-start.34 = (bf16[1408,1024]{1,0:T(8,128)(2,1)}, bf16[1408,1024]{1,0:T(8,128)(2,1)S(1)}, u32[]{:S(2)}, u32[]{:S(2)}) collective-permute-start(bf16[1408,1024]{1,0:T(8,128)(2,1)} %shard_map.223), channel_id=1, source_target_pairs={{0,16},{16,0},{1,17},{17,1},{2,18},{18,2},{3,19},{19,3},{4,20},{20... | collective-permute-start | bytes 8650760 | tf_op jit(solution)/shard_map/ppermute | solution.py:415
  259.2 30.9 %collective-permute-start.33 = (bf16[256,2048]{1,0:T(8,128)(2,1)}, bf16[256,2048]{1,0:T(8,128)(2,1)}, u32[]{:S(2)}, u32[]{:S(2)}) collective-permute-start(bf16[256,2048]{1,0:T(8,128)(2,1)} %add_convert_fusion.6), channel_id=1, source_target_pairs={{0,1},{1,2},{2,3},{3,0},{4,5},{5,6},{6,7},{7,4},{8,9},{9,10},{10,1... | collective-permute-start | bytes 3145736 | tf_op jit(solution)/shard_map/ppermute | solution.py:418
  293.8 29.7 %collective-permute-start.35 = (bf16[256,2048]{1,0:T(8,128)(2,1)}, bf16[256,2048]{1,0:T(8,128)(2,1)}, u32[]{:S(2)}, u32[]{:S(2)}) collective-permute-start(bf16[256,2048]{1,0:T(8,128)(2,1)} %add_convert_fusion.5), channel_id=1, source_target_pairs={{0,1},{1,2},{2,3},{3,0},{4,5},{5,6},{6,7},{7,4},{8,9},{9,10},{10,1... | collective-permute-start | bytes 3145736 | tf_op jit(solution)/shard_map/ppermute | solution.py:418
  299.1 24.4 %collective-permute-start.36 = (bf16[1408,512]{1,0:T(8,128)(2,1)}, bf16[1408,512]{1,0:T(8,128)(2,1)}, u32[]{:S(2)}, u32[]{:S(2)}) collective-permute-start(bf16[1408,512]{1,0:T(8,128)(2,1)} %pad_maximum_fusion.6), channel_id=1, source_target_pairs={{0,4},{4,0},{8,12},{12,8},{16,24},{20,28},{24,16},{28,20},{1,5},{5... | collective-permute-start | bytes 4325384 | tf_op jit(solution)/shard_map/ppermute | solution.py:410
  325.9 23.7 %collective-permute-start.39 = (bf16[1408,256]{1,0:T(8,128)(2,1)}, bf16[1408,256]{1,0:T(8,128)(2,1)}, u32[]{:S(2)}, u32[]{:S(2)}) collective-permute-start(bf16[1408,256]{1,0:T(8,128)(2,1)} %add_convert_fusion.9), channel_id=1, source_target_pairs={{0,8},{4,12},{8,0},{12,4},{16,20},{20,16},{24,28},{28,24},{1,9},{5... | collective-permute-start | bytes 2162696 | tf_op jit(solution)/shard_map/ppermute | solution.py:410
  326.3 26.2 %collective-permute-start.40 = (bf16[512,1408]{1,0:T(8,128)(2,1)}, bf16[512,1408]{1,0:T(8,128)(2,1)}, u32[]{:S(2)}, u32[]{:S(2)}) collective-permute-start(bf16[512,1408]{1,0:T(8,128)(2,1)} %pad_maximum_fusion.7), channel_id=1, source_target_pairs={{0,4},{4,0},{8,12},{12,8},{16,24},{20,28},{24,16},{28,20},{1,5},{5... | collective-permute-start | bytes 4325384 | tf_op jit(solution)/shard_map/ppermute | solution.py:410
  327.4 23.6 %collective-permute-start.41 = (bf16[256,2048]{1,0:T(8,128)(2,1)}, bf16[256,2048]{1,0:T(8,128)(2,1)}, u32[]{:S(2)}, u32[]{:S(2)}) collective-permute-start(bf16[256,2048]{1,0:T(8,128)(2,1)} %get-tuple-element.391), channel_id=1, source_target_pairs={{0,1},{1,2},{2,3},{3,0},{4,5},{5,6},{6,7},{7,4},{8,9},{9,10},{10,1... | collective-permute-start | bytes 3145736 | tf_op jit(solution)/shard_map/ppermute | solution.py:418
  352.5 20.7 %collective-permute-start.42 = (bf16[2048,1024]{1,0:T(8,128)(2,1)S(1)}, bf16[2048,1024]{1,0:T(8,128)(2,1)}, u32[]{:S(2)}, u32[]{:S(2)}) collective-permute-start(bf16[2048,1024]{1,0:T(8,128)(2,1)S(1)} %copy-done.30), channel_id=1, source_target_pairs={{0,16},{16,0},{1,17},{17,1},{2,18},{18,2},{3,19},{19,3},{4,20},{20... | collective-permute-start | bytes 12582920 | tf_op jit(solution)/shard_map/ppermute | solution.py:415
  353.4 29.9 %collective-permute-start.44 = (bf16[512,1408]{1,0:T(8,128)(2,1)}, bf16[512,1408]{1,0:T(8,128)(2,1)}, u32[]{:S(2)}, u32[]{:S(2)}) collective-permute-start(bf16[512,1408]{1,0:T(8,128)(2,1)} %pad_maximum_fusion.8), channel_id=1, source_target_pairs={{0,4},{4,0},{8,12},{12,8},{16,24},{20,28},{24,16},{28,20},{1,5},{5... | collective-permute-start | bytes 4325384 | tf_op jit(solution)/shard_map/ppermute | solution.py:410
  356.6 26.7 %collective-permute-start.45 = (bf16[256,2048]{1,0:T(8,128)(2,1)}, bf16[256,2048]{1,0:T(8,128)(2,1)}, u32[]{:S(2)}, u32[]{:S(2)}) collective-permute-start(bf16[256,2048]{1,0:T(8,128)(2,1)} %add_convert_fusion.4), channel_id=1, source_target_pairs={{0,1},{1,2},{2,3},{3,0},{4,5},{5,6},{6,7},{7,4},{8,9},{9,10},{10,1... | collective-permute-start | bytes 3145736 | tf_op jit(solution)/shard_map/ppermute | solution.py:418
  359.0 24.3 %collective-permute-start.43 = (bf16[256,1408]{1,0:T(8,128)(2,1)}, bf16[256,1408]{1,0:T(8,128)(2,1)}, u32[]{:S(2)}, u32[]{:S(2)}) collective-permute-start(bf16[256,1408]{1,0:T(8,128)(2,1)} %add_convert_fusion.8), channel_id=1, source_target_pairs={{0,8},{4,12},{8,0},{12,4},{16,20},{20,16},{24,28},{28,24},{1,9},{5... | collective-permute-start | bytes 2162696 | tf_op jit(solution)/shard_map/ppermute | solution.py:410
  383.3 21.5 %collective-permute-start.49 = (bf16[1024,512]{1,0:T(8,128)(2,1)S(1)}, bf16[1024,512]{1,0:T(8,128)(2,1)S(1)}, u32[]{:S(2)}, u32[]{:S(2)}) collective-permute-start(bf16[1024,512]{1,0:T(8,128)(2,1)S(1)} %pad_maximum_fusion.10), channel_id=1, source_target_pairs={{0,4},{4,0},{8,12},{12,8},{16,24},{20,28},{24,16},{28,20},{1,5},{5... | collective-permute-start | bytes 3145736 | tf_op jit(solution)/shard_map/ppermute | solution.py:410
  385.7 18.2 %collective-permute-start.48 = (bf16[256,1408]{1,0:T(8,128)(2,1)S(1)}, bf16[256,1408]{1,0:T(8,128)(2,1)S(1)}, u32[]{:S(2)}, u32[]{:S(2)}) collective-permute-start(bf16[256,1408]{1,0:T(8,128)(2,1)S(1)} %add_convert_fusion.7), channel_id=1, source_target_pairs={{0,8},{4,12},{8,0},{12,4},{16,20},{20,16},{24,28},{28,24},{1,9},{5... | collective-permute-start | bytes 2162696 | tf_op jit(solution)/shard_map/ppermute | solution.py:410
  410.7 27.8 %collective-permute-start.55 = (bf16[256,2048]{1,0:T(8,128)(2,1)S(1)}, bf16[256,2048]{1,0:T(8,128)(2,1)}, u32[]{:S(2)}, u32[]{:S(2)}) collective-permute-start(bf16[256,2048]{1,0:T(8,128)(2,1)S(1)} %add_convert_fusion.3), channel_id=1, source_target_pairs={{0,1},{1,2},{2,3},{3,0},{4,5},{5,6},{6,7},{7,4},{8,9},{9,10},{10,1... | collective-permute-start | bytes 3145736 | tf_op jit(solution)/shard_map/ppermute | solution.py:418
  417.1 21.4 %collective-permute-start.53 = (bf16[512,512]{1,0:T(8,128)(2,1)S(1)}, bf16[512,512]{1,0:T(8,128)(2,1)S(1)}, u32[]{:S(2)}, u32[]{:S(2)}) collective-permute-start(bf16[512,512]{1,0:T(8,128)(2,1)S(1)} %pad_maximum_fusion.15), channel_id=1, source_target_pairs={{0,4},{4,0},{8,12},{12,8},{16,24},{20,28},{24,16},{28,20},{1,5},{5... | collective-permute-start | bytes 1572872 | tf_op jit(solution)/shard_map/ppermute | solution.py:410
  418.2 20.3 %collective-permute-start.54 = (bf16[1024,512]{1,0:T(8,128)(2,1)}, bf16[1024,512]{1,0:T(8,128)(2,1)S(1)}, u32[]{:S(2)}, u32[]{:S(2)}) collective-permute-start(bf16[1024,512]{1,0:T(8,128)(2,1)} %pad_maximum_fusion.11), channel_id=1, source_target_pairs={{0,4},{4,0},{8,12},{12,8},{16,24},{20,28},{24,16},{28,20},{1,5},{5... | collective-permute-start | bytes 3145736 | tf_op jit(solution)/shard_map/ppermute | solution.py:410
  450.6 30.5 %collective-permute-start.62 = (bf16[512,2048]{1,0:T(8,128)(2,1)}, bf16[512,2048]{1,0:T(8,128)(2,1)}, u32[]{:S(2)}, u32[]{:S(2)}) collective-permute-start(bf16[512,2048]{1,0:T(8,128)(2,1)} %pad_maximum_fusion.3), channel_id=1, source_target_pairs={{0,4},{4,0},{8,12},{12,8},{16,24},{20,28},{24,16},{28,20},{1,5},{5... | collective-permute-start | bytes 6291464 | tf_op jit(solution)/shard_map/ppermute | solution.py:410
  454.6 24.0 %collective-permute-start.59 = (bf16[256,512]{1,0:T(8,128)(2,1)S(1)}, bf16[256,512]{1,0:T(8,128)(2,1)S(1)}, u32[]{:S(2)}, u32[]{:S(2)}) collective-permute-start(bf16[256,512]{1,0:T(8,128)(2,1)S(1)} %add_convert_fusion.15), channel_id=1, source_target_pairs={{0,1},{1,0},{2,3},{3,2},{4,5},{5,4},{6,7},{7,6},{8,9},{9,8},{10,11... | collective-permute-start | bytes 786440 | tf_op jit(solution)/shard_map/ppermute | solution.py:426
  457.6 21.1 %collective-permute-start.60 = (bf16[256,512]{1,0:T(8,128)(2,1)S(1)}, bf16[256,512]{1,0:T(8,128)(2,1)S(1)}, u32[]{:S(2)}, u32[]{:S(2)}) collective-permute-start(bf16[256,512]{1,0:T(8,128)(2,1)S(1)} %add_convert_fusion.15), channel_id=1, source_target_pairs={{0,2},{1,3},{2,0},{3,1},{4,6},{5,7},{6,4},{7,5},{8,10},{9,11},{10,... | collective-permute-start | bytes 786440 | tf_op jit(solution)/shard_map/ppermute | solution.py:426
  457.6 23.5 %collective-permute-start.61 = (bf16[256,512]{1,0:T(8,128)(2,1)S(1)}, bf16[256,512]{1,0:T(8,128)(2,1)S(1)}, u32[]{:S(2)}, u32[]{:S(2)}) collective-permute-start(bf16[256,512]{1,0:T(8,128)(2,1)S(1)} %add_convert_fusion.15), channel_id=1, source_target_pairs={{0,3},{1,2},{2,1},{3,0},{4,7},{5,6},{6,5},{7,4},{8,11},{9,10},{10,... | collective-permute-start | bytes 786440 | tf_op jit(solution)/shard_map/ppermute | solution.py:426
  458.8 19.8 %collective-permute-start.63 = (f32[2,2048]{1,0:T(2,128)S(1)}, f32[2,2048]{1,0:T(2,128)S(1)}, u32[]{:S(2)}, u32[]{:S(2)}) collective-permute-start(f32[2,2048]{1,0:T(2,128)S(1)} %add.420), channel_id=1, source_target_pairs={{0,2},{1,3},{2,0},{3,1},{4,6},{5,7},{6,4},{7,5},{8,10},{9,11},{10,... | collective-permute-start | bytes 49160 | tf_op jit(solution)/shard_map/ppermute | solution.py:426
  483.1 24.7 %collective-permute-start.65 = (bf16[256,2048]{1,0:T(8,128)(2,1)S(1)}, bf16[256,2048]{1,0:T(8,128)(2,1)S(1)}, u32[]{:S(2)}, u32[]{:S(2)}) collective-permute-start(bf16[256,2048]{1,0:T(8,128)(2,1)S(1)} %add_convert_fusion.2), channel_id=1, source_target_pairs={{0,8},{4,12},{8,0},{12,4},{16,20},{20,16},{24,28},{28,24},{1,9},{5... | collective-permute-start | bytes 3145736 | tf_op jit(solution)/shard_map/ppermute | solution.py:410
  484.7 23.1 %collective-permute-start.68 = (bf16[512,256]{1,0:T(8,128)(2,1)S(1)}, bf16[512,256]{1,0:T(8,128)(2,1)S(1)}, u32[]{:S(2)}, u32[]{:S(2)}) collective-permute-start(bf16[512,256]{1,0:T(8,128)(2,1)S(1)} %get-tuple-element.615), channel_id=1, source_target_pairs={{0,3},{1,2},{2,1},{3,0},{4,7},{5,6},{6,5},{7,4},{8,11},{9,10},{10,... | collective-permute-start | bytes 786440 | tf_op jit(solution)/shard_map/ppermute | solution.py:426
  507.9 28.5 %collective-permute-start.69 = (bf16[512,512]{1,0:T(8,128)(2,1)S(1)}, bf16[512,512]{1,0:T(8,128)(2,1)S(1)}, u32[]{:S(2)}, u32[]{:S(2)}) collective-permute-start(bf16[512,512]{1,0:T(8,128)(2,1)S(1)} %pad_maximum_fusion.16), channel_id=1, source_target_pairs={{0,8},{4,12},{8,0},{12,4},{16,20},{20,16},{24,28},{28,24},{1,9},{5... | collective-permute-start | bytes 1572872 | tf_op jit(solution)/shard_map/ppermute | solution.py:410
  511.9 24.5 %collective-permute-start.72 = (bf16[256,512]{1,0:T(8,128)(2,1)S(1)}, bf16[256,512]{1,0:T(8,128)(2,1)S(1)}, u32[]{:S(2)}, u32[]{:S(2)}) collective-permute-start(bf16[256,512]{1,0:T(8,128)(2,1)S(1)} %get-tuple-element.611), channel_id=1, source_target_pairs={{0,3},{1,2},{2,1},{3,0},{4,7},{5,6},{6,5},{7,4},{8,11},{9,10},{10,... | collective-permute-start | bytes 786440 | tf_op jit(solution)/shard_map/ppermute | solution.py:426
  (111 other events, 891.5 us)

commit v5 on v4

--- a/solution.py
+++ b/solution.py
@@ -495,8 +495,6 @@
         [rotate(kv_pre[:, :kv_width], cosine, sine), kv_pre[:, kv_width:]], 1
     ).astype(bf16)
 
-    w_mine, w_rest = halves(w_down, 1)
-    w_one = to_near(w_mine, 0)
     kv_own, feeds[1] = fence(kv_own, feeds[1])
     kv_before = [along(kv_own, k) for k in range(reach, 0, -1)]
     for k in range(2, cols - 1):
@@ -512,10 +510,9 @@
     key_ids = lax.dynamic_slice_in_dim(ids_padded, start, span, 0)
     row_ids = key_ids[reach * own :]
 
-    (q_two, w_one, q_matrix, o_mine, o_rest, o_one, w_gate, w_up) = fence(
-        q_two, w_one, q_matrix, o_mine, o_rest, o_one, w_gate, w_up
-    )
-    feeds.append(to_cols(after(feeds[-1], q_two), 1))
+    (q_two, q_matrix, o_mine, o_rest, o_one, w_gate, w_up, w_down) = fence(
+        q_two, q_matrix, o_mine, o_rest, o_one, w_gate, w_up, w_down
+    )
 
     o_two = to_near(jnp.concatenate([o_mine, o_one], 0), 1)
     q_two_other = to_core(q_two)
@@ -523,6 +520,7 @@
     u_mine, u_rest = halves(w_up, 0)
     gu_mine = jnp.concatenate([g_mine, u_mine], 0)
     gu_one = to_near(gu_mine, 0)
+    w_mine, w_rest = halves(w_down, 1)
     o_one_other = to_core(o_one)
     kv_all = jnp.concatenate(list(kv_before) + [kv_own], 0)
     rows_two = q_two.shape[0] // 2
@@ -531,6 +529,7 @@
         q_matrix = put(q_matrix, two[:rows_two], 0, spot(far, e), 0)
         q_matrix = put(q_matrix, two[rows_two:], 0, spot(3, e), 0)
     q_pre = nn(normed, q_matrix)
+    feeds.append(to_cols(after(feeds[-1], q_pre), 1))
     mixed, q_rows, top = attend_forward(q_pre, kv_all, cosine, sine, row_ids, key_ids)
     o_matrix = blank((width, width))
     o_matrix = put(o_matrix, o_mine, 1, spot(0, 0), 0)
@@ -538,13 +537,13 @@
     o_matrix = put(o_matrix, o_one, 1, spot(first, 0), 0)
     o_matrix = put(o_matrix, o_one_other, 1, spot(3 - first, 1), 0)
 
-    (o_two, gu_one, mixed, q_rows, top, feeds, o_matrix, w_mine, w_rest, w_one, gu_mine) = fence(
-        o_two, gu_one, mixed, q_rows, top, feeds, o_matrix, w_mine, w_rest, w_one, gu_mine
+    (o_two, gu_one, mixed, q_rows, top, o_matrix, w_mine, w_rest, gu_mine, feeds) = fence(
+        o_two, gu_one, mixed, q_rows, top, o_matrix, w_mine, w_rest, gu_mine, feeds
     )
     gu_two = to_near(jnp.concatenate([gu_mine, gu_one], 0), 1)
     o_two_other = to_core(o_two)
     gu_one_other = to_core(gu_one)
-    w_one_other = to_core(w_one)
+    w_one = to_near(w_mine, 0)
     rows_two = o_two.shape[0] // 2
     for e, two in ((0, o_two), (1, o_two_other)):
         far = 3 - first if e == 0 else first
@@ -554,8 +553,8 @@
     middle = inputs + keep * branch
     factor_two = norm_factor(middle)
     hidden_own = (middle * factor_two * gain_two).astype(bf16)
-    hidden_own, o_matrix, gu_one_other, w_one_other, gu_one, w_one, gu_mine, g_rest, u_rest = fence(
-        hidden_own, o_matrix, gu_one_other, w_one_other, gu_one, w_one, gu_mine, g_rest, u_rest
+    hidden_own, o_matrix, gu_one_other, gu_one, gu_mine, g_rest, u_rest = fence(
+        hidden_own, o_matrix, gu_one_other, gu_one, gu_mine, g_rest, u_rest
     )
     chunks = [hidden_own, to_cols(hidden_own, 1)]
     g_matrix, u_matrix = blank((width, units)), blank((width, units))
@@ -570,8 +569,6 @@
     d_matrix = blank((units, width))
     d_matrix = put(d_matrix, w_mine, 1, spot(0, 0), 0)
     d_matrix = put(d_matrix, w_rest, 1, spot(0, 1), 0)
-    d_matrix = put(d_matrix, w_one, 1, spot(first, 0), 0)
-    d_matrix = put(d_matrix, w_one_other, 1, spot(3 - first, 1), 0)
 
     gu_two, g_matrix, u_matrix, d_matrix, w_mine, w_one, chunks = fence(
         gu_two, g_matrix, u_matrix, d_matrix, w_mine, w_one, chunks
@@ -579,6 +576,9 @@
     chunks = list(chunks)
     w_two = to_near(jnp.concatenate([w_mine, w_one], 0), 1)
     gu_two_other = to_core(gu_two)
+    w_one_other = to_core(w_one)
+    d_matrix = put(d_matrix, w_one, 1, spot(first, 0), 0)
+    d_matrix = put(d_matrix, w_one_other, 1, spot(3 - first, 1), 0)
     for e, two in ((0, gu_two), (1, gu_two_other)):
         far = 3 - first if e == 0 else first
         for n, at in enumerate((spot(far, e), spot(3, e))):

time: 552 us -> 552 us (level)
  starting transfers between devices: 81 us -> 86.7 us
    ppermute x12, waiting for transfers between devices: 39.3 us -> 29.8 us  [to_cols(): lax.ppermute(value, 'cols', [(i, (i + k) % cols) for i in range(cols)])]
    unnamed x170 -> x166, local copies, waits for them, and re-layouts: 20.6 us -> 20.4 us
  transfers between devices with their start and end apart: 77 -> 77, of which waited for: 36 -> 33; matrix products, arithmetic and copies ran while one was open for 20% -> 19% of each run, Pallas kernels for 28% -> 28%
where the time goes in v5:
time: 552 us; the launch traced here: 542 us
  waiting for transfers between devices  167 us (30%)
  Pallas kernels  154 us (28%)
  starting transfers between devices  86.7 us (16%)
  other arithmetic  68 us (12%)
  local copies, waits for them, and re-layouts  46.4 us (8%)
  matrix products  15.6 us (3%)
    ppermute x28, waiting for transfers between devices, to_near(): return lax.ppermute(value, ('dp', 'rows'), pairs)  61.6 us
    pallas_call x10, Pallas kernels, token_sums(): call(kernel, (pl.cdiv(rows_out, tile),), specs, [out] * many, [jax.ShapeD...  57.9 us
    ppermute x14, waiting for transfers between devices, to_xor_cols(): return lax.ppermute(value, 'cols', [(i, i ^ k) for i in range(cols)])  50 us
    pallas_call x7, Pallas kernels, rows_products(): call(kernel, (columns // tile,), specs, [pl.BlockSpec((count, tile), lamb...  47.9 us
    ppermute x12, waiting for transfers between devices, to_cols(): lax.ppermute(value, 'cols', [(i, (i + k) % cols) for i in range(cols)])  29.8 us
    ppermute x28, starting transfers between devices, to_near(): return lax.ppermute(value, ('dp', 'rows'), pairs)  21.5 us
    ppermute x4, waiting for transfers between devices, along(): lax.ppermute(value, 'cols', [(i, i + k) for i in range(cols) if 0 <= i +...  20.6 us
    unnamed x166, local copies, waits for them, and re-layouts  20.4 us
  transfers between devices with their start and end apart: 77, of which 33 were waited for; matrix products, arithmetic and copies ran while one was open for 19% of the time, Pallas kernels for 28%

profile of v5, /device:TPU:11, one launch (start us, length us, event | category | flops | bytes accessed | tf_op | source)
XLA Modules:
  0.0 542.4 jit_solution(13315981826122899792)
XLA Ops:
  33.8 3.6 collective-permute-done.9
  37.3 11.2 %collective-permute-done.5 = bf16[256,2048]{1,0:T(8,128)(2,1)S(1)} collective-permute-done((bf16[256,2048]{1,0:T(8,128)(2,1)S(1)}, bf16[256,2048]{1,0:T(8,128)(2,1)S(1)}, u32[]{:S(2)}, u32[]{:S(2)}) %collective-permute-start.5) | collective-permute-done | bytes 1048608 | tf_op jit(solution)/shard_map/ppermute | solution.py:410
  55.5 3.8 collective-permute-start.16
  61.5 9.1 %collective-permute-done.16 = bf16[256,512]{1,0:T(8,128)(2,1)S(1)} collective-permute-done((bf16[256,512]{1,0:T(8,128)(2,1)S(1)}, bf16[256,512]{1,0:T(8,128)(2,1)S(1)}, u32[]{:S(2)}, u32[]{:S(2)}) %collective-permute-start.16) | collective-permute-done | bytes 262176 | tf_op jit(solution)/shard_map/ppermute | solution.py:421
  70.6 5.6 %collective-permute-done.17 = bf16[256,512]{1,0:T(8,128)(2,1)S(1)} collective-permute-done((bf16[256,512]{1,0:T(8,128)(2,1)S(1)}, bf16[256,512]{1,0:T(8,128)(2,1)S(1)}, u32[]{:S(2)}, u32[]{:S(2)}) %collective-permute-start.17) | collective-permute-done | bytes 262176 | tf_op jit(solution)/shard_map/ppermute | solution.py:421
  88.1 10.6 %collective-permute-done.19 = bf16[256,2048]{1,0:T(8,128)(2,1)} collective-permute-done((bf16[256,2048]{1,0:T(8,128)(2,1)S(1)}, bf16[256,2048]{1,0:T(8,128)(2,1)}, u32[]{:S(2)}, u32[]{:S(2)}) %collective-permute-start.19) | collective-permute-done | bytes 1048608 | tf_op jit(solution)/shard_map/ppermute | solution.py:418
  101.8 10.8 %shard_map.214 = (bf16[256,2048]{1,0:T(8,128)(2,1)S(1)}, bf16[256,2048]{1,0:T(8,128)(2,1)S(1)}, f32[16,1,256]{2,1,0:T(1,128)S(1)}) custom-call(f32[256,2048]{1,0:T(8,128)S(1)} %fusion.40.pre_ref, bf16[768,512]{1,0:T(8,128)(2,1)S(1)} %constant_dynamic-update-slice_fusion.3.k_ref.v_ref, bf16[768,512]{1,0:T(8,128)(2,1)S(1)} %constant_dynamic-update-slice_fusion.3.k_ref.v_ref, ...), custom_call_target="tpu_custom_call" | custom-call | tf_op jit(solution)/shard_map/pallas_call | solution.py:68
  112.6 3.3 collective-permute-done.13
  115.9 4.2 collective-permute-done.12
  120.1 3.1 collective-permute-done.20
  140.4 4.3 collective-permute-done.24
  144.8 22.0 %collective-permute-done.23 = bf16[1024,1408]{1,0:T(8,128)(2,1)} collective-permute-done((bf16[1024,1408]{1,0:T(8,128)(2,1)S(1)}, bf16[1024,1408]{1,0:T(8,128)(2,1)}, u32[]{:S(2)}, u32[]{:S(2)}) %collective-permute-start.23) | collective-permute-done | bytes 2883616 | tf_op jit(solution)/shard_map/ppermute | solution.py:410
  178.4 5.0 fusion.42.gate_ref
  183.4 5.0 fusion.43.up_ref
  188.4 5.1 collective-permute-done.29
  201.1 9.2 %shard_map.219 = (bf16[512,1408]{1,0:T(8,128)(2,1)S(1)}, bf16[512,1408]{1,0:T(8,128)(2,1)S(1)}, bf16[512,1408]{1,0:T(8,128)(2,1)S(1)}) custom-call(bf16[512,2048]{1,0:T(8,128)(2,1)} %copy-done, f32[512,1408]{1,0:T(8,128)} %fusion.42.gate_ref, f32[512,1408]{1,0:T(8,128)} %fusion.43.up_ref, bf16[1408,2048]{1,0:T(8,128)(2,1)} %slice_dynamic-update-slice_fusion.8.d_ref.refs_0_), custom_call_target="tpu_custom_call" | custom-call | tf_op jit(solution)/shard_map/pallas_call | solution.py:217
  210.3 6.9 %shard_map.220 = bf16[256,2048]{1,0:T(8,128)(2,1)S(1)} custom-call(bf16[2048,1408]{1,0:T(8,128)(2,1)} %copy-done.10, bf16[2048,1408]{1,0:T(8,128)(2,1)} %copy-done.9, bf16[512,1408]{1,0:T(8,128)(2,1)S(1)} %get-tuple-element.370.refs_2_.refs_4_, bf16[512,1408]{1,0:T(8,128)(2,1)S(1)} %get-tuple-element.372.refs_3_.refs_5_.refs_4_), custom_call_target="tpu_custom_call" | custom-call | tf_op jit(solution)/shard_map/pallas_call | solution.py:248
  217.2 3.1 collective-permute-done.31
  227.2 15.1 %shard_map.221 = (bf16[512,1408]{1,0:T(8,128)(2,1)S(1)}, bf16[512,1408]{1,0:T(8,128)(2,1)S(1)}, bf16[512,1408]{1,0:T(8,128)(2,1)S(1)}) custom-call(bf16[512,2048]{1,0:T(8,128)(2,1)} %copy-done.17, bf16[512,2048]{1,0:T(8,128)(2,1)} %copy-done.16, bf16[2048,1408]{1,0:T(8,128)(2,1)} %copy-done.10, bf16[2048,1408]{1,0:T(8,128)(2,1)} %copy-done.9, ...), custom_call_target="tpu_custom_call" | custom-call | tf_op jit(solution)/shard_map/pallas_call | solution.py:193
  242.3 7.1 %shard_map.222 = f32[256,2048]{1,0:T(8,128)S(1)} custom-call(bf16[2048,1408]{1,0:T(8,128)(2,1)} %copy-done.10, bf16[2048,1408]{1,0:T(8,128)(2,1)} %copy-done.9, bf16[512,1408]{1,0:T(8,128)(2,1)S(1)} %get-tuple-element.371.refs_2_.refs_3_, bf16[512,1408]{1,0:T(8,128)(2,1)S(1)} %get-tuple-element.373.refs_3_.refs_5_), custom_call_target="tpu_custom_call" | custom-call | tf_op jit(solution)/shard_map/pallas_call | solution.py:248
  249.4 7.0 %shard_map.223 = bf16[1408,1024]{1,0:T(8,128)(2,1)} custom-call(bf16[512,1408]{1,0:T(8,128)(2,1)S(1)} %get-tuple-element.378.refs_0_.refs_1_, bf16[512,1408]{1,0:T(8,128)(2,1)S(1)} %get-tuple-element.384.refs_1_, bf16[512,2048]{1,0:T(8,128)(2,1)S(1)} %copy-done.1, bf16[512,2048]{1,0:T(8,128)(2,1)} %copy-done.16), custom_call_target="tpu_custom_call" | custom-call | tf_op jit(solution)/shard_map/pallas_call | solution.py:291
  260.1 10.1 %shard_map.224 = (f32[256,2048]{1,0:T(8,128)}, f32[256,2048]{1,0:T(8,128)}) custom-call(bf16[2048,1408]{1,0:T(8,128)(2,1)} %copy-done.10, bf16[2048,1408]{1,0:T(8,128)(2,1)} %copy-done.9, bf16[512,1408]{1,0:T(8,128)(2,1)S(1)} %get-tuple-element.371.refs_2_.refs_3_, bf16[512,1408]{1,0:T(8,128)(2,1)S(1)} %get-tuple-element.373.refs_3_.refs_5_, ...), custom_call_target="tpu_custom_call" | custom-call | tf_op jit(solution)/shard_map/pallas_call | solution.py:248
  270.2 9.3 %shard_map.226 = (bf16[1024,1408]{1,0:T(8,128)(2,1)}, bf16[1024,1408]{1,0:T(8,128)(2,1)}) custom-call(bf16[512,2048]{1,0:T(8,128)(2,1)} %copy-done.24, bf16[512,2048]{1,0:T(8,128)(2,1)} %copy-done.17, bf16[512,1408]{1,0:T(8,128)(2,1)S(1)} %get-tuple-element.370.refs_2_.refs_4_, bf16[512,1408]{1,0:T(8,128)(2,1)S(1)} %get-tuple-element.371.refs_2_.refs_3_, ...), custom_call_target="tpu_custom_call" | custom-call | tf_op jit(solution)/shard_map/pallas_call | solution.py:291
  281.1 7.7 %shard_map.225 = bf16[1408,1024]{1,0:T(8,128)(2,1)} custom-call(bf16[512,1408]{1,0:T(8,128)(2,1)S(1)} %get-tuple-element.378.refs_0_.refs_1_, bf16[512,1408]{1,0:T(8,128)(2,1)S(1)} %get-tuple-element.384.refs_1_, bf16[512,2048]{1,0:T(8,128)(2,1)S(1)} %copy-done.1, bf16[512,2048]{1,0:T(8,128)(2,1)} %copy-done.16, bf16[1408,1024]{1,0:T(8,128)(2,1)} %copy-done.38), custom_call_target="tpu_custom_call" | custom-call | tf_op jit(solution)/shard_map/pallas_call | solution.py:291
  288.8 3.2 add_convert_fusion.5
  292.6 3.6 collective-permute-start.35
  297.6 5.8 %shard_map.228 = bf16[512,2048]{1,0:T(8,128)(2,1)S(1)} custom-call(bf16[1408,2048]{1,0:T(8,128)(2,1)} %slice_dynamic-update-slice_fusion.8.d_ref.refs_0_, bf16[512,1408]{1,0:T(8,128)(2,1)S(1)} %get-tuple-element.378.refs_0_.refs_1_), custom_call_target="tpu_custom_call" | custom-call | tf_op jit(solution)/shard_map/pallas_call | solution.py:248
  305.0 9.8 %shard_map.227 = (bf16[1024,1408]{1,0:T(8,128)(2,1)}, bf16[1024,1408]{1,0:T(8,128)(2,1)}) custom-call(bf16[512,2048]{1,0:T(8,128)(2,1)} %copy-done.24, bf16[512,2048]{1,0:T(8,128)(2,1)} %copy-done.17, bf16[512,1408]{1,0:T(8,128)(2,1)S(1)} %get-tuple-element.370.refs_2_.refs_4_, bf16[512,1408]{1,0:T(8,128)(2,1)S(1)} %get-tuple-element.371.refs_2_.refs_3_, ...), custom_call_target="tpu_custom_call" | custom-call | tf_op jit(solution)/shard_map/pallas_call | solution.py:291
  314.8 4.4 broadcast_select_fusion.7
  328.5 3.4 multiply_convert_fusion
  331.9 5.0 shard_map.230
  337.0 5.6 %shard_map.229.back_ref = bf16[256,2048]{1,0:T(8,128)(2,1)S(1)} custom-call(bf16[2048,2048]{1,0:T(8,128)(2,1)} %copy-done.11, bf16[256,2048]{1,0:T(8,128)(2,1)S(1)} %get-tuple-element.391.refs_1_), custom_call_target="tpu_custom_call" | custom-call | tf_op jit(solution)/shard_map/pallas_call | solution.py:248
  342.6 5.9 %shard_map.231 = bf16[512,2048]{1,0:T(8,128)(2,1)S(1)} custom-call(bf16[1408,2048]{1,0:T(8,128)(2,1)} %slice_dynamic-update-slice_fusion.8.d_ref.refs_0_, bf16[512,1408]{1,0:T(8,128)(2,1)S(1)} %get-tuple-element.384.refs_1_), custom_call_target="tpu_custom_call" | custom-call | tf_op jit(solution)/shard_map/pallas_call | solution.py:248
  358.9 13.4 %shard_map.232 = (bf16[256,2048]{1,0:T(8,128)(2,1)S(1)}, f32[768,256]{1,0:T(8,128)S(1)}, f32[768,256]{1,0:T(8,128)S(1)}) custom-call(bf16[256,2048]{1,0:T(8,128)(2,1)S(1)} %copy-done.8, bf16[768,512]{1,0:T(8,128)(2,1)S(1)} %constant_dynamic-update-slice_fusion.3.k_ref.v_ref, bf16[768,512]{1,0:T(8,128)(2,1)S(1)} %constant_dynamic-update-slice_fusion.3.k_ref.v_ref, ...), custom_call_target="tpu_custom_call" | custom-call | tf_op jit(solution)/shard_map/pallas_call | solution.py:128
  372.3 7.6 %shard_map.233 = bf16[2048,1024]{1,0:T(8,128)(2,1)} custom-call(bf16[256,2048]{1,0:T(8,128)(2,1)S(1)} %copy-done.6, bf16[256,2048]{1,0:T(8,128)(2,1)S(1)} %get-tuple-element.391.refs_1_, bf16[2048,1024]{1,0:T(8,128)(2,1)} %collective-permute-done.42.refs_2_), custom_call_target="tpu_custom_call" | custom-call | tf_op jit(solution)/shard_map/pallas_call | solution.py:291
  385.7 3.5 collective-permute-start.46
  391.4 3.5 shard_map.234
  395.9 5.9 %collective-permute-done.47 = bf16[256,512]{1,0:T(8,128)(2,1)S(1)} collective-permute-done((bf16[256,512]{1,0:T(8,128)(2,1)S(1)}, bf16[256,512]{1,0:T(8,128)(2,1)S(1)}, u32[]{:S(2)}, u32[]{:S(2)}) %collective-permute-start.47) | collective-permute-done | bytes 262176 | tf_op jit(solution)/shard_map/ppermute | solution.py:421
  417.7 6.5 %shard_map.237 = f32[256,2048]{1,0:T(8,128)S(1)} custom-call(bf16[2048,2048]{1,0:T(8,128)(2,1)} %copy-done.12, bf16[2048,512]{1,0:T(8,128)(2,1)S(1)} %copy-done.4, bf16[256,2048]{1,0:T(8,128)(2,1)S(1)} %get-tuple-element.400.refs_1_.refs_2_, bf16[256,512]{1,0:T(8,128)(2,1)S(1)} %pad_maximum_fusion.18.refs_1_.refs_3_), custom_call_target="tpu_custom_call" | custom-call | tf_op jit(solution)/shard_map/pallas_call | solution.py:248
  427.2 5.7 %shard_map.238 = bf16[1024,2048]{1,0:T(8,128)(2,1)} custom-call(bf16[256,2048]{1,0:T(8,128)(2,1)S(1)} %fusion.2.refs_0_, bf16[256,2048]{1,0:T(8,128)(2,1)S(1)} %get-tuple-element.400.refs_1_.refs_2_, bf16[1024,2048]{1,0:T(8,128)(2,1)} %copy-done.31), custom_call_target="tpu_custom_call" | custom-call | tf_op jit(solution)/shard_map/pallas_call | solution.py:291
  433.1 4.2 collective-permute-done.55
  439.1 2.9 collective-permute-start.58
  444.0 4.6 collective-permute-done.57
  452.7 3.0 collective-permute-start.59
  458.3 18.3 %collective-permute-done.63 = f32[2,2048]{1,0:T(2,128)S(1)} collective-permute-done((f32[2,2048]{1,0:T(2,128)S(1)}, f32[2,2048]{1,0:T(2,128)S(1)}, u32[]{:S(2)}, u32[]{:S(2)}) %collective-permute-start.63) | collective-permute-done | bytes 16416 | tf_op jit(solution)/shard_map/ppermute | solution.py:426
  487.8 2.9 convert_add_fusion.4
  496.2 11.1 %collective-permute-done.68 = bf16[512,256]{1,0:T(8,128)(2,1)S(1)} collective-permute-done((bf16[512,256]{1,0:T(8,128)(2,1)S(1)}, bf16[512,256]{1,0:T(8,128)(2,1)S(1)}, u32[]{:S(2)}, u32[]{:S(2)}) %collective-permute-start.68) | collective-permute-done | bytes 262176 | tf_op jit(solution)/shard_map/ppermute | solution.py:426
  518.8 16.1 %collective-permute-done.72 = bf16[256,512]{1,0:T(8,128)(2,1)S(1)} collective-permute-done((bf16[256,512]{1,0:T(8,128)(2,1)S(1)}, bf16[256,512]{1,0:T(8,128)(2,1)S(1)}, u32[]{:S(2)}, u32[]{:S(2)}) %collective-permute-start.72) | collective-permute-done | bytes 262176 | tf_op jit(solution)/shard_map/ppermute | solution.py:426
  (519 shorter events, 199.8 us)
Async XLA Ops:
  1.7 21.6 %collective-permute-start.2 = (bf16[256,512]{1,0:T(8,128)(2,1)S(1)}, bf16[256,512]{1,0:T(8,128)(2,1)}, u32[]{:S(2)}, u32[]{:S(2)}) collective-permute-start(bf16[256,512]{1,0:T(8,128)(2,1)S(1)} %slice_select_fusion), channel_id=1, source_target_pairs={{0,1},{1,0},{2,3},{3,2},{4,5},{5,4},{6,7},{7,6},{8,9},{9,8},{10,11... | collective-permute-start | bytes 786440 | tf_op jit(solution)/shard_map/ppermute | solution.py:426
  1.9 22.7 %collective-permute-start.3 = (bf16[256,512]{1,0:T(8,128)(2,1)S(1)}, bf16[256,512]{1,0:T(8,128)(2,1)}, u32[]{:S(2)}, u32[]{:S(2)}) collective-permute-start(bf16[256,512]{1,0:T(8,128)(2,1)S(1)} %slice_select_fusion), channel_id=1, source_target_pairs={{0,2},{1,3},{2,0},{3,1},{4,6},{5,7},{6,4},{7,5},{8,10},{9,11},{10,... | collective-permute-start | bytes 786440 | tf_op jit(solution)/shard_map/ppermute | solution.py:426
  4.3 22.6 %collective-permute-start.4 = (bf16[256,512]{1,0:T(8,128)(2,1)S(1)}, bf16[256,512]{1,0:T(8,128)(2,1)}, u32[]{:S(2)}, u32[]{:S(2)}) collective-permute-start(bf16[256,512]{1,0:T(8,128)(2,1)S(1)} %slice_select_fusion), channel_id=1, source_target_pairs={{0,3},{1,2},{2,1},{3,0},{4,7},{5,6},{6,5},{7,4},{8,11},{9,10},{10,... | collective-permute-start | bytes 786440 | tf_op jit(solution)/shard_map/ppermute | solution.py:426
  13.7 17.4 %collective-permute-start.7 = (bf16[256,512]{1,0:T(8,128)(2,1)}, bf16[256,512]{1,0:T(8,128)(2,1)S(1)}, u32[]{:S(2)}, u32[]{:S(2)}) collective-permute-start(bf16[256,512]{1,0:T(8,128)(2,1)} %collective-permute-done), channel_id=1, source_target_pairs={{0,16},{16,0},{1,17},{17,1},{2,18},{18,2},{3,19},{19,3},{4,20},{20... | collective-permute-start | bytes 786440 | tf_op jit(solution)/shard_map/ppermute | solution.py:415
  28.3 20.3 %collective-permute-start.5 = (bf16[256,2048]{1,0:T(8,128)(2,1)S(1)}, bf16[256,2048]{1,0:T(8,128)(2,1)S(1)}, u32[]{:S(2)}, u32[]{:S(2)}) collective-permute-start(bf16[256,2048]{1,0:T(8,128)(2,1)S(1)} %get-tuple-element.618), channel_id=1, source_target_pairs={{0,4},{4,0},{8,12},{12,8},{16,24},{20,28},{24,16},{28,20},{1,5},{5... | collective-permute-start | bytes 3145736 | tf_op jit(solution)/shard_map/ppermute | solution.py:410
  29.6 19.0 %collective-permute-start.6 = (bf16[256,2048]{1,0:T(8,128)(2,1)S(1)}, bf16[256,2048]{1,0:T(8,128)(2,1)S(1)}, u32[]{:S(2)}, u32[]{:S(2)}) collective-permute-start(bf16[256,2048]{1,0:T(8,128)(2,1)S(1)} %get-tuple-element.618), channel_id=1, source_target_pairs={{0,16},{16,0},{1,17},{17,1},{2,18},{18,2},{3,19},{19,3},{4,20},{20... | collective-permute-start | bytes 3145736 | tf_op jit(solution)/shard_map/ppermute | solution.py:415
  31.2 24.3 %collective-permute-start.15 = (bf16[256,2048]{1,0:T(8,128)(2,1)S(1)}, bf16[256,2048]{1,0:T(8,128)(2,1)S(1)}, u32[]{:S(2)}, u32[]{:S(2)}) collective-permute-start(bf16[256,2048]{1,0:T(8,128)(2,1)S(1)} %multiply_convert_fusion.2), channel_id=1, source_target_pairs={{0,1},{1,2},{2,3},{3,0},{4,5},{5,6},{6,7},{7,4},{8,9},{9,10},{10,1... | collective-permute-start | bytes 3145736 | tf_op jit(solution)/shard_map/ppermute | solution.py:418
  48.9 27.4 %collective-permute-start.11 = (bf16[256,2048]{1,0:T(8,128)(2,1)S(1)}, bf16[256,2048]{1,0:T(8,128)(2,1)S(1)}, u32[]{:S(2)}, u32[]{:S(2)}) collective-permute-start(bf16[256,2048]{1,0:T(8,128)(2,1)S(1)} %collective-permute-done.5), channel_id=1, source_target_pairs={{0,16},{16,0},{1,17},{17,1},{2,18},{18,2},{3,19},{19,3},{4,20},{20... | collective-permute-start | bytes 3145736 | tf_op jit(solution)/shard_map/ppermute | solution.py:415
  51.1 25.3 %collective-permute-start.10 = (bf16[512,2048]{1,0:T(8,128)(2,1)S(1)}, bf16[512,2048]{1,0:T(8,128)(2,1)S(1)}, u32[]{:S(2)}, u32[]{:S(2)}) collective-permute-start(bf16[512,2048]{1,0:T(8,128)(2,1)S(1)} %pad_maximum_fusion.1), channel_id=1, source_target_pairs={{0,8},{4,12},{8,0},{12,4},{16,20},{20,16},{24,28},{28,24},{1,9},{5... | collective-permute-start | bytes 6291464 | tf_op jit(solution)/shard_map/ppermute | solution.py:410
  55.5 15.1 %collective-permute-start.16 = (bf16[256,512]{1,0:T(8,128)(2,1)S(1)}, bf16[256,512]{1,0:T(8,128)(2,1)S(1)}, u32[]{:S(2)}, u32[]{:S(2)}) collective-permute-start(bf16[256,512]{1,0:T(8,128)(2,1)S(1)} %pad_maximum_fusion.17), channel_id=1, source_target_pairs={{0,2},{1,3},{4,6},{5,7},{8,10},{9,11},{12,14},{13,15},{16,18},{17,... | collective-permute-start | bytes 786440 | tf_op jit(solution)/shard_map/ppermute | solution.py:421
  59.3 17.0 %collective-permute-start.17 = (bf16[256,512]{1,0:T(8,128)(2,1)S(1)}, bf16[256,512]{1,0:T(8,128)(2,1)S(1)}, u32[]{:S(2)}, u32[]{:S(2)}) collective-permute-start(bf16[256,512]{1,0:T(8,128)(2,1)S(1)} %pad_maximum_fusion.17), channel_id=1, source_target_pairs={{0,1},{1,2},{2,3},{4,5},{5,6},{6,7},{8,9},{9,10},{10,11},{12,13},{... | collective-permute-start | bytes 786440 | tf_op jit(solution)/shard_map/ppermute | solution.py:421
  61.2 37.5 %collective-permute-start.19 = (bf16[256,2048]{1,0:T(8,128)(2,1)S(1)}, bf16[256,2048]{1,0:T(8,128)(2,1)}, u32[]{:S(2)}, u32[]{:S(2)}) collective-permute-start(bf16[256,2048]{1,0:T(8,128)(2,1)S(1)} %collective-permute-done.15), channel_id=1, source_target_pairs={{0,1},{1,2},{2,3},{3,0},{4,5},{5,6},{6,7},{7,4},{8,9},{9,10},{10,1... | collective-permute-start | bytes 3145736 | tf_op jit(solution)/shard_map/ppermute | solution.py:418
  76.4 25.2 %collective-permute-start.18 = (bf16[2048,256]{1,0:T(8,128)(2,1)S(1)}, bf16[2048,256]{1,0:T(8,128)(2,1)S(1)}, u32[]{:S(2)}, u32[]{:S(2)}) collective-permute-start(bf16[2048,256]{1,0:T(8,128)(2,1)S(1)} %collective-permute-done.9), channel_id=1, source_target_pairs={{0,16},{16,0},{1,17},{17,1},{2,18},{18,2},{3,19},{19,3},{4,20},{20... | collective-permute-start | bytes 3145736 | tf_op jit(solution)/shard_map/ppermute | solution.py:415
  79.2 40.9 %collective-permute-start.12 = (bf16[4096,256]{1,0:T(8,128)(2,1)}, bf16[4096,256]{1,0:T(8,128)(2,1)}, u32[]{:S(2)}, u32[]{:S(2)}) collective-permute-start(bf16[4096,256]{1,0:T(8,128)(2,1)} %pad_maximum_fusion.2), channel_id=1, source_target_pairs={{0,8},{4,12},{8,0},{12,4},{16,20},{20,16},{24,28},{28,24},{1,9},{5... | collective-permute-start | bytes 6291464 | tf_op jit(solution)/shard_map/ppermute | solution.py:410
  82.0 33.8 %collective-permute-start.13 = (bf16[512,1408]{1,0:T(8,128)(2,1)S(1)}, bf16[512,1408]{1,0:T(8,128)(2,1)S(1)}, u32[]{:S(2)}, u32[]{:S(2)}) collective-permute-start(bf16[512,1408]{1,0:T(8,128)(2,1)S(1)} %pad_maximum_fusion.4), channel_id=1, source_target_pairs={{0,4},{4,0},{8,12},{12,8},{16,24},{20,28},{24,16},{28,20},{1,5},{5... | collective-permute-start | bytes 4325384 | tf_op jit(solution)/shard_map/ppermute | solution.py:410
  98.7 24.5 %collective-permute-start.20 = (bf16[256,2048]{1,0:T(8,128)(2,1)}, bf16[256,2048]{1,0:T(8,128)(2,1)S(1)}, u32[]{:S(2)}, u32[]{:S(2)}) collective-permute-start(bf16[256,2048]{1,0:T(8,128)(2,1)} %collective-permute-done.19), channel_id=1, source_target_pairs={{0,1},{1,2},{2,3},{3,0},{4,5},{5,6},{6,7},{7,4},{8,9},{9,10},{10,1... | collective-permute-start | bytes 3145736 | tf_op jit(solution)/shard_map/ppermute | solution.py:418
  125.2 41.5 %collective-permute-start.23 = (bf16[1024,1408]{1,0:T(8,128)(2,1)S(1)}, bf16[1024,1408]{1,0:T(8,128)(2,1)}, u32[]{:S(2)}, u32[]{:S(2)}) collective-permute-start(bf16[1024,1408]{1,0:T(8,128)(2,1)S(1)} %pad_maximum_fusion), channel_id=1, source_target_pairs={{0,8},{4,12},{8,0},{12,4},{16,20},{20,16},{24,28},{28,24},{1,9},{5... | collective-permute-start | bytes 8650760 | tf_op jit(solution)/shard_map/ppermute | solution.py:410
  126.5 18.3 %collective-permute-start.24 = (bf16[1408,256]{1,0:T(8,128)(2,1)S(1)}, bf16[1408,256]{1,0:T(8,128)(2,1)S(1)}, u32[]{:S(2)}, u32[]{:S(2)}) collective-permute-start(bf16[1408,256]{1,0:T(8,128)(2,1)S(1)} %get-tuple-element.307), channel_id=1, source_target_pairs={{0,4},{4,0},{8,12},{12,8},{16,24},{20,28},{24,16},{28,20},{1,5},{5... | collective-permute-start | bytes 2162696 | tf_op jit(solution)/shard_map/ppermute | solution.py:410
  136.2 30.6 %collective-permute-start.25 = (bf16[256,2048]{1,0:T(8,128)(2,1)S(1)}, bf16[256,2048]{1,0:T(8,128)(2,1)S(1)}, u32[]{:S(2)}, u32[]{:S(2)}) collective-permute-start(bf16[256,2048]{1,0:T(8,128)(2,1)S(1)} %multiply_convert_fusion.1), channel_id=1, source_target_pairs={{0,1},{1,2},{2,3},{3,0},{4,5},{5,6},{6,7},{7,4},{8,9},{9,10},{10,1... | collective-permute-start | bytes 3145736 | tf_op jit(solution)/shard_map/ppermute | solution.py:418
  168.3 25.3 %collective-permute-start.27 = (bf16[2816,256]{1,0:T(8,128)(2,1)S(1)}, bf16[2816,256]{1,0:T(8,128)(2,1)S(1)}, u32[]{:S(2)}, u32[]{:S(2)}) collective-permute-start(bf16[2816,256]{1,0:T(8,128)(2,1)S(1)} %pad_maximum_fusion.5), channel_id=1, source_target_pairs={{0,8},{4,12},{8,0},{12,4},{16,20},{20,16},{24,28},{28,24},{1,9},{5... | collective-permute-start | bytes 4325384 | tf_op jit(solution)/shard_map/ppermute | solution.py:410
  168.8 24.8 %collective-permute-start.29 = (bf16[256,2048]{1,0:T(8,128)(2,1)S(1)}, bf16[256,2048]{1,0:T(8,128)(2,1)}, u32[]{:S(2)}, u32[]{:S(2)}) collective-permute-start(bf16[256,2048]{1,0:T(8,128)(2,1)S(1)} %collective-permute-done.25), channel_id=1, source_target_pairs={{0,1},{1,2},{2,3},{3,0},{4,5},{5,6},{6,7},{7,4},{8,9},{9,10},{10,1... | collective-permute-start | bytes 3145736 | tf_op jit(solution)/shard_map/ppermute | solution.py:418
  195.0 25.2 %collective-permute-start.31 = (bf16[256,2048]{1,0:T(8,128)(2,1)}, bf16[256,2048]{1,0:T(8,128)(2,1)S(1)}, u32[]{:S(2)}, u32[]{:S(2)}) collective-permute-start(bf16[256,2048]{1,0:T(8,128)(2,1)} %collective-permute-done.29), channel_id=1, source_target_pairs={{0,1},{1,2},{2,3},{3,0},{4,5},{5,6},{6,7},{7,4},{8,9},{9,10},{10,1... | collective-permute-start | bytes 3145736 | tf_op jit(solution)/shard_map/ppermute | solution.py:418
  220.3 36.1 %collective-permute-start.32 = (bf16[256,2048]{1,0:T(8,128)(2,1)S(1)}, bf16[256,2048]{1,0:T(8,128)(2,1)}, u32[]{:S(2)}, u32[]{:S(2)}) collective-permute-start(bf16[256,2048]{1,0:T(8,128)(2,1)S(1)} %shard_map.220), channel_id=1, source_target_pairs={{0,1},{1,2},{2,3},{3,0},{4,5},{5,6},{6,7},{7,4},{8,9},{9,10},{10,1... | collective-permute-start | bytes 3145736 | tf_op jit(solution)/shard_map/ppermute | solution.py:418
  258.9 20.7 %collective-permute-start.34 = (bf16[1408,1024]{1,0:T(8,128)(2,1)}, bf16[1408,1024]{1,0:T(8,128)(2,1)S(1)}, u32[]{:S(2)}, u32[]{:S(2)}) collective-permute-start(bf16[1408,1024]{1,0:T(8,128)(2,1)} %shard_map.223), channel_id=1, source_target_pairs={{0,16},{16,0},{1,17},{17,1},{2,18},{18,2},{3,19},{19,3},{4,20},{20... | collective-permute-start | bytes 8650760 | tf_op jit(solution)/shard_map/ppermute | solution.py:415
  259.9 28.9 %collective-permute-start.33 = (bf16[256,2048]{1,0:T(8,128)(2,1)}, bf16[256,2048]{1,0:T(8,128)(2,1)}, u32[]{:S(2)}, u32[]{:S(2)}) collective-permute-start(bf16[256,2048]{1,0:T(8,128)(2,1)} %add_convert_fusion.6), channel_id=1, source_target_pairs={{0,1},{1,2},{2,3},{3,0},{4,5},{5,6},{6,7},{7,4},{8,9},{9,10},{10,1... | collective-permute-start | bytes 3145736 | tf_op jit(solution)/shard_map/ppermute | solution.py:418
  292.6 29.1 %collective-permute-start.35 = (bf16[256,2048]{1,0:T(8,128)(2,1)}, bf16[256,2048]{1,0:T(8,128)(2,1)}, u32[]{:S(2)}, u32[]{:S(2)}) collective-permute-start(bf16[256,2048]{1,0:T(8,128)(2,1)} %add_convert_fusion.5), channel_id=1, source_target_pairs={{0,1},{1,2},{2,3},{3,0},{4,5},{5,6},{6,7},{7,4},{8,9},{9,10},{10,1... | collective-permute-start | bytes 3145736 | tf_op jit(solution)/shard_map/ppermute | solution.py:418
  297.5 24.2 %collective-permute-start.36 = (bf16[1408,512]{1,0:T(8,128)(2,1)}, bf16[1408,512]{1,0:T(8,128)(2,1)}, u32[]{:S(2)}, u32[]{:S(2)}) collective-permute-start(bf16[1408,512]{1,0:T(8,128)(2,1)} %pad_maximum_fusion.6), channel_id=1, source_target_pairs={{0,4},{4,0},{8,12},{12,8},{16,24},{20,28},{24,16},{28,20},{1,5},{5... | collective-permute-start | bytes 4325384 | tf_op jit(solution)/shard_map/ppermute | solution.py:410
  324.1 24.6 %collective-permute-start.39 = (bf16[1408,256]{1,0:T(8,128)(2,1)}, bf16[1408,256]{1,0:T(8,128)(2,1)}, u32[]{:S(2)}, u32[]{:S(2)}) collective-permute-start(bf16[1408,256]{1,0:T(8,128)(2,1)} %add_convert_fusion.9), channel_id=1, source_target_pairs={{0,8},{4,12},{8,0},{12,4},{16,20},{20,16},{24,28},{28,24},{1,9},{5... | collective-permute-start | bytes 2162696 | tf_op jit(solution)/shard_map/ppermute | solution.py:410
  325.1 26.2 %collective-permute-start.40 = (bf16[512,1408]{1,0:T(8,128)(2,1)}, bf16[512,1408]{1,0:T(8,128)(2,1)}, u32[]{:S(2)}, u32[]{:S(2)}) collective-permute-start(bf16[512,1408]{1,0:T(8,128)(2,1)} %pad_maximum_fusion.7), channel_id=1, source_target_pairs={{0,4},{4,0},{8,12},{12,8},{16,24},{20,28},{24,16},{28,20},{1,5},{5... | collective-permute-start | bytes 4325384 | tf_op jit(solution)/shard_map/ppermute | solution.py:410
  326.5 24.6 %collective-permute-start.41 = (bf16[256,2048]{1,0:T(8,128)(2,1)}, bf16[256,2048]{1,0:T(8,128)(2,1)}, u32[]{:S(2)}, u32[]{:S(2)}) collective-permute-start(bf16[256,2048]{1,0:T(8,128)(2,1)} %get-tuple-element.385), channel_id=1, source_target_pairs={{0,1},{1,2},{2,3},{3,0},{4,5},{5,6},{6,7},{7,4},{8,9},{9,10},{10,1... | collective-permute-start | bytes 3145736 | tf_op jit(solution)/shard_map/ppermute | solution.py:418
  351.3 21.0 %collective-permute-start.42 = (bf16[2048,1024]{1,0:T(8,128)(2,1)S(1)}, bf16[2048,1024]{1,0:T(8,128)(2,1)}, u32[]{:S(2)}, u32[]{:S(2)}) collective-permute-start(bf16[2048,1024]{1,0:T(8,128)(2,1)S(1)} %copy-done.30), channel_id=1, source_target_pairs={{0,16},{16,0},{1,17},{17,1},{2,18},{18,2},{3,19},{19,3},{4,20},{20... | collective-permute-start | bytes 12582920 | tf_op jit(solution)/shard_map/ppermute | solution.py:415
  352.5 29.9 %collective-permute-start.44 = (bf16[512,1408]{1,0:T(8,128)(2,1)}, bf16[512,1408]{1,0:T(8,128)(2,1)}, u32[]{:S(2)}, u32[]{:S(2)}) collective-permute-start(bf16[512,1408]{1,0:T(8,128)(2,1)} %pad_maximum_fusion.8), channel_id=1, source_target_pairs={{0,4},{4,0},{8,12},{12,8},{16,24},{20,28},{24,16},{28,20},{1,5},{5... | collective-permute-start | bytes 4325384 | tf_op jit(solution)/shard_map/ppermute | solution.py:410
  355.1 27.2 %collective-permute-start.45 = (bf16[256,2048]{1,0:T(8,128)(2,1)}, bf16[256,2048]{1,0:T(8,128)(2,1)}, u32[]{:S(2)}, u32[]{:S(2)}) collective-permute-start(bf16[256,2048]{1,0:T(8,128)(2,1)} %add_convert_fusion.4), channel_id=1, source_target_pairs={{0,1},{1,2},{2,3},{3,0},{4,5},{5,6},{6,7},{7,4},{8,9},{9,10},{10,1... | collective-permute-start | bytes 3145736 | tf_op jit(solution)/shard_map/ppermute | solution.py:418
  357.9 24.5 %collective-permute-start.43 = (bf16[256,1408]{1,0:T(8,128)(2,1)}, bf16[256,1408]{1,0:T(8,128)(2,1)}, u32[]{:S(2)}, u32[]{:S(2)}) collective-permute-start(bf16[256,1408]{1,0:T(8,128)(2,1)} %add_convert_fusion.8), channel_id=1, source_target_pairs={{0,8},{4,12},{8,0},{12,4},{16,20},{20,16},{24,28},{28,24},{1,9},{5... | collective-permute-start | bytes 2162696 | tf_op jit(solution)/shard_map/ppermute | solution.py:410
  382.4 21.6 %collective-permute-start.49 = (bf16[1024,512]{1,0:T(8,128)(2,1)S(1)}, bf16[1024,512]{1,0:T(8,128)(2,1)S(1)}, u32[]{:S(2)}, u32[]{:S(2)}) collective-permute-start(bf16[1024,512]{1,0:T(8,128)(2,1)S(1)} %pad_maximum_fusion.10), channel_id=1, source_target_pairs={{0,4},{4,0},{8,12},{12,8},{16,24},{20,28},{24,16},{28,20},{1,5},{5... | collective-permute-start | bytes 3145736 | tf_op jit(solution)/shard_map/ppermute | solution.py:410
  384.6 18.2 %collective-permute-start.48 = (bf16[256,1408]{1,0:T(8,128)(2,1)S(1)}, bf16[256,1408]{1,0:T(8,128)(2,1)S(1)}, u32[]{:S(2)}, u32[]{:S(2)}) collective-permute-start(bf16[256,1408]{1,0:T(8,128)(2,1)S(1)} %add_convert_fusion.7), channel_id=1, source_target_pairs={{0,8},{4,12},{8,0},{12,4},{16,20},{20,16},{24,28},{28,24},{1,9},{5... | collective-permute-start | bytes 2162696 | tf_op jit(solution)/shard_map/ppermute | solution.py:410
  409.8 27.5 %collective-permute-start.55 = (bf16[256,2048]{1,0:T(8,128)(2,1)S(1)}, bf16[256,2048]{1,0:T(8,128)(2,1)}, u32[]{:S(2)}, u32[]{:S(2)}) collective-permute-start(bf16[256,2048]{1,0:T(8,128)(2,1)S(1)} %add_convert_fusion.3), channel_id=1, source_target_pairs={{0,1},{1,2},{2,3},{3,0},{4,5},{5,6},{6,7},{7,4},{8,9},{9,10},{10,1... | collective-permute-start | bytes 3145736 | tf_op jit(solution)/shard_map/ppermute | solution.py:418
  416.2 21.1 %collective-permute-start.53 = (bf16[512,512]{1,0:T(8,128)(2,1)S(1)}, bf16[512,512]{1,0:T(8,128)(2,1)S(1)}, u32[]{:S(2)}, u32[]{:S(2)}) collective-permute-start(bf16[512,512]{1,0:T(8,128)(2,1)S(1)} %pad_maximum_fusion.15), channel_id=1, source_target_pairs={{0,4},{4,0},{8,12},{12,8},{16,24},{20,28},{24,16},{28,20},{1,5},{5... | collective-permute-start | bytes 1572872 | tf_op jit(solution)/shard_map/ppermute | solution.py:410
  416.9 20.4 %collective-permute-start.54 = (bf16[1024,512]{1,0:T(8,128)(2,1)}, bf16[1024,512]{1,0:T(8,128)(2,1)S(1)}, u32[]{:S(2)}, u32[]{:S(2)}) collective-permute-start(bf16[1024,512]{1,0:T(8,128)(2,1)} %pad_maximum_fusion.11), channel_id=1, source_target_pairs={{0,4},{4,0},{8,12},{12,8},{16,24},{20,28},{24,16},{28,20},{1,5},{5... | collective-permute-start | bytes 3145736 | tf_op jit(solution)/shard_map/ppermute | solution.py:410
  449.4 29.5 %collective-permute-start.62 = (bf16[512,2048]{1,0:T(8,128)(2,1)}, bf16[512,2048]{1,0:T(8,128)(2,1)}, u32[]{:S(2)}, u32[]{:S(2)}) collective-permute-start(bf16[512,2048]{1,0:T(8,128)(2,1)} %pad_maximum_fusion.3), channel_id=1, source_target_pairs={{0,4},{4,0},{8,12},{12,8},{16,24},{20,28},{24,16},{28,20},{1,5},{5... | collective-permute-start | bytes 6291464 | tf_op jit(solution)/shard_map/ppermute | solution.py:410
  452.7 24.0 %collective-permute-start.59 = (bf16[256,512]{1,0:T(8,128)(2,1)S(1)}, bf16[256,512]{1,0:T(8,128)(2,1)S(1)}, u32[]{:S(2)}, u32[]{:S(2)}) collective-permute-start(bf16[256,512]{1,0:T(8,128)(2,1)S(1)} %add_convert_fusion.15), channel_id=1, source_target_pairs={{0,1},{1,0},{2,3},{3,2},{4,5},{5,4},{6,7},{7,6},{8,9},{9,8},{10,11... | collective-permute-start | bytes 786440 | tf_op jit(solution)/shard_map/ppermute | solution.py:426
  455.7 21.0 %collective-permute-start.60 = (bf16[256,512]{1,0:T(8,128)(2,1)S(1)}, bf16[256,512]{1,0:T(8,128)(2,1)S(1)}, u32[]{:S(2)}, u32[]{:S(2)}) collective-permute-start(bf16[256,512]{1,0:T(8,128)(2,1)S(1)} %add_convert_fusion.15), channel_id=1, source_target_pairs={{0,2},{1,3},{2,0},{3,1},{4,6},{5,7},{6,4},{7,5},{8,10},{9,11},{10,... | collective-permute-start | bytes 786440 | tf_op jit(solution)/shard_map/ppermute | solution.py:426
  455.7 23.2 %collective-permute-start.61 = (bf16[256,512]{1,0:T(8,128)(2,1)S(1)}, bf16[256,512]{1,0:T(8,128)(2,1)S(1)}, u32[]{:S(2)}, u32[]{:S(2)}) collective-permute-start(bf16[256,512]{1,0:T(8,128)(2,1)S(1)} %add_convert_fusion.15), channel_id=1, source_target_pairs={{0,3},{1,2},{2,1},{3,0},{4,7},{5,6},{6,5},{7,4},{8,11},{9,10},{10,... | collective-permute-start | bytes 786440 | tf_op jit(solution)/shard_map/ppermute | solution.py:426
  456.9 19.7 %collective-permute-start.63 = (f32[2,2048]{1,0:T(2,128)S(1)}, f32[2,2048]{1,0:T(2,128)S(1)}, u32[]{:S(2)}, u32[]{:S(2)}) collective-permute-start(f32[2,2048]{1,0:T(2,128)S(1)} %add.420), channel_id=1, source_target_pairs={{0,2},{1,3},{2,0},{3,1},{4,6},{5,7},{6,4},{7,5},{8,10},{9,11},{10,... | collective-permute-start | bytes 49160 | tf_op jit(solution)/shard_map/ppermute | solution.py:426
  481.6 25.7 %collective-permute-start.65 = (bf16[256,2048]{1,0:T(8,128)(2,1)S(1)}, bf16[256,2048]{1,0:T(8,128)(2,1)S(1)}, u32[]{:S(2)}, u32[]{:S(2)}) collective-permute-start(bf16[256,2048]{1,0:T(8,128)(2,1)S(1)} %add_convert_fusion.2), channel_id=1, source_target_pairs={{0,8},{4,12},{8,0},{12,4},{16,20},{20,16},{24,28},{28,24},{1,9},{5... | collective-permute-start | bytes 3145736 | tf_op jit(solution)/shard_map/ppermute | solution.py:410
  484.1 23.3 %collective-permute-start.68 = (bf16[512,256]{1,0:T(8,128)(2,1)S(1)}, bf16[512,256]{1,0:T(8,128)(2,1)S(1)}, u32[]{:S(2)}, u32[]{:S(2)}) collective-permute-start(bf16[512,256]{1,0:T(8,128)(2,1)S(1)} %get-tuple-element.609), channel_id=1, source_target_pairs={{0,3},{1,2},{2,1},{3,0},{4,7},{5,6},{6,5},{7,4},{8,11},{9,10},{10,... | collective-permute-start | bytes 786440 | tf_op jit(solution)/shard_map/ppermute | solution.py:426
  507.4 27.4 %collective-permute-start.69 = (bf16[512,512]{1,0:T(8,128)(2,1)S(1)}, bf16[512,512]{1,0:T(8,128)(2,1)S(1)}, u32[]{:S(2)}, u32[]{:S(2)}) collective-permute-start(bf16[512,512]{1,0:T(8,128)(2,1)S(1)} %pad_maximum_fusion.16), channel_id=1, source_target_pairs={{0,8},{4,12},{8,0},{12,4},{16,20},{20,16},{24,28},{28,24},{1,9},{5... | collective-permute-start | bytes 1572872 | tf_op jit(solution)/shard_map/ppermute | solution.py:410
  510.4 24.4 %collective-permute-start.72 = (bf16[256,512]{1,0:T(8,128)(2,1)S(1)}, bf16[256,512]{1,0:T(8,128)(2,1)S(1)}, u32[]{:S(2)}, u32[]{:S(2)}) collective-permute-start(bf16[256,512]{1,0:T(8,128)(2,1)S(1)} %get-tuple-element.605), channel_id=1, source_target_pairs={{0,3},{1,2},{2,1},{3,0},{4,7},{5,6},{6,5},{7,4},{8,11},{9,10},{10,... | collective-permute-start | bytes 786440 | tf_op jit(solution)/shard_map/ppermute | solution.py:426
  (109 other events, 824.8 us)

commit v6 on v5

--- a/solution.py
+++ b/solution.py
@@ -262,7 +262,7 @@
 def token_sums(lefts, left_lanes, rights, right_lanes, received=None):
     n, many = len(lefts), len(rights)
     start, rows_out = left_lanes
-    tile = min(256, rows_out)
+    tile = min(512 if rows_out >= 2048 else 256, rows_out)
     base, columns = right_lanes
 
     def kernel(*refs):
@@ -616,7 +616,7 @@
         part, carry, arrived, done = fence(part, carry, chunks[k + 2], done)
         done = list(done)
         chunks[k + 2] = arrived
-        part = (part + carry.astype(f32)).astype(bf16)
+        part = (part.astype(f32) + carry.astype(f32)).astype(bf16)
         (part,) = fence(part)
     k = cols - 2
     carry = to_cols(part, 1)
@@ -627,12 +627,12 @@
     h_parts = [near_hidden] + chunks[2:k] + [far_hidden]
     f_parts = [near_feed] + feeds[2:k] + [far_feed]
     low, high, full = (0, half), (half, half), (0, units)
-    part = rows_product((gbs[-1], ubs[-1]), weights, True, f32, 0, own)
+    part = rows_product((gbs[-1], ubs[-1]), weights, True, bf16, 0, own)
     d_sent = token_sum(hids, full, f_parts, high)
     part, carry, d_sent, hids, gbs, ubs, h_parts, f_parts = fence(
         part, carry, d_sent, hids, gbs, ubs, h_parts, f_parts
     )
-    part = (part + carry.astype(f32)).astype(bf16)
+    part = (part.astype(f32) + carry.astype(f32)).astype(bf16)
     part, d_sent, hids, gbs, ubs = fence(part, d_sent, hids, gbs, ubs)
 
     carry = to_cols(part, 1)
@@ -645,7 +645,7 @@
     part, own_part, carry, d_sum, g_sent, u_sent, hids, gbs, ubs = fence(
         part, own_part, carry, d_sum, g_sent, u_sent, hids, gbs, ubs
     )
-    part = (part + carry.astype(f32)).astype(bf16)
+    part = (part.astype(f32) + carry.astype(f32)).astype(bf16)
     part, own_part, d_sum, g_sent, u_sent, gbs, ubs, hids = fence(
         part, own_part, d_sum, g_sent, u_sent, gbs, ubs, hids
     )
@@ -665,8 +665,10 @@
     def around(carry, part):
         return to_cols((part.astype(f32) + carry.astype(f32)).astype(bf16), 1)
 
-    def col_sum(total, axis):
-        pieces = xor_blocks(jnp.split(total.astype(bf16), cols, axis), c)
+    def col_pieces(total, axis):
+        return xor_blocks(jnp.split(total.astype(bf16), cols, axis), c)
+
+    def col_sum(pieces):
         return [pieces[0]] + [to_xor_cols(pieces[k], k) for k in range(1, cols)]
 
     def added(values):
@@ -777,13 +779,14 @@
     out_sum = jnp.concatenate(
         [finish(o_low_kept, o_low_far), finish(o_high_kept, o_high_far)], 0
     ).astype(bf16)
-    total, q_near, gains, out_sum = fence(total, q_near, gains, out_sum)
+    out_pieces = col_pieces(out_sum, 0)
+    total, q_near, gains, out_pieces = fence(total, q_near, gains, out_pieces)
 
     total = added(total).astype(bf16)
     one = to_near(total, 0)
     q_kept, q_theirs = half_way(q_parts, q_near, 0)
     q_far = to_near(q_theirs, 1)
-    out_parts = col_sum(out_sum, 0)
+    out_parts = col_sum(out_pieces)
     one, d_far, g_far, u_far, out_carry = fence(one, d_far, g_far, u_far, out_carry)
     down_grad, gate_grad, up_grad = finish(d_kept, d_far), finish(g_kept, g_far), finish(u_kept, u_far)
     piece = out_last.astype(f32) + out_carry.astype(f32)
@@ -795,7 +798,7 @@
     two = to_near(jnp.concatenate([total, one], 0), 1)
     gains = gains + to_near(gains, 0)
     gains = gains + to_near(gains, 1)
-    q_cols = col_sum(finish(q_kept, q_far), 1)
+    q_cols = col_sum(col_pieces(finish(q_kept, q_far), 1))
     out_grad = added(out_parts)
     two, q_cols, out_grad, gains = fence(two, q_cols, out_grad, gains)
     mine = jnp.concatenate([total, one, two], 0)

time: 552 us -> 553 us (level)
  waiting for transfers between devices: 167 us -> 176 us
    ppermute x12, waiting for transfers between devices: 29.8 us -> 37.4 us  [to_cols(): lax.ppermute(value, 'cols', [(i, (i + k) % cols) for i in range(cols)])]
    unnamed x166 -> x160, local copies, waits for them, and re-layouts: 20.4 us -> 20.9 us
  transfers between devices with their start and end apart: 77 -> 77, of which waited for: 33 -> 36; matrix products, arithmetic and copies ran while one was open for 19% -> 19% of each run, Pallas kernels for 28% -> 28%
where the time goes in v6:
time: 553 us; the launch traced here: 544 us
  waiting for transfers between devices  176 us (32%)
  Pallas kernels  151 us (27%)
  starting transfers between devices  86.4 us (16%)
  other arithmetic  63.2 us (11%)
  local copies, waits for them, and re-layouts  47.9 us (9%)
  matrix products  15.7 us (3%)
    ppermute x28, waiting for transfers between devices, to_near(): return lax.ppermute(value, ('dp', 'rows'), pairs)  65.5 us
    pallas_call x10, Pallas kernels, token_sums(): call(kernel, (pl.cdiv(rows_out, tile),), specs, [out] * many, [jax.ShapeD...  54.4 us
    ppermute x14, waiting for transfers between devices, to_xor_cols(): return lax.ppermute(value, 'cols', [(i, i ^ k) for i in range(cols)])  50.1 us
    pallas_call x7, Pallas kernels, rows_products(): call(kernel, (columns // tile,), specs, [pl.BlockSpec((count, tile), lamb...  47.8 us
    ppermute x12, waiting for transfers between devices, to_cols(): lax.ppermute(value, 'cols', [(i, (i + k) % cols) for i in range(cols)])  37.4 us
    ppermute x28, starting transfers between devices, to_near(): return lax.ppermute(value, ('dp', 'rows'), pairs)  21.2 us
    unnamed x160, local copies, waits for them, and re-layouts  20.9 us
    ppermute x12, starting transfers between devices, to_cols(): lax.ppermute(value, 'cols', [(i, (i + k) % cols) for i in range(cols)])  19.3 us
  transfers between devices with their start and end apart: 77, of which 36 were waited for; matrix products, arithmetic and copies ran while one was open for 19% of the time, Pallas kernels for 28%

profile of v6, /device:TPU:11, one launch (start us, length us, event | category | flops | bytes accessed | tf_op | source)
XLA Modules:
  0.0 544.1 jit_solution(5279276915359573359)
XLA Ops:
  33.8 3.7 collective-permute-done.9
  37.4 11.2 %collective-permute-done.5 = bf16[256,2048]{1,0:T(8,128)(2,1)S(1)} collective-permute-done((bf16[256,2048]{1,0:T(8,128)(2,1)S(1)}, bf16[256,2048]{1,0:T(8,128)(2,1)S(1)}, u32[]{:S(2)}, u32[]{:S(2)}) %collective-permute-start.5) | collective-permute-done | bytes 1048608 | tf_op jit(solution)/shard_map/ppermute | solution.py:410
  55.6 3.6 collective-permute-start.16
  61.4 8.8 %collective-permute-done.16 = bf16[256,512]{1,0:T(8,128)(2,1)S(1)} collective-permute-done((bf16[256,512]{1,0:T(8,128)(2,1)S(1)}, bf16[256,512]{1,0:T(8,128)(2,1)S(1)}, u32[]{:S(2)}, u32[]{:S(2)}) %collective-permute-start.16) | collective-permute-done | bytes 262176 | tf_op jit(solution)/shard_map/ppermute | solution.py:421
  70.2 5.6 %collective-permute-done.17 = bf16[256,512]{1,0:T(8,128)(2,1)S(1)} collective-permute-done((bf16[256,512]{1,0:T(8,128)(2,1)S(1)}, bf16[256,512]{1,0:T(8,128)(2,1)S(1)}, u32[]{:S(2)}, u32[]{:S(2)}) %collective-permute-start.17) | collective-permute-done | bytes 262176 | tf_op jit(solution)/shard_map/ppermute | solution.py:421
  87.0 11.4 %collective-permute-done.19 = bf16[256,2048]{1,0:T(8,128)(2,1)} collective-permute-done((bf16[256,2048]{1,0:T(8,128)(2,1)}, bf16[256,2048]{1,0:T(8,128)(2,1)}, u32[]{:S(2)}, u32[]{:S(2)}) %collective-permute-start.19) | collective-permute-done | bytes 1048608 | tf_op jit(solution)/shard_map/ppermute | solution.py:418
  101.4 10.8 %shard_map.214 = (bf16[256,2048]{1,0:T(8,128)(2,1)S(1)}, bf16[256,2048]{1,0:T(8,128)(2,1)S(1)}, f32[16,1,256]{2,1,0:T(1,128)S(1)}) custom-call(f32[256,2048]{1,0:T(8,128)S(1)} %fusion.40.pre_ref, bf16[768,512]{1,0:T(8,128)(2,1)S(1)} %constant_dynamic-update-slice_fusion.3.k_ref.v_ref, bf16[768,512]{1,0:T(8,128)(2,1)S(1)} %constant_dynamic-update-slice_fusion.3.k_ref.v_ref, ...), custom_call_target="tpu_custom_call" | custom-call | tf_op jit(solution)/shard_map/pallas_call | solution.py:68
  114.8 4.0 collective-permute-done.12
  118.8 3.7 collective-permute-done.20
  140.6 3.8 collective-permute-done.24
  144.4 22.0 %collective-permute-done.23 = bf16[1024,1408]{1,0:T(8,128)(2,1)} collective-permute-done((bf16[1024,1408]{1,0:T(8,128)(2,1)S(1)}, bf16[1024,1408]{1,0:T(8,128)(2,1)}, u32[]{:S(2)}, u32[]{:S(2)}) %collective-permute-start.23) | collective-permute-done | bytes 2883616 | tf_op jit(solution)/shard_map/ppermute | solution.py:410
  178.0 5.1 fusion.42.gate_ref
  183.0 5.0 fusion.43.up_ref
  188.0 4.6 collective-permute-done.29
  202.0 9.2 %shard_map.219 = (bf16[512,1408]{1,0:T(8,128)(2,1)S(1)}, bf16[512,1408]{1,0:T(8,128)(2,1)S(1)}, bf16[512,1408]{1,0:T(8,128)(2,1)S(1)}) custom-call(bf16[512,2048]{1,0:T(8,128)(2,1)} %copy-done, f32[512,1408]{1,0:T(8,128)} %fusion.42.gate_ref, f32[512,1408]{1,0:T(8,128)} %fusion.43.up_ref, bf16[1408,2048]{1,0:T(8,128)(2,1)} %slice_dynamic-update-slice_fusion.8.d_ref.refs_0_), custom_call_target="tpu_custom_call" | custom-call | tf_op jit(solution)/shard_map/pallas_call | solution.py:217
  211.2 6.9 %shard_map.220 = bf16[256,2048]{1,0:T(8,128)(2,1)S(1)} custom-call(bf16[2048,1408]{1,0:T(8,128)(2,1)} %copy-done.10, bf16[2048,1408]{1,0:T(8,128)(2,1)} %copy-done.9, bf16[512,1408]{1,0:T(8,128)(2,1)S(1)} %get-tuple-element.373.refs_2_.refs_4_, bf16[512,1408]{1,0:T(8,128)(2,1)S(1)} %get-tuple-element.375.refs_3_.refs_5_.refs_4_), custom_call_target="tpu_custom_call" | custom-call | tf_op jit(solution)/shard_map/pallas_call | solution.py:248
  218.1 3.1 collective-permute-done.31
  224.5 3.1 constant_dynamic-update-slice_fusion.12
  228.6 15.2 %shard_map.221 = (bf16[512,1408]{1,0:T(8,128)(2,1)S(1)}, bf16[512,1408]{1,0:T(8,128)(2,1)S(1)}, bf16[512,1408]{1,0:T(8,128)(2,1)S(1)}) custom-call(bf16[512,2048]{1,0:T(8,128)(2,1)} %constant_dynamic-update-slice_fusion.11.h_ref.refs_1_, bf16[512,2048]{1,0:T(8,128)(2,1)} %copy-done.16, bf16[2048,1408]{1,0:T(8,128)(2,1)} %copy-done.10, ...), custom_call_target="tpu_custom_call" | custom-call | tf_op jit(solution)/shard_map/pallas_call | solution.py:193
  243.8 7.0 %shard_map.222 = bf16[256,2048]{1,0:T(8,128)(2,1)S(1)} custom-call(bf16[2048,1408]{1,0:T(8,128)(2,1)} %copy-done.10, bf16[2048,1408]{1,0:T(8,128)(2,1)} %copy-done.9, bf16[512,1408]{1,0:T(8,128)(2,1)S(1)} %get-tuple-element.374.refs_2_.refs_3_, bf16[512,1408]{1,0:T(8,128)(2,1)S(1)} %get-tuple-element.376.refs_3_.refs_5_), custom_call_target="tpu_custom_call" | custom-call | tf_op jit(solution)/shard_map/pallas_call | solution.py:248
  250.9 6.9 %shard_map.223 = bf16[1408,1024]{1,0:T(8,128)(2,1)} custom-call(bf16[512,1408]{1,0:T(8,128)(2,1)S(1)} %get-tuple-element.381.refs_0_.refs_1_, bf16[512,1408]{1,0:T(8,128)(2,1)S(1)} %get-tuple-element.387.refs_1_, bf16[512,2048]{1,0:T(8,128)(2,1)S(1)} %copy-done.1, bf16[512,2048]{1,0:T(8,128)(2,1)} %copy-done.16), custom_call_target="tpu_custom_call" | custom-call | tf_op jit(solution)/shard_map/pallas_call | solution.py:291
  261.6 10.2 %shard_map.224 = (f32[256,2048]{1,0:T(8,128)}, f32[256,2048]{1,0:T(8,128)}) custom-call(bf16[2048,1408]{1,0:T(8,128)(2,1)} %copy-done.10, bf16[2048,1408]{1,0:T(8,128)(2,1)} %copy-done.9, bf16[512,1408]{1,0:T(8,128)(2,1)S(1)} %get-tuple-element.374.refs_2_.refs_3_, bf16[512,1408]{1,0:T(8,128)(2,1)S(1)} %get-tuple-element.376.refs_3_.refs_5_, ...), custom_call_target="tpu_custom_call" | custom-call | tf_op jit(solution)/shard_map/pallas_call | solution.py:248
  271.8 9.3 %shard_map.226 = (bf16[1024,1408]{1,0:T(8,128)(2,1)}, bf16[1024,1408]{1,0:T(8,128)(2,1)}) custom-call(bf16[512,2048]{1,0:T(8,128)(2,1)} %copy-done.24, bf16[512,2048]{1,0:T(8,128)(2,1)} %constant_dynamic-update-slice_fusion.11.h_ref.refs_1_, bf16[512,1408]{1,0:T(8,128)(2,1)S(1)} %get-tuple-element.373.refs_2_.refs_4_, ...), custom_call_target="tpu_custom_call" | custom-call | tf_op jit(solution)/shard_map/pallas_call | solution.py:291
  281.1 7.8 %shard_map.225 = bf16[1408,1024]{1,0:T(8,128)(2,1)} custom-call(bf16[512,1408]{1,0:T(8,128)(2,1)S(1)} %get-tuple-element.381.refs_0_.refs_1_, bf16[512,1408]{1,0:T(8,128)(2,1)S(1)} %get-tuple-element.387.refs_1_, bf16[512,2048]{1,0:T(8,128)(2,1)S(1)} %copy-done.1, bf16[512,2048]{1,0:T(8,128)(2,1)} %copy-done.16, ...), custom_call_target="tpu_custom_call" | custom-call | tf_op jit(solution)/shard_map/pallas_call | solution.py:291
  292.1 3.6 collective-permute-start.35
  297.5 5.8 %shard_map.228 = bf16[512,2048]{1,0:T(8,128)(2,1)S(1)} custom-call(bf16[1408,2048]{1,0:T(8,128)(2,1)} %slice_dynamic-update-slice_fusion.8.d_ref.refs_0_, bf16[512,1408]{1,0:T(8,128)(2,1)S(1)} %get-tuple-element.381.refs_0_.refs_1_), custom_call_target="tpu_custom_call" | custom-call | tf_op jit(solution)/shard_map/pallas_call | solution.py:248
  305.0 9.8 %shard_map.227 = (bf16[1024,1408]{1,0:T(8,128)(2,1)}, bf16[1024,1408]{1,0:T(8,128)(2,1)}) custom-call(bf16[512,2048]{1,0:T(8,128)(2,1)} %copy-done.24, bf16[512,2048]{1,0:T(8,128)(2,1)} %constant_dynamic-update-slice_fusion.11.h_ref.refs_1_, bf16[512,1408]{1,0:T(8,128)(2,1)S(1)} %get-tuple-element.373.refs_2_.refs_4_, ...), custom_call_target="tpu_custom_call" | custom-call | tf_op jit(solution)/shard_map/pallas_call | solution.py:291
  314.8 4.2 broadcast_select_fusion.7
  329.6 3.5 shard_map.230
  333.1 5.6 %shard_map.229.back_ref = bf16[256,2048]{1,0:T(8,128)(2,1)S(1)} custom-call(bf16[2048,2048]{1,0:T(8,128)(2,1)} %copy-done.11, bf16[256,2048]{1,0:T(8,128)(2,1)S(1)} %get-tuple-element.394.refs_1_), custom_call_target="tpu_custom_call" | custom-call | tf_op jit(solution)/shard_map/pallas_call | solution.py:248
  338.7 5.9 %shard_map.231 = bf16[512,2048]{1,0:T(8,128)(2,1)S(1)} custom-call(bf16[1408,2048]{1,0:T(8,128)(2,1)} %slice_dynamic-update-slice_fusion.8.d_ref.refs_0_, bf16[512,1408]{1,0:T(8,128)(2,1)S(1)} %get-tuple-element.387.refs_1_), custom_call_target="tpu_custom_call" | custom-call | tf_op jit(solution)/shard_map/pallas_call | solution.py:248
  344.8 5.9 %collective-permute-done.41 = bf16[256,2048]{1,0:T(8,128)(2,1)} collective-permute-done((bf16[256,2048]{1,0:T(8,128)(2,1)}, bf16[256,2048]{1,0:T(8,128)(2,1)}, u32[]{:S(2)}, u32[]{:S(2)}) %collective-permute-start.41) | collective-permute-done | bytes 1048608 | tf_op jit(solution)/shard_map/ppermute | solution.py:418
  358.6 13.4 %shard_map.232 = (bf16[256,2048]{1,0:T(8,128)(2,1)S(1)}, f32[768,256]{1,0:T(8,128)S(1)}, f32[768,256]{1,0:T(8,128)S(1)}) custom-call(bf16[256,2048]{1,0:T(8,128)(2,1)S(1)} %copy-done.8, bf16[768,512]{1,0:T(8,128)(2,1)S(1)} %constant_dynamic-update-slice_fusion.3.k_ref.v_ref, bf16[768,512]{1,0:T(8,128)(2,1)S(1)} %constant_dynamic-update-slice_fusion.3.k_ref.v_ref, ...), custom_call_target="tpu_custom_call" | custom-call | tf_op jit(solution)/shard_map/pallas_call | solution.py:128
  372.0 5.7 %shard_map.233 = bf16[2048,1024]{1,0:T(8,128)(2,1)} custom-call(bf16[256,2048]{1,0:T(8,128)(2,1)S(1)} %copy-done.6, bf16[256,2048]{1,0:T(8,128)(2,1)S(1)} %get-tuple-element.394.refs_1_, bf16[2048,1024]{1,0:T(8,128)(2,1)} %collective-permute-done.42.refs_2_), custom_call_target="tpu_custom_call" | custom-call | tf_op jit(solution)/shard_map/pallas_call | solution.py:291
  383.9 3.5 collective-permute-start.46
  389.6 3.5 shard_map.234
  394.2 4.3 collective-permute-done.47
  398.5 3.1 collective-permute-done.48
  416.3 6.4 %shard_map.237 = f32[256,2048]{1,0:T(8,128)S(1)} custom-call(bf16[2048,2048]{1,0:T(8,128)(2,1)} %copy-done.12, bf16[2048,512]{1,0:T(8,128)(2,1)S(1)} %copy-done.4, bf16[256,2048]{1,0:T(8,128)(2,1)S(1)} %get-tuple-element.403.refs_1_.refs_2_, bf16[256,512]{1,0:T(8,128)(2,1)S(1)} %pad_maximum_fusion.17.refs_1_.refs_3_), custom_call_target="tpu_custom_call" | custom-call | tf_op jit(solution)/shard_map/pallas_call | solution.py:248
  425.8 5.7 %shard_map.238 = bf16[1024,2048]{1,0:T(8,128)(2,1)} custom-call(bf16[256,2048]{1,0:T(8,128)(2,1)S(1)} %fusion.2.refs_0_, bf16[256,2048]{1,0:T(8,128)(2,1)S(1)} %get-tuple-element.403.refs_1_.refs_2_, bf16[1024,2048]{1,0:T(8,128)(2,1)} %copy-done.31), custom_call_target="tpu_custom_call" | custom-call | tf_op jit(solution)/shard_map/pallas_call | solution.py:291
  431.6 6.5 %collective-permute-done.55 = bf16[256,2048]{1,0:T(8,128)(2,1)} collective-permute-done((bf16[256,2048]{1,0:T(8,128)(2,1)}, bf16[256,2048]{1,0:T(8,128)(2,1)}, u32[]{:S(2)}, u32[]{:S(2)}) %collective-permute-start.55) | collective-permute-done | bytes 1048608 | tf_op jit(solution)/shard_map/ppermute | solution.py:418
  440.5 3.0 collective-permute-start.58
  445.4 4.6 collective-permute-done.57
  453.5 3.0 collective-permute-start.59
  459.2 18.8 %collective-permute-done.63 = f32[2,2048]{1,0:T(2,128)S(1)} collective-permute-done((f32[2,2048]{1,0:T(2,128)S(1)}, f32[2,2048]{1,0:T(2,128)S(1)}, u32[]{:S(2)}, u32[]{:S(2)}) %collective-permute-start.63) | collective-permute-done | bytes 16416 | tf_op jit(solution)/shard_map/ppermute | solution.py:426
  489.1 2.9 convert_add_fusion.4
  497.5 10.8 %collective-permute-done.68 = bf16[512,256]{1,0:T(8,128)(2,1)S(1)} collective-permute-done((bf16[512,256]{1,0:T(8,128)(2,1)S(1)}, bf16[512,256]{1,0:T(8,128)(2,1)S(1)}, u32[]{:S(2)}, u32[]{:S(2)}) %collective-permute-start.68) | collective-permute-done | bytes 262176 | tf_op jit(solution)/shard_map/ppermute | solution.py:426
  521.3 15.3 %collective-permute-done.72 = bf16[256,512]{1,0:T(8,128)(2,1)S(1)} collective-permute-done((bf16[256,512]{1,0:T(8,128)(2,1)S(1)}, bf16[256,512]{1,0:T(8,128)(2,1)S(1)}, u32[]{:S(2)}, u32[]{:S(2)}) %collective-permute-start.72) | collective-permute-done | bytes 262176 | tf_op jit(solution)/shard_map/ppermute | solution.py:426
  (512 shorter events, 203.4 us)
Async XLA Ops:
  1.7 21.6 %collective-permute-start.2 = (bf16[256,512]{1,0:T(8,128)(2,1)S(1)}, bf16[256,512]{1,0:T(8,128)(2,1)}, u32[]{:S(2)}, u32[]{:S(2)}) collective-permute-start(bf16[256,512]{1,0:T(8,128)(2,1)S(1)} %slice_select_fusion), channel_id=1, source_target_pairs={{0,1},{1,0},{2,3},{3,2},{4,5},{5,4},{6,7},{7,6},{8,9},{9,8},{10,11... | collective-permute-start | bytes 786440 | tf_op jit(solution)/shard_map/ppermute | solution.py:426
  1.9 22.7 %collective-permute-start.3 = (bf16[256,512]{1,0:T(8,128)(2,1)S(1)}, bf16[256,512]{1,0:T(8,128)(2,1)}, u32[]{:S(2)}, u32[]{:S(2)}) collective-permute-start(bf16[256,512]{1,0:T(8,128)(2,1)S(1)} %slice_select_fusion), channel_id=1, source_target_pairs={{0,2},{1,3},{2,0},{3,1},{4,6},{5,7},{6,4},{7,5},{8,10},{9,11},{10,... | collective-permute-start | bytes 786440 | tf_op jit(solution)/shard_map/ppermute | solution.py:426
  4.3 22.6 %collective-permute-start.4 = (bf16[256,512]{1,0:T(8,128)(2,1)S(1)}, bf16[256,512]{1,0:T(8,128)(2,1)}, u32[]{:S(2)}, u32[]{:S(2)}) collective-permute-start(bf16[256,512]{1,0:T(8,128)(2,1)S(1)} %slice_select_fusion), channel_id=1, source_target_pairs={{0,3},{1,2},{2,1},{3,0},{4,7},{5,6},{6,5},{7,4},{8,11},{9,10},{10,... | collective-permute-start | bytes 786440 | tf_op jit(solution)/shard_map/ppermute | solution.py:426
  13.7 17.4 %collective-permute-start.7 = (bf16[256,512]{1,0:T(8,128)(2,1)}, bf16[256,512]{1,0:T(8,128)(2,1)S(1)}, u32[]{:S(2)}, u32[]{:S(2)}) collective-permute-start(bf16[256,512]{1,0:T(8,128)(2,1)} %collective-permute-done), channel_id=1, source_target_pairs={{0,16},{16,0},{1,17},{17,1},{2,18},{18,2},{3,19},{19,3},{4,20},{20... | collective-permute-start | bytes 786440 | tf_op jit(solution)/shard_map/ppermute | solution.py:415
  28.3 20.4 %collective-permute-start.5 = (bf16[256,2048]{1,0:T(8,128)(2,1)S(1)}, bf16[256,2048]{1,0:T(8,128)(2,1)S(1)}, u32[]{:S(2)}, u32[]{:S(2)}) collective-permute-start(bf16[256,2048]{1,0:T(8,128)(2,1)S(1)} %get-tuple-element.624), channel_id=1, source_target_pairs={{0,4},{4,0},{8,12},{12,8},{16,24},{20,28},{24,16},{28,20},{1,5},{5... | collective-permute-start | bytes 3145736 | tf_op jit(solution)/shard_map/ppermute | solution.py:410
  29.6 19.1 %collective-permute-start.6 = (bf16[256,2048]{1,0:T(8,128)(2,1)S(1)}, bf16[256,2048]{1,0:T(8,128)(2,1)S(1)}, u32[]{:S(2)}, u32[]{:S(2)}) collective-permute-start(bf16[256,2048]{1,0:T(8,128)(2,1)S(1)} %get-tuple-element.624), channel_id=1, source_target_pairs={{0,16},{16,0},{1,17},{17,1},{2,18},{18,2},{3,19},{19,3},{4,20},{20... | collective-permute-start | bytes 3145736 | tf_op jit(solution)/shard_map/ppermute | solution.py:415
  31.2 24.4 %collective-permute-start.15 = (bf16[256,2048]{1,0:T(8,128)(2,1)S(1)}, bf16[256,2048]{1,0:T(8,128)(2,1)}, u32[]{:S(2)}, u32[]{:S(2)}) collective-permute-start(bf16[256,2048]{1,0:T(8,128)(2,1)S(1)} %multiply_convert_fusion.2), channel_id=1, source_target_pairs={{0,1},{1,2},{2,3},{3,0},{4,5},{5,6},{6,7},{7,4},{8,9},{9,10},{10,1... | collective-permute-start | bytes 3145736 | tf_op jit(solution)/shard_map/ppermute | solution.py:418
  48.9 27.0 %collective-permute-start.11 = (bf16[256,2048]{1,0:T(8,128)(2,1)S(1)}, bf16[256,2048]{1,0:T(8,128)(2,1)S(1)}, u32[]{:S(2)}, u32[]{:S(2)}) collective-permute-start(bf16[256,2048]{1,0:T(8,128)(2,1)S(1)} %collective-permute-done.5), channel_id=1, source_target_pairs={{0,16},{16,0},{1,17},{17,1},{2,18},{18,2},{3,19},{19,3},{4,20},{20... | collective-permute-start | bytes 3145736 | tf_op jit(solution)/shard_map/ppermute | solution.py:415
  51.0 25.3 %collective-permute-start.10 = (bf16[512,2048]{1,0:T(8,128)(2,1)S(1)}, bf16[512,2048]{1,0:T(8,128)(2,1)S(1)}, u32[]{:S(2)}, u32[]{:S(2)}) collective-permute-start(bf16[512,2048]{1,0:T(8,128)(2,1)S(1)} %pad_maximum_fusion.1), channel_id=1, source_target_pairs={{0,8},{4,12},{8,0},{12,4},{16,20},{20,16},{24,28},{28,24},{1,9},{5... | collective-permute-start | bytes 6291464 | tf_op jit(solution)/shard_map/ppermute | solution.py:410
  55.6 14.6 %collective-permute-start.16 = (bf16[256,512]{1,0:T(8,128)(2,1)S(1)}, bf16[256,512]{1,0:T(8,128)(2,1)S(1)}, u32[]{:S(2)}, u32[]{:S(2)}) collective-permute-start(bf16[256,512]{1,0:T(8,128)(2,1)S(1)} %pad_maximum_fusion.16), channel_id=1, source_target_pairs={{0,2},{1,3},{4,6},{5,7},{8,10},{9,11},{12,14},{13,15},{16,18},{17,... | collective-permute-start | bytes 786440 | tf_op jit(solution)/shard_map/ppermute | solution.py:421
  59.1 16.7 %collective-permute-start.17 = (bf16[256,512]{1,0:T(8,128)(2,1)S(1)}, bf16[256,512]{1,0:T(8,128)(2,1)S(1)}, u32[]{:S(2)}, u32[]{:S(2)}) collective-permute-start(bf16[256,512]{1,0:T(8,128)(2,1)S(1)} %pad_maximum_fusion.16), channel_id=1, source_target_pairs={{0,1},{1,2},{2,3},{4,5},{5,6},{6,7},{8,9},{9,10},{10,11},{12,13},{... | collective-permute-start | bytes 786440 | tf_op jit(solution)/shard_map/ppermute | solution.py:421
  61.1 37.3 %collective-permute-start.19 = (bf16[256,2048]{1,0:T(8,128)(2,1)}, bf16[256,2048]{1,0:T(8,128)(2,1)}, u32[]{:S(2)}, u32[]{:S(2)}) collective-permute-start(bf16[256,2048]{1,0:T(8,128)(2,1)} %collective-permute-done.15), channel_id=1, source_target_pairs={{0,1},{1,2},{2,3},{3,0},{4,5},{5,6},{6,7},{7,4},{8,9},{9,10},{10,1... | collective-permute-start | bytes 3145736 | tf_op jit(solution)/shard_map/ppermute | solution.py:418
  76.3 24.9 %collective-permute-start.18 = (bf16[2048,256]{1,0:T(8,128)(2,1)S(1)}, bf16[2048,256]{1,0:T(8,128)(2,1)S(1)}, u32[]{:S(2)}, u32[]{:S(2)}) collective-permute-start(bf16[2048,256]{1,0:T(8,128)(2,1)S(1)} %collective-permute-done.9), channel_id=1, source_target_pairs={{0,16},{16,0},{1,17},{17,1},{2,18},{18,2},{3,19},{19,3},{4,20},{20... | collective-permute-start | bytes 3145736 | tf_op jit(solution)/shard_map/ppermute | solution.py:415
  78.0 40.8 %collective-permute-start.12 = (bf16[4096,256]{1,0:T(8,128)(2,1)S(1)}, bf16[4096,256]{1,0:T(8,128)(2,1)}, u32[]{:S(2)}, u32[]{:S(2)}) collective-permute-start(bf16[4096,256]{1,0:T(8,128)(2,1)S(1)} %pad_maximum_fusion.2), channel_id=1, source_target_pairs={{0,8},{4,12},{8,0},{12,4},{16,20},{20,16},{24,28},{28,24},{1,9},{5... | collective-permute-start | bytes 6291464 | tf_op jit(solution)/shard_map/ppermute | solution.py:410
  80.9 33.8 %collective-permute-start.13 = (bf16[512,1408]{1,0:T(8,128)(2,1)S(1)}, bf16[512,1408]{1,0:T(8,128)(2,1)S(1)}, u32[]{:S(2)}, u32[]{:S(2)}) collective-permute-start(bf16[512,1408]{1,0:T(8,128)(2,1)S(1)} %pad_maximum_fusion.4), channel_id=1, source_target_pairs={{0,4},{4,0},{8,12},{12,8},{16,24},{20,28},{24,16},{28,20},{1,5},{5... | collective-permute-start | bytes 4325384 | tf_op jit(solution)/shard_map/ppermute | solution.py:410
  98.4 24.1 %collective-permute-start.20 = (bf16[256,2048]{1,0:T(8,128)(2,1)}, bf16[256,2048]{1,0:T(8,128)(2,1)S(1)}, u32[]{:S(2)}, u32[]{:S(2)}) collective-permute-start(bf16[256,2048]{1,0:T(8,128)(2,1)} %collective-permute-done.19), channel_id=1, source_target_pairs={{0,1},{1,2},{2,3},{3,0},{4,5},{5,6},{6,7},{7,4},{8,9},{9,10},{10,1... | collective-permute-start | bytes 3145736 | tf_op jit(solution)/shard_map/ppermute | solution.py:418
  124.8 41.5 %collective-permute-start.23 = (bf16[1024,1408]{1,0:T(8,128)(2,1)S(1)}, bf16[1024,1408]{1,0:T(8,128)(2,1)}, u32[]{:S(2)}, u32[]{:S(2)}) collective-permute-start(bf16[1024,1408]{1,0:T(8,128)(2,1)S(1)} %pad_maximum_fusion), channel_id=1, source_target_pairs={{0,8},{4,12},{8,0},{12,4},{16,20},{20,16},{24,28},{28,24},{1,9},{5... | collective-permute-start | bytes 8650760 | tf_op jit(solution)/shard_map/ppermute | solution.py:410
  126.1 18.3 %collective-permute-start.24 = (bf16[1408,256]{1,0:T(8,128)(2,1)S(1)}, bf16[1408,256]{1,0:T(8,128)(2,1)S(1)}, u32[]{:S(2)}, u32[]{:S(2)}) collective-permute-start(bf16[1408,256]{1,0:T(8,128)(2,1)S(1)} %get-tuple-element.310), channel_id=1, source_target_pairs={{0,4},{4,0},{8,12},{12,8},{16,24},{20,28},{24,16},{28,20},{1,5},{5... | collective-permute-start | bytes 2162696 | tf_op jit(solution)/shard_map/ppermute | solution.py:410
  136.3 30.0 %collective-permute-start.25 = (bf16[256,2048]{1,0:T(8,128)(2,1)S(1)}, bf16[256,2048]{1,0:T(8,128)(2,1)S(1)}, u32[]{:S(2)}, u32[]{:S(2)}) collective-permute-start(bf16[256,2048]{1,0:T(8,128)(2,1)S(1)} %multiply_convert_fusion.1), channel_id=1, source_target_pairs={{0,1},{1,2},{2,3},{3,0},{4,5},{5,6},{6,7},{7,4},{8,9},{9,10},{10,1... | collective-permute-start | bytes 3145736 | tf_op jit(solution)/shard_map/ppermute | solution.py:418
  167.9 24.7 %collective-permute-start.27 = (bf16[2816,256]{1,0:T(8,128)(2,1)S(1)}, bf16[2816,256]{1,0:T(8,128)(2,1)S(1)}, u32[]{:S(2)}, u32[]{:S(2)}) collective-permute-start(bf16[2816,256]{1,0:T(8,128)(2,1)S(1)} %pad_maximum_fusion.5), channel_id=1, source_target_pairs={{0,8},{4,12},{8,0},{12,4},{16,20},{20,16},{24,28},{28,24},{1,9},{5... | collective-permute-start | bytes 4325384 | tf_op jit(solution)/shard_map/ppermute | solution.py:410
  168.4 24.2 %collective-permute-start.29 = (bf16[256,2048]{1,0:T(8,128)(2,1)S(1)}, bf16[256,2048]{1,0:T(8,128)(2,1)}, u32[]{:S(2)}, u32[]{:S(2)}) collective-permute-start(bf16[256,2048]{1,0:T(8,128)(2,1)S(1)} %collective-permute-done.25), channel_id=1, source_target_pairs={{0,1},{1,2},{2,3},{3,0},{4,5},{5,6},{6,7},{7,4},{8,9},{9,10},{10,1... | collective-permute-start | bytes 3145736 | tf_op jit(solution)/shard_map/ppermute | solution.py:418
  195.9 25.2 %collective-permute-start.31 = (bf16[256,2048]{1,0:T(8,128)(2,1)}, bf16[256,2048]{1,0:T(8,128)(2,1)S(1)}, u32[]{:S(2)}, u32[]{:S(2)}) collective-permute-start(bf16[256,2048]{1,0:T(8,128)(2,1)} %collective-permute-done.29), channel_id=1, source_target_pairs={{0,1},{1,2},{2,3},{3,0},{4,5},{5,6},{6,7},{7,4},{8,9},{9,10},{10,1... | collective-permute-start | bytes 3145736 | tf_op jit(solution)/shard_map/ppermute | solution.py:418
  221.1 36.7 %collective-permute-start.32 = (bf16[256,2048]{1,0:T(8,128)(2,1)S(1)}, bf16[256,2048]{1,0:T(8,128)(2,1)}, u32[]{:S(2)}, u32[]{:S(2)}) collective-permute-start(bf16[256,2048]{1,0:T(8,128)(2,1)S(1)} %shard_map.220), channel_id=1, source_target_pairs={{0,1},{1,2},{2,3},{3,0},{4,5},{5,6},{6,7},{7,4},{8,9},{9,10},{10,1... | collective-permute-start | bytes 3145736 | tf_op jit(solution)/shard_map/ppermute | solution.py:418
  260.4 20.7 %collective-permute-start.34 = (bf16[1408,1024]{1,0:T(8,128)(2,1)}, bf16[1408,1024]{1,0:T(8,128)(2,1)}, u32[]{:S(2)}, u32[]{:S(2)}) collective-permute-start(bf16[1408,1024]{1,0:T(8,128)(2,1)} %shard_map.223), channel_id=1, source_target_pairs={{0,16},{16,0},{1,17},{17,1},{2,18},{18,2},{3,19},{19,3},{4,20},{20... | collective-permute-start | bytes 8650760 | tf_op jit(solution)/shard_map/ppermute | solution.py:415
  261.4 27.5 %collective-permute-start.33 = (bf16[256,2048]{1,0:T(8,128)(2,1)}, bf16[256,2048]{1,0:T(8,128)(2,1)}, u32[]{:S(2)}, u32[]{:S(2)}) collective-permute-start(bf16[256,2048]{1,0:T(8,128)(2,1)} %add_convert_fusion.6), channel_id=1, source_target_pairs={{0,1},{1,2},{2,3},{3,0},{4,5},{5,6},{6,7},{7,4},{8,9},{9,10},{10,1... | collective-permute-start | bytes 3145736 | tf_op jit(solution)/shard_map/ppermute | solution.py:418
  292.1 29.4 %collective-permute-start.35 = (bf16[256,2048]{1,0:T(8,128)(2,1)}, bf16[256,2048]{1,0:T(8,128)(2,1)S(1)}, u32[]{:S(2)}, u32[]{:S(2)}) collective-permute-start(bf16[256,2048]{1,0:T(8,128)(2,1)} %add_convert_fusion.5), channel_id=1, source_target_pairs={{0,1},{1,2},{2,3},{3,0},{4,5},{5,6},{6,7},{7,4},{8,9},{9,10},{10,1... | collective-permute-start | bytes 3145736 | tf_op jit(solution)/shard_map/ppermute | solution.py:418
  297.0 24.5 %collective-permute-start.36 = (bf16[1408,512]{1,0:T(8,128)(2,1)}, bf16[1408,512]{1,0:T(8,128)(2,1)}, u32[]{:S(2)}, u32[]{:S(2)}) collective-permute-start(bf16[1408,512]{1,0:T(8,128)(2,1)} %pad_maximum_fusion.6), channel_id=1, source_target_pairs={{0,4},{4,0},{8,12},{12,8},{16,24},{20,28},{24,16},{28,20},{1,5},{5... | collective-permute-start | bytes 4325384 | tf_op jit(solution)/shard_map/ppermute | solution.py:410
  324.8 20.0 %collective-permute-start.39 = (bf16[1408,256]{1,0:T(8,128)(2,1)}, bf16[1408,256]{1,0:T(8,128)(2,1)}, u32[]{:S(2)}, u32[]{:S(2)}) collective-permute-start(bf16[1408,256]{1,0:T(8,128)(2,1)} %add_convert_fusion.9), channel_id=1, source_target_pairs={{0,8},{4,12},{8,0},{12,4},{16,20},{20,16},{24,28},{28,24},{1,9},{5... | collective-permute-start | bytes 2162696 | tf_op jit(solution)/shard_map/ppermute | solution.py:410
  325.8 26.2 %collective-permute-start.40 = (bf16[512,1408]{1,0:T(8,128)(2,1)}, bf16[512,1408]{1,0:T(8,128)(2,1)}, u32[]{:S(2)}, u32[]{:S(2)}) collective-permute-start(bf16[512,1408]{1,0:T(8,128)(2,1)} %pad_maximum_fusion.7), channel_id=1, source_target_pairs={{0,4},{4,0},{8,12},{12,8},{16,24},{20,28},{24,16},{28,20},{1,5},{5... | collective-permute-start | bytes 4325384 | tf_op jit(solution)/shard_map/ppermute | solution.py:410
  326.7 24.0 %collective-permute-start.41 = (bf16[256,2048]{1,0:T(8,128)(2,1)}, bf16[256,2048]{1,0:T(8,128)(2,1)}, u32[]{:S(2)}, u32[]{:S(2)}) collective-permute-start(bf16[256,2048]{1,0:T(8,128)(2,1)} %get-tuple-element.388), channel_id=1, source_target_pairs={{0,1},{1,2},{2,3},{3,0},{4,5},{5,6},{6,7},{7,4},{8,9},{9,10},{10,1... | collective-permute-start | bytes 3145736 | tf_op jit(solution)/shard_map/ppermute | solution.py:418
  352.0 20.0 %collective-permute-start.42 = (bf16[2048,1024]{1,0:T(8,128)(2,1)S(1)}, bf16[2048,1024]{1,0:T(8,128)(2,1)}, u32[]{:S(2)}, u32[]{:S(2)}) collective-permute-start(bf16[2048,1024]{1,0:T(8,128)(2,1)S(1)} %copy-done.30), channel_id=1, source_target_pairs={{0,16},{16,0},{1,17},{17,1},{2,18},{18,2},{3,19},{19,3},{4,20},{20... | collective-permute-start | bytes 12582920 | tf_op jit(solution)/shard_map/ppermute | solution.py:415
  352.7 27.4 %collective-permute-start.44 = (bf16[512,1408]{1,0:T(8,128)(2,1)}, bf16[512,1408]{1,0:T(8,128)(2,1)}, u32[]{:S(2)}, u32[]{:S(2)}) collective-permute-start(bf16[512,1408]{1,0:T(8,128)(2,1)} %pad_maximum_fusion.8), channel_id=1, source_target_pairs={{0,4},{4,0},{8,12},{12,8},{16,24},{20,28},{24,16},{28,20},{1,5},{5... | collective-permute-start | bytes 4325384 | tf_op jit(solution)/shard_map/ppermute | solution.py:410
  355.8 25.0 %collective-permute-start.45 = (bf16[256,2048]{1,0:T(8,128)(2,1)}, bf16[256,2048]{1,0:T(8,128)(2,1)}, u32[]{:S(2)}, u32[]{:S(2)}) collective-permute-start(bf16[256,2048]{1,0:T(8,128)(2,1)} %add_convert_fusion.4), channel_id=1, source_target_pairs={{0,1},{1,2},{2,3},{3,0},{4,5},{5,6},{6,7},{7,4},{8,9},{9,10},{10,1... | collective-permute-start | bytes 3145736 | tf_op jit(solution)/shard_map/ppermute | solution.py:418
  358.2 21.9 %collective-permute-start.43 = (bf16[256,1408]{1,0:T(8,128)(2,1)}, bf16[256,1408]{1,0:T(8,128)(2,1)}, u32[]{:S(2)}, u32[]{:S(2)}) collective-permute-start(bf16[256,1408]{1,0:T(8,128)(2,1)} %add_convert_fusion.8), channel_id=1, source_target_pairs={{0,8},{4,12},{8,0},{12,4},{16,20},{20,16},{24,28},{28,24},{1,9},{5... | collective-permute-start | bytes 2162696 | tf_op jit(solution)/shard_map/ppermute | solution.py:410
  380.9 21.6 %collective-permute-start.49 = (bf16[1024,512]{1,0:T(8,128)(2,1)S(1)}, bf16[1024,512]{1,0:T(8,128)(2,1)S(1)}, u32[]{:S(2)}, u32[]{:S(2)}) collective-permute-start(bf16[1024,512]{1,0:T(8,128)(2,1)S(1)} %pad_maximum_fusion.10), channel_id=1, source_target_pairs={{0,4},{4,0},{8,12},{12,8},{16,24},{20,28},{24,16},{28,20},{1,5},{5... | collective-permute-start | bytes 3145736 | tf_op jit(solution)/shard_map/ppermute | solution.py:410
  383.4 18.2 %collective-permute-start.48 = (bf16[256,1408]{1,0:T(8,128)(2,1)S(1)}, bf16[256,1408]{1,0:T(8,128)(2,1)S(1)}, u32[]{:S(2)}, u32[]{:S(2)}) collective-permute-start(bf16[256,1408]{1,0:T(8,128)(2,1)S(1)} %add_convert_fusion.7), channel_id=1, source_target_pairs={{0,8},{4,12},{8,0},{12,4},{16,20},{20,16},{24,28},{28,24},{1,9},{5... | collective-permute-start | bytes 2162696 | tf_op jit(solution)/shard_map/ppermute | solution.py:410
  409.4 28.7 %collective-permute-start.55 = (bf16[256,2048]{1,0:T(8,128)(2,1)}, bf16[256,2048]{1,0:T(8,128)(2,1)}, u32[]{:S(2)}, u32[]{:S(2)}) collective-permute-start(bf16[256,2048]{1,0:T(8,128)(2,1)} %add_convert_fusion.3), channel_id=1, source_target_pairs={{0,1},{1,2},{2,3},{3,0},{4,5},{5,6},{6,7},{7,4},{8,9},{9,10},{10,1... | collective-permute-start | bytes 3145736 | tf_op jit(solution)/shard_map/ppermute | solution.py:418
  414.7 23.4 %collective-permute-start.53 = (bf16[512,512]{1,0:T(8,128)(2,1)S(1)}, bf16[512,512]{1,0:T(8,128)(2,1)S(1)}, u32[]{:S(2)}, u32[]{:S(2)}) collective-permute-start(bf16[512,512]{1,0:T(8,128)(2,1)S(1)} %pad_maximum_fusion.14), channel_id=1, source_target_pairs={{0,4},{4,0},{8,12},{12,8},{16,24},{20,28},{24,16},{28,20},{1,5},{5... | collective-permute-start | bytes 1572872 | tf_op jit(solution)/shard_map/ppermute | solution.py:410
  415.6 22.4 %collective-permute-start.54 = (bf16[1024,512]{1,0:T(8,128)(2,1)}, bf16[1024,512]{1,0:T(8,128)(2,1)S(1)}, u32[]{:S(2)}, u32[]{:S(2)}) collective-permute-start(bf16[1024,512]{1,0:T(8,128)(2,1)} %pad_maximum_fusion.11), channel_id=1, source_target_pairs={{0,4},{4,0},{8,12},{12,8},{16,24},{20,28},{24,16},{28,20},{1,5},{5... | collective-permute-start | bytes 3145736 | tf_op jit(solution)/shard_map/ppermute | solution.py:410
  450.8 29.4 %collective-permute-start.62 = (bf16[512,2048]{1,0:T(8,128)(2,1)}, bf16[512,2048]{1,0:T(8,128)(2,1)}, u32[]{:S(2)}, u32[]{:S(2)}) collective-permute-start(bf16[512,2048]{1,0:T(8,128)(2,1)} %pad_maximum_fusion.3), channel_id=1, source_target_pairs={{0,4},{4,0},{8,12},{12,8},{16,24},{20,28},{24,16},{28,20},{1,5},{5... | collective-permute-start | bytes 6291464 | tf_op jit(solution)/shard_map/ppermute | solution.py:410
  453.5 24.5 %collective-permute-start.59 = (bf16[256,512]{1,0:T(8,128)(2,1)S(1)}, bf16[256,512]{1,0:T(8,128)(2,1)S(1)}, u32[]{:S(2)}, u32[]{:S(2)}) collective-permute-start(bf16[256,512]{1,0:T(8,128)(2,1)S(1)} %add_convert_fusion.15), channel_id=1, source_target_pairs={{0,1},{1,0},{2,3},{3,2},{4,5},{5,4},{6,7},{7,6},{8,9},{9,8},{10,11... | collective-permute-start | bytes 786440 | tf_op jit(solution)/shard_map/ppermute | solution.py:426
  456.5 21.5 %collective-permute-start.60 = (bf16[256,512]{1,0:T(8,128)(2,1)S(1)}, bf16[256,512]{1,0:T(8,128)(2,1)S(1)}, u32[]{:S(2)}, u32[]{:S(2)}) collective-permute-start(bf16[256,512]{1,0:T(8,128)(2,1)S(1)} %add_convert_fusion.15), channel_id=1, source_target_pairs={{0,2},{1,3},{2,0},{3,1},{4,6},{5,7},{6,4},{7,5},{8,10},{9,11},{10,... | collective-permute-start | bytes 786440 | tf_op jit(solution)/shard_map/ppermute | solution.py:426
  456.5 23.6 %collective-permute-start.61 = (bf16[256,512]{1,0:T(8,128)(2,1)S(1)}, bf16[256,512]{1,0:T(8,128)(2,1)S(1)}, u32[]{:S(2)}, u32[]{:S(2)}) collective-permute-start(bf16[256,512]{1,0:T(8,128)(2,1)S(1)} %add_convert_fusion.15), channel_id=1, source_target_pairs={{0,3},{1,2},{2,1},{3,0},{4,7},{5,6},{6,5},{7,4},{8,11},{9,10},{10,... | collective-permute-start | bytes 786440 | tf_op jit(solution)/shard_map/ppermute | solution.py:426
  457.8 20.2 %collective-permute-start.63 = (f32[2,2048]{1,0:T(2,128)S(1)}, f32[2,2048]{1,0:T(2,128)S(1)}, u32[]{:S(2)}, u32[]{:S(2)}) collective-permute-start(f32[2,2048]{1,0:T(2,128)S(1)} %add.420), channel_id=1, source_target_pairs={{0,2},{1,3},{2,0},{3,1},{4,6},{5,7},{6,4},{7,5},{8,10},{9,11},{10,... | collective-permute-start | bytes 49160 | tf_op jit(solution)/shard_map/ppermute | solution.py:426
  483.9 24.4 %collective-permute-start.65 = (bf16[256,2048]{1,0:T(8,128)(2,1)S(1)}, bf16[256,2048]{1,0:T(8,128)(2,1)S(1)}, u32[]{:S(2)}, u32[]{:S(2)}) collective-permute-start(bf16[256,2048]{1,0:T(8,128)(2,1)S(1)} %add_convert_fusion.2), channel_id=1, source_target_pairs={{0,8},{4,12},{8,0},{12,4},{16,20},{20,16},{24,28},{28,24},{1,9},{5... | collective-permute-start | bytes 3145736 | tf_op jit(solution)/shard_map/ppermute | solution.py:410
  485.3 22.9 %collective-permute-start.68 = (bf16[512,256]{1,0:T(8,128)(2,1)S(1)}, bf16[512,256]{1,0:T(8,128)(2,1)S(1)}, u32[]{:S(2)}, u32[]{:S(2)}) collective-permute-start(bf16[512,256]{1,0:T(8,128)(2,1)S(1)} %get-tuple-element.450), channel_id=1, source_target_pairs={{0,3},{1,2},{2,1},{3,0},{4,7},{5,6},{6,5},{7,4},{8,11},{9,10},{10,... | collective-permute-start | bytes 786440 | tf_op jit(solution)/shard_map/ppermute | solution.py:426
  508.3 28.3 %collective-permute-start.69 = (bf16[512,512]{1,0:T(8,128)(2,1)S(1)}, bf16[512,512]{1,0:T(8,128)(2,1)S(1)}, u32[]{:S(2)}, u32[]{:S(2)}) collective-permute-start(bf16[512,512]{1,0:T(8,128)(2,1)S(1)} %pad_maximum_fusion.15), channel_id=1, source_target_pairs={{0,8},{4,12},{8,0},{12,4},{16,20},{20,16},{24,28},{28,24},{1,9},{5... | collective-permute-start | bytes 1572872 | tf_op jit(solution)/shard_map/ppermute | solution.py:410
  512.1 24.5 %collective-permute-start.72 = (bf16[256,512]{1,0:T(8,128)(2,1)S(1)}, bf16[256,512]{1,0:T(8,128)(2,1)S(1)}, u32[]{:S(2)}, u32[]{:S(2)}) collective-permute-start(bf16[256,512]{1,0:T(8,128)(2,1)S(1)} %get-tuple-element.611), channel_id=1, source_target_pairs={{0,3},{1,2},{2,1},{3,0},{4,7},{5,6},{6,5},{7,4},{8,11},{9,10},{10,... | collective-permute-start | bytes 786440 | tf_op jit(solution)/shard_map/ppermute | solution.py:426
  (106 other events, 1040.0 us)

commit v7 on v5

--- a/solution.py
+++ b/solution.py
@@ -262,7 +262,7 @@
 def token_sums(lefts, left_lanes, rights, right_lanes, received=None):
     n, many = len(lefts), len(rights)
     start, rows_out = left_lanes
-    tile = min(256, rows_out)
+    tile = min(512 if rows_out >= 2048 else 256, rows_out)
     base, columns = right_lanes
 
     def kernel(*refs):

time: 552 us -> 552 us (level)
  no operation moved by 1% of the time
where the time goes in v7:
time: 552 us; the launch traced here: 542 us
  waiting for transfers between devices  171 us (31%)
  Pallas kernels  150 us (27%)
  starting transfers between devices  87.4 us (16%)
  other arithmetic  68 us (12%)
  local copies, waits for them, and re-layouts  45.9 us (8%)
  matrix products  15.6 us (3%)
    ppermute x28, waiting for transfers between devices, to_near(): return lax.ppermute(value, ('dp', 'rows'), pairs)  64.8 us
    pallas_call x10, Pallas kernels, token_sums(): call(kernel, (pl.cdiv(rows_out, tile),), specs, [out] * many, [jax.ShapeD...  54.4 us
    ppermute x14, waiting for transfers between devices, to_xor_cols(): return lax.ppermute(value, 'cols', [(i, i ^ k) for i in range(cols)])  49.8 us
    pallas_call x7, Pallas kernels, rows_products(): call(kernel, (columns // tile,), specs, [pl.BlockSpec((count, tile), lamb...  47.5 us
    ppermute x12, waiting for transfers between devices, to_cols(): lax.ppermute(value, 'cols', [(i, (i + k) % cols) for i in range(cols)])  32.8 us
    ppermute x28, starting transfers between devices, to_near(): return lax.ppermute(value, ('dp', 'rows'), pairs)  22.2 us
    ppermute x12, starting transfers between devices, to_cols(): lax.ppermute(value, 'cols', [(i, (i + k) % cols) for i in range(cols)])  20.4 us
    unnamed x166, local copies, waits for them, and re-layouts  20 us
  transfers between devices with their start and end apart: 77, of which 33 were waited for; matrix products, arithmetic and copies ran while one was open for 19% of the time, Pallas kernels for 28%

profile of v7, /device:TPU:11, one launch (start us, length us, event | category | flops | bytes accessed | tf_op | source)
XLA Modules:
  0.0 542.5 jit_solution(4838166988987522423)
XLA Ops:
  33.8 3.6 collective-permute-done.9
  37.3 11.2 %collective-permute-done.5 = bf16[256,2048]{1,0:T(8,128)(2,1)S(1)} collective-permute-done((bf16[256,2048]{1,0:T(8,128)(2,1)S(1)}, bf16[256,2048]{1,0:T(8,128)(2,1)S(1)}, u32[]{:S(2)}, u32[]{:S(2)}) %collective-permute-start.5) | collective-permute-done | bytes 1048608 | tf_op jit(solution)/shard_map/ppermute | solution.py:410
  55.5 3.8 collective-permute-start.16
  61.5 9.1 %collective-permute-done.16 = bf16[256,512]{1,0:T(8,128)(2,1)S(1)} collective-permute-done((bf16[256,512]{1,0:T(8,128)(2,1)S(1)}, bf16[256,512]{1,0:T(8,128)(2,1)S(1)}, u32[]{:S(2)}, u32[]{:S(2)}) %collective-permute-start.16) | collective-permute-done | bytes 262176 | tf_op jit(solution)/shard_map/ppermute | solution.py:421
  70.6 5.6 %collective-permute-done.17 = bf16[256,512]{1,0:T(8,128)(2,1)S(1)} collective-permute-done((bf16[256,512]{1,0:T(8,128)(2,1)S(1)}, bf16[256,512]{1,0:T(8,128)(2,1)S(1)}, u32[]{:S(2)}, u32[]{:S(2)}) %collective-permute-start.17) | collective-permute-done | bytes 262176 | tf_op jit(solution)/shard_map/ppermute | solution.py:421
  88.1 10.6 %collective-permute-done.19 = bf16[256,2048]{1,0:T(8,128)(2,1)} collective-permute-done((bf16[256,2048]{1,0:T(8,128)(2,1)S(1)}, bf16[256,2048]{1,0:T(8,128)(2,1)}, u32[]{:S(2)}, u32[]{:S(2)}) %collective-permute-start.19) | collective-permute-done | bytes 1048608 | tf_op jit(solution)/shard_map/ppermute | solution.py:418
  101.8 10.8 %shard_map.214 = (bf16[256,2048]{1,0:T(8,128)(2,1)S(1)}, bf16[256,2048]{1,0:T(8,128)(2,1)S(1)}, f32[16,1,256]{2,1,0:T(1,128)S(1)}) custom-call(f32[256,2048]{1,0:T(8,128)S(1)} %fusion.40.pre_ref, bf16[768,512]{1,0:T(8,128)(2,1)S(1)} %constant_dynamic-update-slice_fusion.3.k_ref.v_ref, bf16[768,512]{1,0:T(8,128)(2,1)S(1)} %constant_dynamic-update-slice_fusion.3.k_ref.v_ref, ...), custom_call_target="tpu_custom_call" | custom-call | tf_op jit(solution)/shard_map/pallas_call | solution.py:68
  112.6 3.3 collective-permute-done.13
  115.9 4.2 collective-permute-done.12
  120.1 3.1 collective-permute-done.20
  140.4 4.3 collective-permute-done.24
  144.8 22.0 %collective-permute-done.23 = bf16[1024,1408]{1,0:T(8,128)(2,1)} collective-permute-done((bf16[1024,1408]{1,0:T(8,128)(2,1)S(1)}, bf16[1024,1408]{1,0:T(8,128)(2,1)}, u32[]{:S(2)}, u32[]{:S(2)}) %collective-permute-start.23) | collective-permute-done | bytes 2883616 | tf_op jit(solution)/shard_map/ppermute | solution.py:410
  178.4 5.0 fusion.42.gate_ref
  183.4 5.0 fusion.43.up_ref
  188.4 5.1 collective-permute-done.29
  201.1 9.2 %shard_map.219 = (bf16[512,1408]{1,0:T(8,128)(2,1)S(1)}, bf16[512,1408]{1,0:T(8,128)(2,1)S(1)}, bf16[512,1408]{1,0:T(8,128)(2,1)S(1)}) custom-call(bf16[512,2048]{1,0:T(8,128)(2,1)} %copy-done, f32[512,1408]{1,0:T(8,128)} %fusion.42.gate_ref, f32[512,1408]{1,0:T(8,128)} %fusion.43.up_ref, bf16[1408,2048]{1,0:T(8,128)(2,1)} %slice_dynamic-update-slice_fusion.8.d_ref.refs_0_), custom_call_target="tpu_custom_call" | custom-call | tf_op jit(solution)/shard_map/pallas_call | solution.py:217
  210.3 6.9 %shard_map.220 = bf16[256,2048]{1,0:T(8,128)(2,1)S(1)} custom-call(bf16[2048,1408]{1,0:T(8,128)(2,1)} %copy-done.10, bf16[2048,1408]{1,0:T(8,128)(2,1)} %copy-done.9, bf16[512,1408]{1,0:T(8,128)(2,1)S(1)} %get-tuple-element.370.refs_2_.refs_4_, bf16[512,1408]{1,0:T(8,128)(2,1)S(1)} %get-tuple-element.372.refs_3_.refs_5_.refs_4_), custom_call_target="tpu_custom_call" | custom-call | tf_op jit(solution)/shard_map/pallas_call | solution.py:248
  227.2 15.1 %shard_map.221 = (bf16[512,1408]{1,0:T(8,128)(2,1)S(1)}, bf16[512,1408]{1,0:T(8,128)(2,1)S(1)}, bf16[512,1408]{1,0:T(8,128)(2,1)S(1)}) custom-call(bf16[512,2048]{1,0:T(8,128)(2,1)} %copy-done.17, bf16[512,2048]{1,0:T(8,128)(2,1)} %copy-done.16, bf16[2048,1408]{1,0:T(8,128)(2,1)} %copy-done.10, bf16[2048,1408]{1,0:T(8,128)(2,1)} %copy-done.9, ...), custom_call_target="tpu_custom_call" | custom-call | tf_op jit(solution)/shard_map/pallas_call | solution.py:193
  242.3 7.1 %shard_map.222 = f32[256,2048]{1,0:T(8,128)S(1)} custom-call(bf16[2048,1408]{1,0:T(8,128)(2,1)} %copy-done.10, bf16[2048,1408]{1,0:T(8,128)(2,1)} %copy-done.9, bf16[512,1408]{1,0:T(8,128)(2,1)S(1)} %get-tuple-element.371.refs_2_.refs_3_, bf16[512,1408]{1,0:T(8,128)(2,1)S(1)} %get-tuple-element.373.refs_3_.refs_5_), custom_call_target="tpu_custom_call" | custom-call | tf_op jit(solution)/shard_map/pallas_call | solution.py:248
  249.4 7.0 %shard_map.223 = bf16[1408,1024]{1,0:T(8,128)(2,1)} custom-call(bf16[512,1408]{1,0:T(8,128)(2,1)S(1)} %get-tuple-element.378.refs_0_.refs_1_, bf16[512,1408]{1,0:T(8,128)(2,1)S(1)} %get-tuple-element.384.refs_1_, bf16[512,2048]{1,0:T(8,128)(2,1)S(1)} %copy-done.1, bf16[512,2048]{1,0:T(8,128)(2,1)} %copy-done.16), custom_call_target="tpu_custom_call" | custom-call | tf_op jit(solution)/shard_map/pallas_call | solution.py:291
  260.1 10.1 %shard_map.224 = (f32[256,2048]{1,0:T(8,128)}, f32[256,2048]{1,0:T(8,128)}) custom-call(bf16[2048,1408]{1,0:T(8,128)(2,1)} %copy-done.10, bf16[2048,1408]{1,0:T(8,128)(2,1)} %copy-done.9, bf16[512,1408]{1,0:T(8,128)(2,1)S(1)} %get-tuple-element.371.refs_2_.refs_3_, bf16[512,1408]{1,0:T(8,128)(2,1)S(1)} %get-tuple-element.373.refs_3_.refs_5_, ...), custom_call_target="tpu_custom_call" | custom-call | tf_op jit(solution)/shard_map/pallas_call | solution.py:248
  270.2 9.3 %shard_map.226 = (bf16[1024,1408]{1,0:T(8,128)(2,1)}, bf16[1024,1408]{1,0:T(8,128)(2,1)}) custom-call(bf16[512,2048]{1,0:T(8,128)(2,1)} %copy-done.24, bf16[512,2048]{1,0:T(8,128)(2,1)} %copy-done.17, bf16[512,1408]{1,0:T(8,128)(2,1)S(1)} %get-tuple-element.370.refs_2_.refs_4_, bf16[512,1408]{1,0:T(8,128)(2,1)S(1)} %get-tuple-element.371.refs_2_.refs_3_, ...), custom_call_target="tpu_custom_call" | custom-call | tf_op jit(solution)/shard_map/pallas_call | solution.py:291
  281.1 7.7 %shard_map.225 = bf16[1408,1024]{1,0:T(8,128)(2,1)} custom-call(bf16[512,1408]{1,0:T(8,128)(2,1)S(1)} %get-tuple-element.378.refs_0_.refs_1_, bf16[512,1408]{1,0:T(8,128)(2,1)S(1)} %get-tuple-element.384.refs_1_, bf16[512,2048]{1,0:T(8,128)(2,1)S(1)} %copy-done.1, bf16[512,2048]{1,0:T(8,128)(2,1)} %copy-done.16, bf16[1408,1024]{1,0:T(8,128)(2,1)} %copy-done.38), custom_call_target="tpu_custom_call" | custom-call | tf_op jit(solution)/shard_map/pallas_call | solution.py:291
  288.8 3.2 add_convert_fusion.5
  292.6 3.6 collective-permute-start.35
  297.6 5.8 %shard_map.228 = bf16[512,2048]{1,0:T(8,128)(2,1)S(1)} custom-call(bf16[1408,2048]{1,0:T(8,128)(2,1)} %slice_dynamic-update-slice_fusion.8.d_ref.refs_0_, bf16[512,1408]{1,0:T(8,128)(2,1)S(1)} %get-tuple-element.378.refs_0_.refs_1_), custom_call_target="tpu_custom_call" | custom-call | tf_op jit(solution)/shard_map/pallas_call | solution.py:248
  305.0 9.8 %shard_map.227 = (bf16[1024,1408]{1,0:T(8,128)(2,1)}, bf16[1024,1408]{1,0:T(8,128)(2,1)}) custom-call(bf16[512,2048]{1,0:T(8,128)(2,1)} %copy-done.24, bf16[512,2048]{1,0:T(8,128)(2,1)} %copy-done.17, bf16[512,1408]{1,0:T(8,128)(2,1)S(1)} %get-tuple-element.370.refs_2_.refs_4_, bf16[512,1408]{1,0:T(8,128)(2,1)S(1)} %get-tuple-element.371.refs_2_.refs_3_, ...), custom_call_target="tpu_custom_call" | custom-call | tf_op jit(solution)/shard_map/pallas_call | solution.py:291
  314.8 4.4 broadcast_select_fusion.7
  328.5 3.4 multiply_convert_fusion
  331.9 3.5 shard_map.230
  335.5 5.6 %shard_map.229.back_ref = bf16[256,2048]{1,0:T(8,128)(2,1)S(1)} custom-call(bf16[2048,2048]{1,0:T(8,128)(2,1)} %copy-done.11, bf16[256,2048]{1,0:T(8,128)(2,1)S(1)} %get-tuple-element.391.refs_1_), custom_call_target="tpu_custom_call" | custom-call | tf_op jit(solution)/shard_map/pallas_call | solution.py:248
  341.1 5.9 %shard_map.231 = bf16[512,2048]{1,0:T(8,128)(2,1)S(1)} custom-call(bf16[1408,2048]{1,0:T(8,128)(2,1)} %slice_dynamic-update-slice_fusion.8.d_ref.refs_0_, bf16[512,1408]{1,0:T(8,128)(2,1)S(1)} %get-tuple-element.384.refs_1_), custom_call_target="tpu_custom_call" | custom-call | tf_op jit(solution)/shard_map/pallas_call | solution.py:248
  347.2 3.9 collective-permute-done.41
  358.3 13.4 %shard_map.232 = (bf16[256,2048]{1,0:T(8,128)(2,1)S(1)}, f32[768,256]{1,0:T(8,128)S(1)}, f32[768,256]{1,0:T(8,128)S(1)}) custom-call(bf16[256,2048]{1,0:T(8,128)(2,1)S(1)} %copy-done.8, bf16[768,512]{1,0:T(8,128)(2,1)S(1)} %constant_dynamic-update-slice_fusion.3.k_ref.v_ref, bf16[768,512]{1,0:T(8,128)(2,1)S(1)} %constant_dynamic-update-slice_fusion.3.k_ref.v_ref, ...), custom_call_target="tpu_custom_call" | custom-call | tf_op jit(solution)/shard_map/pallas_call | solution.py:128
  371.7 5.6 %shard_map.233 = bf16[2048,1024]{1,0:T(8,128)(2,1)} custom-call(bf16[256,2048]{1,0:T(8,128)(2,1)S(1)} %copy-done.6, bf16[256,2048]{1,0:T(8,128)(2,1)S(1)} %get-tuple-element.391.refs_1_, bf16[2048,1024]{1,0:T(8,128)(2,1)} %collective-permute-done.42.refs_2_), custom_call_target="tpu_custom_call" | custom-call | tf_op jit(solution)/shard_map/pallas_call | solution.py:291
  383.9 3.2 collective-permute-start.46
  389.4 3.5 shard_map.234
  393.9 4.4 collective-permute-done.47
  398.4 3.3 collective-permute-done.48
  407.8 3.4 collective-permute-start.55
  416.2 6.1 %shard_map.237 = f32[256,2048]{1,0:T(8,128)S(1)} custom-call(bf16[2048,2048]{1,0:T(8,128)(2,1)} %copy-done.12, bf16[2048,512]{1,0:T(8,128)(2,1)S(1)} %copy-done.4, bf16[256,2048]{1,0:T(8,128)(2,1)S(1)} %get-tuple-element.400.refs_1_.refs_2_, bf16[256,512]{1,0:T(8,128)(2,1)S(1)} %pad_maximum_fusion.18.refs_1_.refs_3_), custom_call_target="tpu_custom_call" | custom-call | tf_op jit(solution)/shard_map/pallas_call | solution.py:248
  425.3 5.7 %shard_map.238 = bf16[1024,2048]{1,0:T(8,128)(2,1)} custom-call(bf16[256,2048]{1,0:T(8,128)(2,1)S(1)} %fusion.2.refs_0_, bf16[256,2048]{1,0:T(8,128)(2,1)S(1)} %get-tuple-element.400.refs_1_.refs_2_, bf16[1024,2048]{1,0:T(8,128)(2,1)} %copy-done.31), custom_call_target="tpu_custom_call" | custom-call | tf_op jit(solution)/shard_map/pallas_call | solution.py:291
  431.1 5.7 %collective-permute-done.55 = bf16[256,2048]{1,0:T(8,128)(2,1)} collective-permute-done((bf16[256,2048]{1,0:T(8,128)(2,1)S(1)}, bf16[256,2048]{1,0:T(8,128)(2,1)}, u32[]{:S(2)}, u32[]{:S(2)}) %collective-permute-start.55) | collective-permute-done | bytes 1048608 | tf_op jit(solution)/shard_map/ppermute | solution.py:418
  443.6 4.5 collective-permute-done.57
  451.7 3.1 collective-permute-start.59
  457.5 18.3 %collective-permute-done.63 = f32[2,2048]{1,0:T(2,128)S(1)} collective-permute-done((f32[2,2048]{1,0:T(2,128)S(1)}, f32[2,2048]{1,0:T(2,128)S(1)}, u32[]{:S(2)}, u32[]{:S(2)}) %collective-permute-start.63) | collective-permute-done | bytes 16416 | tf_op jit(solution)/shard_map/ppermute | solution.py:426
  495.8 10.9 %collective-permute-done.68 = bf16[512,256]{1,0:T(8,128)(2,1)S(1)} collective-permute-done((bf16[512,256]{1,0:T(8,128)(2,1)S(1)}, bf16[512,256]{1,0:T(8,128)(2,1)S(1)}, u32[]{:S(2)}, u32[]{:S(2)}) %collective-permute-start.68) | collective-permute-done | bytes 262176 | tf_op jit(solution)/shard_map/ppermute | solution.py:426
  519.9 15.1 %collective-permute-done.72 = bf16[256,512]{1,0:T(8,128)(2,1)S(1)} collective-permute-done((bf16[256,512]{1,0:T(8,128)(2,1)S(1)}, bf16[256,512]{1,0:T(8,128)(2,1)S(1)}, u32[]{:S(2)}, u32[]{:S(2)}) %collective-permute-start.72) | collective-permute-done | bytes 262176 | tf_op jit(solution)/shard_map/ppermute | solution.py:426
  (519 shorter events, 203.5 us)
Async XLA Ops:
  1.7 21.6 %collective-permute-start.2 = (bf16[256,512]{1,0:T(8,128)(2,1)S(1)}, bf16[256,512]{1,0:T(8,128)(2,1)}, u32[]{:S(2)}, u32[]{:S(2)}) collective-permute-start(bf16[256,512]{1,0:T(8,128)(2,1)S(1)} %slice_select_fusion), channel_id=1, source_target_pairs={{0,1},{1,0},{2,3},{3,2},{4,5},{5,4},{6,7},{7,6},{8,9},{9,8},{10,11... | collective-permute-start | bytes 786440 | tf_op jit(solution)/shard_map/ppermute | solution.py:426
  1.9 22.7 %collective-permute-start.3 = (bf16[256,512]{1,0:T(8,128)(2,1)S(1)}, bf16[256,512]{1,0:T(8,128)(2,1)}, u32[]{:S(2)}, u32[]{:S(2)}) collective-permute-start(bf16[256,512]{1,0:T(8,128)(2,1)S(1)} %slice_select_fusion), channel_id=1, source_target_pairs={{0,2},{1,3},{2,0},{3,1},{4,6},{5,7},{6,4},{7,5},{8,10},{9,11},{10,... | collective-permute-start | bytes 786440 | tf_op jit(solution)/shard_map/ppermute | solution.py:426
  4.3 22.6 %collective-permute-start.4 = (bf16[256,512]{1,0:T(8,128)(2,1)S(1)}, bf16[256,512]{1,0:T(8,128)(2,1)}, u32[]{:S(2)}, u32[]{:S(2)}) collective-permute-start(bf16[256,512]{1,0:T(8,128)(2,1)S(1)} %slice_select_fusion), channel_id=1, source_target_pairs={{0,3},{1,2},{2,1},{3,0},{4,7},{5,6},{6,5},{7,4},{8,11},{9,10},{10,... | collective-permute-start | bytes 786440 | tf_op jit(solution)/shard_map/ppermute | solution.py:426
  13.7 17.4 %collective-permute-start.7 = (bf16[256,512]{1,0:T(8,128)(2,1)}, bf16[256,512]{1,0:T(8,128)(2,1)S(1)}, u32[]{:S(2)}, u32[]{:S(2)}) collective-permute-start(bf16[256,512]{1,0:T(8,128)(2,1)} %collective-permute-done), channel_id=1, source_target_pairs={{0,16},{16,0},{1,17},{17,1},{2,18},{18,2},{3,19},{19,3},{4,20},{20... | collective-permute-start | bytes 786440 | tf_op jit(solution)/shard_map/ppermute | solution.py:415
  28.3 20.3 %collective-permute-start.5 = (bf16[256,2048]{1,0:T(8,128)(2,1)S(1)}, bf16[256,2048]{1,0:T(8,128)(2,1)S(1)}, u32[]{:S(2)}, u32[]{:S(2)}) collective-permute-start(bf16[256,2048]{1,0:T(8,128)(2,1)S(1)} %get-tuple-element.618), channel_id=1, source_target_pairs={{0,4},{4,0},{8,12},{12,8},{16,24},{20,28},{24,16},{28,20},{1,5},{5... | collective-permute-start | bytes 3145736 | tf_op jit(solution)/shard_map/ppermute | solution.py:410
  29.6 19.0 %collective-permute-start.6 = (bf16[256,2048]{1,0:T(8,128)(2,1)S(1)}, bf16[256,2048]{1,0:T(8,128)(2,1)S(1)}, u32[]{:S(2)}, u32[]{:S(2)}) collective-permute-start(bf16[256,2048]{1,0:T(8,128)(2,1)S(1)} %get-tuple-element.618), channel_id=1, source_target_pairs={{0,16},{16,0},{1,17},{17,1},{2,18},{18,2},{3,19},{19,3},{4,20},{20... | collective-permute-start | bytes 3145736 | tf_op jit(solution)/shard_map/ppermute | solution.py:415
  31.2 24.3 %collective-permute-start.15 = (bf16[256,2048]{1,0:T(8,128)(2,1)S(1)}, bf16[256,2048]{1,0:T(8,128)(2,1)S(1)}, u32[]{:S(2)}, u32[]{:S(2)}) collective-permute-start(bf16[256,2048]{1,0:T(8,128)(2,1)S(1)} %multiply_convert_fusion.2), channel_id=1, source_target_pairs={{0,1},{1,2},{2,3},{3,0},{4,5},{5,6},{6,7},{7,4},{8,9},{9,10},{10,1... | collective-permute-start | bytes 3145736 | tf_op jit(solution)/shard_map/ppermute | solution.py:418
  48.9 27.4 %collective-permute-start.11 = (bf16[256,2048]{1,0:T(8,128)(2,1)S(1)}, bf16[256,2048]{1,0:T(8,128)(2,1)S(1)}, u32[]{:S(2)}, u32[]{:S(2)}) collective-permute-start(bf16[256,2048]{1,0:T(8,128)(2,1)S(1)} %collective-permute-done.5), channel_id=1, source_target_pairs={{0,16},{16,0},{1,17},{17,1},{2,18},{18,2},{3,19},{19,3},{4,20},{20... | collective-permute-start | bytes 3145736 | tf_op jit(solution)/shard_map/ppermute | solution.py:415
  51.1 25.3 %collective-permute-start.10 = (bf16[512,2048]{1,0:T(8,128)(2,1)S(1)}, bf16[512,2048]{1,0:T(8,128)(2,1)S(1)}, u32[]{:S(2)}, u32[]{:S(2)}) collective-permute-start(bf16[512,2048]{1,0:T(8,128)(2,1)S(1)} %pad_maximum_fusion.1), channel_id=1, source_target_pairs={{0,8},{4,12},{8,0},{12,4},{16,20},{20,16},{24,28},{28,24},{1,9},{5... | collective-permute-start | bytes 6291464 | tf_op jit(solution)/shard_map/ppermute | solution.py:410
  55.5 15.1 %collective-permute-start.16 = (bf16[256,512]{1,0:T(8,128)(2,1)S(1)}, bf16[256,512]{1,0:T(8,128)(2,1)S(1)}, u32[]{:S(2)}, u32[]{:S(2)}) collective-permute-start(bf16[256,512]{1,0:T(8,128)(2,1)S(1)} %pad_maximum_fusion.17), channel_id=1, source_target_pairs={{0,2},{1,3},{4,6},{5,7},{8,10},{9,11},{12,14},{13,15},{16,18},{17,... | collective-permute-start | bytes 786440 | tf_op jit(solution)/shard_map/ppermute | solution.py:421
  59.3 17.0 %collective-permute-start.17 = (bf16[256,512]{1,0:T(8,128)(2,1)S(1)}, bf16[256,512]{1,0:T(8,128)(2,1)S(1)}, u32[]{:S(2)}, u32[]{:S(2)}) collective-permute-start(bf16[256,512]{1,0:T(8,128)(2,1)S(1)} %pad_maximum_fusion.17), channel_id=1, source_target_pairs={{0,1},{1,2},{2,3},{4,5},{5,6},{6,7},{8,9},{9,10},{10,11},{12,13},{... | collective-permute-start | bytes 786440 | tf_op jit(solution)/shard_map/ppermute | solution.py:421
  61.2 37.5 %collective-permute-start.19 = (bf16[256,2048]{1,0:T(8,128)(2,1)S(1)}, bf16[256,2048]{1,0:T(8,128)(2,1)}, u32[]{:S(2)}, u32[]{:S(2)}) collective-permute-start(bf16[256,2048]{1,0:T(8,128)(2,1)S(1)} %collective-permute-done.15), channel_id=1, source_target_pairs={{0,1},{1,2},{2,3},{3,0},{4,5},{5,6},{6,7},{7,4},{8,9},{9,10},{10,1... | collective-permute-start | bytes 3145736 | tf_op jit(solution)/shard_map/ppermute | solution.py:418
  76.4 25.2 %collective-permute-start.18 = (bf16[2048,256]{1,0:T(8,128)(2,1)S(1)}, bf16[2048,256]{1,0:T(8,128)(2,1)S(1)}, u32[]{:S(2)}, u32[]{:S(2)}) collective-permute-start(bf16[2048,256]{1,0:T(8,128)(2,1)S(1)} %collective-permute-done.9), channel_id=1, source_target_pairs={{0,16},{16,0},{1,17},{17,1},{2,18},{18,2},{3,19},{19,3},{4,20},{20... | collective-permute-start | bytes 3145736 | tf_op jit(solution)/shard_map/ppermute | solution.py:415
  79.2 40.9 %collective-permute-start.12 = (bf16[4096,256]{1,0:T(8,128)(2,1)}, bf16[4096,256]{1,0:T(8,128)(2,1)}, u32[]{:S(2)}, u32[]{:S(2)}) collective-permute-start(bf16[4096,256]{1,0:T(8,128)(2,1)} %pad_maximum_fusion.2), channel_id=1, source_target_pairs={{0,8},{4,12},{8,0},{12,4},{16,20},{20,16},{24,28},{28,24},{1,9},{5... | collective-permute-start | bytes 6291464 | tf_op jit(solution)/shard_map/ppermute | solution.py:410
  82.0 33.8 %collective-permute-start.13 = (bf16[512,1408]{1,0:T(8,128)(2,1)S(1)}, bf16[512,1408]{1,0:T(8,128)(2,1)S(1)}, u32[]{:S(2)}, u32[]{:S(2)}) collective-permute-start(bf16[512,1408]{1,0:T(8,128)(2,1)S(1)} %pad_maximum_fusion.4), channel_id=1, source_target_pairs={{0,4},{4,0},{8,12},{12,8},{16,24},{20,28},{24,16},{28,20},{1,5},{5... | collective-permute-start | bytes 4325384 | tf_op jit(solution)/shard_map/ppermute | solution.py:410
  98.7 24.5 %collective-permute-start.20 = (bf16[256,2048]{1,0:T(8,128)(2,1)}, bf16[256,2048]{1,0:T(8,128)(2,1)S(1)}, u32[]{:S(2)}, u32[]{:S(2)}) collective-permute-start(bf16[256,2048]{1,0:T(8,128)(2,1)} %collective-permute-done.19), channel_id=1, source_target_pairs={{0,1},{1,2},{2,3},{3,0},{4,5},{5,6},{6,7},{7,4},{8,9},{9,10},{10,1... | collective-permute-start | bytes 3145736 | tf_op jit(solution)/shard_map/ppermute | solution.py:418
  125.2 41.5 %collective-permute-start.23 = (bf16[1024,1408]{1,0:T(8,128)(2,1)S(1)}, bf16[1024,1408]{1,0:T(8,128)(2,1)}, u32[]{:S(2)}, u32[]{:S(2)}) collective-permute-start(bf16[1024,1408]{1,0:T(8,128)(2,1)S(1)} %pad_maximum_fusion), channel_id=1, source_target_pairs={{0,8},{4,12},{8,0},{12,4},{16,20},{20,16},{24,28},{28,24},{1,9},{5... | collective-permute-start | bytes 8650760 | tf_op jit(solution)/shard_map/ppermute | solution.py:410
  126.5 18.3 %collective-permute-start.24 = (bf16[1408,256]{1,0:T(8,128)(2,1)S(1)}, bf16[1408,256]{1,0:T(8,128)(2,1)S(1)}, u32[]{:S(2)}, u32[]{:S(2)}) collective-permute-start(bf16[1408,256]{1,0:T(8,128)(2,1)S(1)} %get-tuple-element.307), channel_id=1, source_target_pairs={{0,4},{4,0},{8,12},{12,8},{16,24},{20,28},{24,16},{28,20},{1,5},{5... | collective-permute-start | bytes 2162696 | tf_op jit(solution)/shard_map/ppermute | solution.py:410
  136.2 30.6 %collective-permute-start.25 = (bf16[256,2048]{1,0:T(8,128)(2,1)S(1)}, bf16[256,2048]{1,0:T(8,128)(2,1)S(1)}, u32[]{:S(2)}, u32[]{:S(2)}) collective-permute-start(bf16[256,2048]{1,0:T(8,128)(2,1)S(1)} %multiply_convert_fusion.1), channel_id=1, source_target_pairs={{0,1},{1,2},{2,3},{3,0},{4,5},{5,6},{6,7},{7,4},{8,9},{9,10},{10,1... | collective-permute-start | bytes 3145736 | tf_op jit(solution)/shard_map/ppermute | solution.py:418
  168.3 25.3 %collective-permute-start.27 = (bf16[2816,256]{1,0:T(8,128)(2,1)S(1)}, bf16[2816,256]{1,0:T(8,128)(2,1)S(1)}, u32[]{:S(2)}, u32[]{:S(2)}) collective-permute-start(bf16[2816,256]{1,0:T(8,128)(2,1)S(1)} %pad_maximum_fusion.5), channel_id=1, source_target_pairs={{0,8},{4,12},{8,0},{12,4},{16,20},{20,16},{24,28},{28,24},{1,9},{5... | collective-permute-start | bytes 4325384 | tf_op jit(solution)/shard_map/ppermute | solution.py:410
  168.8 24.8 %collective-permute-start.29 = (bf16[256,2048]{1,0:T(8,128)(2,1)S(1)}, bf16[256,2048]{1,0:T(8,128)(2,1)}, u32[]{:S(2)}, u32[]{:S(2)}) collective-permute-start(bf16[256,2048]{1,0:T(8,128)(2,1)S(1)} %collective-permute-done.25), channel_id=1, source_target_pairs={{0,1},{1,2},{2,3},{3,0},{4,5},{5,6},{6,7},{7,4},{8,9},{9,10},{10,1... | collective-permute-start | bytes 3145736 | tf_op jit(solution)/shard_map/ppermute | solution.py:418
  195.0 25.2 %collective-permute-start.31 = (bf16[256,2048]{1,0:T(8,128)(2,1)}, bf16[256,2048]{1,0:T(8,128)(2,1)S(1)}, u32[]{:S(2)}, u32[]{:S(2)}) collective-permute-start(bf16[256,2048]{1,0:T(8,128)(2,1)} %collective-permute-done.29), channel_id=1, source_target_pairs={{0,1},{1,2},{2,3},{3,0},{4,5},{5,6},{6,7},{7,4},{8,9},{9,10},{10,1... | collective-permute-start | bytes 3145736 | tf_op jit(solution)/shard_map/ppermute | solution.py:418
  220.3 36.1 %collective-permute-start.32 = (bf16[256,2048]{1,0:T(8,128)(2,1)S(1)}, bf16[256,2048]{1,0:T(8,128)(2,1)}, u32[]{:S(2)}, u32[]{:S(2)}) collective-permute-start(bf16[256,2048]{1,0:T(8,128)(2,1)S(1)} %shard_map.220), channel_id=1, source_target_pairs={{0,1},{1,2},{2,3},{3,0},{4,5},{5,6},{6,7},{7,4},{8,9},{9,10},{10,1... | collective-permute-start | bytes 3145736 | tf_op jit(solution)/shard_map/ppermute | solution.py:418
  258.9 20.7 %collective-permute-start.34 = (bf16[1408,1024]{1,0:T(8,128)(2,1)}, bf16[1408,1024]{1,0:T(8,128)(2,1)S(1)}, u32[]{:S(2)}, u32[]{:S(2)}) collective-permute-start(bf16[1408,1024]{1,0:T(8,128)(2,1)} %shard_map.223), channel_id=1, source_target_pairs={{0,16},{16,0},{1,17},{17,1},{2,18},{18,2},{3,19},{19,3},{4,20},{20... | collective-permute-start | bytes 8650760 | tf_op jit(solution)/shard_map/ppermute | solution.py:415
  259.9 28.9 %collective-permute-start.33 = (bf16[256,2048]{1,0:T(8,128)(2,1)}, bf16[256,2048]{1,0:T(8,128)(2,1)}, u32[]{:S(2)}, u32[]{:S(2)}) collective-permute-start(bf16[256,2048]{1,0:T(8,128)(2,1)} %add_convert_fusion.6), channel_id=1, source_target_pairs={{0,1},{1,2},{2,3},{3,0},{4,5},{5,6},{6,7},{7,4},{8,9},{9,10},{10,1... | collective-permute-start | bytes 3145736 | tf_op jit(solution)/shard_map/ppermute | solution.py:418
  292.6 29.1 %collective-permute-start.35 = (bf16[256,2048]{1,0:T(8,128)(2,1)}, bf16[256,2048]{1,0:T(8,128)(2,1)}, u32[]{:S(2)}, u32[]{:S(2)}) collective-permute-start(bf16[256,2048]{1,0:T(8,128)(2,1)} %add_convert_fusion.5), channel_id=1, source_target_pairs={{0,1},{1,2},{2,3},{3,0},{4,5},{5,6},{6,7},{7,4},{8,9},{9,10},{10,1... | collective-permute-start | bytes 3145736 | tf_op jit(solution)/shard_map/ppermute | solution.py:418
  297.5 24.2 %collective-permute-start.36 = (bf16[1408,512]{1,0:T(8,128)(2,1)}, bf16[1408,512]{1,0:T(8,128)(2,1)}, u32[]{:S(2)}, u32[]{:S(2)}) collective-permute-start(bf16[1408,512]{1,0:T(8,128)(2,1)} %pad_maximum_fusion.6), channel_id=1, source_target_pairs={{0,4},{4,0},{8,12},{12,8},{16,24},{20,28},{24,16},{28,20},{1,5},{5... | collective-permute-start | bytes 4325384 | tf_op jit(solution)/shard_map/ppermute | solution.py:410
  324.1 23.1 %collective-permute-start.39 = (bf16[1408,256]{1,0:T(8,128)(2,1)}, bf16[1408,256]{1,0:T(8,128)(2,1)}, u32[]{:S(2)}, u32[]{:S(2)}) collective-permute-start(bf16[1408,256]{1,0:T(8,128)(2,1)} %add_convert_fusion.9), channel_id=1, source_target_pairs={{0,8},{4,12},{8,0},{12,4},{16,20},{20,16},{24,28},{28,24},{1,9},{5... | collective-permute-start | bytes 2162696 | tf_op jit(solution)/shard_map/ppermute | solution.py:410
  325.1 26.2 %collective-permute-start.40 = (bf16[512,1408]{1,0:T(8,128)(2,1)}, bf16[512,1408]{1,0:T(8,128)(2,1)}, u32[]{:S(2)}, u32[]{:S(2)}) collective-permute-start(bf16[512,1408]{1,0:T(8,128)(2,1)} %pad_maximum_fusion.7), channel_id=1, source_target_pairs={{0,4},{4,0},{8,12},{12,8},{16,24},{20,28},{24,16},{28,20},{1,5},{5... | collective-permute-start | bytes 4325384 | tf_op jit(solution)/shard_map/ppermute | solution.py:410
  326.5 24.6 %collective-permute-start.41 = (bf16[256,2048]{1,0:T(8,128)(2,1)}, bf16[256,2048]{1,0:T(8,128)(2,1)}, u32[]{:S(2)}, u32[]{:S(2)}) collective-permute-start(bf16[256,2048]{1,0:T(8,128)(2,1)} %get-tuple-element.385), channel_id=1, source_target_pairs={{0,1},{1,2},{2,3},{3,0},{4,5},{5,6},{6,7},{7,4},{8,9},{9,10},{10,1... | collective-permute-start | bytes 3145736 | tf_op jit(solution)/shard_map/ppermute | solution.py:418
  351.3 20.4 %collective-permute-start.42 = (bf16[2048,1024]{1,0:T(8,128)(2,1)S(1)}, bf16[2048,1024]{1,0:T(8,128)(2,1)}, u32[]{:S(2)}, u32[]{:S(2)}) collective-permute-start(bf16[2048,1024]{1,0:T(8,128)(2,1)S(1)} %copy-done.30), channel_id=1, source_target_pairs={{0,16},{16,0},{1,17},{17,1},{2,18},{18,2},{3,19},{19,3},{4,20},{20... | collective-permute-start | bytes 12582920 | tf_op jit(solution)/shard_map/ppermute | solution.py:415
  352.5 27.3 %collective-permute-start.44 = (bf16[512,1408]{1,0:T(8,128)(2,1)}, bf16[512,1408]{1,0:T(8,128)(2,1)}, u32[]{:S(2)}, u32[]{:S(2)}) collective-permute-start(bf16[512,1408]{1,0:T(8,128)(2,1)} %pad_maximum_fusion.8), channel_id=1, source_target_pairs={{0,4},{4,0},{8,12},{12,8},{16,24},{20,28},{24,16},{28,20},{1,5},{5... | collective-permute-start | bytes 4325384 | tf_op jit(solution)/shard_map/ppermute | solution.py:410
  355.1 24.6 %collective-permute-start.45 = (bf16[256,2048]{1,0:T(8,128)(2,1)}, bf16[256,2048]{1,0:T(8,128)(2,1)}, u32[]{:S(2)}, u32[]{:S(2)}) collective-permute-start(bf16[256,2048]{1,0:T(8,128)(2,1)} %add_convert_fusion.4), channel_id=1, source_target_pairs={{0,1},{1,2},{2,3},{3,0},{4,5},{5,6},{6,7},{7,4},{8,9},{9,10},{10,1... | collective-permute-start | bytes 3145736 | tf_op jit(solution)/shard_map/ppermute | solution.py:418
  357.8 21.9 %collective-permute-start.43 = (bf16[256,1408]{1,0:T(8,128)(2,1)}, bf16[256,1408]{1,0:T(8,128)(2,1)}, u32[]{:S(2)}, u32[]{:S(2)}) collective-permute-start(bf16[256,1408]{1,0:T(8,128)(2,1)} %add_convert_fusion.8), channel_id=1, source_target_pairs={{0,8},{4,12},{8,0},{12,4},{16,20},{20,16},{24,28},{28,24},{1,9},{5... | collective-permute-start | bytes 2162696 | tf_op jit(solution)/shard_map/ppermute | solution.py:410
  379.8 22.6 %collective-permute-start.49 = (bf16[1024,512]{1,0:T(8,128)(2,1)S(1)}, bf16[1024,512]{1,0:T(8,128)(2,1)S(1)}, u32[]{:S(2)}, u32[]{:S(2)}) collective-permute-start(bf16[1024,512]{1,0:T(8,128)(2,1)S(1)} %pad_maximum_fusion.10), channel_id=1, source_target_pairs={{0,4},{4,0},{8,12},{12,8},{16,24},{20,28},{24,16},{28,20},{1,5},{5... | collective-permute-start | bytes 3145736 | tf_op jit(solution)/shard_map/ppermute | solution.py:410
  383.4 18.3 %collective-permute-start.48 = (bf16[256,1408]{1,0:T(8,128)(2,1)S(1)}, bf16[256,1408]{1,0:T(8,128)(2,1)S(1)}, u32[]{:S(2)}, u32[]{:S(2)}) collective-permute-start(bf16[256,1408]{1,0:T(8,128)(2,1)S(1)} %add_convert_fusion.7), channel_id=1, source_target_pairs={{0,8},{4,12},{8,0},{12,4},{16,20},{20,16},{24,28},{28,24},{1,9},{5... | collective-permute-start | bytes 2162696 | tf_op jit(solution)/shard_map/ppermute | solution.py:410
  407.8 29.0 %collective-permute-start.55 = (bf16[256,2048]{1,0:T(8,128)(2,1)S(1)}, bf16[256,2048]{1,0:T(8,128)(2,1)}, u32[]{:S(2)}, u32[]{:S(2)}) collective-permute-start(bf16[256,2048]{1,0:T(8,128)(2,1)S(1)} %add_convert_fusion.3), channel_id=1, source_target_pairs={{0,1},{1,2},{2,3},{3,0},{4,5},{5,6},{6,7},{7,4},{8,9},{9,10},{10,1... | collective-permute-start | bytes 3145736 | tf_op jit(solution)/shard_map/ppermute | solution.py:418
  414.1 22.8 %collective-permute-start.53 = (bf16[512,512]{1,0:T(8,128)(2,1)S(1)}, bf16[512,512]{1,0:T(8,128)(2,1)S(1)}, u32[]{:S(2)}, u32[]{:S(2)}) collective-permute-start(bf16[512,512]{1,0:T(8,128)(2,1)S(1)} %pad_maximum_fusion.15), channel_id=1, source_target_pairs={{0,4},{4,0},{8,12},{12,8},{16,24},{20,28},{24,16},{28,20},{1,5},{5... | collective-permute-start | bytes 1572872 | tf_op jit(solution)/shard_map/ppermute | solution.py:410
  415.5 21.3 %collective-permute-start.54 = (bf16[1024,512]{1,0:T(8,128)(2,1)}, bf16[1024,512]{1,0:T(8,128)(2,1)S(1)}, u32[]{:S(2)}, u32[]{:S(2)}) collective-permute-start(bf16[1024,512]{1,0:T(8,128)(2,1)} %pad_maximum_fusion.11), channel_id=1, source_target_pairs={{0,4},{4,0},{8,12},{12,8},{16,24},{20,28},{24,16},{28,20},{1,5},{5... | collective-permute-start | bytes 3145736 | tf_op jit(solution)/shard_map/ppermute | solution.py:410
  448.9 29.2 %collective-permute-start.62 = (bf16[512,2048]{1,0:T(8,128)(2,1)}, bf16[512,2048]{1,0:T(8,128)(2,1)}, u32[]{:S(2)}, u32[]{:S(2)}) collective-permute-start(bf16[512,2048]{1,0:T(8,128)(2,1)} %pad_maximum_fusion.3), channel_id=1, source_target_pairs={{0,4},{4,0},{8,12},{12,8},{16,24},{20,28},{24,16},{28,20},{1,5},{5... | collective-permute-start | bytes 6291464 | tf_op jit(solution)/shard_map/ppermute | solution.py:410
  451.7 24.1 %collective-permute-start.59 = (bf16[256,512]{1,0:T(8,128)(2,1)S(1)}, bf16[256,512]{1,0:T(8,128)(2,1)S(1)}, u32[]{:S(2)}, u32[]{:S(2)}) collective-permute-start(bf16[256,512]{1,0:T(8,128)(2,1)S(1)} %add_convert_fusion.15), channel_id=1, source_target_pairs={{0,1},{1,0},{2,3},{3,2},{4,5},{5,4},{6,7},{7,6},{8,9},{9,8},{10,11... | collective-permute-start | bytes 786440 | tf_op jit(solution)/shard_map/ppermute | solution.py:426
  454.8 21.0 %collective-permute-start.60 = (bf16[256,512]{1,0:T(8,128)(2,1)S(1)}, bf16[256,512]{1,0:T(8,128)(2,1)S(1)}, u32[]{:S(2)}, u32[]{:S(2)}) collective-permute-start(bf16[256,512]{1,0:T(8,128)(2,1)S(1)} %add_convert_fusion.15), channel_id=1, source_target_pairs={{0,2},{1,3},{2,0},{3,1},{4,6},{5,7},{6,4},{7,5},{8,10},{9,11},{10,... | collective-permute-start | bytes 786440 | tf_op jit(solution)/shard_map/ppermute | solution.py:426
  454.8 23.3 %collective-permute-start.61 = (bf16[256,512]{1,0:T(8,128)(2,1)S(1)}, bf16[256,512]{1,0:T(8,128)(2,1)S(1)}, u32[]{:S(2)}, u32[]{:S(2)}) collective-permute-start(bf16[256,512]{1,0:T(8,128)(2,1)S(1)} %add_convert_fusion.15), channel_id=1, source_target_pairs={{0,3},{1,2},{2,1},{3,0},{4,7},{5,6},{6,5},{7,4},{8,11},{9,10},{10,... | collective-permute-start | bytes 786440 | tf_op jit(solution)/shard_map/ppermute | solution.py:426
  456.1 19.7 %collective-permute-start.63 = (f32[2,2048]{1,0:T(2,128)S(1)}, f32[2,2048]{1,0:T(2,128)S(1)}, u32[]{:S(2)}, u32[]{:S(2)}) collective-permute-start(f32[2,2048]{1,0:T(2,128)S(1)} %add.420), channel_id=1, source_target_pairs={{0,2},{1,3},{2,0},{3,1},{4,6},{5,7},{6,4},{7,5},{8,10},{9,11},{10,... | collective-permute-start | bytes 49160 | tf_op jit(solution)/shard_map/ppermute | solution.py:426
  482.0 24.6 %collective-permute-start.65 = (bf16[256,2048]{1,0:T(8,128)(2,1)S(1)}, bf16[256,2048]{1,0:T(8,128)(2,1)S(1)}, u32[]{:S(2)}, u32[]{:S(2)}) collective-permute-start(bf16[256,2048]{1,0:T(8,128)(2,1)S(1)} %add_convert_fusion.2), channel_id=1, source_target_pairs={{0,8},{4,12},{8,0},{12,4},{16,20},{20,16},{24,28},{28,24},{1,9},{5... | collective-permute-start | bytes 3145736 | tf_op jit(solution)/shard_map/ppermute | solution.py:410
  483.6 23.0 %collective-permute-start.68 = (bf16[512,256]{1,0:T(8,128)(2,1)S(1)}, bf16[512,256]{1,0:T(8,128)(2,1)S(1)}, u32[]{:S(2)}, u32[]{:S(2)}) collective-permute-start(bf16[512,256]{1,0:T(8,128)(2,1)S(1)} %get-tuple-element.609), channel_id=1, source_target_pairs={{0,3},{1,2},{2,1},{3,0},{4,7},{5,6},{6,5},{7,4},{8,11},{9,10},{10,... | collective-permute-start | bytes 786440 | tf_op jit(solution)/shard_map/ppermute | solution.py:426
  506.7 28.3 %collective-permute-start.69 = (bf16[512,512]{1,0:T(8,128)(2,1)S(1)}, bf16[512,512]{1,0:T(8,128)(2,1)S(1)}, u32[]{:S(2)}, u32[]{:S(2)}) collective-permute-start(bf16[512,512]{1,0:T(8,128)(2,1)S(1)} %pad_maximum_fusion.16), channel_id=1, source_target_pairs={{0,8},{4,12},{8,0},{12,4},{16,20},{20,16},{24,28},{28,24},{1,9},{5... | collective-permute-start | bytes 1572872 | tf_op jit(solution)/shard_map/ppermute | solution.py:410
  510.5 24.5 %collective-permute-start.72 = (bf16[256,512]{1,0:T(8,128)(2,1)S(1)}, bf16[256,512]{1,0:T(8,128)(2,1)S(1)}, u32[]{:S(2)}, u32[]{:S(2)}) collective-permute-start(bf16[256,512]{1,0:T(8,128)(2,1)S(1)} %get-tuple-element.605), channel_id=1, source_target_pairs={{0,3},{1,2},{2,1},{3,0},{4,7},{5,6},{6,5},{7,4},{8,11},{9,10},{10,... | collective-permute-start | bytes 786440 | tf_op jit(solution)/shard_map/ppermute | solution.py:426
  (109 other events, 834.2 us)
